TPU v7x, 32 devices: a whole 2x2x4 slice. The times are simulated.
32 devices in a mesh: tm: 4 (over x, core), space: 8 (over z, y).
Axes of the slice: x: 2, y: 2, z: 4, core: 2. Of those that a mesh axis runs over, the one named last changes fastest.
Arguments:
- state: bfloat16 [24, 16, 8, 8, 128], P('tm', None, 'space'), may hold values from -6 to 6
- noise: bfloat16 [24, 16, 8, 8, 128], P('tm', None, 'space'), may hold values from -6 to 6
- conv_one: bfloat16 [64, 16, 3, 3, 3], replicated, may hold values from -0.3125 to 0.3125
- bias_one: float32 [64], replicated, may hold values from -3 to 3
- conv_two: bfloat16 [64, 64, 3, 3, 3], replicated, may hold values from -0.15625 to 0.15625
- bias_two: float32 [64], replicated, may hold values from -3 to 3
- conv_three: bfloat16 [16, 64, 3, 3, 3], replicated, may hold values from -0.15625 to 0.15625
- bias_three: float32 [16], replicated, may hold values from -3 to 3
- day_of_frame: int32 [24], P('tm'), may hold values from 0 to 1, never falling along the last dimension, each value on 1 to 23 neighbouring positions
- observed: float32 [2, 8, 8, 128], P(None, 'space'), may hold values from -18 to 18
- obs_mask: int32 [8, 8, 128], P('space'), may hold values 0 or 1
Outputs:
- updated: bfloat16 [24, 16, 8, 8, 128], P('tm', None, 'space')
Inputs may be any that keep to these rules, and one draw needn't show every extreme that they name: `day_of_frame`: frames of one observation period are consecutive and periods never go back; every period has 1 to 23 frames and one has exactly 23.
All inputs are finite; a program needn't handle non-finite values. No bound on the sum of `obs_mask` on one device may be relied on, other than what follows from the above.
Results may differ from a plain program's by a relative error of at most 0.0028.
Values may be sent and summed in bfloat16 or wider, within the bound.
No kernel may reach another device: no remote copies, remote signals or barrier semaphores. Data moves between devices by JAX's collectives and lax.ppermute only.
A program may use at most 64 MiB of HBM per device.

v0:
```python
import jax
import jax.numpy as jnp
from jax import lax
from jax.sharding import PartitionSpec as P


def passed_along(value, axis, steps):
    count = lax.axis_size(axis)
    leading, last = (max(0, -steps), min(count, count - steps))
    return lax.ppermute(value, axis, [(source, source + steps) for source in range(leading, last)])


def with_halo(block, sides, width):
    for axis, dim in sides:
        count = lax.axis_size(axis)
        forward = [(i, i + 1) for i in range(count - 1)]
        backward = [(target, source) for source, target in forward]
        low = lax.ppermute(
            lax.slice_in_dim(block, block.shape[dim] - width, None, axis=dim), axis, forward
        )
        high = lax.ppermute(lax.slice_in_dim(block, 0, width, axis=dim), axis, backward)
        block = jnp.concatenate([low, block, high], axis=dim)
    return block


def space_rim(field, margin):
    from_west = passed_along(field[..., -margin:], "space", 1)
    from_east = passed_along(field[..., :margin], "space", -1)
    widened = jnp.concatenate([from_west, field, from_east], axis=-1)
    pad_spec = [(0, 0)] * (widened.ndim - 2) + [(margin, margin), (0, 0)]
    return jnp.pad(widened, pad_spec)


def time_rim(field, margin):
    return with_halo(field, (("tm", 0),), margin)


def extend(field, margin):
    return space_rim(time_rim(field, margin), margin)


def conv_valid(field, kernel, bias):
    out = lax.conv_general_dilated(
        field[None],
        kernel,
        (1, 1, 1),
        "VALID",
        dimension_numbers=("NDCHW", "OIDHW", "NDCHW"),
        preferred_element_type=jnp.float32,
    )
    return out[0] + bias[None, :, None, None]


def body(
    state,
    noise,
    conv_one,
    bias_one,
    conv_two,
    bias_two,
    conv_three,
    bias_three,
    day_of_frame,
    observed,
    obs_mask,
):
    current = state[:, :, 0]
    frames, tile_rows, tile_cols = (current.shape[0], current.shape[2], current.shape[3])
    hidden_one = jax.nn.silu(conv_valid(extend(current, 1), conv_one, bias_one)).astype(
        jnp.bfloat16
    )
    hidden_two = jax.nn.silu(conv_valid(extend(hidden_one, 1), conv_two, bias_two)).astype(
        jnp.bfloat16
    )
    score = conv_valid(extend(hidden_two, 1), conv_three, bias_three)
    estimate = current[:, 0].astype(jnp.float32) + 0.5 * score[:, 0]
    flat_cells = estimate.reshape(frames, -1)
    day_count = observed.shape[0]
    obs_flat = observed[:, 0].reshape(day_count, -1)
    mask_flat = obs_mask[0].reshape(1, -1).astype(jnp.float32)
    onehot = (day_of_frame[:, None] == jnp.arange(day_count, dtype=jnp.int32)[None, :]).astype(
        jnp.float32
    )
    partial_tot = jnp.dot(onehot.T, flat_cells, precision=lax.Precision.HIGHEST)
    totals = lax.psum(partial_tot, "tm")
    misfit = mask_flat * (totals - obs_flat)
    per_frame = jnp.dot(onehot, misfit, precision=lax.Precision.HIGHEST)
    moved = current.astype(jnp.float32) + 0.8 * score + 0.5 * noise[:, :, 0].astype(jnp.float32)
    moved = moved.at[:, 0].add(-0.15 * per_frame.reshape(frames, tile_rows, tile_cols))
    return moved.astype(jnp.bfloat16)[:, :, None]


def solution(mesh):
    in_specs = (
        P("tm", None, "space", None, None),
        P("tm", None, "space", None, None),
        P(),
        P(),
        P(),
        P(),
        P(),
        P(),
        P("tm"),
        P(None, "space", None, None),
        P("space", None, None),
    )
    out_specs = P("tm", None, "space", None, None)
    return jax.shard_map(body, mesh=mesh, in_specs=in_specs, out_specs=out_specs, check_vma=False)
```

profile of v0, /device:TPU:0, one launch (start us, length us, event | category | flops | bytes accessed | tf_op | source)
XLA Modules:
  0.0 149.7 jit_solution(3385110747795471758)
XLA Ops:
  0.8 2.4 %collective-permute-start = (bf16[1,16,8,128]{3,1,2,0:T(8,128)(2,1)S(1)}, bf16[1,16,8,128]{3,1,2,0:T(8,128)(2,1)S(1)}, u32[]{:S(2)}, u32[]{:S(2)}) collective-permute-start(bf16[1,16,8,128]{3,1,2,0:T(8,128)(2,1)S(1)} %bitcast.107), channel_id=1, source_target_pairs={{0,8},{8,16},{16,24},{1,9},{9,17},{17,25},{2,10},{10,18},{18,26},{... | collective-permute-start | bytes 98312 | tf_op jit(solution)/shard_map/ppermute | solution.py:18
  3.2 1.3 collective-permute-start.1
  5.5 2.9 %collective-permute-done.1 = bf16[1,16,8,128]{3,1,2,0:T(8,128)(2,1)S(1)} collective-permute-done((bf16[1,16,8,128]{3,1,2,0:T(8,128)(2,1)S(1)}, bf16[1,16,8,128]{3,1,2,0:T(8,128)(2,1)S(1)}, u32[]{:S(2)}, u32[]{:S(2)}) %collective-permute-start.1) | collective-permute-done | bytes 32800 | tf_op jit(solution)/shard_map/ppermute | solution.py:21
  8.6 3.4 %collective-permute-start.2 = (bf16[8,16,8,1]{3,1,2,0:T(8,128)(2,1)S(1)}, bf16[8,16,8,1]{3,1,2,0:T(8,128)(2,1)S(1)}, u32[]{:S(2)}, u32[]{:S(2)}) collective-permute-start(bf16[8,16,8,1]{3,1,2,0:T(8,128)(2,1)S(1)} %get-tuple-element.27), channel_id=1, source_target_pairs={{0,1},{1,2},{2,3},{3,4},{4,5},{5,6},{6,7},{8,9},{9,10},{10,11},{11... | collective-permute-start | bytes 6152 | tf_op jit(solution)/shard_map/ppermute | solution.py:10
  12.1 1.3 collective-permute-start.3
  13.4 3.6 %collective-permute-done.2 = bf16[8,16,8,1]{3,1,2,0:T(8,128)(2,1)S(1)} collective-permute-done((bf16[8,16,8,1]{3,1,2,0:T(8,128)(2,1)S(1)}, bf16[8,16,8,1]{3,1,2,0:T(8,128)(2,1)S(1)}, u32[]{:S(2)}, u32[]{:S(2)}) %collective-permute-start.2) | collective-permute-done | bytes 2080 | tf_op jit(solution)/shard_map/ppermute | solution.py:10
  17.0 4.7 %collective-permute-done.3 = bf16[8,16,8,1]{3,1,2,0:T(8,128)(2,1)S(1)} collective-permute-done((bf16[8,16,8,1]{3,1,2,0:T(8,128)(2,1)S(1)}, bf16[8,16,8,1]{3,1,2,0:T(8,128)(2,1)S(1)}, u32[]{:S(2)}, u32[]{:S(2)}) %collective-permute-start.3) | collective-permute-done | bytes 2080 | tf_op jit(solution)/shard_map/ppermute | solution.py:10
  23.0 3.3 %reshape.72 = bf16[8,16,10,1,8,17]{5,4,1,2,0,3:T(8,128)(2,1)S(1)} reshape(bf16[8,16,10,1,136]{4,1,2,0,3:T(8,128)(2,1)} %pad.16) | data formatting | bytes 696320 | tf_op jit(solution)/shard_map/conv_general_dilated | solution.py:43
  26.4 5.3 %copy.20 = bf16[8,16,10,1,8,17]{1,4,5,2,0,3:T(8,128)(2,1)} copy(bf16[8,16,10,1,8,17]{5,4,1,2,0,3:T(8,128)(2,1)S(1)} %reshape.72) | data formatting | bytes 696320 | tf_op jit(solution)/shard_map/conv_general_dilated | solution.py:43
  31.7 1.1 slice.100
  32.8 6.0 %fusion.40 = f32[6,8,8,17,64]{4,2,3,1,0:T(8,128)S(1)} fusion(bf16[64,16,3,3,3]{0,1,4,3,2:T(8,128)(2,1)S(1)} %copy-done.7, bf16[8,16,10,1,7,2]{1,4,5,2,0,3:T(8,128)(2,1)S(1)} %slice.100, bf16[8,16,10,1,8,17]{1,4,5,2,0,3:T(8,128)(2,1)} %copy.20, pred[8,17]{0,1:T(8,128)(4,1)S(1)} %copy-done.11), kind=kOutput, calls=%fused_computation.49 | convolution fusion | flops 362557440 | bytes 2110600 | tf_op jit(solution)/shard_map/conv_general_dilated | solution.py:43
  40.3 4.7 %collective-permute-start.4 = (bf16[1,64,8,128]{1,2,3,0:T(8,128)(2,1)S(1)}, bf16[1,64,8,128]{1,2,3,0:T(8,128)(2,1)S(1)}, u32[]{:S(2)}, u32[]{:S(2)}) collective-permute-start(bf16[1,64,8,128]{1,2,3,0:T(8,128)(2,1)S(1)} %get-tuple-element.25), channel_id=1, source_target_pairs={{0,8},{8,16},{16,24},{1,9},{9,17},{17,25},{2,10},{10,18},{18,26},{... | collective-permute-start | bytes 393224 | tf_op jit(solution)/shard_map/ppermute | solution.py:18
  44.9 1.3 collective-permute-start.5
  46.3 2.1 %collective-permute-done.5 = bf16[1,64,8,128]{1,2,3,0:T(8,128)(2,1)S(1)} collective-permute-done((bf16[1,64,8,128]{1,2,3,0:T(8,128)(2,1)S(1)}, bf16[1,64,8,128]{1,2,3,0:T(8,128)(2,1)S(1)}, u32[]{:S(2)}, u32[]{:S(2)}) %collective-permute-start.5) | collective-permute-done | bytes 131104 | tf_op jit(solution)/shard_map/ppermute | solution.py:21
  48.4 4.1 %collective-permute-start.6 = (bf16[8,64,8,1]{1,2,3,0:T(8,128)(2,1)S(1)}, bf16[8,64,8,1]{1,2,3,0:T(8,128)(2,1)S(1)}, u32[]{:S(2)}, u32[]{:S(2)}) collective-permute-start(bf16[8,64,8,1]{1,2,3,0:T(8,128)(2,1)S(1)} %get-tuple-element.21), channel_id=1, source_target_pairs={{0,1},{1,2},{2,3},{3,4},{4,5},{5,6},{6,7},{8,9},{9,10},{10,11},{11... | collective-permute-start | bytes 24584 | tf_op jit(solution)/shard_map/ppermute | solution.py:10
  52.5 1.3 collective-permute-start.7
  53.9 4.8 %collective-permute-done.7 = bf16[8,64,8,1]{1,2,3,0:T(8,128)(2,1)S(1)} collective-permute-done((bf16[8,64,8,1]{1,2,3,0:T(8,128)(2,1)S(1)}, bf16[8,64,8,1]{1,2,3,0:T(8,128)(2,1)S(1)}, u32[]{:S(2)}, u32[]{:S(2)}) %collective-permute-start.7) | collective-permute-done | bytes 8224 | tf_op jit(solution)/shard_map/ppermute | solution.py:10
  58.7 4.1 %fusion.5 = bf16[8,64,10,1,130]{1,2,4,0,3:T(8,128)(2,1)S(1)} fusion(bf16[8,64,8,1]{1,2,3,0:T(8,128)(2,1)S(1)} %collective-permute-done.7, bf16[8,64,8,1]{1,2,3,0:T(8,128)(2,1)S(1)} %collective-permute-done.6, bf16[1,64,8,128]{1,2,3,0:T(8,128)(2,1)S(1)} %collective-permute-done.5, bf16[6,64,8,128]{1,2,3,0:T(8,128)(2,1)S(1)} %multiply_convert_fusion.1, ...), kind=kLoop, calls=%fused_computation.14 | loop fusion | flops 11980800 | bytes 2396160 | tf_op jit(solution)/shard_map/broadcast_in_dim | solution.py:44
  62.8 1.1 pad.18
  64.7 24.8 %fusion.34 = f32[6,8,8,17,64]{4,2,3,1,0:T(8,128)S(1)} fusion(bf16[64,64,3,3,3]{1,0,4,3,2:T(8,128)(2,1)S(1)} %copy-done, bf16[8,64,10,1,7,2]{1,4,5,2,0,3:T(8,128)(2,1)S(1)} %slice.104, bf16[8,64,10,1,8,17]{1,4,5,2,0,3:T(8,128)(2,1)S(1)} %copy.24, pred[8,17]{0,1:T(8,128)(4,1)S(1)} %copy-done.11), kind=kOutput, calls=%fused_computation.47 | convolution fusion | flops 1448976384 | bytes 3428488 | tf_op jit(solution)/shard_map/conv_general_dilated | solution.py:43
  91.1 5.0 %collective-permute-start.8 = (bf16[1,64,8,128]{1,2,3,0:T(8,128)(2,1)S(1)}, bf16[1,64,8,128]{1,2,3,0:T(8,128)(2,1)S(1)}, u32[]{:S(2)}, u32[]{:S(2)}) collective-permute-start(bf16[1,64,8,128]{1,2,3,0:T(8,128)(2,1)S(1)} %get-tuple-element.23), channel_id=1, source_target_pairs={{0,8},{8,16},{16,24},{1,9},{9,17},{17,25},{2,10},{10,18},{18,26},{... | collective-permute-start | bytes 393224 | tf_op jit(solution)/shard_map/ppermute | solution.py:18
  96.1 1.3 collective-permute-start.9
  97.4 2.6 %collective-permute-done.9 = bf16[1,64,8,128]{1,2,3,0:T(8,128)(2,1)S(1)} collective-permute-done((bf16[1,64,8,128]{1,2,3,0:T(8,128)(2,1)S(1)}, bf16[1,64,8,128]{1,2,3,0:T(8,128)(2,1)S(1)}, u32[]{:S(2)}, u32[]{:S(2)}) %collective-permute-start.9) | collective-permute-done | bytes 131104 | tf_op jit(solution)/shard_map/ppermute | solution.py:21
  100.0 4.8 %collective-permute-start.10 = (bf16[8,64,8,1]{1,2,3,0:T(8,128)(2,1)S(1)}, bf16[8,64,8,1]{1,2,3,0:T(8,128)(2,1)S(1)}, u32[]{:S(2)}, u32[]{:S(2)}) collective-permute-start(bf16[8,64,8,1]{1,2,3,0:T(8,128)(2,1)S(1)} %get-tuple-element.19), channel_id=1, source_target_pairs={{0,1},{1,2},{2,3},{3,4},{4,5},{5,6},{6,7},{8,9},{9,10},{10,11},{11... | collective-permute-start | bytes 24584 | tf_op jit(solution)/shard_map/ppermute | solution.py:10
  104.8 1.3 collective-permute-start.11
  106.3 4.2 %collective-permute-done.11 = bf16[8,64,8,1]{1,2,3,0:T(8,128)(2,1)S(1)} collective-permute-done((bf16[8,64,8,1]{1,2,3,0:T(8,128)(2,1)S(1)}, bf16[8,64,8,1]{1,2,3,0:T(8,128)(2,1)S(1)}, u32[]{:S(2)}, u32[]{:S(2)}) %collective-permute-start.11) | collective-permute-done | bytes 8224 | tf_op jit(solution)/shard_map/ppermute | solution.py:10
  110.5 3.9 %fusion.4 = bf16[8,64,10,1,130]{1,2,4,0,3:T(8,128)(2,1)S(1)} fusion(bf16[8,64,8,1]{1,2,3,0:T(8,128)(2,1)S(1)} %collective-permute-done.11, bf16[8,64,8,1]{1,2,3,0:T(8,128)(2,1)S(1)} %collective-permute-done.10, bf16[1,64,8,128]{1,2,3,0:T(8,128)(2,1)S(1)} %collective-permute-done.9, bf16[6,64,8,128]{1,2,3,0:T(8,128)(2,1)S(1)} %multiply_convert_fusion, ...), kind=kLoop, calls=%fused_computation.9 | loop fusion | flops 11980800 | bytes 2396160 | tf_op jit(solution)/shard_map/broadcast_in_dim | solution.py:44
  114.3 1.1 pad.20
  116.3 14.3 %fusion.37 = f32[6,8,8,17,16]{4,2,3,1,0:T(8,128)} fusion(bf16[16,64,3,3,3]{1,0,4,3,2:T(8,128)(2,1)S(1)} %copy-done.8, bf16[8,64,10,1,7,2]{1,4,5,2,0,3:T(8,128)(2,1)S(1)} %slice.108, bf16[8,64,10,1,8,17]{1,4,5,2,0,3:T(8,128)(2,1)S(1)} %copy.28, pred[8,17]{0,1:T(8,128)(4,1)S(1)} %copy-done.11), kind=kOutput, calls=%fused_computation.48 | convolution fusion | flops 365746176 | bytes 2009224 | tf_op jit(solution)/shard_map/conv_general_dilated | solution.py:43
  130.6 5.5 %copy.29 = f32[6,8,8,17,16]{3,2,4,1,0:T(8,128)} copy(f32[6,8,8,17,16]{4,2,3,1,0:T(8,128)} %fusion.37) | data formatting | bytes 835584 | tf_op jit(solution)/shard_map/conv_general_dilated | solution.py:43
  136.2 2.4 %reshape.90 = f32[6,8,1,136,16]{3,4,1,0,2:T(8,128)S(1)} reshape(f32[6,8,8,17,16]{3,2,4,1,0:T(8,128)} %copy.29) | data formatting | bytes 835584 | tf_op jit(solution)/shard_map/conv_general_dilated | solution.py:43
  139.1 9.1 %psum.7 = f32[2,1024]{1,0:T(2,128)S(1)} all-reduce(f32[2,1024]{1,0:T(2,128)S(1)} %fusion.55), channel_id=1, replica_groups=mesh['tm'=4,'space'=8] {'tm'}, use_global_device_ids=true, to_apply=%region_0.1 | all-reduce | flops 2048 | bytes 16384 | tf_op jit(solution)/shard_map/psum | solution.py:85
  (59 shorter events, 9.9 us)
Async XLA Ops:
  0.0 64.7 %copy-start = (bf16[64,64,3,3,3]{1,0,4,3,2:T(8,128)(2,1)S(1)}, bf16[64,64,3,3,3]{1,0,4,3,2:T(8,128)(2,1)}, u32[]{:S(2)}) copy-start(bf16[64,64,3,3,3]{1,0,4,3,2:T(8,128)(2,1)} %param.17) | copy-start | bytes 663556
  0.8 4.6 %collective-permute-start = (bf16[1,16,8,128]{3,1,2,0:T(8,128)(2,1)S(1)}, bf16[1,16,8,128]{3,1,2,0:T(8,128)(2,1)S(1)}, u32[]{:S(2)}, u32[]{:S(2)}) collective-permute-start(bf16[1,16,8,128]{3,1,2,0:T(8,128)(2,1)S(1)} %bitcast.107), channel_id=1, source_target_pairs={{0,8},{8,16},{16,24},{1,9},{9,17},{17,25},{2,10},{10,18},{18,26},{... | collective-permute-start | bytes 98312 | tf_op jit(solution)/shard_map/ppermute | solution.py:18
  3.2 5.2 %collective-permute-start.1 = (bf16[1,16,8,128]{3,1,2,0:T(8,128)(2,1)S(1)}, bf16[1,16,8,128]{3,1,2,0:T(8,128)(2,1)S(1)}, u32[]{:S(2)}, u32[]{:S(2)}) collective-permute-start(bf16[1,16,8,128]{3,1,2,0:T(8,128)(2,1)S(1)} %bitcast.108), channel_id=1, source_target_pairs={{8,0},{16,8},{24,16},{9,1},{17,9},{25,17},{10,2},{18,10},{26,18},{... | collective-permute-start | bytes 98312 | tf_op jit(solution)/shard_map/ppermute | solution.py:21
  8.6 8.4 %collective-permute-start.2 = (bf16[8,16,8,1]{3,1,2,0:T(8,128)(2,1)S(1)}, bf16[8,16,8,1]{3,1,2,0:T(8,128)(2,1)S(1)}, u32[]{:S(2)}, u32[]{:S(2)}) collective-permute-start(bf16[8,16,8,1]{3,1,2,0:T(8,128)(2,1)S(1)} %get-tuple-element.27), channel_id=1, source_target_pairs={{0,1},{1,2},{2,3},{3,4},{4,5},{5,6},{6,7},{8,9},{9,10},{10,11},{11... | collective-permute-start | bytes 6152 | tf_op jit(solution)/shard_map/ppermute | solution.py:10
  12.1 9.6 %collective-permute-start.3 = (bf16[8,16,8,1]{3,1,2,0:T(8,128)(2,1)S(1)}, bf16[8,16,8,1]{3,1,2,0:T(8,128)(2,1)S(1)}, u32[]{:S(2)}, u32[]{:S(2)}) collective-permute-start(bf16[8,16,8,1]{3,1,2,0:T(8,128)(2,1)S(1)} %get-tuple-element.28), channel_id=1, source_target_pairs={{1,0},{2,1},{3,2},{4,3},{5,4},{6,5},{7,6},{9,8},{10,9},{11,10},{12... | collective-permute-start | bytes 6152 | tf_op jit(solution)/shard_map/ppermute | solution.py:10
  26.4 6.4 %copy-start.7 = (bf16[64,16,3,3,3]{0,1,4,3,2:T(8,128)(2,1)S(1)}, bf16[64,16,3,3,3]{0,1,4,3,2:T(8,128)(2,1)}, u32[]{:S(2)}) copy-start(bf16[64,16,3,3,3]{0,1,4,3,2:T(8,128)(2,1)} %param.15) | copy-start | bytes 165892
  26.4 6.4 %copy-start.11 = (pred[8,17]{0,1:T(8,128)(4,1)S(1)}, pred[8,17]{0,1:T(8,128)(4,1)}, u32[]{:S(2)}) copy-start(pred[8,17]{0,1:T(8,128)(4,1)} %constant.64) | copy-start | bytes 412
  38.7 0.7 copy-start.4
  40.3 6.0 %collective-permute-start.4 = (bf16[1,64,8,128]{1,2,3,0:T(8,128)(2,1)S(1)}, bf16[1,64,8,128]{1,2,3,0:T(8,128)(2,1)S(1)}, u32[]{:S(2)}, u32[]{:S(2)}) collective-permute-start(bf16[1,64,8,128]{1,2,3,0:T(8,128)(2,1)S(1)} %get-tuple-element.25), channel_id=1, source_target_pairs={{0,8},{8,16},{16,24},{1,9},{9,17},{17,25},{2,10},{10,18},{18,26},{... | collective-permute-start | bytes 393224 | tf_op jit(solution)/shard_map/ppermute | solution.py:18
  44.9 3.4 %collective-permute-start.5 = (bf16[1,64,8,128]{1,2,3,0:T(8,128)(2,1)S(1)}, bf16[1,64,8,128]{1,2,3,0:T(8,128)(2,1)S(1)}, u32[]{:S(2)}, u32[]{:S(2)}) collective-permute-start(bf16[1,64,8,128]{1,2,3,0:T(8,128)(2,1)S(1)} %get-tuple-element.26), channel_id=1, source_target_pairs={{8,0},{16,8},{24,16},{9,1},{17,9},{25,17},{10,2},{18,10},{26,18},{... | collective-permute-start | bytes 393224 | tf_op jit(solution)/shard_map/ppermute | solution.py:21
  48.4 5.5 %collective-permute-start.6 = (bf16[8,64,8,1]{1,2,3,0:T(8,128)(2,1)S(1)}, bf16[8,64,8,1]{1,2,3,0:T(8,128)(2,1)S(1)}, u32[]{:S(2)}, u32[]{:S(2)}) collective-permute-start(bf16[8,64,8,1]{1,2,3,0:T(8,128)(2,1)S(1)} %get-tuple-element.21), channel_id=1, source_target_pairs={{0,1},{1,2},{2,3},{3,4},{4,5},{5,6},{6,7},{8,9},{9,10},{10,11},{11... | collective-permute-start | bytes 24584 | tf_op jit(solution)/shard_map/ppermute | solution.py:10
  52.5 6.2 %collective-permute-start.7 = (bf16[8,64,8,1]{1,2,3,0:T(8,128)(2,1)S(1)}, bf16[8,64,8,1]{1,2,3,0:T(8,128)(2,1)S(1)}, u32[]{:S(2)}, u32[]{:S(2)}) collective-permute-start(bf16[8,64,8,1]{1,2,3,0:T(8,128)(2,1)S(1)} %get-tuple-element.22), channel_id=1, source_target_pairs={{1,0},{2,1},{3,2},{4,3},{5,4},{6,5},{7,6},{9,8},{10,9},{11,10},{12... | collective-permute-start | bytes 24584 | tf_op jit(solution)/shard_map/ppermute | solution.py:10
  89.5 0.7 copy-start.5
  90.2 16.0 %copy-start.3 = (s32[1,8,128]{2,1,0:T(8,128)S(1)}, s32[1,8,128]{2,1,0:T(8,128)}, u32[]{:S(2)}) copy-start(s32[1,8,128]{2,1,0:T(8,128)} %param.23) | copy-start | bytes 12292
  91.1 6.3 %collective-permute-start.8 = (bf16[1,64,8,128]{1,2,3,0:T(8,128)(2,1)S(1)}, bf16[1,64,8,128]{1,2,3,0:T(8,128)(2,1)S(1)}, u32[]{:S(2)}, u32[]{:S(2)}) collective-permute-start(bf16[1,64,8,128]{1,2,3,0:T(8,128)(2,1)S(1)} %get-tuple-element.23), channel_id=1, source_target_pairs={{0,8},{8,16},{16,24},{1,9},{9,17},{17,25},{2,10},{10,18},{18,26},{... | collective-permute-start | bytes 393224 | tf_op jit(solution)/shard_map/ppermute | solution.py:18
  96.1 3.9 %collective-permute-start.9 = (bf16[1,64,8,128]{1,2,3,0:T(8,128)(2,1)S(1)}, bf16[1,64,8,128]{1,2,3,0:T(8,128)(2,1)S(1)}, u32[]{:S(2)}, u32[]{:S(2)}) collective-permute-start(bf16[1,64,8,128]{1,2,3,0:T(8,128)(2,1)S(1)} %get-tuple-element.24), channel_id=1, source_target_pairs={{8,0},{16,8},{24,16},{9,1},{17,9},{25,17},{10,2},{18,10},{26,18},{... | collective-permute-start | bytes 393224 | tf_op jit(solution)/shard_map/ppermute | solution.py:21
  100.0 6.2 %collective-permute-start.10 = (bf16[8,64,8,1]{1,2,3,0:T(8,128)(2,1)S(1)}, bf16[8,64,8,1]{1,2,3,0:T(8,128)(2,1)S(1)}, u32[]{:S(2)}, u32[]{:S(2)}) collective-permute-start(bf16[8,64,8,1]{1,2,3,0:T(8,128)(2,1)S(1)} %get-tuple-element.19), channel_id=1, source_target_pairs={{0,1},{1,2},{2,3},{3,4},{4,5},{5,6},{6,7},{8,9},{9,10},{10,11},{11... | collective-permute-start | bytes 24584 | tf_op jit(solution)/shard_map/ppermute | solution.py:10
  104.8 5.6 %collective-permute-start.11 = (bf16[8,64,8,1]{1,2,3,0:T(8,128)(2,1)S(1)}, bf16[8,64,8,1]{1,2,3,0:T(8,128)(2,1)S(1)}, u32[]{:S(2)}, u32[]{:S(2)}) collective-permute-start(bf16[8,64,8,1]{1,2,3,0:T(8,128)(2,1)S(1)} %get-tuple-element.20), channel_id=1, source_target_pairs={{1,0},{2,1},{3,2},{4,3},{5,4},{6,5},{7,6},{9,8},{10,9},{11,10},{12... | collective-permute-start | bytes 24584 | tf_op jit(solution)/shard_map/ppermute | solution.py:10
  115.4 0.9 copy-start.8
  136.1 2.4 %copy-start.1 = (bf16[6,16,1,8,128]{4,3,2,1,0:T(8,128)(2,1)S(1)}, bf16[6,16,1,8,128]{4,3,2,1,0:T(8,128)(2,1)}, u32[]{:S(2)}) copy-start(bf16[6,16,1,8,128]{4,3,2,1,0:T(8,128)(2,1)} %param.13) | copy-start | bytes 589828
  136.1 2.5 %copy-start.2 = (bf16[6,16,1,8,128]{4,3,2,1,0:T(8,128)(2,1)S(1)}, bf16[6,16,1,8,128]{4,3,2,1,0:T(8,128)(2,1)}, u32[]{:S(2)}) copy-start(bf16[6,16,1,8,128]{4,3,2,1,0:T(8,128)(2,1)} %param.14) | copy-start | bytes 589828
  136.1 2.5 %copy-start.6 = (f32[16]{0:T(128)S(1)}, f32[16]{0:T(128)}, u32[]{:S(2)}) copy-start(f32[16]{0:T(128)} %param.20) | copy-start | bytes 196
  136.1 2.7 %copy-start.10 = (s32[6]{0:T(128)S(1)}, s32[6]{0:T(128)}, u32[]{:S(2)}) copy-start(s32[6]{0:T(128)} %param.21) | copy-start | bytes 76
  136.2 12.1 %copy-start.9 = (f32[2,1,8,128]{3,2,1,0:T(8,128)S(1)}, f32[2,1,8,128]{3,2,1,0:T(8,128)}, u32[]{:S(2)}) copy-start(f32[2,1,8,128]{3,2,1,0:T(8,128)} %param.22) | copy-start | bytes 24580
where the time goes:
time: 152 us; the launch traced here: 150 us
  matrix products  45.5 us (30%)
  starting transfers between devices  32.2 us (21%)
  local copies, waits for them, and re-layouts  26.6 us (18%)
  waiting for transfers between devices  25.3 us (17%)
  other arithmetic  10.3 us (7%)
  blocking collectives  9.12 us (6%)
    conv_general_dilated x3, matrix products, conv_valid(): lax.conv_general_dilated(field[None], kernel, (1, 1, 1), 'VALID', dimensi...  45.1 us
    conv_general_dilated x11, local copies, waits for them, and re-layouts, conv_valid(): lax.conv_general_dilated(field[None], kernel, (1, 1, 1), 'VALID', dimensi...  20.4 us
    ppermute x6, waiting for transfers between devices, passed_along(): lax.ppermute(value, axis, [(source, source + steps) for source in range(l...  17.6 us
    ppermute x6, starting transfers between devices, passed_along(): lax.ppermute(value, axis, [(source, source + steps) for source in range(l...  16.2 us
    ppermute x3, starting transfers between devices, with_halo(): lax.ppermute(lax.slice_in_dim(block, block.shape[dim] - width, None, axis...  12.1 us
    psum x1, blocking collectives, body(): totals = lax.psum(partial_tot, 'tm')  9.12 us
    broadcast_in_dim x3, other arithmetic, conv_valid(): field[None]  8.3 us
    ppermute x3, waiting for transfers between devices, with_halo(): lax.ppermute(lax.slice_in_dim(block, 0, width, axis=dim), axis, backward)  7.66 us
  transfers between devices with their start and end apart: 12, of which 9 were waited for; matrix products, arithmetic and copies ran while one was open for 1% of the time, Pallas kernels for 0%

commit v1 on v0

v1 whole, which is shorter than its diff:
```python
import functools

import jax
import jax.numpy as jnp
from jax import lax
from jax.experimental import pallas as pl
from jax.experimental.pallas import tpu as pltpu
from jax.sharding import PartitionSpec as P

BF = jnp.bfloat16
F32 = jnp.float32
LANES = 128
DEPTH = 3
PITCH = 16
VMEM = pl.BlockSpec(memory_space=pltpu.VMEM)
SMEM = pl.BlockSpec(memory_space=pltpu.SMEM)
LIMIT = 48 * 1024 * 1024


def params():
    return pltpu.CompilerParams(vmem_limit_bytes=LIMIT)


def silu(v):
    half = 0.5 * v
    return half + half * jnp.tanh(half)


def lanes(shape):
    return lax.broadcasted_iota(jnp.int32, shape, len(shape) - 1)


def turn(v, steps):
    steps = steps % LANES
    if steps == 0:
        return v
    return pltpu.roll(v, steps, 1)


def tile(i):
    return slice(i * LANES, (i + 1) * LANES)


def rows_kernel(state_ref, w1_ref, w2_ref, w3_ref, own_ref, lo_ref, hi_ref, k1_ref, k2_ref, k3_ref, scr):
    frames, chans, rows, _ = state_ref.shape
    for f in range(frames):
        scr[f] = state_ref[f].astype(F32).reshape(chans * rows, LANES)
    for f in range(frames):
        for y in range(rows):
            v = scr[f, pl.ds(y, chans, stride=rows), :].astype(BF)
            own_ref[f, :, tile(y)] = v
            if f < DEPTH:
                lo_ref[f, :, tile(y)] = v
            if f >= frames - DEPTH:
                hi_ref[f - (frames - DEPTH), :, tile(y)] = v
    hid = w2_ref.shape[1]
    k1_ref[...] = w1_ref[...].astype(F32).T.astype(BF)
    for t in range(27):
        k2_ref[:, t * hid : (t + 1) * hid] = w2_ref[t]
        k3_ref[:, t * hid : (t + 1) * hid] = w3_ref[t]


def make_rows(state, w1, w2, w3):
    frames, chans, rows, _ = state.shape
    hid, fields = w2.shape[1], w3.shape[1]
    slab = jax.ShapeDtypeStruct((DEPTH, chans, rows * LANES), BF)
    return pl.pallas_call(
        rows_kernel,
        out_shape=(
            jax.ShapeDtypeStruct((frames, chans, rows * LANES), BF),
            slab,
            slab,
            jax.ShapeDtypeStruct((hid, 27 * chans), BF),
            jax.ShapeDtypeStruct((hid, 27 * hid), BF),
            jax.ShapeDtypeStruct((fields, 27 * hid), BF),
        ),
        in_specs=[VMEM] * 4,
        out_specs=(VMEM,) * 6,
        scratch_shapes=[pltpu.VMEM((frames, chans * rows, LANES), F32)],
        compiler_params=params(),
        name="rows",
    )(state, w1, w2, w3)


def edges_kernel(own_ref, below_ref, above_ref, west_ref, east_ref):
    frames = own_ref.shape[0]
    rows = own_ref.shape[2] // LANES
    shape = (own_ref.shape[1], LANES)
    lane = lanes(shape)
    group, place = lane // PITCH, lane % PITCH
    for f in range(frames + 2 * DEPTH):
        if f < DEPTH:
            src, g = below_ref, f
        elif f < DEPTH + frames:
            src, g = own_ref, f - DEPTH
        else:
            src, g = above_ref, f - DEPTH - frames
        west = jnp.zeros(shape, BF)
        east = jnp.zeros(shape, BF)
        for y in range(rows):
            v = src[g, :, tile(y)]
            here = group == y
            west = jnp.where(here & (place >= DEPTH), turn(v, y * PITCH + DEPTH), west)
            east = jnp.where(here & (place < PITCH - DEPTH), turn(v, y * PITCH + PITCH - DEPTH), east)
        west_ref[f] = west
        east_ref[f] = east


def make_edges(own, below, above):
    frames, chans, _ = own.shape
    strip = jax.ShapeDtypeStruct((frames + 2 * DEPTH, chans, LANES), BF)
    return pl.pallas_call(
        edges_kernel,
        out_shape=(strip, strip),
        in_specs=[VMEM] * 3,
        out_specs=(VMEM,) * 2,
        compiler_params=params(),
        name="edges",
    )(own, below, above)


def spread(dst, f, y, v):
    chans = v.shape[0]
    at = tile(y + 1)
    dst[f, 0:chans, at] = turn(v, 1)
    dst[f, chans : 2 * chans, at] = v
    dst[f, 2 * chans : 3 * chans, at] = turn(v, -1)


def window(src, f, y):
    return jnp.concatenate(
        [src[f + dt, :, (y + dy) * LANES : (y + dy + 2) * LANES] for dt in range(3) for dy in range(3)], axis=0
    )


def in_trajectory(local, frames):
    step = lax.axis_index("tm") * frames + local
    return (step >= 0) & (step < frames * lax.axis_size("tm"))


def main_kernel(own_ref, below_ref, above_ref, k1_ref, k2_ref, k3_ref, b1_ref, b2_ref, score_ref, s1, s2, s3):
    frames = own_ref.shape[0]
    rows = own_ref.shape[2] // LANES
    for s in (s1, s2, s3):
        s[:, :, tile(0)] = jnp.zeros(s.shape[:2] + (LANES,), BF)
        s[:, :, tile(rows + 1)] = jnp.zeros(s.shape[:2] + (LANES,), BF)
    for f in range(frames + 2 * DEPTH):
        if f < DEPTH:
            src, g = below_ref, f
        elif f < DEPTH + frames:
            src, g = own_ref, f - DEPTH
        else:
            src, g = above_ref, f - DEPTH - frames
        for y in range(rows):
            spread(s1, f, y, src[g, :, tile(y)])

    def layer(src, dst, k_ref, b_ref, count, first):
        def step(f, carry):
            keep = in_trajectory(f + first, frames)
            for y in range(0, rows, 2):
                acc = jnp.dot(k_ref[...], window(src, f, y), preferred_element_type=F32)
                h = jnp.where(keep, silu(acc + b_ref[...]), 0.0).astype(BF)
                spread(dst, f, y, h[:, tile(0)])
                spread(dst, f, y + 1, h[:, tile(1)])
            return carry

        lax.fori_loop(0, count, step, 0)

    layer(s1, s2, k1_ref, b1_ref, frames + 4, -2)
    layer(s2, s3, k2_ref, b2_ref, frames + 2, -1)

    def last(f, carry):
        for y in range(0, rows, 2):
            score_ref[f, :, y * LANES : (y + 2) * LANES] = jnp.dot(
                k3_ref[...], window(s3, f, y), preferred_element_type=F32
            )
        return carry

    lax.fori_loop(0, frames, last, 0)


def make_main(own, below, above, k1, k2, k3, b1, b2):
    frames, chans, width = own.shape
    hid, fields = k2.shape[0], k3.shape[0]
    wide = width + 2 * LANES
    return pl.pallas_call(
        main_kernel,
        out_shape=jax.ShapeDtypeStruct((frames, fields, width), F32),
        in_specs=[VMEM] * 8,
        out_specs=VMEM,
        scratch_shapes=[
            pltpu.VMEM((frames + 6, 3 * chans, wide), BF),
            pltpu.VMEM((frames + 4, 3 * hid, wide), BF),
            pltpu.VMEM((frames + 2, 3 * hid, wide), BF),
        ],
        compiler_params=params(),
        cost_estimate=pl.CostEstimate(flops=5_000_000_000, bytes_accessed=4_000_000, transcendentals=1_000_000),
        name="main",
    )(own, below, above, k1, k2, k3, b1, b2)


def spread_side(dst, f, v):
    chans = v.shape[0]
    lane = lanes((chans, LANES))
    for half in range(2):
        w = v[:, tile(half)]
        for i, shifted in enumerate((turn(w, 1), w, turn(w, -1))):
            down = jnp.where(lane >= PITCH, turn(shifted, PITCH), jnp.zeros_like(shifted))
            up = jnp.where(lane < LANES - PITCH, turn(shifted, -PITCH), jnp.zeros_like(shifted))
            for dy, piece in enumerate((down, shifted, up)):
                at = (dy * 3 + i) * chans
                dst[f, at : at + chans, tile(half)] = piece


def finish_kernel(
    score_ref, west_ref, east_ref, from_west_ref, from_east_ref, k1_ref, k2_ref, k3_ref, b1_ref, b2_ref, b3_ref,
    state_ref, noise_ref, day_ref, out_ref, first_ref, part_ref, t1, t2, t3, scr,
):
    frames, fields = state_ref.shape[:2]
    rows = state_ref.shape[2]
    chans = west_ref.shape[1]
    lane = lanes((chans, LANES)) % PITCH
    for f in range(frames + 2 * DEPTH):
        west = jnp.where(lane < DEPTH, turn(from_west_ref[f], 2 * DEPTH - PITCH), west_ref[f])
        east = jnp.where(lane >= PITCH - DEPTH, turn(from_east_ref[f], PITCH - 2 * DEPTH), east_ref[f])
        spread_side(t1, f, jnp.concatenate([west, east], axis=1))

    me, last = lax.axis_index("space"), lax.axis_size("space") - 1
    pair = lanes((1, 2 * LANES))
    place = pair % PITCH
    outside = ((pair < LANES) & (place < DEPTH) & (me == 0)) | (
        (pair >= LANES) & (place >= PITCH - DEPTH) & (me == last)
    )

    def layer(src, dst, k_ref, b_ref, count, first):
        def step(f, carry):
            keep = in_trajectory(f + first, frames)
            z = jnp.concatenate([src[f + dt] for dt in range(3)], axis=0)
            acc = jnp.dot(k_ref[...], z, preferred_element_type=F32)
            h = jnp.where(keep & ~outside, silu(acc + b_ref[...]), 0.0).astype(BF)
            spread_side(dst, f, h)
            return carry

        lax.fori_loop(0, count, step, 0)

    layer(t1, t2, k1_ref, b1_ref, frames + 4, -2)
    layer(t2, t3, k2_ref, b2_ref, frames + 2, -1)

    col = lanes((fields, LANES))
    days = part_ref.shape[0]
    totals = [jnp.zeros((rows, LANES), F32) for _ in range(days)]
    for f in range(frames):
        z = jnp.concatenate([t3[f + dt] for dt in range(3)], axis=0)
        side = jnp.dot(k3_ref[...], z, preferred_element_type=F32)
        west, east = side[:, tile(0)], side[:, tile(1)]
        for y in range(rows):
            v = score_ref[f, :, tile(y)]
            v = jnp.where(col < DEPTH, turn(west, -(y * PITCH + DEPTH)), v)
            v = jnp.where(col >= LANES - DEPTH, turn(east, DEPTH - (y + 1) * PITCH), v)
            scr[f, pl.ds(y, fields, stride=rows), :] = v + b3_ref[...]
        score = scr[f].reshape(fields, rows, LANES)
        now = state_ref[f].astype(F32)
        moved = now + 0.8 * score + 0.5 * noise_ref[f].astype(F32)
        out_ref[f] = moved.astype(BF)
        first_ref[f] = moved[0]
        estimate = now[0] + 0.5 * score[0]
        for d in range(days):
            totals[d] = totals[d] + jnp.where(day_ref[f] == d, estimate, 0.0)
    for d in range(days):
        part_ref[d] = totals[d]


def make_finish(score, west, east, from_west, from_east, k1, k2, k3, b1, b2, b3, state, noise, day, days):
    frames, fields, rows, _ = state.shape
    chans, hid = west.shape[1], k2.shape[0]
    return pl.pallas_call(
        finish_kernel,
        out_shape=(
            jax.ShapeDtypeStruct(state.shape, BF),
            jax.ShapeDtypeStruct((frames, rows, LANES), F32),
            jax.ShapeDtypeStruct((days, rows, LANES), F32),
        ),
        in_specs=[VMEM] * 13 + [SMEM],
        out_specs=(VMEM,) * 3,
        scratch_shapes=[
            pltpu.VMEM((frames + 6, 9 * chans, 2 * LANES), BF),
            pltpu.VMEM((frames + 4, 9 * hid, 2 * LANES), BF),
            pltpu.VMEM((frames + 2, 9 * hid, 2 * LANES), BF),
            pltpu.VMEM((frames, fields * rows, LANES), F32),
        ],
        compiler_params=params(),
        name="finish",
    )(score, west, east, from_west, from_east, k1, k2, k3, b1, b2, b3, state, noise, day)


def correct_kernel(count, *refs):
    parts = refs[:count]
    observed_ref, mask_ref, first_ref, day_ref, _, out_ref, buf, sem = refs[count:]
    frames = first_ref.shape[0]
    days = observed_ref.shape[0]
    mask = mask_ref[...].astype(F32)
    misfit = []
    for d in range(days):
        total = parts[0][d]
        for p in parts[1:]:
            total = total + p[d]
        misfit.append(0.15 * (mask * (total - observed_ref[d])))
    for f in range(frames):
        v = first_ref[f]
        for d in range(days):
            v = v - jnp.where(day_ref[f] == d, misfit[d], 0.0)
        buf[f, 0] = v.astype(BF)
    copy = pltpu.make_async_copy(buf, out_ref.at[:, 0:1], sem)
    copy.start()
    copy.wait()


def make_correct(parts, observed, mask, first, day, out):
    frames, rows, _ = first.shape
    anywhere = pl.BlockSpec(memory_space=pl.ANY)
    return pl.pallas_call(
        functools.partial(correct_kernel, len(parts)),
        out_shape=jax.ShapeDtypeStruct(out.shape, BF),
        in_specs=[VMEM] * (len(parts) + 3) + [SMEM, anywhere],
        out_specs=anywhere,
        scratch_shapes=[pltpu.VMEM((frames, 1, rows, LANES), BF), pltpu.SemaphoreType.DMA],
        input_output_aliases={len(parts) + 4: 0},
        compiler_params=params(),
        name="correct",
    )(*parts, observed, mask, first, day, out)


def passed(value, axis, steps):
    count = lax.axis_size(axis)
    return lax.ppermute(value, axis, [(i, i + steps) for i in range(count) if 0 <= i + steps < count])


def body(
    state, noise, conv_one, bias_one, conv_two, bias_two, conv_three, bias_three, day_of_frame, observed, obs_mask
):
    state, noise = state[:, :, 0], noise[:, :, 0]
    hid, chans = conv_one.shape[:2]
    fields = conv_three.shape[0]
    w1 = conv_one.transpose(2, 3, 4, 1, 0).reshape(27 * chans, hid)
    w2 = conv_two.transpose(2, 3, 4, 0, 1).reshape(27, hid, hid)
    w3 = conv_three.transpose(2, 3, 4, 0, 1).reshape(27, fields, hid)
    b1, b2, b3 = bias_one[:, None], bias_two[:, None], bias_three[:, None]
    own, lo, hi, k1, k2, k3 = make_rows(state, w1, w2, w3)
    below = passed(hi, "tm", 1)
    above = passed(lo, "tm", -1)
    west, east = make_edges(own, below, above)
    from_west = passed(east, "space", 1)
    from_east = passed(west, "space", -1)
    score = make_main(own, below, above, k1, k2, k3, b1, b2)
    out, first, part = make_finish(
        score, west, east, from_west, from_east, k1, k2, k3, b1, b2, b3, state, noise, day_of_frame, observed.shape[0]
    )
    count = lax.axis_size("tm")
    if count <= 4:
        parts = [part] + [
            lax.ppermute(part, "tm", [(i, (i + s) % count) for i in range(count)]) for s in range(1, count)
        ]
    else:
        parts = [lax.psum(part, "tm")]
    out = make_correct(parts, observed[:, 0], obs_mask[0], first, day_of_frame, out)
    return out[:, :, None]


def solution(mesh):
    in_specs = (
        P("tm", None, "space", None, None),
        P("tm", None, "space", None, None),
        P(),
        P(),
        P(),
        P(),
        P(),
        P(),
        P("tm"),
        P(None, "space", None, None),
        P("space", None, None),
    )
    out_specs = P("tm", None, "space", None, None)
    return jax.shard_map(body, mesh=mesh, in_specs=in_specs, out_specs=out_specs, check_vma=False)
```

time: 152 us -> 50.6 us (0.33)
  matrix products: 45.5 us -> 0 us
  Pallas kernels: 0 us -> 26.1 us
  waiting for transfers between devices: 25.3 us -> 4.52 us
  local copies, waits for them, and re-layouts: 26.6 us -> 5.97 us
  starting transfers between devices: 32.2 us -> 12.9 us
  other arithmetic: 10.3 us -> 0 us
  blocking collectives: 9.12 us -> 0 us
    conv_general_dilated x3 -> x0, matrix products: 45.1 us -> none  [conv_valid(): lax.conv_general_dilated(field[None], kernel, (1, 1, 1), 'VALID', dimensi...]
    pallas_call x0 -> x5, Pallas kernels: none -> 26.1 us  [the longest x1 14.5 us: make_main(): pl.pallas_call(main_kernel, out_shape=jax.ShapeDtypeStruct((frames, field...]
    ppermute x12 -> x7, waiting for transfers between devices: 25.3 us -> 4.52 us  [the longest x4 2.41 us: passed(): lax.ppermute(value, axis, [(i, i + steps) for i in range(count) if 0 <= i...]
    conv_general_dilated x11 -> x0, local copies, waits for them, and re-layouts: 20.4 us -> none  [conv_valid(): lax.conv_general_dilated(field[None], kernel, (1, 1, 1), 'VALID', dimensi...]
    ppermute x12 -> x7, starting transfers between devices: 32.2 us -> 12.9 us  [the longest x4 8.37 us: passed(): lax.ppermute(value, axis, [(i, i + steps) for i in range(count) if 0 <= i...]
    psum x1 -> x0, blocking collectives: 9.12 us -> none  [body(): totals = lax.psum(partial_tot, 'tm')]
    broadcast_in_dim x4 -> x0, other arithmetic: 8.33 us -> none  [the longest x3 8.3 us: conv_valid(): field[None]]
    unnamed x28 -> x24, local copies, waits for them, and re-layouts: 1.22 us -> 5.69 us
  transfers between devices with their start and end apart: 12 -> 7, of which waited for: 9 -> 2; matrix products, arithmetic and copies ran while one was open for 1% -> 1% of each run, Pallas kernels for 0% -> 29%
where the time goes in v1:
time: 50.6 us; the launch traced here: 49.6 us
  Pallas kernels  26.1 us (52%)
  starting transfers between devices  12.9 us (25%)
  local copies, waits for them, and re-layouts  5.97 us (12%)
  waiting for transfers between devices  4.52 us (9%)
    pallas_call x1, Pallas kernels, make_main(): pl.pallas_call(main_kernel, out_shape=jax.ShapeDtypeStruct((frames, field...  14.5 us
    pallas_call x1, Pallas kernels, make_finish(): pl.pallas_call(finish_kernel, out_shape=(jax.ShapeDtypeStruct(state.shape...  9.89 us
    ppermute x4, starting transfers between devices, passed(): lax.ppermute(value, axis, [(i, i + steps) for i in range(count) if 0 <= i...  8.37 us
    unnamed x24, local copies, waits for them, and re-layouts  5.69 us
    ppermute x3, starting transfers between devices, body(): lax.ppermute(part, 'tm', [(i, (i + s) % count) for i in range(count)])  4.5 us
    ppermute x4, waiting for transfers between devices, passed(): lax.ppermute(value, axis, [(i, i + steps) for i in range(count) if 0 <= i...  2.41 us
    ppermute x3, waiting for transfers between devices, body(): lax.ppermute(part, 'tm', [(i, (i + s) % count) for i in range(count)])  2.11 us
    pallas_call x1, Pallas kernels, make_correct(): pl.pallas_call(functools.partial(correct_kernel, len(parts)), out_shape=j...  1.17 us
  transfers between devices with their start and end apart: 7, of which 2 were waited for; matrix products, arithmetic and copies ran while one was open for 1% of the time, Pallas kernels for 29%

profile of v1, /device:TPU:0, one launch (start us, length us, event | category | flops | bytes accessed | tf_op | source)
XLA Modules:
  0.0 49.6 jit_solution(9129016208251450376)
XLA Ops:
  0.0 0.9 %copy-done = bf16[6,16,1,8,128]{4,3,2,1,0:T(8,128)(2,1)S(1)} copy-done((bf16[6,16,1,8,128]{4,3,2,1,0:T(8,128)(2,1)S(1)}, bf16[6,16,1,8,128]{4,3,2,1,0:T(8,128)(2,1)}, u32[]{:S(2)}) %copy-start) | copy-done | bytes 196632
  0.9 1.0 %copy-done.2 = bf16[64,64,3,3,3]{1,0,4,3,2:T(8,128)(2,1)S(1)} copy-done((bf16[64,64,3,3,3]{1,0,4,3,2:T(8,128)(2,1)S(1)}, bf16[64,64,3,3,3]{1,0,4,3,2:T(8,128)(2,1)}, u32[]{:S(2)}) %copy-start.2) | copy-done | bytes 221208
  1.9 0.9 %copy-done.4 = bf16[64,16,3,3,3]{0,1,4,3,2:T(8,128)(2,1)S(1)} copy-done((bf16[64,16,3,3,3]{0,1,4,3,2:T(8,128)(2,1)S(1)}, bf16[64,16,3,3,3]{0,1,4,3,2:T(8,128)(2,1)}, u32[]{:S(2)}) %copy-start.4) | copy-done | bytes 55320
  2.8 0.9 %copy-done.5 = bf16[16,64,3,3,3]{1,0,4,3,2:T(8,128)(2,1)S(1)} copy-done((bf16[16,64,3,3,3]{1,0,4,3,2:T(8,128)(2,1)S(1)}, bf16[16,64,3,3,3]{1,0,4,3,2:T(8,128)(2,1)}, u32[]{:S(2)}) %copy-start.5) | copy-done | bytes 55320
  3.7 0.3 rows.1
  4.1 2.4 %collective-permute-start = (bf16[3,16,1024]{2,1,0:T(8,128)(2,1)S(1)}, bf16[3,16,1024]{2,1,0:T(8,128)(2,1)S(1)}, u32[]{:S(2)}, u32[]{:S(2)}) collective-permute-start(bf16[3,16,1024]{2,1,0:T(8,128)(2,1)S(1)} %get-tuple-element.17), channel_id=1, source_target_pairs={{0,8},{8,16},{16,24},{1,9},{9,17},{17,25},{2,10},{10,18},{18,26},{... | collective-permute-start | bytes 294920 | tf_op jit(solution)/shard_map/ppermute | solution.py:335
  6.4 0.0 copy-start.9
  6.4 1.3 %collective-permute-start.1 = (bf16[3,16,1024]{2,1,0:T(8,128)(2,1)S(1)}, bf16[3,16,1024]{2,1,0:T(8,128)(2,1)S(1)}, u32[]{:S(2)}, u32[]{:S(2)}) collective-permute-start(bf16[3,16,1024]{2,1,0:T(8,128)(2,1)S(1)} %get-tuple-element.18), channel_id=1, source_target_pairs={{8,0},{16,8},{24,16},{9,1},{17,9},{25,17},{10,2},{18,10},{26,18},{... | collective-permute-start | bytes 294920 | tf_op jit(solution)/shard_map/ppermute | solution.py:335
  7.8 0.1 copy.13.b1_ref
  7.9 0.7 %copy-done.10 = f32[64]{0:T(128)S(1)} copy-done((f32[64]{0:T(128)S(1)}, f32[64]{0:T(128)}, u32[]{:S(2)}) %copy-start.10) | copy-done | bytes 280
  8.5 0.1 copy.14.b2_ref
  8.6 0.7 %copy-done.11 = f32[16]{0:T(128)S(1)} copy-done((f32[16]{0:T(128)S(1)}, f32[16]{0:T(128)}, u32[]{:S(2)}) %copy-start.11) | copy-done | bytes 88
  9.3 0.1 copy.17.b3_ref
  9.3 0.0 collective-permute-done.below_ref
  9.3 2.4 %collective-permute-done.1.above_ref = bf16[3,16,1024]{2,1,0:T(8,128)(2,1)S(1)} collective-permute-done((bf16[3,16,1024]{2,1,0:T(8,128)(2,1)S(1)}, bf16[3,16,1024]{2,1,0:T(8,128)(2,1)S(1)}, u32[]{:S(2)}, u32[]{:S(2)}) %collective-permute-start.1) | collective-permute-done | bytes 98336 | tf_op jit(solution)/shard_map/ppermute | solution.py:335
  11.7 0.3 edges.1
  12.0 3.4 %collective-permute-start.2 = (bf16[12,16,128]{2,1,0:T(8,128)(2,1)S(1)}, bf16[12,16,128]{2,1,0:T(8,128)(2,1)S(1)}, u32[]{:S(2)}, u32[]{:S(2)}) collective-permute-start(bf16[12,16,128]{2,1,0:T(8,128)(2,1)S(1)} %get-tuple-element.23.east_ref), channel_id=1, source_target_pairs={{0,1},{1,2},{2,3},{3,4},{4,5},{5,6},{6,7},{8,9},{9,10},{10,11},{11... | collective-permute-start | bytes 147464 | tf_op jit(solution)/shard_map/ppermute | solution.py:335
  15.4 1.3 %collective-permute-start.3 = (bf16[12,16,128]{2,1,0:T(8,128)(2,1)S(1)}, bf16[12,16,128]{2,1,0:T(8,128)(2,1)S(1)}, u32[]{:S(2)}, u32[]{:S(2)}) collective-permute-start(bf16[12,16,128]{2,1,0:T(8,128)(2,1)S(1)} %get-tuple-element.22.west_ref), channel_id=1, source_target_pairs={{1,0},{2,1},{3,2},{4,3},{5,4},{6,5},{7,6},{9,8},{10,9},{11,10},{12... | collective-permute-start | bytes 147464 | tf_op jit(solution)/shard_map/ppermute | solution.py:335
  16.7 0.0 copy-start.1
  16.8 0.0 copy-start.3
  16.8 14.5 %main.1.score_ref = f32[6,16,1024]{2,1,0:T(8,128)S(1)} custom-call(bf16[6,16,1024]{2,1,0:T(8,128)(2,1)S(1)} %get-tuple-element.16.own_ref, bf16[3,16,1024]{2,1,0:T(8,128)(2,1)S(1)} %collective-permute-done.below_ref, bf16[3,16,1024]{2,1,0:T(8,128)(2,1)S(1)} %collective-permute-done.1.above_ref, bf16[64,432]{1,0:T(8,128)(2,1)S(1)} %get-tuple-element.19.k1_ref, ...), custom_call_target="tpu_custom_call" | custom-call | flops 5000000000 | bytes 4000000 | tf_op jit(solution)/shard_map/main/pallas_call | solution.py:186
  31.3 0.0 collective-permute-done.2.from_west_ref
  31.3 0.0 collective-permute-done.3.from_east_ref
  31.3 0.6 %copy-done.8 = s32[6]{0:T(128)S(1)} copy-done((s32[6]{0:T(128)S(1)}, s32[6]{0:T(128)}, u32[]{:S(2)}) %copy-start.8) | copy-done | bytes 48
  31.9 9.9 %finish.1 = (bf16[6,16,8,128]{3,2,1,0:T(8,128)(2,1)}, f32[6,8,128]{2,1,0:T(8,128)S(1)}, f32[2,8,128]{2,1,0:T(8,128)S(1)}) custom-call(f32[6,16,1024]{2,1,0:T(8,128)S(1)} %main.1.score_ref, bf16[12,16,128]{2,1,0:T(8,128)(2,1)S(1)} %get-tuple-element.22.west_ref, bf16[12,16,128]{2,1,0:T(8,128)(2,1)S(1)} %get-tuple-element.23.east_ref, ...), custom_call_target="tpu_custom_call" | custom-call | tf_op jit(solution)/shard_map/finish/pallas_call | solution.py:276
  41.8 3.0 %collective-permute-start.4 = (f32[2,8,128]{2,1,0:T(8,128)S(1)}, f32[2,8,128]{2,1,0:T(8,128)S(1)}, u32[]{:S(2)}, u32[]{:S(2)}) collective-permute-start(f32[2,8,128]{2,1,0:T(8,128)S(1)} %get-tuple-element.24.refs_0_), channel_id=1, source_target_pairs={{0,8},{8,16},{16,24},{24,0},{1,9},{9,17},{17,25},{25,1},{2,10},{10... | collective-permute-start | bytes 24584 | tf_op jit(solution)/shard_map/ppermute | solution.py:361
  44.8 0.1 collective-permute-start.5
  44.9 1.4 %collective-permute-start.6 = (f32[2,8,128]{2,1,0:T(8,128)S(1)}, f32[2,8,128]{2,1,0:T(8,128)S(1)}, u32[]{:S(2)}, u32[]{:S(2)}) collective-permute-start(f32[2,8,128]{2,1,0:T(8,128)S(1)} %get-tuple-element.24.refs_0_), channel_id=1, source_target_pairs={{0,24},{8,0},{16,8},{24,16},{1,25},{9,1},{17,9},{25,17},{2,26},{10... | collective-permute-start | bytes 24584 | tf_op jit(solution)/shard_map/ppermute | solution.py:361
  46.3 0.0 collective-permute-done.4.refs_1_
  46.3 2.1 %collective-permute-done.5.refs_2_ = f32[2,8,128]{2,1,0:T(8,128)S(1)} collective-permute-done((f32[2,8,128]{2,1,0:T(8,128)S(1)}, f32[2,8,128]{2,1,0:T(8,128)S(1)}, u32[]{:S(2)}, u32[]{:S(2)}) %collective-permute-start.5) | collective-permute-done | bytes 8224 | tf_op jit(solution)/shard_map/ppermute | solution.py:361
  48.4 0.0 collective-permute-done.6.refs_3_
  48.4 1.2 %correct.1 = bf16[6,16,8,128]{3,2,1,0:T(8,128)(2,1)} custom-call(f32[2,8,128]{2,1,0:T(8,128)S(1)} %get-tuple-element.24.refs_0_, f32[2,8,128]{2,1,0:T(8,128)S(1)} %collective-permute-done.4.refs_1_, f32[2,8,128]{2,1,0:T(8,128)S(1)} %collective-permute-done.5.refs_2_, ...), custom_call_target="tpu_custom_call", output_to_operand_aliasing={{}: (8, {})} | custom-call | tf_op jit(solution)/shard_map/correct/pallas_call | solution.py:321
  (14 shorter events, 0.0 us)
Async XLA Ops:
  0.0 0.9 %copy-start = (bf16[6,16,1,8,128]{4,3,2,1,0:T(8,128)(2,1)S(1)}, bf16[6,16,1,8,128]{4,3,2,1,0:T(8,128)(2,1)}, u32[]{:S(2)}) copy-start(bf16[6,16,1,8,128]{4,3,2,1,0:T(8,128)(2,1)} %param.11) | copy-start | bytes 589828
  0.9 1.0 %copy-start.2 = (bf16[64,64,3,3,3]{1,0,4,3,2:T(8,128)(2,1)S(1)}, bf16[64,64,3,3,3]{1,0,4,3,2:T(8,128)(2,1)}, u32[]{:S(2)}) copy-start(bf16[64,64,3,3,3]{1,0,4,3,2:T(8,128)(2,1)} %param.15) | copy-start | bytes 663556
  1.9 0.9 %copy-start.4 = (bf16[64,16,3,3,3]{0,1,4,3,2:T(8,128)(2,1)S(1)}, bf16[64,16,3,3,3]{0,1,4,3,2:T(8,128)(2,1)}, u32[]{:S(2)}) copy-start(bf16[64,16,3,3,3]{0,1,4,3,2:T(8,128)(2,1)} %param.13) | copy-start | bytes 165892
  2.8 0.9 %copy-start.5 = (bf16[16,64,3,3,3]{1,0,4,3,2:T(8,128)(2,1)S(1)}, bf16[16,64,3,3,3]{1,0,4,3,2:T(8,128)(2,1)}, u32[]{:S(2)}) copy-start(bf16[16,64,3,3,3]{1,0,4,3,2:T(8,128)(2,1)} %param.17) | copy-start | bytes 165892
  4.1 5.3 %collective-permute-start = (bf16[3,16,1024]{2,1,0:T(8,128)(2,1)S(1)}, bf16[3,16,1024]{2,1,0:T(8,128)(2,1)S(1)}, u32[]{:S(2)}, u32[]{:S(2)}) collective-permute-start(bf16[3,16,1024]{2,1,0:T(8,128)(2,1)S(1)} %get-tuple-element.17), channel_id=1, source_target_pairs={{0,8},{8,16},{16,24},{1,9},{9,17},{17,25},{2,10},{10,18},{18,26},{... | collective-permute-start | bytes 294920 | tf_op jit(solution)/shard_map/ppermute | solution.py:335
  6.4 1.3 %copy-start.9 = (f32[64]{0:T(128)S(1)}, f32[64]{0:T(128)}, u32[]{:S(2)}) copy-start(f32[64]{0:T(128)} %param.14) | copy-start | bytes 772
  6.4 5.3 %collective-permute-start.1 = (bf16[3,16,1024]{2,1,0:T(8,128)(2,1)S(1)}, bf16[3,16,1024]{2,1,0:T(8,128)(2,1)S(1)}, u32[]{:S(2)}, u32[]{:S(2)}) collective-permute-start(bf16[3,16,1024]{2,1,0:T(8,128)(2,1)S(1)} %get-tuple-element.18), channel_id=1, source_target_pairs={{8,0},{16,8},{24,16},{9,1},{17,9},{25,17},{10,2},{18,10},{26,18},{... | collective-permute-start | bytes 294920 | tf_op jit(solution)/shard_map/ppermute | solution.py:335
  7.9 0.7 %copy-start.10 = (f32[64]{0:T(128)S(1)}, f32[64]{0:T(128)}, u32[]{:S(2)}) copy-start(f32[64]{0:T(128)} %param.16) | copy-start | bytes 772
  8.6 0.7 %copy-start.11 = (f32[16]{0:T(128)S(1)}, f32[16]{0:T(128)}, u32[]{:S(2)}) copy-start(f32[16]{0:T(128)} %param.18) | copy-start | bytes 196
  12.0 19.3 %collective-permute-start.2 = (bf16[12,16,128]{2,1,0:T(8,128)(2,1)S(1)}, bf16[12,16,128]{2,1,0:T(8,128)(2,1)S(1)}, u32[]{:S(2)}, u32[]{:S(2)}) collective-permute-start(bf16[12,16,128]{2,1,0:T(8,128)(2,1)S(1)} %get-tuple-element.23.east_ref), channel_id=1, source_target_pairs={{0,1},{1,2},{2,3},{3,4},{4,5},{5,6},{6,7},{8,9},{9,10},{10,11},{11... | collective-permute-start | bytes 147464 | tf_op jit(solution)/shard_map/ppermute | solution.py:335
  15.4 15.8 %collective-permute-start.3 = (bf16[12,16,128]{2,1,0:T(8,128)(2,1)S(1)}, bf16[12,16,128]{2,1,0:T(8,128)(2,1)S(1)}, u32[]{:S(2)}, u32[]{:S(2)}) collective-permute-start(bf16[12,16,128]{2,1,0:T(8,128)(2,1)S(1)} %get-tuple-element.22.west_ref), channel_id=1, source_target_pairs={{1,0},{2,1},{3,2},{4,3},{5,4},{6,5},{7,6},{9,8},{10,9},{11,10},{12... | collective-permute-start | bytes 147464 | tf_op jit(solution)/shard_map/ppermute | solution.py:335
  16.7 14.5 %copy-start.1 = (bf16[6,16,1,8,128]{4,3,2,1,0:T(8,128)(2,1)S(1)}, bf16[6,16,1,8,128]{4,3,2,1,0:T(8,128)(2,1)}, u32[]{:S(2)}) copy-start(bf16[6,16,1,8,128]{4,3,2,1,0:T(8,128)(2,1)} %param.11) | copy-start | bytes 589828
  16.8 14.5 %copy-start.3 = (bf16[6,16,1,8,128]{4,3,2,1,0:T(8,128)(2,1)S(1)}, bf16[6,16,1,8,128]{4,3,2,1,0:T(8,128)(2,1)}, u32[]{:S(2)}) copy-start(bf16[6,16,1,8,128]{4,3,2,1,0:T(8,128)(2,1)} %param.12) | copy-start | bytes 589828
  31.3 0.7 %copy-start.8 = (s32[6]{0:T(128)S(1)}, s32[6]{0:T(128)}, u32[]{:S(2)}) copy-start(s32[6]{0:T(128)} %refs_7_.1) | copy-start | bytes 76
  31.9 16.5 %copy-start.7 = (s32[1,8,128]{2,1,0:T(8,128)S(1)}, s32[1,8,128]{2,1,0:T(8,128)}, u32[]{:S(2)}) copy-start(s32[1,8,128]{2,1,0:T(8,128)} %param.21) | copy-start | bytes 12292
  41.8 6.6 %copy-start.6 = (f32[2,1,8,128]{3,2,1,0:T(8,128)S(1)}, f32[2,1,8,128]{3,2,1,0:T(8,128)}, u32[]{:S(2)}) copy-start(f32[2,1,8,128]{3,2,1,0:T(8,128)} %param.20) | copy-start | bytes 24580
  41.8 4.5 %collective-permute-start.4 = (f32[2,8,128]{2,1,0:T(8,128)S(1)}, f32[2,8,128]{2,1,0:T(8,128)S(1)}, u32[]{:S(2)}, u32[]{:S(2)}) collective-permute-start(f32[2,8,128]{2,1,0:T(8,128)S(1)} %get-tuple-element.24.refs_0_), channel_id=1, source_target_pairs={{0,8},{8,16},{16,24},{24,0},{1,9},{9,17},{17,25},{25,1},{2,10},{10... | collective-permute-start | bytes 24584 | tf_op jit(solution)/shard_map/ppermute | solution.py:361
  44.8 3.7 %collective-permute-start.5 = (f32[2,8,128]{2,1,0:T(8,128)S(1)}, f32[2,8,128]{2,1,0:T(8,128)S(1)}, u32[]{:S(2)}, u32[]{:S(2)}) collective-permute-start(f32[2,8,128]{2,1,0:T(8,128)S(1)} %get-tuple-element.24.refs_0_), channel_id=1, source_target_pairs={{0,16},{8,24},{16,0},{24,8},{1,17},{9,25},{17,1},{25,9},{2,18},{10... | collective-permute-start | bytes 24584 | tf_op jit(solution)/shard_map/ppermute | solution.py:361
  44.9 3.5 %collective-permute-start.6 = (f32[2,8,128]{2,1,0:T(8,128)S(1)}, f32[2,8,128]{2,1,0:T(8,128)S(1)}, u32[]{:S(2)}, u32[]{:S(2)}) collective-permute-start(f32[2,8,128]{2,1,0:T(8,128)S(1)} %get-tuple-element.24.refs_0_), channel_id=1, source_target_pairs={{0,24},{8,0},{16,8},{24,16},{1,25},{9,1},{17,9},{25,17},{2,26},{10... | collective-permute-start | bytes 24584 | tf_op jit(solution)/shard_map/ppermute | solution.py:361

commit v2 on v0

v2 whole, which is shorter than its diff:
```python
import jax
import jax.numpy as jnp
from jax import lax
from jax.experimental import pallas as pl
from jax.experimental.pallas import tpu as pltpu
from jax.sharding import PartitionSpec as P

BF = jnp.bfloat16
F32 = jnp.float32
LANES = 128
DEPTH = 3
PITCH = 16
VMEM = pl.BlockSpec(memory_space=pltpu.VMEM)
SMEM = pl.BlockSpec(memory_space=pltpu.SMEM)
ANYWHERE = pl.BlockSpec(memory_space=pltpu.HBM)
LIMIT = 24 * 1024 * 1024


def shape_of(dims, kind):
    return jax.ShapeDtypeStruct(dims, kind)


def call(kernel, name, outs, specs, scratch=(), cost=None, alias=None, out_specs=None):
    return pl.pallas_call(
        kernel,
        out_shape=outs,
        in_specs=specs,
        out_specs=out_specs or (VMEM,) * len(outs),
        scratch_shapes=list(scratch),
        input_output_aliases=alias or {},
        compiler_params=pltpu.CompilerParams(vmem_limit_bytes=LIMIT),
        cost_estimate=cost and pl.CostEstimate(flops=cost, bytes_accessed=1_000_000, transcendentals=0),
        name=name,
    )


def silu(v):
    half = 0.5 * v
    return half + half * jnp.tanh(half)


def lanes(shape):
    return lax.broadcasted_iota(jnp.int32, shape, len(shape) - 1)


def turn(v, steps):
    steps = steps % LANES
    return pltpu.roll(v, steps, 1) if steps else v


def tile(i):
    return slice(i * LANES, (i + 1) * LANES)


def is_even(axis):
    return lax.axis_index(axis) % 2 == 0


def rows_kernel(state_ref, own_ref, first_ref, second_ref, raw, scr, sems):
    frames, chans, rows, _ = state_ref.shape
    copies = [pltpu.make_async_copy(state_ref.at[f], raw.at[f], sems.at[f]) for f in range(frames)]
    for c in copies:
        c.start()
    for f in range(frames):
        copies[f].wait()
        scr[f] = raw[f].astype(F32).reshape(chans * rows, LANES)
        for y in range(rows):
            own_ref[f, :, tile(y)] = scr[f, pl.ds(y, chans, stride=rows), :].astype(BF)
    even = is_even("tm")
    to_first = jnp.where(even, frames - DEPTH, 0)
    to_second = jnp.where(even, 0, frames - DEPTH)
    for f in range(DEPTH):
        first_ref[f] = own_ref[to_first + f]
        second_ref[f] = own_ref[to_second + f]


def make_rows(state):
    frames, chans, rows, _ = state.shape
    slab = shape_of((DEPTH, chans, rows * LANES), BF)
    return call(
        rows_kernel,
        "rows",
        (shape_of((frames, chans, rows * LANES), BF), slab, slab),
        [ANYWHERE],
        [
            pltpu.VMEM(state.shape, BF),
            pltpu.VMEM((frames, chans * rows, LANES), F32),
            pltpu.SemaphoreType.DMA((frames,)),
        ],
    )(state)


def column(ref):
    n = ref.shape[1]
    return jnp.broadcast_to(ref[...], (8, n)).T[:, 0:1]


def weights_kernel(
    w1_ref, w2_ref, w3_ref, b1_ref, b2_ref, b3_ref,
    m1_ref, m2_ref, m3_ref, s1_ref, s2_ref, s3_ref, c1_ref, c2_ref, c3_ref, r1, r2, r3, sems,
):
    copies = [
        pltpu.make_async_copy(a, b, sems.at[i])
        for i, (a, b) in enumerate(((w1_ref, r1), (w2_ref, r2), (w3_ref, r3)))
    ]
    for c in copies:
        c.start()
    c1_ref[...], c2_ref[...], c3_ref[...] = column(b1_ref), column(b2_ref), column(b3_ref)
    for ref in (m1_ref, m2_ref, m3_ref, s1_ref, s2_ref, s3_ref):
        ref[...] = jnp.zeros_like(ref)
    hid = c1_ref.shape[0]
    chans = r1.shape[0] // 27
    fields = c3_ref.shape[0]
    frames = m3_ref.shape[0] // fields
    copies[0].wait()
    flat = r1[...].astype(F32).T.astype(BF)
    for p in range(2):
        m1_ref[p * hid : (p + 1) * hid, p * 9 * chans : (p + 3) * 9 * chans] = flat
        for dt in range(3):
            for dy in range(3):
                at = (dt * 3 + dy) * 3 * chans
                s1_ref[(p * 3 + dy) * hid : (p * 3 + dy + 1) * hid, (dt + p) * 3 * chans : (dt + p + 1) * 3 * chans] = (
                    flat[:, at : at + 3 * chans]
                )

    def place(raw, main, side, count, outs):
        for dt in range(3):
            for dy in range(3):
                for dx in range(3):
                    w = raw[(dt * 3 + dy) * 3 + dx]
                    for p in range(count):
                        at = (((dt + p) * 3 + dy) * 3 + dx) * hid
                        main[p * outs : (p + 1) * outs, at : at + hid] = w
                        at = ((dt + p) * 3 + dx) * hid
                        side[(p * 3 + dy) * outs : (p * 3 + dy + 1) * outs, at : at + hid] = w

    copies[1].wait()
    place(r2, m2_ref, s2_ref, 2, hid)
    copies[2].wait()
    place(r3, m3_ref, s3_ref, frames, fields)


def make_weights(w1, w2, w3, b1, b2, b3, frames):
    hid, fields, chans = w2.shape[1], w3.shape[1], w1.shape[0] // 27
    return call(
        weights_kernel,
        "weights",
        (
            shape_of((2 * hid, 4 * 9 * chans), BF),
            shape_of((2 * hid, 4 * 9 * hid), BF),
            shape_of((frames * fields, (frames + 2) * 9 * hid), BF),
            shape_of((6 * hid, 4 * 3 * chans), BF),
            shape_of((6 * hid, 4 * 3 * hid), BF),
            shape_of((frames * 3 * fields, (frames + 2) * 3 * hid), BF),
            shape_of((hid, 1), F32),
            shape_of((hid, 1), F32),
            shape_of((fields, 1), F32),
        ),
        [ANYWHERE] * 3 + [VMEM] * 3,
        [pltpu.VMEM(w.shape, BF) for w in (w1, w2, w3)] + [pltpu.SemaphoreType.DMA((3,))],
        cost=1_000_000_000,
    )(w1, w2, w3, b1, b2, b3)


def slab_order(frames):
    even = is_even("tm")
    return jnp.where(even, frames + DEPTH, 0), jnp.where(even, 0, frames + DEPTH)


def edges_kernel(own_ref, first_ref, second_ref, west_ref, east_ref, send1_ref, send2_ref):
    frames = own_ref.shape[0]
    rows = own_ref.shape[2] // LANES
    shape = (own_ref.shape[1], LANES)
    lane = lanes(shape)
    group, place = lane // PITCH, lane % PITCH
    at1, at2 = slab_order(frames)
    even = is_even("space")
    for src, base, count in ((own_ref, DEPTH, frames), (first_ref, at1, DEPTH), (second_ref, at2, DEPTH)):
        for f in range(count):
            west = jnp.zeros(shape, BF)
            east = jnp.zeros(shape, BF)
            for y in range(rows):
                v = src[f, :, tile(y)]
                here = group == y
                west = jnp.where(here & (place >= DEPTH), turn(v, y * PITCH + DEPTH), west)
                east = jnp.where(here & (place < PITCH - DEPTH), turn(v, y * PITCH + PITCH - DEPTH), east)
            west_ref[base + f] = west
            east_ref[base + f] = east
            send1_ref[base + f] = jnp.where(even, east, west)
            send2_ref[base + f] = jnp.where(even, west, east)


def make_edges(own, first, second):
    frames, chans, _ = own.shape
    strip = shape_of((frames + 2 * DEPTH, chans, LANES), BF)
    return call(edges_kernel, "edges", (strip,) * 4, [VMEM] * 3)(own, first, second)


def spread(dst, f, y, v):
    chans = v.shape[0]
    at = tile(y + 1)
    dst[f, 0:chans, at] = turn(v, 1)
    dst[f, chans : 2 * chans, at] = v
    dst[f, 2 * chans : 3 * chans, at] = turn(v, -1)


def window(src, f, count, y):
    return jnp.concatenate(
        [src[f + j, :, (y + dy) * LANES : (y + dy + 2) * LANES] for j in range(count) for dy in range(3)], axis=0
    )


def in_trajectory(local, frames):
    step = lax.axis_index("tm") * frames + local
    return (step >= 0) & (step < frames * lax.axis_size("tm"))


def main_kernel(
    own_ref, first_ref, second_ref, m1_ref, m2_ref, m3_ref, c1_ref, c2_ref, score_ref, s1, s2, s3
):
    frames = own_ref.shape[0]
    rows = own_ref.shape[2] // LANES
    hid = c1_ref.shape[0]
    for s in (s1, s2, s3):
        s[:, :, tile(0)] = jnp.zeros(s.shape[:2] + (LANES,), BF)
        s[:, :, tile(rows + 1)] = jnp.zeros(s.shape[:2] + (LANES,), BF)
    at1, at2 = slab_order(frames)
    for src, base, count in ((own_ref, DEPTH, frames), (first_ref, at1, DEPTH), (second_ref, at2, DEPTH)):
        for f in range(count):
            for y in range(rows):
                spread(s1, base + f, y, src[f, :, tile(y)])

    def layer(src, dst, m_ref, c_ref, count, first):
        def step(i, carry):
            f = 2 * i
            for y in range(0, rows, 2):
                acc = jnp.dot(m_ref[...], window(src, f, 4, y), preferred_element_type=F32)
                for p in range(2):
                    h = silu(acc[p * hid : (p + 1) * hid] + c_ref[...]).astype(BF)
                    h = jnp.where(in_trajectory(f + p + first, frames), h, jnp.zeros_like(h))
                    spread(dst, f + p, y, h[:, tile(0)])
                    spread(dst, f + p, y + 1, h[:, tile(1)])
            return carry

        lax.fori_loop(0, count // 2, step, 0, unroll=UNROLL)

    layer(s1, s2, m1_ref, c1_ref, frames + 4, -2)
    layer(s2, s3, m2_ref, c2_ref, frames + 2, -1)
    for y in range(0, rows, 2):
        acc = jnp.dot(m3_ref[...], window(s3, 0, frames + 2, y), preferred_element_type=F32)
        score_ref[y], score_ref[y + 1] = acc[:, tile(0)], acc[:, tile(1)]


UNROLL = False


def make_main(own, first, second, m1, m2, m3, c1, c2):
    frames, chans, width = own.shape
    hid = c1.shape[0]
    wide = width + 2 * LANES
    return call(
        main_kernel,
        "main",
        (shape_of((width // LANES, m3.shape[0], LANES), F32),),
        [VMEM] * 8,
        [
            pltpu.VMEM((frames + 6, 3 * chans, wide), BF),
            pltpu.VMEM((frames + 4, 3 * hid, wide), BF),
            pltpu.VMEM((frames + 2, 3 * hid, wide), BF),
        ],
        cost=5_000_000_000,
    )(own, first, second, m1, m2, m3, c1, c2)[0]


def spread_side(dst, f, v):
    chans = v.shape[0]
    for half in range(2):
        w = v[:, tile(half)]
        dst[f, 0:chans, tile(half)] = turn(w, 1)
        dst[f, chans : 2 * chans, tile(half)] = w
        dst[f, 2 * chans : 3 * chans, tile(half)] = turn(w, -1)


def over_rows(acc, at, outs):
    halves = []
    for half in range(2):
        up, mid, down = (acc[at + d * outs : at + (d + 1) * outs, tile(half)] for d in range(3))
        lane = lanes((outs, LANES))
        up = jnp.where(lane >= PITCH, turn(up, PITCH), 0.0)
        down = jnp.where(lane < LANES - PITCH, turn(down, -PITCH), 0.0)
        halves.append(mid + up + down)
    return jnp.concatenate(halves, axis=1)


def patched(v, west, east, y):
    col = lanes(v.shape)
    v = jnp.where(col < DEPTH, turn(west, -(y * PITCH + DEPTH)), v)
    return jnp.where(col >= LANES - DEPTH, turn(east, DEPTH - (y + 1) * PITCH), v)


def side_kernel(
    score_ref, west_ref, east_ref, first_ref, second_ref, s1_ref, s2_ref, s3_ref, c1_ref, c2_ref, c3_ref,
    state_ref, day_ref, side_ref, part_ref, t1, t2, t3,
):
    frames, fields, rows, _ = state_ref.shape
    chans, hid = west_ref.shape[1], c1_ref.shape[0]
    place = lanes((chans, LANES)) % PITCH
    even = is_even("space")
    for f in range(frames + 2 * DEPTH):
        a, b = first_ref[f], second_ref[f]
        west = jnp.where(place < DEPTH, turn(jnp.where(even, b, a), 2 * DEPTH - PITCH), west_ref[f])
        east = jnp.where(place >= PITCH - DEPTH, turn(jnp.where(even, a, b), PITCH - 2 * DEPTH), east_ref[f])
        spread_side(t1, f, jnp.concatenate([west, east], axis=1))

    me, last = lax.axis_index("space"), lax.axis_size("space") - 1
    pair = lanes((1, 2 * LANES))
    place = pair % PITCH
    outside = ((pair < LANES) & (place < DEPTH) & (me == 0)) | (
        (pair >= LANES) & (place >= PITCH - DEPTH) & (me == last)
    )

    def layer(src, dst, m_ref, c_ref, count, first):
        for f in range(0, count, 2):
            z = jnp.concatenate([src[f + j] for j in range(4)], axis=0)
            acc = jnp.dot(m_ref[...], z, preferred_element_type=F32)
            for p in range(2):
                h = silu(over_rows(acc, p * 3 * hid, hid) + c_ref[...])
                keep = in_trajectory(f + p + first, frames) & ~outside
                spread_side(dst, f + p, jnp.where(keep, h, 0.0).astype(BF))

    layer(t1, t2, s1_ref, c1_ref, frames + 4, -2)
    layer(t2, t3, s2_ref, c2_ref, frames + 2, -1)
    z = jnp.concatenate([t3[j] for j in range(frames + 2)], axis=0)
    acc = jnp.dot(s3_ref[...], z, preferred_element_type=F32)
    for f in range(frames):
        both = over_rows(acc, f * 3 * fields, fields)
        for half in range(2):
            side_ref[half, f * fields : (f + 1) * fields] = both[:, tile(half)]

    days = part_ref.shape[0]
    heads = pl.ds(0, frames, stride=fields)
    west, east = side_ref[0, heads], side_ref[1, heads]
    row = lax.broadcasted_iota(jnp.int32, (frames, LANES), 0)
    day = jnp.zeros((frames, LANES), jnp.int32)
    for f in range(frames):
        day = jnp.where(row == f, day_ref[f], day)
    for y in range(rows):
        v = patched(score_ref[y, heads], west, east, y)
        for d in range(days):
            part_ref[d, y : y + 1, :] = jnp.sum(jnp.where(day == d, v, 0.0), axis=0, keepdims=True)
    base = c3_ref[0:1, 0:1]
    for d in range(days):
        total = 0.5 * part_ref[d]
        for f in range(frames):
            total = total + jnp.where(day_ref[f] == d, state_ref[f, 0].astype(F32) + 0.5 * base, 0.0)
        part_ref[d] = total


def make_side(score, west, east, first, second, s1, s2, s3, c1, c2, c3, state, day, days):
    frames, fields, rows, _ = state.shape
    chans, hid = west.shape[1], c1.shape[0]
    return call(
        side_kernel,
        "side",
        (shape_of((2, frames * fields, LANES), F32), shape_of((days, rows, LANES), F32)),
        [VMEM] * 12 + [SMEM],
        [
            pltpu.VMEM((frames + 6, 3 * chans, 2 * LANES), BF),
            pltpu.VMEM((frames + 4, 3 * hid, 2 * LANES), BF),
            pltpu.VMEM((frames + 2, 3 * hid, 2 * LANES), BF),
        ],
    )(score, west, east, first, second, s1, s2, s3, c1, c2, c3, state, day)


def update_kernel(score_ref, side_ref, c3_ref, state_ref, noise_ref, out_ref, head_ref, scr):
    frames, fields, rows, _ = state_ref.shape
    for f in range(frames):
        at = slice(f * fields, (f + 1) * fields)
        west, east = side_ref[0, at], side_ref[1, at]
        for y in range(rows):
            scr[f, pl.ds(y, fields, stride=rows), :] = (
                patched(score_ref[y, at], west, east, y) + c3_ref[...]
            )
        score = scr[f].reshape(fields, rows, LANES)
        moved = state_ref[f].astype(F32) + 0.8 * score + 0.5 * noise_ref[f].astype(F32)
        out_ref[f] = moved.astype(BF)
        head_ref[f] = moved[0]


def make_update(score, side, c3, state, noise):
    frames, fields, rows, _ = state.shape
    return call(
        update_kernel,
        "update",
        (shape_of(state.shape, BF), shape_of((frames, rows, LANES), F32)),
        [VMEM] * 5,
        [pltpu.VMEM((frames, fields * rows, LANES), F32)],
        cost=1_000_000_000,
    )(score, side, c3, state, noise)


def correct_kernel(mine_ref, theirs_ref, observed_ref, mask_ref, head_ref, day_ref, _, out_ref, buf, sem):
    frames = head_ref.shape[0]
    days = observed_ref.shape[0]
    mask = mask_ref[...].astype(F32)
    misfit = [0.15 * (mask * (mine_ref[d] + theirs_ref[d] - observed_ref[d])) for d in range(days)]
    for f in range(frames):
        v = head_ref[f]
        for d in range(days):
            v = v - jnp.where(day_ref[f] == d, misfit[d], 0.0)
        buf[f, 0] = v.astype(BF)
    copy = pltpu.make_async_copy(buf, out_ref.at[:, 0:1], sem)
    copy.start()
    copy.wait()


def make_correct(mine, theirs, observed, mask, head, day, out):
    frames, rows, _ = head.shape
    return call(
        correct_kernel,
        "correct",
        (shape_of(out.shape, BF),),
        [VMEM] * 5 + [SMEM, ANYWHERE],
        [pltpu.VMEM((frames, 1, rows, LANES), BF), pltpu.SemaphoreType.DMA],
        alias={6: 0},
        out_specs=(ANYWHERE,),
    )(mine, theirs, observed, mask, head, day, out)[0]


def exchanged(value, axis, start):
    pairs = [(i, i + 1) for i in range(start, lax.axis_size(axis) - 1, 2)]
    return lax.ppermute(value, axis, pairs + [(j, i) for i, j in pairs])


def body(
    state, noise, conv_one, bias_one, conv_two, bias_two, conv_three, bias_three, day_of_frame, observed, obs_mask
):
    state, noise = state[:, :, 0], noise[:, :, 0]
    hid, chans = conv_one.shape[:2]
    fields = conv_three.shape[0]
    w1 = conv_one.transpose(2, 3, 4, 1, 0).reshape(27 * chans, hid)
    w2 = conv_two.transpose(2, 3, 4, 0, 1).reshape(27, hid, hid)
    w3 = conv_three.transpose(2, 3, 4, 0, 1).reshape(27, fields, hid)
    own, send1, send2 = make_rows(state)
    first, second = exchanged(send1, "tm", 0), exchanged(send2, "tm", 1)
    m1, m2, m3, s1, s2, s3, c1, c2, c3 = make_weights(
        w1, w2, w3, bias_one[None], bias_two[None], bias_three[None], state.shape[0]
    )
    west, east, send1, send2 = make_edges(own, first, second)
    near, far = exchanged(send1, "space", 0), exchanged(send2, "space", 1)
    score = make_main(own, first, second, m1, m2, m3, c1, c2)
    side, mine = make_side(
        score, west, east, near, far, s1, s2, s3, c1, c2, c3, state, day_of_frame, observed.shape[0]
    )
    out, head = make_update(score, side, c3, state, noise)
    count = lax.axis_size("tm")
    reach = 1
    while True:
        theirs = lax.ppermute(mine, "tm", [(i, i ^ reach) for i in range(count)])
        reach *= 2
        if reach >= count:
            break
        mine = mine + theirs
    out = make_correct(mine, theirs, observed[:, 0], obs_mask[0], head, day_of_frame, out)
    return out[:, :, None]


def solution(mesh):
    in_specs = (
        P("tm", None, "space", None, None),
        P("tm", None, "space", None, None),
        P(),
        P(),
        P(),
        P(),
        P(),
        P(),
        P("tm"),
        P(None, "space", None, None),
        P("space", None, None),
    )
    out_specs = P("tm", None, "space", None, None)
    return jax.shard_map(body, mesh=mesh, in_specs=in_specs, out_specs=out_specs, check_vma=False)
```

time: 152 us -> 32.2 us (0.21)
  the two profiles are of different devices: /device:TPU:0 before, /device:TPU:20 now
where the time goes in v2:
time: 32.2 us; the launch traced here: 32 us
  Pallas kernels  16.2 us (50%)
  starting transfers between devices  9.52 us (30%)
  local copies, waits for them, and re-layouts  4.15 us (13%)
  waiting for transfers between devices  1.98 us (6%)
    pallas_call x1, Pallas kernels, make_main(): call(main_kernel, 'main', (shape_of((width // LANES, m3.shape[0], LANES),...  8.69 us
    ppermute x4, starting transfers between devices, exchanged(): return lax.ppermute(value, axis, pairs + [(j, i) for i, j in pairs])  5.74 us
    unnamed x24, local copies, waits for them, and re-layouts  4.15 us
    ppermute x2, starting transfers between devices, body(): theirs = lax.ppermute(mine, 'tm', [(i, i ^ reach) for i in range(count)])  3.78 us
    pallas_call x1, Pallas kernels, make_side(): call(side_kernel, 'side', (shape_of((2, frames * fields, LANES), F32), sh...  3.03 us
    ppermute x2, waiting for transfers between devices, body(): theirs = lax.ppermute(mine, 'tm', [(i, i ^ reach) for i in range(count)])  1.97 us
    pallas_call x1, Pallas kernels, make_weights(): call(weights_kernel, 'weights', (shape_of((2 * hid, 4 * 9 * chans), BF),...  1.5 us
    pallas_call x1, Pallas kernels, make_correct(): call(correct_kernel, 'correct', (shape_of(out.shape, BF),), [VMEM] * 5 +...  1.17 us
  transfers between devices with their start and end apart: 6, of which 2 were waited for; matrix products, arithmetic and copies ran while one was open for 0% of the time, Pallas kernels for 35%

profile of v2, /device:TPU:20, one launch (start us, length us, event | category | flops | bytes accessed | tf_op | source)
XLA Modules:
  0.0 32.0 jit_solution(3505740907748813894)
XLA Ops:
  0.0 0.9 %copy-done = bf16[6,16,1,8,128]{4,3,2,1,0:T(8,128)(2,1)S(1)} copy-done((bf16[6,16,1,8,128]{4,3,2,1,0:T(8,128)(2,1)S(1)}, bf16[6,16,1,8,128]{4,3,2,1,0:T(8,128)(2,1)}, u32[]{:S(2)}) %copy-start) | copy-done | bytes 196632
  0.9 0.4 %rows.1 = (bf16[6,16,1024]{2,1,0:T(8,128)(2,1)S(1)}, bf16[3,16,1024]{2,1,0:T(8,128)(2,1)S(1)}, bf16[3,16,1024]{2,1,0:T(8,128)(2,1)S(1)}) custom-call(bf16[6,16,8,128]{3,2,1,0:T(8,128)(2,1)S(1)} %bitcast.19), custom_call_target="tpu_custom_call" | custom-call | tf_op jit(solution)/shard_map/rows/pallas_call | solution.py:80
  1.4 0.1 collective-permute-start
  1.5 0.7 %collective-permute-start.1 = (bf16[3,16,1024]{2,1,0:T(8,128)(2,1)S(1)}, bf16[3,16,1024]{2,1,0:T(8,128)(2,1)S(1)}, u32[]{:S(2)}, u32[]{:S(2)}) collective-permute-start(bf16[3,16,1024]{2,1,0:T(8,128)(2,1)S(1)} %get-tuple-element.27), channel_id=1, source_target_pairs={{8,16},{16,8},{9,17},{17,9},{10,18},{18,10},{11,19},{19,11},{12,20... | collective-permute-start | bytes 294920 | tf_op jit(solution)/shard_map/ppermute | solution.py:432
  2.1 0.0 copy-start.9
  2.1 0.0 copy-start.10
  2.1 0.0 copy-start.11
  2.2 0.6 %copy-done.9 = f32[64]{0:T(128)S(1)} copy-done((f32[64]{0:T(128)S(1)}, f32[64]{0:T(128)}, u32[]{:S(2)}) %copy-start.9) | copy-done | bytes 280
  2.8 0.0 copy-done.10
  2.8 0.0 copy-done.11
  2.8 1.0 %copy-done.5 = bf16[64,64,3,3,3]{1,0,4,3,2:T(8,128)(2,1)S(1)} copy-done((bf16[64,64,3,3,3]{1,0,4,3,2:T(8,128)(2,1)S(1)}, bf16[64,64,3,3,3]{1,0,4,3,2:T(8,128)(2,1)}, u32[]{:S(2)}) %copy-start.5) | copy-done | bytes 221208
  3.8 0.9 %copy-done.8 = bf16[16,64,3,3,3]{1,0,4,3,2:T(8,128)(2,1)S(1)} copy-done((bf16[16,64,3,3,3]{1,0,4,3,2:T(8,128)(2,1)S(1)}, bf16[16,64,3,3,3]{1,0,4,3,2:T(8,128)(2,1)}, u32[]{:S(2)}) %copy-start.8) | copy-done | bytes 55320
  4.7 1.5 %weights.1 = (bf16[128,576]{1,0:T(8,128)(2,1)S(1)}, bf16[128,2304]{1,0:T(8,128)(2,1)S(1)}, bf16[96,4608]{1,0:T(8,128)(2,1)S(1)}, bf16[384,192]{1,0:T(8,128)(2,1)...) custom-call(bf16[432,64]{1,0:T(8,128)(2,1)S(1)} %bitcast.26, ...), custom_call_target="tpu_custom_call" | custom-call | flops 1000000000 | bytes 1000000 | tf_op jit(solution)/shard_map/weights/pallas_call | solution.py:145
  6.2 0.0 collective-permute-done.first_ref
  6.2 0.0 collective-permute-done.1.second_ref
  6.3 0.3 edges.1
  6.5 0.6 %collective-permute-start.2 = (bf16[12,16,128]{2,1,0:T(8,128)(2,1)S(1)}, bf16[12,16,128]{2,1,0:T(8,128)(2,1)S(1)}, u32[]{:S(2)}, u32[]{:S(2)}) collective-permute-start(bf16[12,16,128]{2,1,0:T(8,128)(2,1)S(1)} %get-tuple-element.35), channel_id=1, source_target_pairs={{0,1},{2,3},{4,5},{6,7},{1,0},{3,2},{5,4},{7,6},{8,9},{10,11},{12,... | collective-permute-start | bytes 147464 | tf_op jit(solution)/shard_map/ppermute | solution.py:432
  7.1 4.4 %collective-permute-start.3 = (bf16[12,16,128]{2,1,0:T(8,128)(2,1)S(1)}, bf16[12,16,128]{2,1,0:T(8,128)(2,1)S(1)}, u32[]{:S(2)}, u32[]{:S(2)}) collective-permute-start(bf16[12,16,128]{2,1,0:T(8,128)(2,1)S(1)} %get-tuple-element.36), channel_id=1, source_target_pairs={{1,2},{3,4},{5,6},{2,1},{4,3},{6,5},{9,10},{11,12},{13,14},{10,9},... | collective-permute-start | bytes 147464 | tf_op jit(solution)/shard_map/ppermute | solution.py:432
  11.5 0.0 copy-start.1
  11.6 8.7 %main.1.score_ref = f32[8,96,128]{2,1,0:T(8,128)S(1)} custom-call(bf16[6,16,1024]{2,1,0:T(8,128)(2,1)S(1)} %get-tuple-element.25.own_ref, bf16[3,16,1024]{2,1,0:T(8,128)(2,1)S(1)} %collective-permute-done.first_ref, bf16[3,16,1024]{2,1,0:T(8,128)(2,1)S(1)} %collective-permute-done.1.second_ref, bf16[128,576]{1,0:T(8,128)(2,1)S(1)} %get-tuple-element.28.m1_ref, ...), custom_call_target="tpu_custom_call" | custom-call | flops 5000000000 | bytes 1000000 | tf_op jit(solution)/shard_map/main/pallas_call | solution.py:261
  20.2 0.0 collective-permute-done.2.first_ref
  20.3 0.0 collective-permute-done.3.second_ref
  20.3 0.0 copy-start.4
  20.3 0.6 %copy-done.4 = s32[6]{0:T(128)S(1)} copy-done((s32[6]{0:T(128)S(1)}, s32[6]{0:T(128)}, u32[]{:S(2)}) %copy-start.4) | copy-done | bytes 48
  20.9 3.0 %side.1 = (f32[2,96,128]{2,1,0:T(8,128)S(1)}, f32[2,8,128]{2,1,0:T(8,128)S(1)}) custom-call(f32[8,96,128]{2,1,0:T(8,128)S(1)} %main.1.score_ref, bf16[12,16,128]{2,1,0:T(8,128)(2,1)S(1)} %get-tuple-element.33.west_ref, bf16[12,16,128]{2,1,0:T(8,128)(2,1)S(1)} %get-tuple-element.34.east_ref, bf16[12,16,128]{2,1,0:T(8,128)(2,1)S(1)} %collective-permute-done.2.first_ref, ...), custom_call_target="tpu_custom_call" | custom-call | tf_op jit(solution)/shard_map/side/pallas_call | solution.py:362
  24.0 2.4 %collective-permute-start.4 = (f32[2,8,128]{2,1,0:T(8,128)S(1)}, f32[2,8,128]{2,1,0:T(8,128)S(1)}, u32[]{:S(2)}, u32[]{:S(2)}) collective-permute-start(f32[2,8,128]{2,1,0:T(8,128)S(1)} %get-tuple-element.41), channel_id=1, source_target_pairs={{0,8},{8,0},{16,24},{24,16},{1,9},{9,1},{17,25},{25,17},{2,10},{10... | collective-permute-start | bytes 24584 | tf_op jit(solution)/shard_map/ppermute | solution.py:459
  26.3 0.8 %collective-permute-done.4 = f32[2,8,128]{2,1,0:T(8,128)S(1)} collective-permute-done((f32[2,8,128]{2,1,0:T(8,128)S(1)}, f32[2,8,128]{2,1,0:T(8,128)S(1)}, u32[]{:S(2)}, u32[]{:S(2)}) %collective-permute-start.4) | collective-permute-done | bytes 8224 | tf_op jit(solution)/shard_map/ppermute | solution.py:459
  27.2 1.4 %collective-permute-start.5 = (f32[2,8,128]{2,1,0:T(8,128)S(1)}, f32[2,8,128]{2,1,0:T(8,128)S(1)}, u32[]{:S(2)}, u32[]{:S(2)}) collective-permute-start(f32[2,8,128]{2,1,0:T(8,128)S(1)} %add.3.mine_ref), channel_id=1, source_target_pairs={{0,16},{8,24},{16,0},{24,8},{1,17},{9,25},{17,1},{25,9},{2,18},{10... | collective-permute-start | bytes 24584 | tf_op jit(solution)/shard_map/ppermute | solution.py:459
  28.6 0.0 copy-done.6
  28.6 1.1 %update.1 = (bf16[6,16,8,128]{3,2,1,0:T(8,128)(2,1)}, f32[6,8,128]{2,1,0:T(8,128)S(1)}) custom-call(f32[8,96,128]{2,1,0:T(8,128)S(1)} %main.1.score_ref, f32[2,96,128]{2,1,0:T(8,128)S(1)} %get-tuple-element.42.side_ref, f32[16,1]{1,0:T(8,128)S(1)} %get-tuple-element.40.c3_ref, bf16[6,16,8,128]{3,2,1,0:T(8,128)(2,1)S(1)} %bitcast.21, ...), custom_call_target="tpu_custom_call" | custom-call | flops 1000000000 | bytes 1000000 | tf_op jit(solution)/shard_map/update/pallas_call | solution.py:392
  29.7 1.1 %collective-permute-done.5.theirs_ref = f32[2,8,128]{2,1,0:T(8,128)S(1)} collective-permute-done((f32[2,8,128]{2,1,0:T(8,128)S(1)}, f32[2,8,128]{2,1,0:T(8,128)S(1)}, u32[]{:S(2)}, u32[]{:S(2)}) %collective-permute-start.5) | collective-permute-done | bytes 8224 | tf_op jit(solution)/shard_map/ppermute | solution.py:459
  30.8 1.2 %correct.1 = bf16[6,16,8,128]{3,2,1,0:T(8,128)(2,1)} custom-call(f32[2,8,128]{2,1,0:T(8,128)S(1)} %add.3.mine_ref, f32[2,8,128]{2,1,0:T(8,128)S(1)} %collective-permute-done.5.theirs_ref, f32[2,8,128]{2,1,0:T(8,128)S(1)} %bitcast.22, s32[8,128]{1,0:T(8,128)S(1)} %bitcast.23, ...), custom_call_target="tpu_custom_call", output_to_operand_aliasing={{}: (6, {})} | custom-call | tf_op jit(solution)/shard_map/correct/pallas_call | solution.py:419
  (12 shorter events, 0.0 us)
Async XLA Ops:
  0.0 0.9 %copy-start = (bf16[6,16,1,8,128]{4,3,2,1,0:T(8,128)(2,1)S(1)}, bf16[6,16,1,8,128]{4,3,2,1,0:T(8,128)(2,1)}, u32[]{:S(2)}) copy-start(bf16[6,16,1,8,128]{4,3,2,1,0:T(8,128)(2,1)} %param.11) | copy-start | bytes 589828
  0.9 1.2 %copy-start.7 = (bf16[64,16,3,3,3]{0,1,4,3,2:T(8,128)(2,1)S(1)}, bf16[64,16,3,3,3]{0,1,4,3,2:T(8,128)(2,1)}, u32[]{:S(2)}) copy-start(bf16[64,16,3,3,3]{0,1,4,3,2:T(8,128)(2,1)} %param.13) | copy-start | bytes 165892
  1.4 4.9 %collective-permute-start = (bf16[3,16,1024]{2,1,0:T(8,128)(2,1)S(1)}, bf16[3,16,1024]{2,1,0:T(8,128)(2,1)S(1)}, u32[]{:S(2)}, u32[]{:S(2)}) collective-permute-start(bf16[3,16,1024]{2,1,0:T(8,128)(2,1)S(1)} %get-tuple-element.26), channel_id=1, source_target_pairs={{0,8},{16,24},{8,0},{24,16},{1,9},{17,25},{9,1},{25,17},{2,10},{18... | collective-permute-start | bytes 294920 | tf_op jit(solution)/shard_map/ppermute | solution.py:432
  1.5 4.8 %collective-permute-start.1 = (bf16[3,16,1024]{2,1,0:T(8,128)(2,1)S(1)}, bf16[3,16,1024]{2,1,0:T(8,128)(2,1)S(1)}, u32[]{:S(2)}, u32[]{:S(2)}) collective-permute-start(bf16[3,16,1024]{2,1,0:T(8,128)(2,1)S(1)} %get-tuple-element.27), channel_id=1, source_target_pairs={{8,16},{16,8},{9,17},{17,9},{10,18},{18,10},{11,19},{19,11},{12,20... | collective-permute-start | bytes 294920 | tf_op jit(solution)/shard_map/ppermute | solution.py:432
  2.1 0.7 %copy-start.9 = (f32[64]{0:T(128)S(1)}, f32[64]{0:T(128)}, u32[]{:S(2)}) copy-start(f32[64]{0:T(128)} %param.14) | copy-start | bytes 772
  2.1 0.7 %copy-start.10 = (f32[64]{0:T(128)S(1)}, f32[64]{0:T(128)}, u32[]{:S(2)}) copy-start(f32[64]{0:T(128)} %param.16) | copy-start | bytes 772
  2.1 0.7 %copy-start.11 = (f32[16]{0:T(128)S(1)}, f32[16]{0:T(128)}, u32[]{:S(2)}) copy-start(f32[16]{0:T(128)} %param.18) | copy-start | bytes 196
  2.8 1.0 %copy-start.5 = (bf16[64,64,3,3,3]{1,0,4,3,2:T(8,128)(2,1)S(1)}, bf16[64,64,3,3,3]{1,0,4,3,2:T(8,128)(2,1)}, u32[]{:S(2)}) copy-start(bf16[64,64,3,3,3]{1,0,4,3,2:T(8,128)(2,1)} %param.15) | copy-start | bytes 663556
  3.8 0.9 %copy-start.8 = (bf16[16,64,3,3,3]{1,0,4,3,2:T(8,128)(2,1)S(1)}, bf16[16,64,3,3,3]{1,0,4,3,2:T(8,128)(2,1)}, u32[]{:S(2)}) copy-start(bf16[16,64,3,3,3]{1,0,4,3,2:T(8,128)(2,1)} %param.17) | copy-start | bytes 165892
  6.5 13.7 %collective-permute-start.2 = (bf16[12,16,128]{2,1,0:T(8,128)(2,1)S(1)}, bf16[12,16,128]{2,1,0:T(8,128)(2,1)S(1)}, u32[]{:S(2)}, u32[]{:S(2)}) collective-permute-start(bf16[12,16,128]{2,1,0:T(8,128)(2,1)S(1)} %get-tuple-element.35), channel_id=1, source_target_pairs={{0,1},{2,3},{4,5},{6,7},{1,0},{3,2},{5,4},{7,6},{8,9},{10,11},{12,... | collective-permute-start | bytes 147464 | tf_op jit(solution)/shard_map/ppermute | solution.py:432
  7.1 13.2 %collective-permute-start.3 = (bf16[12,16,128]{2,1,0:T(8,128)(2,1)S(1)}, bf16[12,16,128]{2,1,0:T(8,128)(2,1)S(1)}, u32[]{:S(2)}, u32[]{:S(2)}) collective-permute-start(bf16[12,16,128]{2,1,0:T(8,128)(2,1)S(1)} %get-tuple-element.36), channel_id=1, source_target_pairs={{1,2},{3,4},{5,6},{2,1},{4,3},{6,5},{9,10},{11,12},{13,14},{10,9},... | collective-permute-start | bytes 147464 | tf_op jit(solution)/shard_map/ppermute | solution.py:432
  11.5 8.7 %copy-start.1 = (bf16[6,16,1,8,128]{4,3,2,1,0:T(8,128)(2,1)S(1)}, bf16[6,16,1,8,128]{4,3,2,1,0:T(8,128)(2,1)}, u32[]{:S(2)}) copy-start(bf16[6,16,1,8,128]{4,3,2,1,0:T(8,128)(2,1)} %param.11) | copy-start | bytes 589828
  20.3 0.7 %copy-start.4 = (s32[6]{0:T(128)S(1)}, s32[6]{0:T(128)}, u32[]{:S(2)}) copy-start(s32[6]{0:T(128)} %day_ref.3) | copy-start | bytes 76
  20.9 7.7 %copy-start.6 = (bf16[6,16,1,8,128]{4,3,2,1,0:T(8,128)(2,1)S(1)}, bf16[6,16,1,8,128]{4,3,2,1,0:T(8,128)(2,1)}, u32[]{:S(2)}) copy-start(bf16[6,16,1,8,128]{4,3,2,1,0:T(8,128)(2,1)} %param.12) | copy-start | bytes 589828
  24.0 3.2 %collective-permute-start.4 = (f32[2,8,128]{2,1,0:T(8,128)S(1)}, f32[2,8,128]{2,1,0:T(8,128)S(1)}, u32[]{:S(2)}, u32[]{:S(2)}) collective-permute-start(f32[2,8,128]{2,1,0:T(8,128)S(1)} %get-tuple-element.41), channel_id=1, source_target_pairs={{0,8},{8,0},{16,24},{24,16},{1,9},{9,1},{17,25},{25,17},{2,10},{10... | collective-permute-start | bytes 24584 | tf_op jit(solution)/shard_map/ppermute | solution.py:459
  27.2 3.7 %collective-permute-start.5 = (f32[2,8,128]{2,1,0:T(8,128)S(1)}, f32[2,8,128]{2,1,0:T(8,128)S(1)}, u32[]{:S(2)}, u32[]{:S(2)}) collective-permute-start(f32[2,8,128]{2,1,0:T(8,128)S(1)} %add.3.mine_ref), channel_id=1, source_target_pairs={{0,16},{8,24},{16,0},{24,8},{1,17},{9,25},{17,1},{25,9},{2,18},{10... | collective-permute-start | bytes 24584 | tf_op jit(solution)/shard_map/ppermute | solution.py:459
  28.6 2.2 %copy-start.2 = (f32[2,1,8,128]{3,2,1,0:T(8,128)S(1)}, f32[2,1,8,128]{3,2,1,0:T(8,128)}, u32[]{:S(2)}) copy-start(f32[2,1,8,128]{3,2,1,0:T(8,128)} %param.20) | copy-start | bytes 24580
  29.7 1.1 %copy-start.3 = (s32[1,8,128]{2,1,0:T(8,128)S(1)}, s32[1,8,128]{2,1,0:T(8,128)}, u32[]{:S(2)}) copy-start(s32[1,8,128]{2,1,0:T(8,128)} %param.21) | copy-start | bytes 12292

commit v3 on v2

--- a/solution.py
+++ b/solution.py
@@ -11,7 +11,6 @@
 DEPTH = 3
 PITCH = 16
 VMEM = pl.BlockSpec(memory_space=pltpu.VMEM)
-SMEM = pl.BlockSpec(memory_space=pltpu.SMEM)
 ANYWHERE = pl.BlockSpec(memory_space=pltpu.HBM)
 LIMIT = 24 * 1024 * 1024
 
@@ -56,14 +55,10 @@
     return lax.axis_index(axis) % 2 == 0
 
 
-def rows_kernel(state_ref, own_ref, first_ref, second_ref, raw, scr, sems):
+def rows_kernel(state_ref, own_ref, first_ref, second_ref, scr):
     frames, chans, rows, _ = state_ref.shape
-    copies = [pltpu.make_async_copy(state_ref.at[f], raw.at[f], sems.at[f]) for f in range(frames)]
-    for c in copies:
-        c.start()
     for f in range(frames):
-        copies[f].wait()
-        scr[f] = raw[f].astype(F32).reshape(chans * rows, LANES)
+        scr[f] = state_ref[f].astype(F32).reshape(chans * rows, LANES)
         for y in range(rows):
             own_ref[f, :, tile(y)] = scr[f, pl.ds(y, chans, stride=rows), :].astype(BF)
     even = is_even("tm")
@@ -81,39 +76,26 @@
         rows_kernel,
         "rows",
         (shape_of((frames, chans, rows * LANES), BF), slab, slab),
-        [ANYWHERE],
-        [
-            pltpu.VMEM(state.shape, BF),
-            pltpu.VMEM((frames, chans * rows, LANES), F32),
-            pltpu.SemaphoreType.DMA((frames,)),
-        ],
+        [VMEM],
+        [pltpu.VMEM((frames, chans * rows, LANES), F32)],
+        cost=4_000_000_000,
     )(state)
 
 
-def column(ref):
-    n = ref.shape[1]
-    return jnp.broadcast_to(ref[...], (8, n)).T[:, 0:1]
-
-
 def weights_kernel(
-    w1_ref, w2_ref, w3_ref, b1_ref, b2_ref, b3_ref,
-    m1_ref, m2_ref, m3_ref, s1_ref, s2_ref, s3_ref, c1_ref, c2_ref, c3_ref, r1, r2, r3, sems,
+    w1_ref, w2_ref, w3_ref, small_ref,
+    m1_ref, m2_ref, m3_ref, s1_ref, s2_ref, s3_ref, c1_ref, c2_ref, c3_ref, days_ref, f2, f3,
 ):
-    copies = [
-        pltpu.make_async_copy(a, b, sems.at[i])
-        for i, (a, b) in enumerate(((w1_ref, r1), (w2_ref, r2), (w3_ref, r3)))
-    ]
-    for c in copies:
-        c.start()
-    c1_ref[...], c2_ref[...], c3_ref[...] = column(b1_ref), column(b2_ref), column(b3_ref)
+    small = jnp.broadcast_to(small_ref[...], (8, small_ref.shape[1])).T[:, 0:1]
+    at = 0
+    for ref in (c1_ref, c2_ref, c3_ref, days_ref):
+        ref[...] = jnp.broadcast_to(small[at : at + ref.shape[0]], ref.shape)
+        at += ref.shape[0]
     for ref in (m1_ref, m2_ref, m3_ref, s1_ref, s2_ref, s3_ref):
         ref[...] = jnp.zeros_like(ref)
-    hid = c1_ref.shape[0]
-    chans = r1.shape[0] // 27
-    fields = c3_ref.shape[0]
-    frames = m3_ref.shape[0] // fields
-    copies[0].wait()
-    flat = r1[...].astype(F32).T.astype(BF)
+    hid, fields, chans = w2_ref.shape[1], w3_ref.shape[1], w1_ref.shape[0] // 27
+    frames = days_ref.shape[0]
+    flat = w1_ref[...].astype(F32).T.astype(BF)
     for p in range(2):
         m1_ref[p * hid : (p + 1) * hid, p * 9 * chans : (p + 3) * 9 * chans] = flat
         for dt in range(3):
@@ -123,24 +105,27 @@
                     flat[:, at : at + 3 * chans]
                 )
 
-    def place(raw, main, side, count, outs):
-        for dt in range(3):
-            for dy in range(3):
-                for dx in range(3):
-                    w = raw[(dt * 3 + dy) * 3 + dx]
-                    for p in range(count):
-                        at = (((dt + p) * 3 + dy) * 3 + dx) * hid
-                        main[p * outs : (p + 1) * outs, at : at + hid] = w
-                        at = ((dt + p) * 3 + dx) * hid
-                        side[(p * 3 + dy) * outs : (p * 3 + dy + 1) * outs, at : at + hid] = w
-
-    copies[1].wait()
-    place(r2, m2_ref, s2_ref, 2, hid)
-    copies[2].wait()
-    place(r3, m3_ref, s3_ref, frames, fields)
-
-
-def make_weights(w1, w2, w3, b1, b2, b3, frames):
+    def place(raw, flat, main, side, count, outs):
+        half = LANES // 2
+        for t in range(27):
+            for k in range(2):
+                flat[k, :, t * hid + k * half : (t + 1) * hid + k * half] = raw[t]
+        for p in range(count):
+            rows, at = slice(p * outs, (p + 1) * outs), p * 9 * hid
+            k = at % LANES // half
+            main[rows, at : at + 27 * hid] = flat[k, :, k * half : k * half + 27 * hid]
+            for dt in range(3):
+                for dy in range(3):
+                    rows = slice((p * 3 + dy) * outs, (p * 3 + dy + 1) * outs)
+                    at, src = (dt + p) * 3 * hid, (dt * 3 + dy) * 3 * hid
+                    k = (at - src) % LANES // half
+                    side[rows, at : at + 3 * hid] = flat[k, :, src + k * half : src + k * half + 3 * hid]
+
+    place(w2_ref, f2, m2_ref, s2_ref, 2, hid)
+    place(w3_ref, f3, m3_ref, s3_ref, frames, fields)
+
+
+def make_weights(w1, w2, w3, small, frames):
     hid, fields, chans = w2.shape[1], w3.shape[1], w1.shape[0] // 27
     return call(
         weights_kernel,
@@ -155,11 +140,12 @@
             shape_of((hid, 1), F32),
             shape_of((hid, 1), F32),
             shape_of((fields, 1), F32),
+            shape_of((frames, LANES), F32),
         ),
-        [ANYWHERE] * 3 + [VMEM] * 3,
-        [pltpu.VMEM(w.shape, BF) for w in (w1, w2, w3)] + [pltpu.SemaphoreType.DMA((3,))],
+        [VMEM] * 4,
+        [pltpu.VMEM((2, w.shape[1], 27 * hid + LANES // 2), BF) for w in (w2, w3)],
         cost=1_000_000_000,
-    )(w1, w2, w3, b1, b2, b3)
+    )(w1, w2, w3, small)
 
 
 def slab_order(frames):
@@ -230,13 +216,13 @@
             for y in range(rows):
                 spread(s1, base + f, y, src[f, :, tile(y)])
 
-    def layer(src, dst, m_ref, c_ref, count, first):
+    def layer(src, dst, m_ref, bias, count, first):
         def step(i, carry):
             f = 2 * i
             for y in range(0, rows, 2):
                 acc = jnp.dot(m_ref[...], window(src, f, 4, y), preferred_element_type=F32)
                 for p in range(2):
-                    h = silu(acc[p * hid : (p + 1) * hid] + c_ref[...]).astype(BF)
+                    h = silu(acc[p * hid : (p + 1) * hid] + bias).astype(BF)
                     h = jnp.where(in_trajectory(f + p + first, frames), h, jnp.zeros_like(h))
                     spread(dst, f + p, y, h[:, tile(0)])
                     spread(dst, f + p, y + 1, h[:, tile(1)])
@@ -244,14 +230,14 @@
 
         lax.fori_loop(0, count // 2, step, 0, unroll=UNROLL)
 
-    layer(s1, s2, m1_ref, c1_ref, frames + 4, -2)
-    layer(s2, s3, m2_ref, c2_ref, frames + 2, -1)
+    layer(s1, s2, m1_ref, c1_ref[...], frames + 4, -2)
+    layer(s2, s3, m2_ref, c2_ref[...], frames + 2, -1)
     for y in range(0, rows, 2):
         acc = jnp.dot(m3_ref[...], window(s3, 0, frames + 2, y), preferred_element_type=F32)
         score_ref[y], score_ref[y + 1] = acc[:, tile(0)], acc[:, tile(1)]
 
 
-UNROLL = False
+UNROLL = True
 
 
 def make_main(own, first, second, m1, m2, m3, c1, c2):
@@ -319,17 +305,17 @@
         (pair >= LANES) & (place >= PITCH - DEPTH) & (me == last)
     )
 
-    def layer(src, dst, m_ref, c_ref, count, first):
+    def layer(src, dst, m_ref, bias, count, first):
         for f in range(0, count, 2):
             z = jnp.concatenate([src[f + j] for j in range(4)], axis=0)
             acc = jnp.dot(m_ref[...], z, preferred_element_type=F32)
             for p in range(2):
-                h = silu(over_rows(acc, p * 3 * hid, hid) + c_ref[...])
+                h = silu(over_rows(acc, p * 3 * hid, hid) + bias)
                 keep = in_trajectory(f + p + first, frames) & ~outside
                 spread_side(dst, f + p, jnp.where(keep, h, 0.0).astype(BF))
 
-    layer(t1, t2, s1_ref, c1_ref, frames + 4, -2)
-    layer(t2, t3, s2_ref, c2_ref, frames + 2, -1)
+    layer(t1, t2, s1_ref, c1_ref[...], frames + 4, -2)
+    layer(t2, t3, s2_ref, c2_ref[...], frames + 2, -1)
     z = jnp.concatenate([t3[j] for j in range(frames + 2)], axis=0)
     acc = jnp.dot(s3_ref[...], z, preferred_element_type=F32)
     for f in range(frames):
@@ -340,10 +326,7 @@
     days = part_ref.shape[0]
     heads = pl.ds(0, frames, stride=fields)
     west, east = side_ref[0, heads], side_ref[1, heads]
-    row = lax.broadcasted_iota(jnp.int32, (frames, LANES), 0)
-    day = jnp.zeros((frames, LANES), jnp.int32)
-    for f in range(frames):
-        day = jnp.where(row == f, day_ref[f], day)
+    day = day_ref[...]
     for y in range(rows):
         v = patched(score_ref[y, heads], west, east, y)
         for d in range(days):
@@ -352,7 +335,7 @@
     for d in range(days):
         total = 0.5 * part_ref[d]
         for f in range(frames):
-            total = total + jnp.where(day_ref[f] == d, state_ref[f, 0].astype(F32) + 0.5 * base, 0.0)
+            total = total + jnp.where(day[f : f + 1] == d, state_ref[f, 0].astype(F32) + 0.5 * base, 0.0)
         part_ref[d] = total
 
 
@@ -363,7 +346,7 @@
         side_kernel,
         "side",
         (shape_of((2, frames * fields, LANES), F32), shape_of((days, rows, LANES), F32)),
-        [VMEM] * 12 + [SMEM],
+        [VMEM] * 13,
         [
             pltpu.VMEM((frames + 6, 3 * chans, 2 * LANES), BF),
             pltpu.VMEM((frames + 4, 3 * hid, 2 * LANES), BF),
@@ -374,12 +357,13 @@
 
 def update_kernel(score_ref, side_ref, c3_ref, state_ref, noise_ref, out_ref, head_ref, scr):
     frames, fields, rows, _ = state_ref.shape
+    bias = c3_ref[...]
     for f in range(frames):
         at = slice(f * fields, (f + 1) * fields)
         west, east = side_ref[0, at], side_ref[1, at]
         for y in range(rows):
             scr[f, pl.ds(y, fields, stride=rows), :] = (
-                patched(score_ref[y, at], west, east, y) + c3_ref[...]
+                patched(score_ref[y, at], west, east, y) + bias
             )
         score = scr[f].reshape(fields, rows, LANES)
         moved = state_ref[f].astype(F32) + 0.8 * score + 0.5 * noise_ref[f].astype(F32)
@@ -407,7 +391,7 @@
     for f in range(frames):
         v = head_ref[f]
         for d in range(days):
-            v = v - jnp.where(day_ref[f] == d, misfit[d], 0.0)
+            v = v - jnp.where(day_ref[f : f + 1] == d, misfit[d], 0.0)
         buf[f, 0] = v.astype(BF)
     copy = pltpu.make_async_copy(buf, out_ref.at[:, 0:1], sem)
     copy.start()
@@ -420,7 +404,7 @@
         correct_kernel,
         "correct",
         (shape_of(out.shape, BF),),
-        [VMEM] * 5 + [SMEM, ANYWHERE],
+        [VMEM] * 6 + [ANYWHERE],
         [pltpu.VMEM((frames, 1, rows, LANES), BF), pltpu.SemaphoreType.DMA],
         alias={6: 0},
         out_specs=(ANYWHERE,),
@@ -443,14 +427,13 @@
     w3 = conv_three.transpose(2, 3, 4, 0, 1).reshape(27, fields, hid)
     own, send1, send2 = make_rows(state)
     first, second = exchanged(send1, "tm", 0), exchanged(send2, "tm", 1)
-    m1, m2, m3, s1, s2, s3, c1, c2, c3 = make_weights(
-        w1, w2, w3, bias_one[None], bias_two[None], bias_three[None], state.shape[0]
-    )
+    small = jnp.concatenate([bias_one, bias_two, bias_three, day_of_frame.astype(F32)])[None]
+    m1, m2, m3, s1, s2, s3, c1, c2, c3, days = make_weights(w1, w2, w3, small, state.shape[0])
     west, east, send1, send2 = make_edges(own, first, second)
     near, far = exchanged(send1, "space", 0), exchanged(send2, "space", 1)
     score = make_main(own, first, second, m1, m2, m3, c1, c2)
     side, mine = make_side(
-        score, west, east, near, far, s1, s2, s3, c1, c2, c3, state, day_of_frame, observed.shape[0]
+        score, west, east, near, far, s1, s2, s3, c1, c2, c3, state, days, observed.shape[0]
     )
     out, head = make_update(score, side, c3, state, noise)
     count = lax.axis_size("tm")
@@ -461,7 +444,7 @@
         if reach >= count:
             break
         mine = mine + theirs
-    out = make_correct(mine, theirs, observed[:, 0], obs_mask[0], head, day_of_frame, out)
+    out = make_correct(mine, theirs, observed[:, 0], obs_mask[0], head, days, out)
     return out[:, :, None]
 
 

time: 32.2 us -> 26.8 us (0.83)
  the two profiles are of different devices: /device:TPU:20 before, /device:TPU:22 now
where the time goes in v3:
time: 26.8 us; the launch traced here: 26.6 us
  Pallas kernels  11.3 us (42%)
  starting transfers between devices  7.86 us (29%)
  waiting for transfers between devices  6.22 us (23%)
  local copies, waits for them, and re-layouts  0.98 us (4%)
    ppermute x4, starting transfers between devices, exchanged(): return lax.ppermute(value, axis, pairs + [(j, i) for i, j in pairs])  7.71 us
    pallas_call x1, Pallas kernels, make_main(): call(main_kernel, 'main', (shape_of((width // LANES, m3.shape[0], LANES),...  5.93 us
    ppermute x2, waiting for transfers between devices, body(): theirs = lax.ppermute(mine, 'tm', [(i, i ^ reach) for i in range(count)])  3.74 us
    pallas_call x1, Pallas kernels, make_side(): call(side_kernel, 'side', (shape_of((2, frames * fields, LANES), F32), sh...  2.56 us
    ppermute x4, waiting for transfers between devices, exchanged(): return lax.ppermute(value, axis, pairs + [(j, i) for i, j in pairs])  2.48 us
    unnamed x24, local copies, waits for them, and re-layouts  0.98 us
    pallas_call x1, Pallas kernels, make_update(): call(update_kernel, 'update', (shape_of(state.shape, BF), shape_of((frame...  0.98 us
    pallas_call x1, Pallas kernels, make_weights(): call(weights_kernel, 'weights', (shape_of((2 * hid, 4 * 9 * chans), BF),...  0.8 us
  transfers between devices with their start and end apart: 6, of which 3 were waited for; matrix products, arithmetic and copies ran while one was open for 0% of the time, Pallas kernels for 29%

profile of v3, /device:TPU:22, one launch (start us, length us, event | category | flops | bytes accessed | tf_op | source)
XLA Modules:
  0.0 26.6 jit_solution(5883922930339653731)
XLA Ops:
  0.0 0.9 %copy-done = bf16[6,16,1,8,128]{4,3,2,1,0:T(8,128)(2,1)S(1)} copy-done((bf16[6,16,1,8,128]{4,3,2,1,0:T(8,128)(2,1)S(1)}, bf16[6,16,1,8,128]{4,3,2,1,0:T(8,128)(2,1)}, u32[]{:S(2)}) %copy-start) | copy-done | bytes 196632
  0.9 0.1 rows.1
  1.1 0.0 copy-start.11
  1.1 0.1 collective-permute-start
  1.1 0.0 copy-start.8
  1.2 0.0 copy-start.9
  1.2 0.0 copy-start.10
  1.2 2.6 %collective-permute-start.1 = (bf16[3,16,1024]{2,1,0:T(8,128)(2,1)S(1)}, bf16[3,16,1024]{2,1,0:T(8,128)(2,1)S(1)}, u32[]{:S(2)}, u32[]{:S(2)}) collective-permute-start(bf16[3,16,1024]{2,1,0:T(8,128)(2,1)S(1)} %get-tuple-element.28), channel_id=1, source_target_pairs={{8,16},{16,8},{9,17},{17,9},{10,18},{18,10},{11,19},{19,11},{12,20... | collective-permute-start | bytes 294920 | tf_op jit(solution)/shard_map/ppermute | solution.py:416
  3.8 0.0 copy-done.11
  3.8 0.0 copy-done.8
  3.9 0.0 copy-done.9
  3.9 0.1 pad_maximum_fusion
  4.0 0.8 %weights.1 = (bf16[128,576]{1,0:T(8,128)(2,1)S(1)}, bf16[128,2304]{1,0:T(8,128)(2,1)S(1)}, bf16[96,4608]{1,0:T(8,128)(2,1)S(1)}, bf16[384,192]{1,0:T(8,128)(2,1)...) custom-call(bf16[432,64]{1,0:T(8,128)(2,1)S(1)} %bitcast.25, ...), custom_call_target="tpu_custom_call" | custom-call | flops 1000000000 | bytes 1000000 | tf_op jit(solution)/shard_map/weights/pallas_call | solution.py:130
  4.8 0.0 collective-permute-done.first_ref
  4.8 2.5 %collective-permute-done.1.second_ref = bf16[3,16,1024]{2,1,0:T(8,128)(2,1)S(1)} collective-permute-done((bf16[3,16,1024]{2,1,0:T(8,128)(2,1)S(1)}, bf16[3,16,1024]{2,1,0:T(8,128)(2,1)S(1)}, u32[]{:S(2)}, u32[]{:S(2)}) %collective-permute-start.1) | collective-permute-done | bytes 98336 | tf_op jit(solution)/shard_map/ppermute | solution.py:416
  7.2 0.3 %edges.1 = (bf16[12,16,128]{2,1,0:T(8,128)(2,1)S(1)}, bf16[12,16,128]{2,1,0:T(8,128)(2,1)S(1)}, bf16[12,16,128]{2,1,0:T(8,128)(2,1)S(1)}, bf16[12,16,128]{2,1,0:T(8,128)(2,1)S(1)}) custom-call(bf16[6,16,1024]{2,1,0:T(8,128)(2,1)S(1)} %get-tuple-element.26.own_ref, bf16[3,16,1024]{2,1,0:T(8,128)(2,1)S(1)} %collective-permute-done.first_ref, ...), custom_call_target="tpu_custom_call" | custom-call | tf_op jit(solution)/shard_map/edges/pallas_call | solution.py:182
  7.5 0.6 %collective-permute-start.2 = (bf16[12,16,128]{2,1,0:T(8,128)(2,1)S(1)}, bf16[12,16,128]{2,1,0:T(8,128)(2,1)S(1)}, u32[]{:S(2)}, u32[]{:S(2)}) collective-permute-start(bf16[12,16,128]{2,1,0:T(8,128)(2,1)S(1)} %get-tuple-element.36), channel_id=1, source_target_pairs={{0,1},{2,3},{4,5},{6,7},{1,0},{3,2},{5,4},{7,6},{8,9},{10,11},{12,... | collective-permute-start | bytes 147464 | tf_op jit(solution)/shard_map/ppermute | solution.py:416
  8.1 4.4 %collective-permute-start.3 = (bf16[12,16,128]{2,1,0:T(8,128)(2,1)S(1)}, bf16[12,16,128]{2,1,0:T(8,128)(2,1)S(1)}, u32[]{:S(2)}, u32[]{:S(2)}) collective-permute-start(bf16[12,16,128]{2,1,0:T(8,128)(2,1)S(1)} %get-tuple-element.37), channel_id=1, source_target_pairs={{1,2},{3,4},{5,6},{2,1},{4,3},{6,5},{9,10},{11,12},{13,14},{10,9},... | collective-permute-start | bytes 147464 | tf_op jit(solution)/shard_map/ppermute | solution.py:416
  12.5 0.0 copy-start.1
  12.5 5.9 %main.1.score_ref = f32[8,96,128]{2,1,0:T(8,128)S(1)} custom-call(bf16[6,16,1024]{2,1,0:T(8,128)(2,1)S(1)} %get-tuple-element.26.own_ref, bf16[3,16,1024]{2,1,0:T(8,128)(2,1)S(1)} %collective-permute-done.first_ref, bf16[3,16,1024]{2,1,0:T(8,128)(2,1)S(1)} %collective-permute-done.1.second_ref, bf16[128,576]{1,0:T(8,128)(2,1)S(1)} %get-tuple-element.29.m1_ref, ...), custom_call_target="tpu_custom_call" | custom-call | flops 5000000000 | bytes 1000000 | tf_op jit(solution)/shard_map/main/pallas_call | solution.py:247
  18.5 0.0 collective-permute-done.2.first_ref
  18.5 0.0 collective-permute-done.3.second_ref
  18.5 0.0 copy-done.1
  18.5 0.0 copy-start.5
  18.5 2.6 %side.1 = (f32[2,96,128]{2,1,0:T(8,128)S(1)}, f32[2,8,128]{2,1,0:T(8,128)S(1)}) custom-call(f32[8,96,128]{2,1,0:T(8,128)S(1)} %main.1.score_ref, bf16[12,16,128]{2,1,0:T(8,128)(2,1)S(1)} %get-tuple-element.34.west_ref, bf16[12,16,128]{2,1,0:T(8,128)(2,1)S(1)} %get-tuple-element.35.east_ref, bf16[12,16,128]{2,1,0:T(8,128)(2,1)S(1)} %collective-permute-done.2.first_ref, ...), custom_call_target="tpu_custom_call" | custom-call | tf_op jit(solution)/shard_map/side/pallas_call | solution.py:345
  21.1 0.1 collective-permute-start.4
  21.2 1.2 %collective-permute-done.4 = f32[2,8,128]{2,1,0:T(8,128)S(1)} collective-permute-done((f32[2,8,128]{2,1,0:T(8,128)S(1)}, f32[2,8,128]{2,1,0:T(8,128)S(1)}, u32[]{:S(2)}, u32[]{:S(2)}) %collective-permute-start.4) | collective-permute-done | bytes 8224 | tf_op jit(solution)/shard_map/ppermute | solution.py:442
  22.3 0.1 collective-permute-start.5
  22.4 1.0 %update.1 = (bf16[6,16,8,128]{3,2,1,0:T(8,128)(2,1)}, f32[6,8,128]{2,1,0:T(8,128)S(1)}) custom-call(f32[8,96,128]{2,1,0:T(8,128)S(1)} %main.1.score_ref, f32[2,96,128]{2,1,0:T(8,128)S(1)} %get-tuple-element.44.side_ref, f32[16,1]{1,0:T(8,128)S(1)} %get-tuple-element.41.c3_ref, bf16[6,16,8,128]{3,2,1,0:T(8,128)(2,1)S(1)} %bitcast.19, ...), custom_call_target="tpu_custom_call" | custom-call | flops 1000000000 | bytes 1000000 | tf_op jit(solution)/shard_map/update/pallas_call | solution.py:376
  23.4 2.6 %collective-permute-done.5.theirs_ref = f32[2,8,128]{2,1,0:T(8,128)S(1)} collective-permute-done((f32[2,8,128]{2,1,0:T(8,128)S(1)}, f32[2,8,128]{2,1,0:T(8,128)S(1)}, u32[]{:S(2)}, u32[]{:S(2)}) %collective-permute-start.5) | collective-permute-done | bytes 8224 | tf_op jit(solution)/shard_map/ppermute | solution.py:442
  26.0 0.0 copy-done.2
  26.0 0.6 %correct.1 = bf16[6,16,8,128]{3,2,1,0:T(8,128)(2,1)} custom-call(f32[2,8,128]{2,1,0:T(8,128)S(1)} %add.3.mine_ref, f32[2,8,128]{2,1,0:T(8,128)S(1)} %collective-permute-done.5.theirs_ref, f32[2,8,128]{2,1,0:T(8,128)S(1)} %bitcast.20, s32[8,128]{1,0:T(8,128)S(1)} %bitcast.21, ...), custom_call_target="tpu_custom_call", output_to_operand_aliasing={{}: (6, {})} | custom-call | tf_op jit(solution)/shard_map/correct/pallas_call | solution.py:403
  (14 shorter events, 0.0 us)
Async XLA Ops:
  0.0 0.9 %copy-start = (bf16[6,16,1,8,128]{4,3,2,1,0:T(8,128)(2,1)S(1)}, bf16[6,16,1,8,128]{4,3,2,1,0:T(8,128)(2,1)}, u32[]{:S(2)}) copy-start(bf16[6,16,1,8,128]{4,3,2,1,0:T(8,128)(2,1)} %param.11) | copy-start | bytes 589828
  0.9 3.0 %copy-start.4 = (bf16[64,64,3,3,3]{1,0,4,3,2:T(8,128)(2,1)S(1)}, bf16[64,64,3,3,3]{1,0,4,3,2:T(8,128)(2,1)}, u32[]{:S(2)}) copy-start(bf16[64,64,3,3,3]{1,0,4,3,2:T(8,128)(2,1)} %param.15) | copy-start | bytes 663556
  0.9 3.0 %copy-start.6 = (bf16[64,16,3,3,3]{0,1,4,3,2:T(8,128)(2,1)S(1)}, bf16[64,16,3,3,3]{0,1,4,3,2:T(8,128)(2,1)}, u32[]{:S(2)}) copy-start(bf16[64,16,3,3,3]{0,1,4,3,2:T(8,128)(2,1)} %param.13) | copy-start | bytes 165892
  0.9 3.0 %copy-start.7 = (bf16[16,64,3,3,3]{1,0,4,3,2:T(8,128)(2,1)S(1)}, bf16[16,64,3,3,3]{1,0,4,3,2:T(8,128)(2,1)}, u32[]{:S(2)}) copy-start(bf16[16,64,3,3,3]{1,0,4,3,2:T(8,128)(2,1)} %param.17) | copy-start | bytes 165892
  1.1 2.8 %copy-start.11 = (s32[6]{0:T(128)S(1)}, s32[6]{0:T(128)}, u32[]{:S(2)}) copy-start(s32[6]{0:T(128)} %param.19) | copy-start | bytes 76
  1.1 3.7 %collective-permute-start = (bf16[3,16,1024]{2,1,0:T(8,128)(2,1)S(1)}, bf16[3,16,1024]{2,1,0:T(8,128)(2,1)S(1)}, u32[]{:S(2)}, u32[]{:S(2)}) collective-permute-start(bf16[3,16,1024]{2,1,0:T(8,128)(2,1)S(1)} %get-tuple-element.27), channel_id=1, source_target_pairs={{0,8},{16,24},{8,0},{24,16},{1,9},{17,25},{9,1},{25,17},{2,10},{18... | collective-permute-start | bytes 294920 | tf_op jit(solution)/shard_map/ppermute | solution.py:416
  1.1 2.7 %copy-start.8 = (f32[16]{0:T(128)S(1)}, f32[16]{0:T(128)}, u32[]{:S(2)}) copy-start(f32[16]{0:T(128)} %param.18) | copy-start | bytes 196
  1.2 2.7 %copy-start.9 = (f32[64]{0:T(128)S(1)}, f32[64]{0:T(128)}, u32[]{:S(2)}) copy-start(f32[64]{0:T(128)} %param.16) | copy-start | bytes 772
  1.2 2.7 %copy-start.10 = (f32[64]{0:T(128)S(1)}, f32[64]{0:T(128)}, u32[]{:S(2)}) copy-start(f32[64]{0:T(128)} %param.14) | copy-start | bytes 772
  1.2 6.1 %collective-permute-start.1 = (bf16[3,16,1024]{2,1,0:T(8,128)(2,1)S(1)}, bf16[3,16,1024]{2,1,0:T(8,128)(2,1)S(1)}, u32[]{:S(2)}, u32[]{:S(2)}) collective-permute-start(bf16[3,16,1024]{2,1,0:T(8,128)(2,1)S(1)} %get-tuple-element.28), channel_id=1, source_target_pairs={{8,16},{16,8},{9,17},{17,9},{10,18},{18,10},{11,19},{19,11},{12,20... | collective-permute-start | bytes 294920 | tf_op jit(solution)/shard_map/ppermute | solution.py:416
  7.5 11.0 %collective-permute-start.2 = (bf16[12,16,128]{2,1,0:T(8,128)(2,1)S(1)}, bf16[12,16,128]{2,1,0:T(8,128)(2,1)S(1)}, u32[]{:S(2)}, u32[]{:S(2)}) collective-permute-start(bf16[12,16,128]{2,1,0:T(8,128)(2,1)S(1)} %get-tuple-element.36), channel_id=1, source_target_pairs={{0,1},{2,3},{4,5},{6,7},{1,0},{3,2},{5,4},{7,6},{8,9},{10,11},{12,... | collective-permute-start | bytes 147464 | tf_op jit(solution)/shard_map/ppermute | solution.py:416
  8.1 10.4 %collective-permute-start.3 = (bf16[12,16,128]{2,1,0:T(8,128)(2,1)S(1)}, bf16[12,16,128]{2,1,0:T(8,128)(2,1)S(1)}, u32[]{:S(2)}, u32[]{:S(2)}) collective-permute-start(bf16[12,16,128]{2,1,0:T(8,128)(2,1)S(1)} %get-tuple-element.37), channel_id=1, source_target_pairs={{1,2},{3,4},{5,6},{2,1},{4,3},{6,5},{9,10},{11,12},{13,14},{10,9},... | collective-permute-start | bytes 147464 | tf_op jit(solution)/shard_map/ppermute | solution.py:416
  12.5 6.0 %copy-start.1 = (bf16[6,16,1,8,128]{4,3,2,1,0:T(8,128)(2,1)S(1)}, bf16[6,16,1,8,128]{4,3,2,1,0:T(8,128)(2,1)}, u32[]{:S(2)}) copy-start(bf16[6,16,1,8,128]{4,3,2,1,0:T(8,128)(2,1)} %param.11) | copy-start | bytes 589828
  18.5 3.9 %copy-start.5 = (bf16[6,16,1,8,128]{4,3,2,1,0:T(8,128)(2,1)S(1)}, bf16[6,16,1,8,128]{4,3,2,1,0:T(8,128)(2,1)}, u32[]{:S(2)}) copy-start(bf16[6,16,1,8,128]{4,3,2,1,0:T(8,128)(2,1)} %param.12) | copy-start | bytes 589828
  21.1 1.2 %collective-permute-start.4 = (f32[2,8,128]{2,1,0:T(8,128)S(1)}, f32[2,8,128]{2,1,0:T(8,128)S(1)}, u32[]{:S(2)}, u32[]{:S(2)}) collective-permute-start(f32[2,8,128]{2,1,0:T(8,128)S(1)} %get-tuple-element.43), channel_id=1, source_target_pairs={{0,8},{8,0},{16,24},{24,16},{1,9},{9,1},{17,25},{25,17},{2,10},{10... | collective-permute-start | bytes 24584 | tf_op jit(solution)/shard_map/ppermute | solution.py:442
  22.3 3.7 %collective-permute-start.5 = (f32[2,8,128]{2,1,0:T(8,128)S(1)}, f32[2,8,128]{2,1,0:T(8,128)S(1)}, u32[]{:S(2)}, u32[]{:S(2)}) collective-permute-start(f32[2,8,128]{2,1,0:T(8,128)S(1)} %add.3.mine_ref), channel_id=1, source_target_pairs={{0,16},{8,24},{16,0},{24,8},{1,17},{9,25},{17,1},{25,9},{2,18},{10... | collective-permute-start | bytes 24584 | tf_op jit(solution)/shard_map/ppermute | solution.py:442
  22.4 3.6 %copy-start.2 = (f32[2,1,8,128]{3,2,1,0:T(8,128)S(1)}, f32[2,1,8,128]{3,2,1,0:T(8,128)}, u32[]{:S(2)}) copy-start(f32[2,1,8,128]{3,2,1,0:T(8,128)} %param.20) | copy-start | bytes 24580
  23.4 2.6 %copy-start.3 = (s32[1,8,128]{2,1,0:T(8,128)S(1)}, s32[1,8,128]{2,1,0:T(8,128)}, u32[]{:S(2)}) copy-start(s32[1,8,128]{2,1,0:T(8,128)} %param.21) | copy-start | bytes 12292

commit v4 on v3

--- a/solution.py
+++ b/solution.py
@@ -55,18 +55,17 @@
     return lax.axis_index(axis) % 2 == 0
 
 
-def rows_kernel(state_ref, own_ref, first_ref, second_ref, scr):
+def rows_kernel(state_ref, own_ref, low_ref, high_ref, scr):
     frames, chans, rows, _ = state_ref.shape
     for f in range(frames):
         scr[f] = state_ref[f].astype(F32).reshape(chans * rows, LANES)
         for y in range(rows):
-            own_ref[f, :, tile(y)] = scr[f, pl.ds(y, chans, stride=rows), :].astype(BF)
-    even = is_even("tm")
-    to_first = jnp.where(even, frames - DEPTH, 0)
-    to_second = jnp.where(even, 0, frames - DEPTH)
-    for f in range(DEPTH):
-        first_ref[f] = own_ref[to_first + f]
-        second_ref[f] = own_ref[to_second + f]
+            v = scr[f, pl.ds(y, chans, stride=rows), :].astype(BF)
+            own_ref[f, :, tile(y)] = v
+            if f < DEPTH:
+                low_ref[f, :, tile(y)] = v
+            if f >= frames - DEPTH:
+                high_ref[f - (frames - DEPTH), :, tile(y)] = v
 
 
 def make_rows(state):
@@ -148,38 +147,38 @@
     )(w1, w2, w3, small)
 
 
-def slab_order(frames):
-    even = is_even("tm")
-    return jnp.where(even, frames + DEPTH, 0), jnp.where(even, 0, frames + DEPTH)
-
-
-def edges_kernel(own_ref, first_ref, second_ref, west_ref, east_ref, send1_ref, send2_ref):
+def widened(own_ref, below_ref, above_ref):
     frames = own_ref.shape[0]
+    step, last = lax.axis_index("tm"), lax.axis_size("tm") - 1
+    parts = (own_ref, DEPTH, None), (below_ref, 0, step > 0), (above_ref, DEPTH + frames, step < last)
+    for src, base, inside in parts:
+        for f in range(src.shape[0]):
+            for y in range(src.shape[2] // LANES):
+                v = src[f, :, tile(y)]
+                yield base + f, y, v if inside is None else jnp.where(inside, v, jnp.zeros_like(v))
+
+
+def edges_kernel(own_ref, below_ref, above_ref, west_ref, east_ref, send1_ref, send2_ref):
     rows = own_ref.shape[2] // LANES
     shape = (own_ref.shape[1], LANES)
     lane = lanes(shape)
     group, place = lane // PITCH, lane % PITCH
-    at1, at2 = slab_order(frames)
     even = is_even("space")
-    for src, base, count in ((own_ref, DEPTH, frames), (first_ref, at1, DEPTH), (second_ref, at2, DEPTH)):
-        for f in range(count):
-            west = jnp.zeros(shape, BF)
-            east = jnp.zeros(shape, BF)
-            for y in range(rows):
-                v = src[f, :, tile(y)]
-                here = group == y
-                west = jnp.where(here & (place >= DEPTH), turn(v, y * PITCH + DEPTH), west)
-                east = jnp.where(here & (place < PITCH - DEPTH), turn(v, y * PITCH + PITCH - DEPTH), east)
-            west_ref[base + f] = west
-            east_ref[base + f] = east
-            send1_ref[base + f] = jnp.where(even, east, west)
-            send2_ref[base + f] = jnp.where(even, west, east)
-
-
-def make_edges(own, first, second):
+    for f, y, v in widened(own_ref, below_ref, above_ref):
+        if y == 0:
+            west, east = jnp.zeros(shape, BF), jnp.zeros(shape, BF)
+        here = group == y
+        west = jnp.where(here & (place >= DEPTH), turn(v, y * PITCH + DEPTH), west)
+        east = jnp.where(here & (place < PITCH - DEPTH), turn(v, y * PITCH + PITCH - DEPTH), east)
+        if y == rows - 1:
+            west_ref[f], east_ref[f] = west, east
+            send1_ref[f], send2_ref[f] = jnp.where(even, east, west), jnp.where(even, west, east)
+
+
+def make_edges(own, below, above):
     frames, chans, _ = own.shape
     strip = shape_of((frames + 2 * DEPTH, chans, LANES), BF)
-    return call(edges_kernel, "edges", (strip,) * 4, [VMEM] * 3)(own, first, second)
+    return call(edges_kernel, "edges", (strip,) * 4, [VMEM] * 3)(own, below, above)
 
 
 def spread(dst, f, y, v):
@@ -202,7 +201,7 @@
 
 
 def main_kernel(
-    own_ref, first_ref, second_ref, m1_ref, m2_ref, m3_ref, c1_ref, c2_ref, score_ref, s1, s2, s3
+    own_ref, below_ref, above_ref, m1_ref, m2_ref, m3_ref, c1_ref, c2_ref, score_ref, s1, s2, s3
 ):
     frames = own_ref.shape[0]
     rows = own_ref.shape[2] // LANES
@@ -210,11 +209,8 @@
     for s in (s1, s2, s3):
         s[:, :, tile(0)] = jnp.zeros(s.shape[:2] + (LANES,), BF)
         s[:, :, tile(rows + 1)] = jnp.zeros(s.shape[:2] + (LANES,), BF)
-    at1, at2 = slab_order(frames)
-    for src, base, count in ((own_ref, DEPTH, frames), (first_ref, at1, DEPTH), (second_ref, at2, DEPTH)):
-        for f in range(count):
-            for y in range(rows):
-                spread(s1, base + f, y, src[f, :, tile(y)])
+    for f, y, v in widened(own_ref, below_ref, above_ref):
+        spread(s1, f, y, v)
 
     def layer(src, dst, m_ref, bias, count, first):
         def step(i, carry):
@@ -240,7 +236,7 @@
 UNROLL = True
 
 
-def make_main(own, first, second, m1, m2, m3, c1, c2):
+def make_main(own, below, above, m1, m2, m3, c1, c2):
     frames, chans, width = own.shape
     hid = c1.shape[0]
     wide = width + 2 * LANES
@@ -255,7 +251,7 @@
             pltpu.VMEM((frames + 2, 3 * hid, wide), BF),
         ],
         cost=5_000_000_000,
-    )(own, first, second, m1, m2, m3, c1, c2)[0]
+    )(own, below, above, m1, m2, m3, c1, c2)[0]
 
 
 def spread_side(dst, f, v):
@@ -292,13 +288,16 @@
     chans, hid = west_ref.shape[1], c1_ref.shape[0]
     place = lanes((chans, LANES)) % PITCH
     even = is_even("space")
+    me, last = lax.axis_index("space"), lax.axis_size("space") - 1
+    none = jnp.zeros((chans, LANES), BF)
     for f in range(frames + 2 * DEPTH):
         a, b = first_ref[f], second_ref[f]
-        west = jnp.where(place < DEPTH, turn(jnp.where(even, b, a), 2 * DEPTH - PITCH), west_ref[f])
-        east = jnp.where(place >= PITCH - DEPTH, turn(jnp.where(even, a, b), PITCH - 2 * DEPTH), east_ref[f])
+        a, b = jnp.where(even, b, a), jnp.where(even, a, b)
+        a, b = jnp.where(me > 0, a, none), jnp.where(me < last, b, none)
+        west = jnp.where(place < DEPTH, turn(a, 2 * DEPTH - PITCH), west_ref[f])
+        east = jnp.where(place >= PITCH - DEPTH, turn(b, PITCH - 2 * DEPTH), east_ref[f])
         spread_side(t1, f, jnp.concatenate([west, east], axis=1))
 
-    me, last = lax.axis_index("space"), lax.axis_size("space") - 1
     pair = lanes((1, 2 * LANES))
     place = pair % PITCH
     outside = ((pair < LANES) & (place < DEPTH) & (me == 0)) | (
@@ -411,9 +410,22 @@
     )(mine, theirs, observed, mask, head, day, out)[0]
 
 
-def exchanged(value, axis, start):
-    pairs = [(i, i + 1) for i in range(start, lax.axis_size(axis) - 1, 2)]
-    return lax.ppermute(value, axis, pairs + [(j, i) for i, j in pairs])
+def shifted(value, axis, steps):
+    count = lax.axis_size(axis)
+    return lax.ppermute(value, axis, [(i, (i + steps) % count) for i in range(count)])
+
+
+def swapped(value, start):
+    blocks, strips = lax.axis_size("tm"), lax.axis_size("space")
+    pairs = []
+    for t in range(blocks):
+        for i in range(strips):
+            other = i + 1 if i % 2 == start else i - 1
+            if 0 <= other < strips:
+                pairs.append((t * strips + i, t * strips + other))
+            elif t ^ 1 < blocks:
+                pairs.append((t * strips + i, (t ^ 1) * strips + i))
+    return lax.ppermute(value, ("tm", "space"), pairs)
 
 
 def body(
@@ -425,13 +437,13 @@
     w1 = conv_one.transpose(2, 3, 4, 1, 0).reshape(27 * chans, hid)
     w2 = conv_two.transpose(2, 3, 4, 0, 1).reshape(27, hid, hid)
     w3 = conv_three.transpose(2, 3, 4, 0, 1).reshape(27, fields, hid)
-    own, send1, send2 = make_rows(state)
-    first, second = exchanged(send1, "tm", 0), exchanged(send2, "tm", 1)
+    own, low, high = make_rows(state)
+    below, above = shifted(high, "tm", 1), shifted(low, "tm", -1)
     small = jnp.concatenate([bias_one, bias_two, bias_three, day_of_frame.astype(F32)])[None]
     m1, m2, m3, s1, s2, s3, c1, c2, c3, days = make_weights(w1, w2, w3, small, state.shape[0])
-    west, east, send1, send2 = make_edges(own, first, second)
-    near, far = exchanged(send1, "space", 0), exchanged(send2, "space", 1)
-    score = make_main(own, first, second, m1, m2, m3, c1, c2)
+    west, east, send1, send2 = make_edges(own, below, above)
+    near, far = swapped(send1, 0), swapped(send2, 1)
+    score = make_main(own, below, above, m1, m2, m3, c1, c2)
     side, mine = make_side(
         score, west, east, near, far, s1, s2, s3, c1, c2, c3, state, days, observed.shape[0]
     )

time: 26.8 us -> 23.8 us (0.89)
  the two profiles are of different devices: /device:TPU:22 before, /device:TPU:0 now
where the time goes in v4:
time: 23.8 us; the launch traced here: 23.7 us
  Pallas kernels  11.1 us (47%)
  starting transfers between devices  6.2 us (26%)
  waiting for transfers between devices  5.23 us (22%)
  local copies, waits for them, and re-layouts  0.97 us (4%)
    pallas_call x1, Pallas kernels, make_main(): call(main_kernel, 'main', (shape_of((width // LANES, m3.shape[0], LANES),...  5.74 us
    ppermute x2, waiting for transfers between devices, body(): theirs = lax.ppermute(mine, 'tm', [(i, i ^ reach) for i in range(count)])  3.07 us
    ppermute x2, starting transfers between devices, swapped(): return lax.ppermute(value, ('tm', 'space'), pairs)  2.86 us
    pallas_call x1, Pallas kernels, make_side(): call(side_kernel, 'side', (shape_of((2, frames * fields, LANES), F32), sh...  2.56 us
    ppermute x2, starting transfers between devices, shifted(): lax.ppermute(value, axis, [(i, (i + steps) % count) for i in range(count)])  2.52 us
    ppermute x2, waiting for transfers between devices, shifted(): lax.ppermute(value, axis, [(i, (i + steps) % count) for i in range(count)])  2.15 us
    pallas_call x1, Pallas kernels, make_update(): call(update_kernel, 'update', (shape_of(state.shape, BF), shape_of((frame...  0.98 us
    unnamed x24, local copies, waits for them, and re-layouts  0.97 us
  transfers between devices with their start and end apart: 6, of which 4 were waited for; matrix products, arithmetic and copies ran while one was open for 0% of the time, Pallas kernels for 32%

profile of v4, /device:TPU:0, one launch (start us, length us, event | category | flops | bytes accessed | tf_op | source)
XLA Modules:
  0.0 23.7 jit_solution(5692771754933051588)
XLA Ops:
  0.0 0.9 %copy-done = bf16[6,16,1,8,128]{4,3,2,1,0:T(8,128)(2,1)S(1)} copy-done((bf16[6,16,1,8,128]{4,3,2,1,0:T(8,128)(2,1)S(1)}, bf16[6,16,1,8,128]{4,3,2,1,0:T(8,128)(2,1)}, u32[]{:S(2)}) %copy-start) | copy-done | bytes 196632
  0.9 0.1 rows.1
  1.1 0.0 copy-start.11
  1.1 0.5 %collective-permute-start = (bf16[3,16,1024]{2,1,0:T(8,128)(2,1)S(1)}, bf16[3,16,1024]{2,1,0:T(8,128)(2,1)S(1)}, u32[]{:S(2)}, u32[]{:S(2)}) collective-permute-start(bf16[3,16,1024]{2,1,0:T(8,128)(2,1)S(1)} %get-tuple-element.27), channel_id=1, source_target_pairs={{0,8},{8,16},{16,24},{24,0},{1,9},{9,17},{17,25},{25,1},{2,10},{10... | collective-permute-start | bytes 294920 | tf_op jit(solution)/shard_map/ppermute | solution.py:415
  1.6 2.0 %collective-permute-start.1 = (bf16[3,16,1024]{2,1,0:T(8,128)(2,1)S(1)}, bf16[3,16,1024]{2,1,0:T(8,128)(2,1)S(1)}, u32[]{:S(2)}, u32[]{:S(2)}) collective-permute-start(bf16[3,16,1024]{2,1,0:T(8,128)(2,1)S(1)} %get-tuple-element.28), channel_id=1, source_target_pairs={{0,24},{8,0},{16,8},{24,16},{1,25},{9,1},{17,9},{25,17},{2,26},{10... | collective-permute-start | bytes 294920 | tf_op jit(solution)/shard_map/ppermute | solution.py:415
  3.6 0.0 copy-done.11
  3.6 0.0 copy-done.8
  3.6 0.0 copy-done.9
  3.6 0.0 copy-done.10
  3.6 0.1 pad_maximum_fusion
  3.7 0.0 copy-done.4
  3.7 0.0 copy-done.6
  3.7 0.0 copy-done.7
  3.7 0.8 %weights.1 = (bf16[128,576]{1,0:T(8,128)(2,1)S(1)}, bf16[128,2304]{1,0:T(8,128)(2,1)S(1)}, bf16[96,4608]{1,0:T(8,128)(2,1)S(1)}, bf16[384,192]{1,0:T(8,128)(2,1)...) custom-call(bf16[432,64]{1,0:T(8,128)(2,1)S(1)} %bitcast.25, ...), custom_call_target="tpu_custom_call" | custom-call | flops 1000000000 | bytes 1000000 | tf_op jit(solution)/shard_map/weights/pallas_call | solution.py:129
  4.5 1.3 %collective-permute-done.below_ref = bf16[3,16,1024]{2,1,0:T(8,128)(2,1)S(1)} collective-permute-done((bf16[3,16,1024]{2,1,0:T(8,128)(2,1)S(1)}, bf16[3,16,1024]{2,1,0:T(8,128)(2,1)S(1)}, u32[]{:S(2)}, u32[]{:S(2)}) %collective-permute-start) | collective-permute-done | bytes 98336 | tf_op jit(solution)/shard_map/ppermute | solution.py:415
  5.8 0.9 %collective-permute-done.1.above_ref = bf16[3,16,1024]{2,1,0:T(8,128)(2,1)S(1)} collective-permute-done((bf16[3,16,1024]{2,1,0:T(8,128)(2,1)S(1)}, bf16[3,16,1024]{2,1,0:T(8,128)(2,1)S(1)}, u32[]{:S(2)}, u32[]{:S(2)}) %collective-permute-start.1) | collective-permute-done | bytes 98336 | tf_op jit(solution)/shard_map/ppermute | solution.py:415
  6.7 0.3 %edges.1 = (bf16[12,16,128]{2,1,0:T(8,128)(2,1)S(1)}, bf16[12,16,128]{2,1,0:T(8,128)(2,1)S(1)}, bf16[12,16,128]{2,1,0:T(8,128)(2,1)S(1)}, bf16[12,16,128]{2,1,0:T(8,128)(2,1)S(1)}) custom-call(bf16[6,16,1024]{2,1,0:T(8,128)(2,1)S(1)} %get-tuple-element.26.own_ref, bf16[3,16,1024]{2,1,0:T(8,128)(2,1)S(1)} %collective-permute-done.below_ref, ...), custom_call_target="tpu_custom_call" | custom-call | tf_op jit(solution)/shard_map/edges/pallas_call | solution.py:181
  6.9 1.6 %collective-permute-start.2 = (bf16[12,16,128]{2,1,0:T(8,128)(2,1)S(1)}, bf16[12,16,128]{2,1,0:T(8,128)(2,1)S(1)}, u32[]{:S(2)}, u32[]{:S(2)}) collective-permute-start(bf16[12,16,128]{2,1,0:T(8,128)(2,1)S(1)} %get-tuple-element.36), channel_id=1, source_target_pairs={{0,1},{1,0},{2,3},{3,2},{4,5},{5,4},{6,7},{7,6},{8,9},{9,8},{10,11... | collective-permute-start | bytes 147464 | tf_op jit(solution)/shard_map/ppermute | solution.py:428
  8.5 1.3 %collective-permute-start.3 = (bf16[12,16,128]{2,1,0:T(8,128)(2,1)S(1)}, bf16[12,16,128]{2,1,0:T(8,128)(2,1)S(1)}, u32[]{:S(2)}, u32[]{:S(2)}) collective-permute-start(bf16[12,16,128]{2,1,0:T(8,128)(2,1)S(1)} %get-tuple-element.37), channel_id=1, source_target_pairs={{0,8},{1,2},{2,1},{3,4},{4,3},{5,6},{6,5},{7,15},{8,0},{9,10},{10,... | collective-permute-start | bytes 147464 | tf_op jit(solution)/shard_map/ppermute | solution.py:428
  9.8 5.7 %main.1.score_ref = f32[8,96,128]{2,1,0:T(8,128)S(1)} custom-call(bf16[6,16,1024]{2,1,0:T(8,128)(2,1)S(1)} %get-tuple-element.26.own_ref, bf16[3,16,1024]{2,1,0:T(8,128)(2,1)S(1)} %collective-permute-done.below_ref, bf16[3,16,1024]{2,1,0:T(8,128)(2,1)S(1)} %collective-permute-done.1.above_ref, bf16[128,576]{1,0:T(8,128)(2,1)S(1)} %get-tuple-element.29.m1_ref, ...), custom_call_target="tpu_custom_call" | custom-call | flops 5000000000 | bytes 1000000 | tf_op jit(solution)/shard_map/main/pallas_call | solution.py:243
  15.6 0.0 collective-permute-done.2.first_ref
  15.6 0.0 collective-permute-done.3.second_ref
  15.6 0.0 copy-done.1
  15.6 0.0 copy-start.5
  15.6 2.6 %side.1 = (f32[2,96,128]{2,1,0:T(8,128)S(1)}, f32[2,8,128]{2,1,0:T(8,128)S(1)}) custom-call(f32[8,96,128]{2,1,0:T(8,128)S(1)} %main.1.score_ref, bf16[12,16,128]{2,1,0:T(8,128)(2,1)S(1)} %get-tuple-element.34.west_ref, bf16[12,16,128]{2,1,0:T(8,128)(2,1)S(1)} %get-tuple-element.35.east_ref, bf16[12,16,128]{2,1,0:T(8,128)(2,1)S(1)} %collective-permute-done.2.first_ref, ...), custom_call_target="tpu_custom_call" | custom-call | tf_op jit(solution)/shard_map/side/pallas_call | solution.py:344
  18.2 0.1 collective-permute-start.4
  18.2 1.2 %collective-permute-done.4 = f32[2,8,128]{2,1,0:T(8,128)S(1)} collective-permute-done((f32[2,8,128]{2,1,0:T(8,128)S(1)}, f32[2,8,128]{2,1,0:T(8,128)S(1)}, u32[]{:S(2)}, u32[]{:S(2)}) %collective-permute-start.4) | collective-permute-done | bytes 8224 | tf_op jit(solution)/shard_map/ppermute | solution.py:454
  19.4 0.7 %collective-permute-start.5 = (f32[2,8,128]{2,1,0:T(8,128)S(1)}, f32[2,8,128]{2,1,0:T(8,128)S(1)}, u32[]{:S(2)}, u32[]{:S(2)}) collective-permute-start(f32[2,8,128]{2,1,0:T(8,128)S(1)} %add.3.mine_ref), channel_id=1, source_target_pairs={{0,16},{8,24},{16,0},{24,8},{1,17},{9,25},{17,1},{25,9},{2,18},{10... | collective-permute-start | bytes 24584 | tf_op jit(solution)/shard_map/ppermute | solution.py:454
  20.2 1.0 %update.1 = (bf16[6,16,8,128]{3,2,1,0:T(8,128)(2,1)}, f32[6,8,128]{2,1,0:T(8,128)S(1)}) custom-call(f32[8,96,128]{2,1,0:T(8,128)S(1)} %main.1.score_ref, f32[2,96,128]{2,1,0:T(8,128)S(1)} %get-tuple-element.44.side_ref, f32[16,1]{1,0:T(8,128)S(1)} %get-tuple-element.41.c3_ref, bf16[6,16,8,128]{3,2,1,0:T(8,128)(2,1)S(1)} %bitcast.19, ...), custom_call_target="tpu_custom_call" | custom-call | flops 1000000000 | bytes 1000000 | tf_op jit(solution)/shard_map/update/pallas_call | solution.py:375
  21.1 1.9 %collective-permute-done.5.theirs_ref = f32[2,8,128]{2,1,0:T(8,128)S(1)} collective-permute-done((f32[2,8,128]{2,1,0:T(8,128)S(1)}, f32[2,8,128]{2,1,0:T(8,128)S(1)}, u32[]{:S(2)}, u32[]{:S(2)}) %collective-permute-start.5) | collective-permute-done | bytes 8224 | tf_op jit(solution)/shard_map/ppermute | solution.py:454
  23.1 0.0 copy-done.3
  23.1 0.6 %correct.1 = bf16[6,16,8,128]{3,2,1,0:T(8,128)(2,1)} custom-call(f32[2,8,128]{2,1,0:T(8,128)S(1)} %add.3.mine_ref, f32[2,8,128]{2,1,0:T(8,128)S(1)} %collective-permute-done.5.theirs_ref, f32[2,8,128]{2,1,0:T(8,128)S(1)} %bitcast.20, s32[8,128]{1,0:T(8,128)S(1)} %bitcast.21, ...), custom_call_target="tpu_custom_call", output_to_operand_aliasing={{}: (6, {})} | custom-call | tf_op jit(solution)/shard_map/correct/pallas_call | solution.py:402
  (14 shorter events, 0.0 us)
Async XLA Ops:
  0.0 0.9 %copy-start = (bf16[6,16,1,8,128]{4,3,2,1,0:T(8,128)(2,1)S(1)}, bf16[6,16,1,8,128]{4,3,2,1,0:T(8,128)(2,1)}, u32[]{:S(2)}) copy-start(bf16[6,16,1,8,128]{4,3,2,1,0:T(8,128)(2,1)} %param.11) | copy-start | bytes 589828
  0.9 2.8 %copy-start.4 = (bf16[64,64,3,3,3]{1,0,4,3,2:T(8,128)(2,1)S(1)}, bf16[64,64,3,3,3]{1,0,4,3,2:T(8,128)(2,1)}, u32[]{:S(2)}) copy-start(bf16[64,64,3,3,3]{1,0,4,3,2:T(8,128)(2,1)} %param.15) | copy-start | bytes 663556
  0.9 2.8 %copy-start.6 = (bf16[64,16,3,3,3]{0,1,4,3,2:T(8,128)(2,1)S(1)}, bf16[64,16,3,3,3]{0,1,4,3,2:T(8,128)(2,1)}, u32[]{:S(2)}) copy-start(bf16[64,16,3,3,3]{0,1,4,3,2:T(8,128)(2,1)} %param.13) | copy-start | bytes 165892
  0.9 2.8 %copy-start.7 = (bf16[16,64,3,3,3]{1,0,4,3,2:T(8,128)(2,1)S(1)}, bf16[16,64,3,3,3]{1,0,4,3,2:T(8,128)(2,1)}, u32[]{:S(2)}) copy-start(bf16[16,64,3,3,3]{1,0,4,3,2:T(8,128)(2,1)} %param.17) | copy-start | bytes 165892
  1.1 2.5 %copy-start.11 = (s32[6]{0:T(128)S(1)}, s32[6]{0:T(128)}, u32[]{:S(2)}) copy-start(s32[6]{0:T(128)} %param.19) | copy-start | bytes 76
  1.1 4.7 %collective-permute-start = (bf16[3,16,1024]{2,1,0:T(8,128)(2,1)S(1)}, bf16[3,16,1024]{2,1,0:T(8,128)(2,1)S(1)}, u32[]{:S(2)}, u32[]{:S(2)}) collective-permute-start(bf16[3,16,1024]{2,1,0:T(8,128)(2,1)S(1)} %get-tuple-element.27), channel_id=1, source_target_pairs={{0,8},{8,16},{16,24},{24,0},{1,9},{9,17},{17,25},{25,1},{2,10},{10... | collective-permute-start | bytes 294920 | tf_op jit(solution)/shard_map/ppermute | solution.py:415
  1.6 2.0 %copy-start.8 = (f32[16]{0:T(128)S(1)}, f32[16]{0:T(128)}, u32[]{:S(2)}) copy-start(f32[16]{0:T(128)} %param.18) | copy-start | bytes 196
  1.6 2.0 %copy-start.9 = (f32[64]{0:T(128)S(1)}, f32[64]{0:T(128)}, u32[]{:S(2)}) copy-start(f32[64]{0:T(128)} %param.16) | copy-start | bytes 772
  1.6 2.0 %copy-start.10 = (f32[64]{0:T(128)S(1)}, f32[64]{0:T(128)}, u32[]{:S(2)}) copy-start(f32[64]{0:T(128)} %param.14) | copy-start | bytes 772
  1.6 5.1 %collective-permute-start.1 = (bf16[3,16,1024]{2,1,0:T(8,128)(2,1)S(1)}, bf16[3,16,1024]{2,1,0:T(8,128)(2,1)S(1)}, u32[]{:S(2)}, u32[]{:S(2)}) collective-permute-start(bf16[3,16,1024]{2,1,0:T(8,128)(2,1)S(1)} %get-tuple-element.28), channel_id=1, source_target_pairs={{0,24},{8,0},{16,8},{24,16},{1,25},{9,1},{17,9},{25,17},{2,26},{10... | collective-permute-start | bytes 294920 | tf_op jit(solution)/shard_map/ppermute | solution.py:415
  6.9 8.6 %collective-permute-start.2 = (bf16[12,16,128]{2,1,0:T(8,128)(2,1)S(1)}, bf16[12,16,128]{2,1,0:T(8,128)(2,1)S(1)}, u32[]{:S(2)}, u32[]{:S(2)}) collective-permute-start(bf16[12,16,128]{2,1,0:T(8,128)(2,1)S(1)} %get-tuple-element.36), channel_id=1, source_target_pairs={{0,1},{1,0},{2,3},{3,2},{4,5},{5,4},{6,7},{7,6},{8,9},{9,8},{10,11... | collective-permute-start | bytes 147464 | tf_op jit(solution)/shard_map/ppermute | solution.py:428
  8.5 7.0 %collective-permute-start.3 = (bf16[12,16,128]{2,1,0:T(8,128)(2,1)S(1)}, bf16[12,16,128]{2,1,0:T(8,128)(2,1)S(1)}, u32[]{:S(2)}, u32[]{:S(2)}) collective-permute-start(bf16[12,16,128]{2,1,0:T(8,128)(2,1)S(1)} %get-tuple-element.37), channel_id=1, source_target_pairs={{0,8},{1,2},{2,1},{3,4},{4,3},{5,6},{6,5},{7,15},{8,0},{9,10},{10,... | collective-permute-start | bytes 147464 | tf_op jit(solution)/shard_map/ppermute | solution.py:428
  9.8 5.8 %copy-start.1 = (bf16[6,16,1,8,128]{4,3,2,1,0:T(8,128)(2,1)S(1)}, bf16[6,16,1,8,128]{4,3,2,1,0:T(8,128)(2,1)}, u32[]{:S(2)}) copy-start(bf16[6,16,1,8,128]{4,3,2,1,0:T(8,128)(2,1)} %param.11) | copy-start | bytes 589828
  15.6 4.6 %copy-start.5 = (bf16[6,16,1,8,128]{4,3,2,1,0:T(8,128)(2,1)S(1)}, bf16[6,16,1,8,128]{4,3,2,1,0:T(8,128)(2,1)}, u32[]{:S(2)}) copy-start(bf16[6,16,1,8,128]{4,3,2,1,0:T(8,128)(2,1)} %param.12) | copy-start | bytes 589828
  18.2 1.2 %collective-permute-start.4 = (f32[2,8,128]{2,1,0:T(8,128)S(1)}, f32[2,8,128]{2,1,0:T(8,128)S(1)}, u32[]{:S(2)}, u32[]{:S(2)}) collective-permute-start(f32[2,8,128]{2,1,0:T(8,128)S(1)} %get-tuple-element.43), channel_id=1, source_target_pairs={{0,8},{8,0},{16,24},{24,16},{1,9},{9,1},{17,25},{25,17},{2,10},{10... | collective-permute-start | bytes 24584 | tf_op jit(solution)/shard_map/ppermute | solution.py:454
  19.4 3.7 %collective-permute-start.5 = (f32[2,8,128]{2,1,0:T(8,128)S(1)}, f32[2,8,128]{2,1,0:T(8,128)S(1)}, u32[]{:S(2)}, u32[]{:S(2)}) collective-permute-start(f32[2,8,128]{2,1,0:T(8,128)S(1)} %add.3.mine_ref), channel_id=1, source_target_pairs={{0,16},{8,24},{16,0},{24,8},{1,17},{9,25},{17,1},{25,9},{2,18},{10... | collective-permute-start | bytes 24584 | tf_op jit(solution)/shard_map/ppermute | solution.py:454
  20.2 2.9 %copy-start.2 = (f32[2,1,8,128]{3,2,1,0:T(8,128)S(1)}, f32[2,1,8,128]{3,2,1,0:T(8,128)}, u32[]{:S(2)}) copy-start(f32[2,1,8,128]{3,2,1,0:T(8,128)} %param.20) | copy-start | bytes 24580
  21.1 1.9 %copy-start.3 = (s32[1,8,128]{2,1,0:T(8,128)S(1)}, s32[1,8,128]{2,1,0:T(8,128)}, u32[]{:S(2)}) copy-start(s32[1,8,128]{2,1,0:T(8,128)} %param.21) | copy-start | bytes 12292

commit v5 on v4

--- a/solution.py
+++ b/solution.py
@@ -12,6 +12,7 @@
 PITCH = 16
 VMEM = pl.BlockSpec(memory_space=pltpu.VMEM)
 ANYWHERE = pl.BlockSpec(memory_space=pltpu.HBM)
+EARLY = 4
 LIMIT = 24 * 1024 * 1024
 
 
@@ -83,7 +84,7 @@
 
 def weights_kernel(
     w1_ref, w2_ref, w3_ref, small_ref,
-    m1_ref, m2_ref, m3_ref, s1_ref, s2_ref, s3_ref, c1_ref, c2_ref, c3_ref, days_ref, f2, f3,
+    m1_ref, m2_ref, m3_ref, s1_ref, s2_ref, s3_ref, c1_ref, c2_ref, c3_ref, days_ref, head_ref, f2, f3,
 ):
     small = jnp.broadcast_to(small_ref[...], (8, small_ref.shape[1])).T[:, 0:1]
     at = 0
@@ -122,6 +123,9 @@
 
     place(w2_ref, f2, m2_ref, s2_ref, 2, hid)
     place(w3_ref, f3, m3_ref, s3_ref, frames, fields)
+    shape = (head_ref.shape[0], s3_ref.shape[0])
+    pick = lanes(shape) == fields * lax.broadcasted_iota(jnp.int32, shape, 0)
+    head_ref[...] = jnp.dot(pick.astype(F32).astype(BF), s3_ref[...], preferred_element_type=F32).astype(BF)
 
 
 def make_weights(w1, w2, w3, small, frames):
@@ -140,6 +144,7 @@
             shape_of((hid, 1), F32),
             shape_of((fields, 1), F32),
             shape_of((frames, LANES), F32),
+            shape_of((-(-3 * frames // 16) * 16, (frames + 2) * 3 * hid), BF),
         ),
         [VMEM] * 4,
         [pltpu.VMEM((2, w.shape[1], 27 * hid + LANES // 2), BF) for w in (w2, w3)],
@@ -201,7 +206,7 @@
 
 
 def main_kernel(
-    own_ref, below_ref, above_ref, m1_ref, m2_ref, m3_ref, c1_ref, c2_ref, score_ref, s1, s2, s3
+    own_ref, below_ref, above_ref, m1_ref, m2_ref, c1_ref, c2_ref, s3, s1, s2
 ):
     frames = own_ref.shape[0]
     rows = own_ref.shape[2] // LANES
@@ -228,30 +233,26 @@
 
     layer(s1, s2, m1_ref, c1_ref[...], frames + 4, -2)
     layer(s2, s3, m2_ref, c2_ref[...], frames + 2, -1)
-    for y in range(0, rows, 2):
-        acc = jnp.dot(m3_ref[...], window(s3, 0, frames + 2, y), preferred_element_type=F32)
-        score_ref[y], score_ref[y + 1] = acc[:, tile(0)], acc[:, tile(1)]
 
 
 UNROLL = True
 
 
-def make_main(own, below, above, m1, m2, m3, c1, c2):
+def make_main(own, below, above, m1, m2, c1, c2):
     frames, chans, width = own.shape
     hid = c1.shape[0]
     wide = width + 2 * LANES
     return call(
         main_kernel,
         "main",
-        (shape_of((width // LANES, m3.shape[0], LANES), F32),),
-        [VMEM] * 8,
+        (shape_of((frames + 2, 3 * hid, wide), BF),),
+        [VMEM] * 7,
         [
             pltpu.VMEM((frames + 6, 3 * chans, wide), BF),
             pltpu.VMEM((frames + 4, 3 * hid, wide), BF),
-            pltpu.VMEM((frames + 2, 3 * hid, wide), BF),
         ],
         cost=5_000_000_000,
-    )(own, below, above, m1, m2, m3, c1, c2)[0]
+    )(own, below, above, m1, m2, c1, c2)[0]
 
 
 def spread_side(dst, f, v):
@@ -263,14 +264,18 @@
         dst[f, 2 * chans : 3 * chans, tile(half)] = turn(w, -1)
 
 
+def three_rows(up, mid, down):
+    lane = lanes(mid.shape)
+    up = jnp.where(lane >= PITCH, turn(up, PITCH), 0.0)
+    down = jnp.where(lane < LANES - PITCH, turn(down, -PITCH), 0.0)
+    return mid + up + down
+
+
 def over_rows(acc, at, outs):
     halves = []
     for half in range(2):
         up, mid, down = (acc[at + d * outs : at + (d + 1) * outs, tile(half)] for d in range(3))
-        lane = lanes((outs, LANES))
-        up = jnp.where(lane >= PITCH, turn(up, PITCH), 0.0)
-        down = jnp.where(lane < LANES - PITCH, turn(down, -PITCH), 0.0)
-        halves.append(mid + up + down)
+        halves.append(three_rows(up, mid, down))
     return jnp.concatenate(halves, axis=1)
 
 
@@ -281,8 +286,8 @@
 
 
 def side_kernel(
-    score_ref, west_ref, east_ref, first_ref, second_ref, s1_ref, s2_ref, s3_ref, c1_ref, c2_ref, c3_ref,
-    state_ref, day_ref, side_ref, part_ref, t1, t2, t3,
+    wide_ref, west_ref, east_ref, first_ref, second_ref, s1_ref, s2_ref, head_ref, c1_ref, c2_ref, c3_ref,
+    state_ref, day_ref, t3, part_ref, t1, t2, own, ends,
 ):
     frames, fields, rows, _ = state_ref.shape
     chans, hid = west_ref.shape[1], c1_ref.shape[0]
@@ -315,19 +320,21 @@
 
     layer(t1, t2, s1_ref, c1_ref[...], frames + 4, -2)
     layer(t2, t3, s2_ref, c2_ref[...], frames + 2, -1)
+    own[0] = jnp.zeros(own.shape[1:], F32)
+    own[rows + 1] = jnp.zeros(own.shape[1:], F32)
+    for y in range(0, rows, 2):
+        z = jnp.concatenate([wide_ref[j, :, (y + 1) * LANES : (y + 3) * LANES] for j in range(frames + 2)], axis=0)
+        acc = jnp.dot(head_ref[...], z, preferred_element_type=F32)
+        own[y + 1], own[y + 2] = acc[:, tile(0)], acc[:, tile(1)]
     z = jnp.concatenate([t3[j] for j in range(frames + 2)], axis=0)
-    acc = jnp.dot(s3_ref[...], z, preferred_element_type=F32)
-    for f in range(frames):
-        both = over_rows(acc, f * 3 * fields, fields)
-        for half in range(2):
-            side_ref[half, f * fields : (f + 1) * fields] = both[:, tile(half)]
-
+    acc = jnp.dot(head_ref[...], z, preferred_element_type=F32)
+    ends[0], ends[1] = acc[:, tile(0)], acc[:, tile(1)]
+    offsets = [pl.ds(dy, frames, stride=3) for dy in range(3)]
+    west, east = (three_rows(*(ends[half, at] for at in offsets)) for half in range(2))
     days = part_ref.shape[0]
-    heads = pl.ds(0, frames, stride=fields)
-    west, east = side_ref[0, heads], side_ref[1, heads]
     day = day_ref[...]
     for y in range(rows):
-        v = patched(score_ref[y, heads], west, east, y)
+        v = patched(sum(own[y + dy, offsets[dy]] for dy in range(3)), west, east, y)
         for d in range(days):
             part_ref[d, y : y + 1, :] = jnp.sum(jnp.where(day == d, v, 0.0), axis=0, keepdims=True)
     base = c3_ref[0:1, 0:1]
@@ -338,48 +345,82 @@
         part_ref[d] = total
 
 
-def make_side(score, west, east, first, second, s1, s2, s3, c1, c2, c3, state, day, days):
+def make_side(wide, west, east, first, second, s1, s2, head, c1, c2, c3, state, day, days):
     frames, fields, rows, _ = state.shape
     chans, hid = west.shape[1], c1.shape[0]
     return call(
         side_kernel,
         "side",
-        (shape_of((2, frames * fields, LANES), F32), shape_of((days, rows, LANES), F32)),
+        (shape_of((frames + 2, 3 * hid, 2 * LANES), BF), shape_of((days, rows, LANES), F32)),
         [VMEM] * 13,
         [
             pltpu.VMEM((frames + 6, 3 * chans, 2 * LANES), BF),
             pltpu.VMEM((frames + 4, 3 * hid, 2 * LANES), BF),
-            pltpu.VMEM((frames + 2, 3 * hid, 2 * LANES), BF),
+            pltpu.VMEM((rows + 2, head.shape[0], LANES), F32),
+            pltpu.VMEM((2, head.shape[0], LANES), F32),
         ],
-    )(score, west, east, first, second, s1, s2, s3, c1, c2, c3, state, day)
-
-
-def update_kernel(score_ref, side_ref, c3_ref, state_ref, noise_ref, out_ref, head_ref, scr):
+    )(wide, west, east, first, second, s1, s2, head, c1, c2, c3, state, day)
+
+
+def own_score(wide_ref, m3_ref, frames, y):
+    acc = jnp.dot(m3_ref[...], window(wide_ref, 0, frames + 2, y), preferred_element_type=F32)
+    return acc[:, tile(0)], acc[:, tile(1)]
+
+
+def early_kernel(wide_ref, t3, m3_ref, s3_ref, score_ref, side_ref):
+    frames = t3.shape[0] - 2
+    fields = m3_ref.shape[0] // frames
+    for y in range(0, score_ref.shape[0], 2):
+        score_ref[y], score_ref[y + 1] = own_score(wide_ref, m3_ref, frames, y)
+    z = jnp.concatenate([t3[j] for j in range(frames + 2)], axis=0)
+    acc = jnp.dot(s3_ref[...], z, preferred_element_type=F32)
+    for f in range(frames):
+        both = over_rows(acc, f * 3 * fields, fields)
+        for half in range(2):
+            side_ref[half, f * fields : (f + 1) * fields] = both[:, tile(half)]
+
+
+def make_early(wide, t3, m3, s3, count):
+    return call(
+        early_kernel,
+        "early",
+        (shape_of((count, m3.shape[0], LANES), F32), shape_of((2, m3.shape[0], LANES), F32)),
+        [VMEM] * 4,
+        cost=1_000_000_000,
+    )(wide, t3, m3, s3)
+
+
+def update_kernel(wide_ref, m3_ref, score_ref, side_ref, c3_ref, state_ref, noise_ref, out_ref, head_ref, rest, scr):
     frames, fields, rows, _ = state_ref.shape
+    done = score_ref.shape[0]
+    for y in range(done, rows, 2):
+        rest[y - done], rest[y - done + 1] = own_score(wide_ref, m3_ref, frames, y)
     bias = c3_ref[...]
     for f in range(frames):
         at = slice(f * fields, (f + 1) * fields)
         west, east = side_ref[0, at], side_ref[1, at]
         for y in range(rows):
-            scr[f, pl.ds(y, fields, stride=rows), :] = (
-                patched(score_ref[y, at], west, east, y) + bias
-            )
+            v = score_ref[y, at] if y < done else rest[y - done, at]
+            scr[f, pl.ds(y, fields, stride=rows), :] = patched(v, west, east, y) + bias
         score = scr[f].reshape(fields, rows, LANES)
         moved = state_ref[f].astype(F32) + 0.8 * score + 0.5 * noise_ref[f].astype(F32)
         out_ref[f] = moved.astype(BF)
         head_ref[f] = moved[0]
 
 
-def make_update(score, side, c3, state, noise):
+def make_update(wide, m3, score, side, c3, state, noise):
     frames, fields, rows, _ = state.shape
     return call(
         update_kernel,
         "update",
         (shape_of(state.shape, BF), shape_of((frames, rows, LANES), F32)),
-        [VMEM] * 5,
-        [pltpu.VMEM((frames, fields * rows, LANES), F32)],
-        cost=1_000_000_000,
-    )(score, side, c3, state, noise)
+        [VMEM] * 7,
+        [
+            pltpu.VMEM((rows - score.shape[0], frames * fields, LANES), F32),
+            pltpu.VMEM((frames, fields * rows, LANES), F32),
+        ],
+        cost=2_000_000_000,
+    )(wide, m3, score, side, c3, state, noise)
 
 
 def correct_kernel(mine_ref, theirs_ref, observed_ref, mask_ref, head_ref, day_ref, _, out_ref, buf, sem):
@@ -440,14 +481,15 @@
     own, low, high = make_rows(state)
     below, above = shifted(high, "tm", 1), shifted(low, "tm", -1)
     small = jnp.concatenate([bias_one, bias_two, bias_three, day_of_frame.astype(F32)])[None]
-    m1, m2, m3, s1, s2, s3, c1, c2, c3, days = make_weights(w1, w2, w3, small, state.shape[0])
+    m1, m2, m3, s1, s2, s3, c1, c2, c3, days, head = make_weights(w1, w2, w3, small, state.shape[0])
     west, east, send1, send2 = make_edges(own, below, above)
     near, far = swapped(send1, 0), swapped(send2, 1)
-    score = make_main(own, below, above, m1, m2, m3, c1, c2)
-    side, mine = make_side(
-        score, west, east, near, far, s1, s2, s3, c1, c2, c3, state, days, observed.shape[0]
+    wide = make_main(own, below, above, m1, m2, c1, c2)
+    t3, mine = make_side(
+        wide, west, east, near, far, s1, s2, head, c1, c2, c3, state, days, observed.shape[0]
     )
-    out, head = make_update(score, side, c3, state, noise)
+    score, side = make_early(wide, t3, m3, s3, EARLY)
+    out, first = make_update(wide, m3, score, side, c3, state, noise)
     count = lax.axis_size("tm")
     reach = 1
     while True:
@@ -456,7 +498,7 @@
         if reach >= count:
             break
         mine = mine + theirs
-    out = make_correct(mine, theirs, observed[:, 0], obs_mask[0], head, days, out)
+    out = make_correct(mine, theirs, observed[:, 0], obs_mask[0], first, days, out)
     return out[:, :, None]
 
 

time: 23.8 us -> 22.7 us (0.954)
  waiting for transfers between devices: 5.23 us -> 3.21 us
  Pallas kernels: 11.1 us -> 11.8 us
    ppermute x2, waiting for transfers between devices: 3.07 us -> 1.09 us  [body(): theirs = lax.ppermute(mine, 'tm', [(i, i ^ reach) for i in range(count)])]
    pallas_call x1, Pallas kernels: 0.98 us -> 1.65 us  [make_update(): call(update_kernel, 'update', (shape_of(state.shape, BF), shape_of((frame...]
    pallas_call x2 -> x3, Pallas kernels: 8.3 us -> 8.23 us  [the longest x1 4.46 us: make_main(): call(main_kernel, 'main', (shape_of((frames + 2, 3 * hid, wide), BF),), [...]
  transfers between devices with their start and end apart: 6 -> 6, of which waited for: 4 -> 3; matrix products, arithmetic and copies ran while one was open for 0% -> 0% of each run, Pallas kernels for 32% -> 36%
where the time goes in v5:
time: 22.7 us; the launch traced here: 22.6 us
  Pallas kernels  11.8 us (52%)
  starting transfers between devices  6.39 us (28%)
  waiting for transfers between devices  3.21 us (14%)
  local copies, waits for them, and re-layouts  0.98 us (4%)
    pallas_call x1, Pallas kernels, make_main(): call(main_kernel, 'main', (shape_of((frames + 2, 3 * hid, wide), BF),), [...  4.46 us
    ppermute x2, starting transfers between devices, swapped(): return lax.ppermute(value, ('tm', 'space'), pairs)  2.85 us
    pallas_call x1, Pallas kernels, make_side(): call(side_kernel, 'side', (shape_of((frames + 2, 3 * hid, 2 * LANES), BF)...  2.57 us
    ppermute x2, starting transfers between devices, shifted(): lax.ppermute(value, axis, [(i, (i + steps) % count) for i in range(count)])  2.49 us
    ppermute x2, waiting for transfers between devices, shifted(): lax.ppermute(value, axis, [(i, (i + steps) % count) for i in range(count)])  2.11 us
    pallas_call x1, Pallas kernels, make_update(): call(update_kernel, 'update', (shape_of(state.shape, BF), shape_of((frame...  1.65 us
    pallas_call x1, Pallas kernels, make_early(): call(early_kernel, 'early', (shape_of((count, m3.shape[0], LANES), F32),...  1.2 us
    ppermute x2, waiting for transfers between devices, body(): theirs = lax.ppermute(mine, 'tm', [(i, i ^ reach) for i in range(count)])  1.09 us
  transfers between devices with their start and end apart: 6, of which 3 were waited for; matrix products, arithmetic and copies ran while one was open for 0% of the time, Pallas kernels for 36%

profile of v5, /device:TPU:0, one launch (start us, length us, event | category | flops | bytes accessed | tf_op | source)
XLA Modules:
  0.0 22.6 jit_solution(9727306678370373094)
XLA Ops:
  0.0 0.9 %copy-done = bf16[6,16,1,8,128]{4,3,2,1,0:T(8,128)(2,1)S(1)} copy-done((bf16[6,16,1,8,128]{4,3,2,1,0:T(8,128)(2,1)S(1)}, bf16[6,16,1,8,128]{4,3,2,1,0:T(8,128)(2,1)}, u32[]{:S(2)}) %copy-start) | copy-done | bytes 196632
  0.9 0.0 copy-start.4
  0.9 0.0 copy-start.6
  1.0 0.1 rows.1
  1.1 0.5 %collective-permute-start = (bf16[3,16,1024]{2,1,0:T(8,128)(2,1)S(1)}, bf16[3,16,1024]{2,1,0:T(8,128)(2,1)S(1)}, u32[]{:S(2)}, u32[]{:S(2)}) collective-permute-start(bf16[3,16,1024]{2,1,0:T(8,128)(2,1)S(1)} %get-tuple-element.30), channel_id=1, source_target_pairs={{0,8},{8,16},{16,24},{24,0},{1,9},{9,17},{17,25},{25,1},{2,10},{10... | collective-permute-start | bytes 294920 | tf_op jit(solution)/shard_map/ppermute | solution.py:456
  1.6 2.0 %collective-permute-start.1 = (bf16[3,16,1024]{2,1,0:T(8,128)(2,1)S(1)}, bf16[3,16,1024]{2,1,0:T(8,128)(2,1)S(1)}, u32[]{:S(2)}, u32[]{:S(2)}) collective-permute-start(bf16[3,16,1024]{2,1,0:T(8,128)(2,1)S(1)} %get-tuple-element.31), channel_id=1, source_target_pairs={{0,24},{8,0},{16,8},{24,16},{1,25},{9,1},{17,9},{25,17},{2,26},{10... | collective-permute-start | bytes 294920 | tf_op jit(solution)/shard_map/ppermute | solution.py:456
  3.6 0.0 copy-done.11
  3.6 0.0 copy-done.9
  3.6 0.0 copy-done.10
  3.6 0.1 pad_maximum_fusion
  3.7 0.0 copy-done.6
  3.7 0.9 %weights.1 = (bf16[128,576]{1,0:T(8,128)(2,1)S(1)}, bf16[128,2304]{1,0:T(8,128)(2,1)S(1)}, bf16[96,4608]{1,0:T(8,128)(2,1)S(1)}, bf16[384,192]{1,0:T(8,128)(2,1)...) custom-call(bf16[432,64]{1,0:T(8,128)(2,1)S(1)} %bitcast.25, ...), custom_call_target="tpu_custom_call" | custom-call | flops 1000000000 | bytes 1000000 | tf_op jit(solution)/shard_map/weights/pallas_call | solution.py:133
  4.6 1.2 %collective-permute-done.below_ref = bf16[3,16,1024]{2,1,0:T(8,128)(2,1)S(1)} collective-permute-done((bf16[3,16,1024]{2,1,0:T(8,128)(2,1)S(1)}, bf16[3,16,1024]{2,1,0:T(8,128)(2,1)S(1)}, u32[]{:S(2)}, u32[]{:S(2)}) %collective-permute-start) | collective-permute-done | bytes 98336 | tf_op jit(solution)/shard_map/ppermute | solution.py:456
  5.8 0.9 %collective-permute-done.1.above_ref = bf16[3,16,1024]{2,1,0:T(8,128)(2,1)S(1)} collective-permute-done((bf16[3,16,1024]{2,1,0:T(8,128)(2,1)S(1)}, bf16[3,16,1024]{2,1,0:T(8,128)(2,1)S(1)}, u32[]{:S(2)}, u32[]{:S(2)}) %collective-permute-start.1) | collective-permute-done | bytes 98336 | tf_op jit(solution)/shard_map/ppermute | solution.py:456
  6.7 0.3 %edges.1 = (bf16[12,16,128]{2,1,0:T(8,128)(2,1)S(1)}, bf16[12,16,128]{2,1,0:T(8,128)(2,1)S(1)}, bf16[12,16,128]{2,1,0:T(8,128)(2,1)S(1)}, bf16[12,16,128]{2,1,0:T(8,128)(2,1)S(1)}) custom-call(bf16[6,16,1024]{2,1,0:T(8,128)(2,1)S(1)} %get-tuple-element.29.own_ref, bf16[3,16,1024]{2,1,0:T(8,128)(2,1)S(1)} %collective-permute-done.below_ref, ...), custom_call_target="tpu_custom_call" | custom-call | tf_op jit(solution)/shard_map/edges/pallas_call | solution.py:186
  7.0 1.6 %collective-permute-start.2 = (bf16[12,16,128]{2,1,0:T(8,128)(2,1)S(1)}, bf16[12,16,128]{2,1,0:T(8,128)(2,1)S(1)}, u32[]{:S(2)}, u32[]{:S(2)}) collective-permute-start(bf16[12,16,128]{2,1,0:T(8,128)(2,1)S(1)} %get-tuple-element.38), channel_id=1, source_target_pairs={{0,1},{1,0},{2,3},{3,2},{4,5},{5,4},{6,7},{7,6},{8,9},{9,8},{10,11... | collective-permute-start | bytes 147464 | tf_op jit(solution)/shard_map/ppermute | solution.py:469
  8.6 1.3 %collective-permute-start.3 = (bf16[12,16,128]{2,1,0:T(8,128)(2,1)S(1)}, bf16[12,16,128]{2,1,0:T(8,128)(2,1)S(1)}, u32[]{:S(2)}, u32[]{:S(2)}) collective-permute-start(bf16[12,16,128]{2,1,0:T(8,128)(2,1)S(1)} %get-tuple-element.39), channel_id=1, source_target_pairs={{0,8},{1,2},{2,1},{3,4},{4,3},{5,6},{6,5},{7,15},{8,0},{9,10},{10,... | collective-permute-start | bytes 147464 | tf_op jit(solution)/shard_map/ppermute | solution.py:469
  9.8 4.5 %main.1.wide_ref = bf16[8,192,1280]{2,1,0:T(8,128)(2,1)S(1)} custom-call(bf16[6,16,1024]{2,1,0:T(8,128)(2,1)S(1)} %get-tuple-element.29.own_ref, bf16[3,16,1024]{2,1,0:T(8,128)(2,1)S(1)} %collective-permute-done.below_ref, bf16[3,16,1024]{2,1,0:T(8,128)(2,1)S(1)} %collective-permute-done.1.above_ref, bf16[128,576]{1,0:T(8,128)(2,1)S(1)} %get-tuple-element.32.m1_ref, ...), custom_call_target="tpu_custom_call" | custom-call | flops 5000000000 | bytes 1000000 | tf_op jit(solution)/shard_map/main/pallas_call | solution.py:245
  14.3 0.0 collective-permute-done.2.first_ref
  14.3 0.0 collective-permute-done.3.second_ref
  14.3 2.6 %side.1 = (bf16[8,192,256]{2,1,0:T(8,128)(2,1)S(1)}, f32[2,8,128]{2,1,0:T(8,128)S(1)}) custom-call(bf16[8,192,1280]{2,1,0:T(8,128)(2,1)S(1)} %main.1.wide_ref, bf16[12,16,128]{2,1,0:T(8,128)(2,1)S(1)} %get-tuple-element.36.west_ref, bf16[12,16,128]{2,1,0:T(8,128)(2,1)S(1)} %get-tuple-element.37.east_ref, ...), custom_call_target="tpu_custom_call" | custom-call | tf_op jit(solution)/shard_map/side/pallas_call | solution.py:351
  16.9 0.0 copy-start.5
  16.9 0.1 collective-permute-start.4
  17.0 1.2 %early.1 = (f32[4,96,128]{2,1,0:T(8,128)S(1)}, f32[2,96,128]{2,1,0:T(8,128)S(1)}) custom-call(bf16[8,192,1280]{2,1,0:T(8,128)(2,1)S(1)} %main.1.wide_ref, bf16[8,192,256]{2,1,0:T(8,128)(2,1)S(1)} %get-tuple-element.47.t3, bf16[96,4608]{1,0:T(8,128)(2,1)S(1)} %get-tuple-element.46.m3_ref, bf16[288,1536]{1,0:T(8,128)(2,1)S(1)} %get-tuple-element.48.s3_ref), custom_call_target="tpu_custom_call" | custom-call | flops 1000000000 | bytes 1000000 | tf_op jit(solution)/shard_map/early/pallas_call | solution.py:384
  18.2 0.0 copy-start.2
  18.2 0.0 copy-start.3
  18.2 0.0 collective-permute-done.4
  18.2 1.0 %collective-permute-start.5 = (f32[2,8,128]{2,1,0:T(8,128)S(1)}, f32[2,8,128]{2,1,0:T(8,128)S(1)}, u32[]{:S(2)}, u32[]{:S(2)}) collective-permute-start(f32[2,8,128]{2,1,0:T(8,128)S(1)} %add.3.mine_ref), channel_id=1, source_target_pairs={{0,16},{8,24},{16,0},{24,8},{1,17},{9,25},{17,1},{25,9},{2,18},{10... | collective-permute-start | bytes 24584 | tf_op jit(solution)/shard_map/ppermute | solution.py:496
  19.2 1.6 %update.1 = (bf16[6,16,8,128]{3,2,1,0:T(8,128)(2,1)}, f32[6,8,128]{2,1,0:T(8,128)S(1)}) custom-call(bf16[8,192,1280]{2,1,0:T(8,128)(2,1)S(1)} %main.1.wide_ref, bf16[96,4608]{1,0:T(8,128)(2,1)S(1)} %get-tuple-element.46.m3_ref, f32[4,96,128]{2,1,0:T(8,128)S(1)} %get-tuple-element.49.score_ref, f32[2,96,128]{2,1,0:T(8,128)S(1)} %get-tuple-element.50.side_ref, ...), custom_call_target="tpu_custom_call" | custom-call | flops 2000000000 | bytes 1000000 | tf_op jit(solution)/shard_map/update/pallas_call | solution.py:413
  20.9 1.1 %collective-permute-done.5.theirs_ref = f32[2,8,128]{2,1,0:T(8,128)S(1)} collective-permute-done((f32[2,8,128]{2,1,0:T(8,128)S(1)}, f32[2,8,128]{2,1,0:T(8,128)S(1)}, u32[]{:S(2)}, u32[]{:S(2)}) %collective-permute-start.5) | collective-permute-done | bytes 8224 | tf_op jit(solution)/shard_map/ppermute | solution.py:496
  22.0 0.0 copy-done.2
  22.0 0.6 %correct.1 = bf16[6,16,8,128]{3,2,1,0:T(8,128)(2,1)} custom-call(f32[2,8,128]{2,1,0:T(8,128)S(1)} %add.3.mine_ref, f32[2,8,128]{2,1,0:T(8,128)S(1)} %collective-permute-done.5.theirs_ref, f32[2,8,128]{2,1,0:T(8,128)S(1)} %bitcast.20, s32[8,128]{1,0:T(8,128)S(1)} %bitcast.21, ...), custom_call_target="tpu_custom_call", output_to_operand_aliasing={{}: (6, {})} | custom-call | tf_op jit(solution)/shard_map/correct/pallas_call | solution.py:443
  (15 shorter events, 0.0 us)
Async XLA Ops:
  0.0 0.9 %copy-start = (bf16[6,16,1,8,128]{4,3,2,1,0:T(8,128)(2,1)S(1)}, bf16[6,16,1,8,128]{4,3,2,1,0:T(8,128)(2,1)}, u32[]{:S(2)}) copy-start(bf16[6,16,1,8,128]{4,3,2,1,0:T(8,128)(2,1)} %param.11) | copy-start | bytes 589828
  0.9 2.7 %copy-start.11 = (s32[6]{0:T(128)S(1)}, s32[6]{0:T(128)}, u32[]{:S(2)}) copy-start(s32[6]{0:T(128)} %param.19) | copy-start | bytes 76
  0.9 2.7 %copy-start.8 = (f32[16]{0:T(128)S(1)}, f32[16]{0:T(128)}, u32[]{:S(2)}) copy-start(f32[16]{0:T(128)} %param.18) | copy-start | bytes 196
  0.9 2.7 %copy-start.9 = (f32[64]{0:T(128)S(1)}, f32[64]{0:T(128)}, u32[]{:S(2)}) copy-start(f32[64]{0:T(128)} %param.16) | copy-start | bytes 772
  0.9 2.7 %copy-start.10 = (f32[64]{0:T(128)S(1)}, f32[64]{0:T(128)}, u32[]{:S(2)}) copy-start(f32[64]{0:T(128)} %param.14) | copy-start | bytes 772
  0.9 2.8 %copy-start.4 = (bf16[64,64,3,3,3]{1,0,4,3,2:T(8,128)(2,1)S(1)}, bf16[64,64,3,3,3]{1,0,4,3,2:T(8,128)(2,1)}, u32[]{:S(2)}) copy-start(bf16[64,64,3,3,3]{1,0,4,3,2:T(8,128)(2,1)} %param.15) | copy-start | bytes 663556
  0.9 2.7 %copy-start.6 = (bf16[64,16,3,3,3]{0,1,4,3,2:T(8,128)(2,1)S(1)}, bf16[64,16,3,3,3]{0,1,4,3,2:T(8,128)(2,1)}, u32[]{:S(2)}) copy-start(bf16[64,16,3,3,3]{0,1,4,3,2:T(8,128)(2,1)} %param.13) | copy-start | bytes 165892
  1.0 2.7 %copy-start.7 = (bf16[16,64,3,3,3]{1,0,4,3,2:T(8,128)(2,1)S(1)}, bf16[16,64,3,3,3]{1,0,4,3,2:T(8,128)(2,1)}, u32[]{:S(2)}) copy-start(bf16[16,64,3,3,3]{1,0,4,3,2:T(8,128)(2,1)} %param.17) | copy-start | bytes 165892
  1.1 4.7 %collective-permute-start = (bf16[3,16,1024]{2,1,0:T(8,128)(2,1)S(1)}, bf16[3,16,1024]{2,1,0:T(8,128)(2,1)S(1)}, u32[]{:S(2)}, u32[]{:S(2)}) collective-permute-start(bf16[3,16,1024]{2,1,0:T(8,128)(2,1)S(1)} %get-tuple-element.30), channel_id=1, source_target_pairs={{0,8},{8,16},{16,24},{24,0},{1,9},{9,17},{17,25},{25,1},{2,10},{10... | collective-permute-start | bytes 294920 | tf_op jit(solution)/shard_map/ppermute | solution.py:456
  1.6 5.1 %collective-permute-start.1 = (bf16[3,16,1024]{2,1,0:T(8,128)(2,1)S(1)}, bf16[3,16,1024]{2,1,0:T(8,128)(2,1)S(1)}, u32[]{:S(2)}, u32[]{:S(2)}) collective-permute-start(bf16[3,16,1024]{2,1,0:T(8,128)(2,1)S(1)} %get-tuple-element.31), channel_id=1, source_target_pairs={{0,24},{8,0},{16,8},{24,16},{1,25},{9,1},{17,9},{25,17},{2,26},{10... | collective-permute-start | bytes 294920 | tf_op jit(solution)/shard_map/ppermute | solution.py:456
  7.0 7.3 %collective-permute-start.2 = (bf16[12,16,128]{2,1,0:T(8,128)(2,1)S(1)}, bf16[12,16,128]{2,1,0:T(8,128)(2,1)S(1)}, u32[]{:S(2)}, u32[]{:S(2)}) collective-permute-start(bf16[12,16,128]{2,1,0:T(8,128)(2,1)S(1)} %get-tuple-element.38), channel_id=1, source_target_pairs={{0,1},{1,0},{2,3},{3,2},{4,5},{5,4},{6,7},{7,6},{8,9},{9,8},{10,11... | collective-permute-start | bytes 147464 | tf_op jit(solution)/shard_map/ppermute | solution.py:469
  8.6 5.7 %collective-permute-start.3 = (bf16[12,16,128]{2,1,0:T(8,128)(2,1)S(1)}, bf16[12,16,128]{2,1,0:T(8,128)(2,1)S(1)}, u32[]{:S(2)}, u32[]{:S(2)}) collective-permute-start(bf16[12,16,128]{2,1,0:T(8,128)(2,1)S(1)} %get-tuple-element.39), channel_id=1, source_target_pairs={{0,8},{1,2},{2,1},{3,4},{4,3},{5,6},{6,5},{7,15},{8,0},{9,10},{10,... | collective-permute-start | bytes 147464 | tf_op jit(solution)/shard_map/ppermute | solution.py:469
  9.8 4.5 %copy-start.1 = (bf16[6,16,1,8,128]{4,3,2,1,0:T(8,128)(2,1)S(1)}, bf16[6,16,1,8,128]{4,3,2,1,0:T(8,128)(2,1)}, u32[]{:S(2)}) copy-start(bf16[6,16,1,8,128]{4,3,2,1,0:T(8,128)(2,1)} %param.11) | copy-start | bytes 589828
  16.9 2.3 %copy-start.5 = (bf16[6,16,1,8,128]{4,3,2,1,0:T(8,128)(2,1)S(1)}, bf16[6,16,1,8,128]{4,3,2,1,0:T(8,128)(2,1)}, u32[]{:S(2)}) copy-start(bf16[6,16,1,8,128]{4,3,2,1,0:T(8,128)(2,1)} %param.12) | copy-start | bytes 589828
  16.9 1.3 %collective-permute-start.4 = (f32[2,8,128]{2,1,0:T(8,128)S(1)}, f32[2,8,128]{2,1,0:T(8,128)S(1)}, u32[]{:S(2)}, u32[]{:S(2)}) collective-permute-start(f32[2,8,128]{2,1,0:T(8,128)S(1)} %get-tuple-element.45), channel_id=1, source_target_pairs={{0,8},{8,0},{16,24},{24,16},{1,9},{9,1},{17,25},{25,17},{2,10},{10... | collective-permute-start | bytes 24584 | tf_op jit(solution)/shard_map/ppermute | solution.py:496
  18.2 3.8 %copy-start.2 = (f32[2,1,8,128]{3,2,1,0:T(8,128)S(1)}, f32[2,1,8,128]{3,2,1,0:T(8,128)}, u32[]{:S(2)}) copy-start(f32[2,1,8,128]{3,2,1,0:T(8,128)} %param.20) | copy-start | bytes 24580
  18.2 3.8 %copy-start.3 = (s32[1,8,128]{2,1,0:T(8,128)S(1)}, s32[1,8,128]{2,1,0:T(8,128)}, u32[]{:S(2)}) copy-start(s32[1,8,128]{2,1,0:T(8,128)} %param.21) | copy-start | bytes 12292
  18.2 3.7 %collective-permute-start.5 = (f32[2,8,128]{2,1,0:T(8,128)S(1)}, f32[2,8,128]{2,1,0:T(8,128)S(1)}, u32[]{:S(2)}, u32[]{:S(2)}) collective-permute-start(f32[2,8,128]{2,1,0:T(8,128)S(1)} %add.3.mine_ref), channel_id=1, source_target_pairs={{0,16},{8,24},{16,0},{24,8},{1,17},{9,25},{17,1},{25,9},{2,18},{10... | collective-permute-start | bytes 24584 | tf_op jit(solution)/shard_map/ppermute | solution.py:496

commit v6 on v5

--- a/solution.py
+++ b/solution.py
@@ -12,7 +12,7 @@
 PITCH = 16
 VMEM = pl.BlockSpec(memory_space=pltpu.VMEM)
 ANYWHERE = pl.BlockSpec(memory_space=pltpu.HBM)
-EARLY = 4
+EARLY = 2
 LIMIT = 24 * 1024 * 1024
 
 
@@ -152,38 +152,46 @@
     )(w1, w2, w3, small)
 
 
-def widened(own_ref, below_ref, above_ref):
-    frames = own_ref.shape[0]
+def beside(below_ref, above_ref):
     step, last = lax.axis_index("tm"), lax.axis_size("tm") - 1
-    parts = (own_ref, DEPTH, None), (below_ref, 0, step > 0), (above_ref, DEPTH + frames, step < last)
-    for src, base, inside in parts:
-        for f in range(src.shape[0]):
+    for part, src, inside in ((0, below_ref, step > 0), (1, above_ref, step < last)):
+        for f in range(DEPTH):
             for y in range(src.shape[2] // LANES):
                 v = src[f, :, tile(y)]
-                yield base + f, y, v if inside is None else jnp.where(inside, v, jnp.zeros_like(v))
-
-
-def edges_kernel(own_ref, below_ref, above_ref, west_ref, east_ref, send1_ref, send2_ref):
-    rows = own_ref.shape[2] // LANES
-    shape = (own_ref.shape[1], LANES)
-    lane = lanes(shape)
-    group, place = lane // PITCH, lane % PITCH
-    even = is_even("space")
-    for f, y, v in widened(own_ref, below_ref, above_ref):
+                yield part * DEPTH + f, y, jnp.where(inside, v, jnp.zeros_like(v))
+
+
+def strips(rows_of_frames, count):
+    for f, y, v in rows_of_frames:
+        lane = lanes(v.shape)
+        group, place = lane // PITCH, lane % PITCH
         if y == 0:
-            west, east = jnp.zeros(shape, BF), jnp.zeros(shape, BF)
+            west, east = jnp.zeros_like(v), jnp.zeros_like(v)
         here = group == y
         west = jnp.where(here & (place >= DEPTH), turn(v, y * PITCH + DEPTH), west)
         east = jnp.where(here & (place < PITCH - DEPTH), turn(v, y * PITCH + PITCH - DEPTH), east)
-        if y == rows - 1:
-            west_ref[f], east_ref[f] = west, east
-            send1_ref[f], send2_ref[f] = jnp.where(even, east, west), jnp.where(even, west, east)
-
-
-def make_edges(own, below, above):
-    frames, chans, _ = own.shape
+        if y == count - 1:
+            yield f, west, east
+
+
+def edges_kernel(own_west_ref, own_east_ref, below_ref, above_ref, west_ref, east_ref, send1_ref, send2_ref):
+    frames = own_west_ref.shape[0]
+    even = is_even("space")
+
+    def put(f, west, east):
+        west_ref[f], east_ref[f] = west, east
+        send1_ref[f], send2_ref[f] = jnp.where(even, east, west), jnp.where(even, west, east)
+
+    for f in range(frames):
+        put(DEPTH + f, own_west_ref[f], own_east_ref[f])
+    for f, west, east in strips(beside(below_ref, above_ref), below_ref.shape[2] // LANES):
+        put(f if f < DEPTH else f + frames, west, east)
+
+
+def make_edges(own_west, own_east, below, above):
+    frames, chans, _ = own_west.shape
     strip = shape_of((frames + 2 * DEPTH, chans, LANES), BF)
-    return call(edges_kernel, "edges", (strip,) * 4, [VMEM] * 3)(own, below, above)
+    return call(edges_kernel, "edges", (strip,) * 4, [VMEM] * 4)(own_west, own_east, below, above)
 
 
 def spread(dst, f, y, v):
@@ -194,10 +202,17 @@
     dst[f, 2 * chans : 3 * chans, at] = turn(v, -1)
 
 
-def window(src, f, count, y):
-    return jnp.concatenate(
-        [src[f + j, :, (y + dy) * LANES : (y + dy + 2) * LANES] for j in range(count) for dy in range(3)], axis=0
-    )
+def window(src, frames, y):
+    parts = []
+    for f in frames:
+        ref, at = src(f)
+        for dy in range(3):
+            parts.append(ref[at, :, (y + dy) * LANES : (y + dy + 2) * LANES])
+    return jnp.concatenate(parts, axis=0)
+
+
+def plain(ref):
+    return lambda f: (ref, f)
 
 
 def in_trajectory(local, frames):
@@ -205,54 +220,86 @@
     return (step >= 0) & (step < frames * lax.axis_size("tm"))
 
 
-def main_kernel(
-    own_ref, below_ref, above_ref, m1_ref, m2_ref, c1_ref, c2_ref, s3, s1, s2
-):
+def blank_ends(*refs):
+    for s in refs:
+        s[:, :, tile(0)] = jnp.zeros(s.shape[:2] + (LANES,), BF)
+        last = s.shape[2] // LANES - 1
+        s[:, :, tile(last)] = jnp.zeros(s.shape[:2] + (LANES,), BF)
+
+
+def layer(src, dst, m_ref, c_ref, groups, rows, keep):
+    hid = c_ref.shape[0]
+    for f, count in groups:
+        weights = m_ref[...] if count == 2 else m_ref[0:hid, 0 : m_ref.shape[1] // 4 * 3]
+        for y in range(0, rows, 2):
+            acc = jnp.dot(weights, window(src, range(f, f + count + 2), y), preferred_element_type=F32)
+            for p in range(count):
+                h = silu(acc[p * hid : (p + 1) * hid] + c_ref[...]).astype(BF)
+                inside = keep(f + p)
+                h = h if inside is None else jnp.where(inside, h, jnp.zeros_like(h))
+                ref, at = dst(f + p)
+                spread(ref, at, y, h[:, tile(0)])
+                spread(ref, at, y + 1, h[:, tile(1)])
+
+
+def pairs_of(frames):
+    groups = [(f, 2) for f in range(frames[0], frames[-1], 2)]
+    return groups + [(frames[-1], 1)] * (len(frames) % 2)
+
+
+def inner_kernel(own_ref, m1_ref, c1_ref, s1, s2, west_ref, east_ref):
     frames = own_ref.shape[0]
     rows = own_ref.shape[2] // LANES
-    hid = c1_ref.shape[0]
-    for s in (s1, s2, s3):
-        s[:, :, tile(0)] = jnp.zeros(s.shape[:2] + (LANES,), BF)
-        s[:, :, tile(rows + 1)] = jnp.zeros(s.shape[:2] + (LANES,), BF)
-    for f, y, v in widened(own_ref, below_ref, above_ref):
+    each = [(f, y, own_ref[f, :, tile(y)]) for f in range(frames) for y in range(rows)]
+    blank_ends(s1, s2)
+    for f, y, v in each:
         spread(s1, f, y, v)
-
-    def layer(src, dst, m_ref, bias, count, first):
-        def step(i, carry):
-            f = 2 * i
-            for y in range(0, rows, 2):
-                acc = jnp.dot(m_ref[...], window(src, f, 4, y), preferred_element_type=F32)
-                for p in range(2):
-                    h = silu(acc[p * hid : (p + 1) * hid] + bias).astype(BF)
-                    h = jnp.where(in_trajectory(f + p + first, frames), h, jnp.zeros_like(h))
-                    spread(dst, f + p, y, h[:, tile(0)])
-                    spread(dst, f + p, y + 1, h[:, tile(1)])
-            return carry
-
-        lax.fori_loop(0, count // 2, step, 0, unroll=UNROLL)
-
-    layer(s1, s2, m1_ref, c1_ref[...], frames + 4, -2)
-    layer(s2, s3, m2_ref, c2_ref[...], frames + 2, -1)
-
-
-UNROLL = True
-
-
-def make_main(own, below, above, m1, m2, c1, c2):
+    for f, west, east in strips(each, rows):
+        west_ref[f], east_ref[f] = west, east
+    layer(plain(s1), plain(s2), m1_ref, c1_ref, pairs_of(range(frames - 2)), rows, lambda f: None)
+
+
+def make_inner(own, m1, c1):
     frames, chans, width = own.shape
-    hid = c1.shape[0]
-    wide = width + 2 * LANES
+    hid, wide = c1.shape[0], width + 2 * LANES
+    strip = shape_of((frames, chans, LANES), BF)
+    return call(
+        inner_kernel,
+        "inner",
+        (shape_of((frames, 3 * chans, wide), BF), shape_of((frames - 2, 3 * hid, wide), BF), strip, strip),
+        [VMEM] * 3,
+        cost=1_000_000_000,
+    )(own, m1, c1)
+
+
+def main_kernel(own1, own2, below_ref, above_ref, m1_ref, m2_ref, c1_ref, c2_ref, s3, far1, far2):
+    frames = own1.shape[0]
+    rows = below_ref.shape[2] // LANES
+    blank_ends(far1, far2, s3)
+    for f, y, v in beside(below_ref, above_ref):
+        spread(far1, f, y, v)
+
+    def split(own, far, edge):
+        count = own.shape[0]
+        return lambda f: (own, f - edge) if edge <= f < edge + count else (far, f if f < edge else f - count)
+
+    one, two = split(own1, far1, DEPTH), split(own2, far2, DEPTH)
+    groups = pairs_of(range(DEPTH)) + pairs_of(range(frames + 1, frames + 4))
+    layer(one, two, m1_ref, c1_ref, groups, rows, lambda f: in_trajectory(f - 2, frames))
+    layer(two, plain(s3), m2_ref, c2_ref, pairs_of(range(frames + 2)), rows, lambda f: in_trajectory(f - 1, frames))
+
+
+def make_main(own1, own2, below, above, m1, m2, c1, c2):
+    frames, rows1, wide = own1.shape
+    rows2 = own2.shape[1]
     return call(
         main_kernel,
         "main",
-        (shape_of((frames + 2, 3 * hid, wide), BF),),
-        [VMEM] * 7,
-        [
-            pltpu.VMEM((frames + 6, 3 * chans, wide), BF),
-            pltpu.VMEM((frames + 4, 3 * hid, wide), BF),
-        ],
+        (shape_of((frames + 2, rows2, wide), BF),),
+        [VMEM] * 8,
+        [pltpu.VMEM((2 * DEPTH, rows1, wide), BF), pltpu.VMEM((2 * DEPTH, rows2, wide), BF)],
         cost=5_000_000_000,
-    )(own, below, above, m1, m2, c1, c2)[0]
+    )(own1, own2, below, above, m1, m2, c1, c2)[0]
 
 
 def spread_side(dst, f, v):
@@ -312,9 +359,9 @@
     def layer(src, dst, m_ref, bias, count, first):
         for f in range(0, count, 2):
             z = jnp.concatenate([src[f + j] for j in range(4)], axis=0)
-            acc = jnp.dot(m_ref[...], z, preferred_element_type=F32)
             for p in range(2):
-                h = silu(over_rows(acc, p * 3 * hid, hid) + bias)
+                acc = jnp.dot(m_ref[p * 3 * hid : (p + 1) * 3 * hid], z, preferred_element_type=F32)
+                h = silu(over_rows(acc, 0, hid) + bias)
                 keep = in_trajectory(f + p + first, frames) & ~outside
                 spread_side(dst, f + p, jnp.where(keep, h, 0.0).astype(BF))
 
@@ -363,7 +410,7 @@
 
 
 def own_score(wide_ref, m3_ref, frames, y):
-    acc = jnp.dot(m3_ref[...], window(wide_ref, 0, frames + 2, y), preferred_element_type=F32)
+    acc = jnp.dot(m3_ref[...], window(plain(wide_ref), range(frames + 2), y), preferred_element_type=F32)
     return acc[:, tile(0)], acc[:, tile(1)]
 
 
@@ -482,9 +529,10 @@
     below, above = shifted(high, "tm", 1), shifted(low, "tm", -1)
     small = jnp.concatenate([bias_one, bias_two, bias_three, day_of_frame.astype(F32)])[None]
     m1, m2, m3, s1, s2, s3, c1, c2, c3, days, head = make_weights(w1, w2, w3, small, state.shape[0])
-    west, east, send1, send2 = make_edges(own, below, above)
+    own1, own2, west, east = make_inner(own, m1, c1)
+    west, east, send1, send2 = make_edges(west, east, below, above)
     near, far = swapped(send1, 0), swapped(send2, 1)
-    wide = make_main(own, below, above, m1, m2, c1, c2)
+    wide = make_main(own1, own2, below, above, m1, m2, c1, c2)
     t3, mine = make_side(
         wide, west, east, near, far, s1, s2, head, c1, c2, c3, state, days, observed.shape[0]
     )

time: 22.7 us -> 22.2 us (0.978)
  waiting for transfers between devices: 3.21 us -> 2.44 us
  Pallas kernels: 11.8 us -> 12.3 us
    ppermute x2, waiting for transfers between devices: 2.11 us -> 1.2 us  [shifted(): lax.ppermute(value, axis, [(i, (i + steps) % count) for i in range(count)])]
    pallas_call x2 -> x3, Pallas kernels: 4.73 us -> 5.18 us  [the longest x1 4.1 us: make_main(): call(main_kernel, 'main', (shape_of((frames + 2, rows2, wide), BF),), [VM...]
    pallas_call x1, Pallas kernels: 1.2 us -> 0.77 us  [make_early(): call(early_kernel, 'early', (shape_of((count, m3.shape[0], LANES), F32),...]
    pallas_call x1, Pallas kernels: 1.65 us -> 2.02 us  [make_update(): call(update_kernel, 'update', (shape_of(state.shape, BF), shape_of((frame...]
  transfers between devices with their start and end apart: 6 -> 6, of which waited for: 3 -> 4; matrix products, arithmetic and copies ran while one was open for 0% -> 0% of each run, Pallas kernels for 36% -> 39%
where the time goes in v6:
time: 22.2 us; the launch traced here: 22.1 us
  Pallas kernels  12.3 us (55%)
  starting transfers between devices  6.17 us (28%)
  waiting for transfers between devices  2.44 us (11%)
  local copies, waits for them, and re-layouts  0.98 us (4%)
    pallas_call x1, Pallas kernels, make_main(): call(main_kernel, 'main', (shape_of((frames + 2, rows2, wide), BF),), [VM...  4.1 us
    ppermute x2, starting transfers between devices, swapped(): return lax.ppermute(value, ('tm', 'space'), pairs)  2.85 us
    pallas_call x1, Pallas kernels, make_side(): call(side_kernel, 'side', (shape_of((frames + 2, 3 * hid, 2 * LANES), BF)...  2.66 us
    ppermute x2, starting transfers between devices, shifted(): lax.ppermute(value, axis, [(i, (i + steps) % count) for i in range(count)])  2.49 us
    pallas_call x1, Pallas kernels, make_update(): call(update_kernel, 'update', (shape_of(state.shape, BF), shape_of((frame...  2.02 us
    ppermute x2, waiting for transfers between devices, body(): theirs = lax.ppermute(mine, 'tm', [(i, i ^ reach) for i in range(count)])  1.23 us
    ppermute x2, waiting for transfers between devices, shifted(): lax.ppermute(value, axis, [(i, (i + steps) % count) for i in range(count)])  1.2 us
    unnamed x24, local copies, waits for them, and re-layouts  0.98 us
  transfers between devices with their start and end apart: 6, of which 4 were waited for; matrix products, arithmetic and copies ran while one was open for 0% of the time, Pallas kernels for 39%

profile of v6, /device:TPU:0, one launch (start us, length us, event | category | flops | bytes accessed | tf_op | source)
XLA Modules:
  0.0 22.1 jit_solution(12728202592898173048)
XLA Ops:
  0.0 0.9 %copy-done = bf16[6,16,1,8,128]{4,3,2,1,0:T(8,128)(2,1)S(1)} copy-done((bf16[6,16,1,8,128]{4,3,2,1,0:T(8,128)(2,1)S(1)}, bf16[6,16,1,8,128]{4,3,2,1,0:T(8,128)(2,1)}, u32[]{:S(2)}) %copy-start) | copy-done | bytes 196632
  0.9 0.0 copy-start.4
  0.9 0.0 copy-start.6
  1.0 0.0 copy-start.7
  1.0 0.1 rows.1
  1.1 0.5 %collective-permute-start = (bf16[3,16,1024]{2,1,0:T(8,128)(2,1)S(1)}, bf16[3,16,1024]{2,1,0:T(8,128)(2,1)S(1)}, u32[]{:S(2)}, u32[]{:S(2)}) collective-permute-start(bf16[3,16,1024]{2,1,0:T(8,128)(2,1)S(1)} %get-tuple-element.38), channel_id=1, source_target_pairs={{0,8},{8,16},{16,24},{24,0},{1,9},{9,17},{17,25},{25,1},{2,10},{10... | collective-permute-start | bytes 294920 | tf_op jit(solution)/shard_map/ppermute | solution.py:503
  1.6 2.0 %collective-permute-start.1 = (bf16[3,16,1024]{2,1,0:T(8,128)(2,1)S(1)}, bf16[3,16,1024]{2,1,0:T(8,128)(2,1)S(1)}, u32[]{:S(2)}, u32[]{:S(2)}) collective-permute-start(bf16[3,16,1024]{2,1,0:T(8,128)(2,1)S(1)} %get-tuple-element.39), channel_id=1, source_target_pairs={{0,24},{8,0},{16,8},{24,16},{1,25},{9,1},{17,9},{25,17},{2,26},{10... | collective-permute-start | bytes 294920 | tf_op jit(solution)/shard_map/ppermute | solution.py:503
  3.6 0.0 copy-done.11
  3.6 0.0 copy-done.9
  3.6 0.1 pad_maximum_fusion
  3.7 0.9 %weights.1 = (bf16[128,576]{1,0:T(8,128)(2,1)S(1)}, bf16[128,2304]{1,0:T(8,128)(2,1)S(1)}, bf16[96,4608]{1,0:T(8,128)(2,1)S(1)}, bf16[384,192]{1,0:T(8,128)(2,1)...) custom-call(bf16[432,64]{1,0:T(8,128)(2,1)S(1)} %bitcast.25, ...), custom_call_target="tpu_custom_call" | custom-call | flops 1000000000 | bytes 1000000 | tf_op jit(solution)/shard_map/weights/pallas_call | solution.py:133
  4.6 0.9 %inner.1 = (bf16[6,48,1280]{2,1,0:T(8,128)(2,1)S(1)}, bf16[4,192,1280]{2,1,0:T(8,128)(2,1)S(1)}, bf16[6,16,128]{2,1,0:T(8,128)(2,1)S(1)}, bf16[6,16,128]{2,1,0:T(8,128)(2,1)S(1)}) custom-call(bf16[6,16,1024]{2,1,0:T(8,128)(2,1)S(1)} %get-tuple-element.33.own_ref, bf16[128,576]{1,0:T(8,128)(2,1)S(1)} %get-tuple-element.34.m1_ref, ...), custom_call_target="tpu_custom_call" | custom-call | flops 1000000000 | bytes 1000000 | tf_op jit(solution)/shard_map/inner/pallas_call | solution.py:266
  5.5 0.3 %collective-permute-done.below_ref = bf16[3,16,1024]{2,1,0:T(8,128)(2,1)S(1)} collective-permute-done((bf16[3,16,1024]{2,1,0:T(8,128)(2,1)S(1)}, bf16[3,16,1024]{2,1,0:T(8,128)(2,1)S(1)}, u32[]{:S(2)}, u32[]{:S(2)}) %collective-permute-start) | collective-permute-done | bytes 98336 | tf_op jit(solution)/shard_map/ppermute | solution.py:503
  5.8 0.9 %collective-permute-done.1.above_ref = bf16[3,16,1024]{2,1,0:T(8,128)(2,1)S(1)} collective-permute-done((bf16[3,16,1024]{2,1,0:T(8,128)(2,1)S(1)}, bf16[3,16,1024]{2,1,0:T(8,128)(2,1)S(1)}, u32[]{:S(2)}, u32[]{:S(2)}) %collective-permute-start.1) | collective-permute-done | bytes 98336 | tf_op jit(solution)/shard_map/ppermute | solution.py:503
  6.7 0.2 edges.1
  6.9 1.6 %collective-permute-start.2 = (bf16[12,16,128]{2,1,0:T(8,128)(2,1)S(1)}, bf16[12,16,128]{2,1,0:T(8,128)(2,1)S(1)}, u32[]{:S(2)}, u32[]{:S(2)}) collective-permute-start(bf16[12,16,128]{2,1,0:T(8,128)(2,1)S(1)} %get-tuple-element.46), channel_id=1, source_target_pairs={{0,1},{1,0},{2,3},{3,2},{4,5},{5,4},{6,7},{7,6},{8,9},{9,8},{10,11... | collective-permute-start | bytes 147464 | tf_op jit(solution)/shard_map/ppermute | solution.py:516
  8.5 1.3 %collective-permute-start.3 = (bf16[12,16,128]{2,1,0:T(8,128)(2,1)S(1)}, bf16[12,16,128]{2,1,0:T(8,128)(2,1)S(1)}, u32[]{:S(2)}, u32[]{:S(2)}) collective-permute-start(bf16[12,16,128]{2,1,0:T(8,128)(2,1)S(1)} %get-tuple-element.47), channel_id=1, source_target_pairs={{0,8},{1,2},{2,1},{3,4},{4,3},{5,6},{6,5},{7,15},{8,0},{9,10},{10,... | collective-permute-start | bytes 147464 | tf_op jit(solution)/shard_map/ppermute | solution.py:516
  9.7 4.1 %main.1.wide_ref = bf16[8,192,1280]{2,1,0:T(8,128)(2,1)S(1)} custom-call(bf16[6,48,1280]{2,1,0:T(8,128)(2,1)S(1)} %get-tuple-element.36.own1, bf16[4,192,1280]{2,1,0:T(8,128)(2,1)S(1)} %get-tuple-element.37.own2, bf16[3,16,1024]{2,1,0:T(8,128)(2,1)S(1)} %collective-permute-done.below_ref, bf16[3,16,1024]{2,1,0:T(8,128)(2,1)S(1)} %collective-permute-done.1.above_ref, ...), custom_call_target="tpu_custom_call" | custom-call | flops 5000000000 | bytes 1000000 | tf_op jit(solution)/shard_map/main/pallas_call | solution.py:295
  13.8 0.0 collective-permute-done.2.first_ref
  13.8 0.0 collective-permute-done.3.second_ref
  13.9 0.0 copy-done.1
  13.9 2.7 %side.1 = (bf16[8,192,256]{2,1,0:T(8,128)(2,1)S(1)}, f32[2,8,128]{2,1,0:T(8,128)S(1)}) custom-call(bf16[8,192,1280]{2,1,0:T(8,128)(2,1)S(1)} %main.1.wide_ref, bf16[12,16,128]{2,1,0:T(8,128)(2,1)S(1)} %get-tuple-element.44.west_ref, bf16[12,16,128]{2,1,0:T(8,128)(2,1)S(1)} %get-tuple-element.45.east_ref, ...), custom_call_target="tpu_custom_call" | custom-call | tf_op jit(solution)/shard_map/side/pallas_call | solution.py:398
  16.5 0.0 copy-start.5
  16.5 0.1 collective-permute-start.4
  16.6 0.8 %early.1 = (f32[2,96,128]{2,1,0:T(8,128)S(1)}, f32[2,96,128]{2,1,0:T(8,128)S(1)}) custom-call(bf16[8,192,1280]{2,1,0:T(8,128)(2,1)S(1)} %main.1.wide_ref, bf16[8,192,256]{2,1,0:T(8,128)(2,1)S(1)} %get-tuple-element.55.t3, bf16[96,4608]{1,0:T(8,128)(2,1)S(1)} %get-tuple-element.54.m3_ref, bf16[288,1536]{1,0:T(8,128)(2,1)S(1)} %get-tuple-element.56.s3_ref), custom_call_target="tpu_custom_call" | custom-call | flops 1000000000 | bytes 1000000 | tf_op jit(solution)/shard_map/early/pallas_call | solution.py:431
  17.4 0.0 copy-start.2
  17.4 0.0 copy-start.3
  17.4 0.4 %collective-permute-done.4 = f32[2,8,128]{2,1,0:T(8,128)S(1)} collective-permute-done((f32[2,8,128]{2,1,0:T(8,128)S(1)}, f32[2,8,128]{2,1,0:T(8,128)S(1)}, u32[]{:S(2)}, u32[]{:S(2)}) %collective-permute-start.4) | collective-permute-done | bytes 8224 | tf_op jit(solution)/shard_map/ppermute | solution.py:544
  17.8 0.8 %collective-permute-start.5 = (f32[2,8,128]{2,1,0:T(8,128)S(1)}, f32[2,8,128]{2,1,0:T(8,128)S(1)}, u32[]{:S(2)}, u32[]{:S(2)}) collective-permute-start(f32[2,8,128]{2,1,0:T(8,128)S(1)} %add.3.mine_ref), channel_id=1, source_target_pairs={{0,16},{8,24},{16,0},{24,8},{1,17},{9,25},{17,1},{25,9},{2,18},{10... | collective-permute-start | bytes 24584 | tf_op jit(solution)/shard_map/ppermute | solution.py:544
  18.5 2.0 %update.1 = (bf16[6,16,8,128]{3,2,1,0:T(8,128)(2,1)}, f32[6,8,128]{2,1,0:T(8,128)S(1)}) custom-call(bf16[8,192,1280]{2,1,0:T(8,128)(2,1)S(1)} %main.1.wide_ref, bf16[96,4608]{1,0:T(8,128)(2,1)S(1)} %get-tuple-element.54.m3_ref, f32[2,96,128]{2,1,0:T(8,128)S(1)} %get-tuple-element.57.score_ref, f32[2,96,128]{2,1,0:T(8,128)S(1)} %get-tuple-element.58.side_ref, ...), custom_call_target="tpu_custom_call" | custom-call | flops 2000000000 | bytes 1000000 | tf_op jit(solution)/shard_map/update/pallas_call | solution.py:460
  20.6 0.9 %collective-permute-done.5.theirs_ref = f32[2,8,128]{2,1,0:T(8,128)S(1)} collective-permute-done((f32[2,8,128]{2,1,0:T(8,128)S(1)}, f32[2,8,128]{2,1,0:T(8,128)S(1)}, u32[]{:S(2)}, u32[]{:S(2)}) %collective-permute-start.5) | collective-permute-done | bytes 8224 | tf_op jit(solution)/shard_map/ppermute | solution.py:544
  21.4 0.6 %correct.1 = bf16[6,16,8,128]{3,2,1,0:T(8,128)(2,1)} custom-call(f32[2,8,128]{2,1,0:T(8,128)S(1)} %add.3.mine_ref, f32[2,8,128]{2,1,0:T(8,128)S(1)} %collective-permute-done.5.theirs_ref, f32[2,8,128]{2,1,0:T(8,128)S(1)} %bitcast.20, s32[8,128]{1,0:T(8,128)S(1)} %bitcast.21, ...), custom_call_target="tpu_custom_call", output_to_operand_aliasing={{}: (6, {})} | custom-call | tf_op jit(solution)/shard_map/correct/pallas_call | solution.py:490
  (16 shorter events, 0.0 us)
Async XLA Ops:
  0.0 0.9 %copy-start = (bf16[6,16,1,8,128]{4,3,2,1,0:T(8,128)(2,1)S(1)}, bf16[6,16,1,8,128]{4,3,2,1,0:T(8,128)(2,1)}, u32[]{:S(2)}) copy-start(bf16[6,16,1,8,128]{4,3,2,1,0:T(8,128)(2,1)} %param.11) | copy-start | bytes 589828
  0.9 2.7 %copy-start.11 = (s32[6]{0:T(128)S(1)}, s32[6]{0:T(128)}, u32[]{:S(2)}) copy-start(s32[6]{0:T(128)} %param.19) | copy-start | bytes 76
  0.9 2.7 %copy-start.8 = (f32[16]{0:T(128)S(1)}, f32[16]{0:T(128)}, u32[]{:S(2)}) copy-start(f32[16]{0:T(128)} %param.18) | copy-start | bytes 196
  0.9 2.7 %copy-start.9 = (f32[64]{0:T(128)S(1)}, f32[64]{0:T(128)}, u32[]{:S(2)}) copy-start(f32[64]{0:T(128)} %param.16) | copy-start | bytes 772
  0.9 2.7 %copy-start.10 = (f32[64]{0:T(128)S(1)}, f32[64]{0:T(128)}, u32[]{:S(2)}) copy-start(f32[64]{0:T(128)} %param.14) | copy-start | bytes 772
  0.9 2.8 %copy-start.4 = (bf16[64,64,3,3,3]{1,0,4,3,2:T(8,128)(2,1)S(1)}, bf16[64,64,3,3,3]{1,0,4,3,2:T(8,128)(2,1)}, u32[]{:S(2)}) copy-start(bf16[64,64,3,3,3]{1,0,4,3,2:T(8,128)(2,1)} %param.15) | copy-start | bytes 663556
  0.9 2.7 %copy-start.6 = (bf16[64,16,3,3,3]{0,1,4,3,2:T(8,128)(2,1)S(1)}, bf16[64,16,3,3,3]{0,1,4,3,2:T(8,128)(2,1)}, u32[]{:S(2)}) copy-start(bf16[64,16,3,3,3]{0,1,4,3,2:T(8,128)(2,1)} %param.13) | copy-start | bytes 165892
  1.0 2.7 %copy-start.7 = (bf16[16,64,3,3,3]{1,0,4,3,2:T(8,128)(2,1)S(1)}, bf16[16,64,3,3,3]{1,0,4,3,2:T(8,128)(2,1)}, u32[]{:S(2)}) copy-start(bf16[16,64,3,3,3]{1,0,4,3,2:T(8,128)(2,1)} %param.17) | copy-start | bytes 165892
  1.1 4.7 %collective-permute-start = (bf16[3,16,1024]{2,1,0:T(8,128)(2,1)S(1)}, bf16[3,16,1024]{2,1,0:T(8,128)(2,1)S(1)}, u32[]{:S(2)}, u32[]{:S(2)}) collective-permute-start(bf16[3,16,1024]{2,1,0:T(8,128)(2,1)S(1)} %get-tuple-element.38), channel_id=1, source_target_pairs={{0,8},{8,16},{16,24},{24,0},{1,9},{9,17},{17,25},{25,1},{2,10},{10... | collective-permute-start | bytes 294920 | tf_op jit(solution)/shard_map/ppermute | solution.py:503
  1.6 5.1 %collective-permute-start.1 = (bf16[3,16,1024]{2,1,0:T(8,128)(2,1)S(1)}, bf16[3,16,1024]{2,1,0:T(8,128)(2,1)S(1)}, u32[]{:S(2)}, u32[]{:S(2)}) collective-permute-start(bf16[3,16,1024]{2,1,0:T(8,128)(2,1)S(1)} %get-tuple-element.39), channel_id=1, source_target_pairs={{0,24},{8,0},{16,8},{24,16},{1,25},{9,1},{17,9},{25,17},{2,26},{10... | collective-permute-start | bytes 294920 | tf_op jit(solution)/shard_map/ppermute | solution.py:503
  6.9 7.0 %collective-permute-start.2 = (bf16[12,16,128]{2,1,0:T(8,128)(2,1)S(1)}, bf16[12,16,128]{2,1,0:T(8,128)(2,1)S(1)}, u32[]{:S(2)}, u32[]{:S(2)}) collective-permute-start(bf16[12,16,128]{2,1,0:T(8,128)(2,1)S(1)} %get-tuple-element.46), channel_id=1, source_target_pairs={{0,1},{1,0},{2,3},{3,2},{4,5},{5,4},{6,7},{7,6},{8,9},{9,8},{10,11... | collective-permute-start | bytes 147464 | tf_op jit(solution)/shard_map/ppermute | solution.py:516
  8.5 5.4 %collective-permute-start.3 = (bf16[12,16,128]{2,1,0:T(8,128)(2,1)S(1)}, bf16[12,16,128]{2,1,0:T(8,128)(2,1)S(1)}, u32[]{:S(2)}, u32[]{:S(2)}) collective-permute-start(bf16[12,16,128]{2,1,0:T(8,128)(2,1)S(1)} %get-tuple-element.47), channel_id=1, source_target_pairs={{0,8},{1,2},{2,1},{3,4},{4,3},{5,6},{6,5},{7,15},{8,0},{9,10},{10,... | collective-permute-start | bytes 147464 | tf_op jit(solution)/shard_map/ppermute | solution.py:516
  9.7 4.1 %copy-start.1 = (bf16[6,16,1,8,128]{4,3,2,1,0:T(8,128)(2,1)S(1)}, bf16[6,16,1,8,128]{4,3,2,1,0:T(8,128)(2,1)}, u32[]{:S(2)}) copy-start(bf16[6,16,1,8,128]{4,3,2,1,0:T(8,128)(2,1)} %param.11) | copy-start | bytes 589828
  16.5 2.0 %copy-start.5 = (bf16[6,16,1,8,128]{4,3,2,1,0:T(8,128)(2,1)S(1)}, bf16[6,16,1,8,128]{4,3,2,1,0:T(8,128)(2,1)}, u32[]{:S(2)}) copy-start(bf16[6,16,1,8,128]{4,3,2,1,0:T(8,128)(2,1)} %param.12) | copy-start | bytes 589828
  16.5 1.2 %collective-permute-start.4 = (f32[2,8,128]{2,1,0:T(8,128)S(1)}, f32[2,8,128]{2,1,0:T(8,128)S(1)}, u32[]{:S(2)}, u32[]{:S(2)}) collective-permute-start(f32[2,8,128]{2,1,0:T(8,128)S(1)} %get-tuple-element.53), channel_id=1, source_target_pairs={{0,8},{8,0},{16,24},{24,16},{1,9},{9,1},{17,25},{25,17},{2,10},{10... | collective-permute-start | bytes 24584 | tf_op jit(solution)/shard_map/ppermute | solution.py:544
  17.4 4.0 %copy-start.2 = (f32[2,1,8,128]{3,2,1,0:T(8,128)S(1)}, f32[2,1,8,128]{3,2,1,0:T(8,128)}, u32[]{:S(2)}) copy-start(f32[2,1,8,128]{3,2,1,0:T(8,128)} %param.20) | copy-start | bytes 24580
  17.4 4.0 %copy-start.3 = (s32[1,8,128]{2,1,0:T(8,128)S(1)}, s32[1,8,128]{2,1,0:T(8,128)}, u32[]{:S(2)}) copy-start(s32[1,8,128]{2,1,0:T(8,128)} %param.21) | copy-start | bytes 12292
  17.8 3.7 %collective-permute-start.5 = (f32[2,8,128]{2,1,0:T(8,128)S(1)}, f32[2,8,128]{2,1,0:T(8,128)S(1)}, u32[]{:S(2)}, u32[]{:S(2)}) collective-permute-start(f32[2,8,128]{2,1,0:T(8,128)S(1)} %add.3.mine_ref), channel_id=1, source_target_pairs={{0,16},{8,24},{16,0},{24,8},{1,17},{9,25},{17,1},{25,9},{2,18},{10... | collective-permute-start | bytes 24584 | tf_op jit(solution)/shard_map/ppermute | solution.py:544

commit v7 on v6

--- a/solution.py
+++ b/solution.py
@@ -56,17 +56,17 @@
     return lax.axis_index(axis) % 2 == 0
 
 
-def rows_kernel(state_ref, own_ref, low_ref, high_ref, scr):
+def rows_kernel(state_ref, own_ref, far_ref, near_ref, scr):
     frames, chans, rows, _ = state_ref.shape
     for f in range(frames):
         scr[f] = state_ref[f].astype(F32).reshape(chans * rows, LANES)
         for y in range(rows):
             v = scr[f, pl.ds(y, chans, stride=rows), :].astype(BF)
             own_ref[f, :, tile(y)] = v
-            if f < DEPTH:
-                low_ref[f, :, tile(y)] = v
-            if f >= frames - DEPTH:
-                high_ref[f - (frames - DEPTH), :, tile(y)] = v
+    even = is_even("tm")
+    for f in range(DEPTH):
+        low, high = own_ref[f], own_ref[frames - DEPTH + f]
+        near_ref[f], far_ref[f] = jnp.where(even, high, low), jnp.where(even, low, high)
 
 
 def make_rows(state):
@@ -152,29 +152,33 @@
     )(w1, w2, w3, small)
 
 
-def beside(below_ref, above_ref):
+def beside(near_ref, far_ref):
     step, last = lax.axis_index("tm"), lax.axis_size("tm") - 1
-    for part, src, inside in ((0, below_ref, step > 0), (1, above_ref, step < last)):
-        for f in range(DEPTH):
-            for y in range(src.shape[2] // LANES):
-                v = src[f, :, tile(y)]
-                yield part * DEPTH + f, y, jnp.where(inside, v, jnp.zeros_like(v))
+    even = is_even("tm")
+    for f in range(DEPTH):
+        for y in range(near_ref.shape[2] // LANES):
+            a, b = near_ref[f, :, tile(y)], far_ref[f, :, tile(y)]
+            none = jnp.zeros_like(a)
+            yield f, y, jnp.where(step > 0, jnp.where(even, b, a), none)
+            yield DEPTH + f, y, jnp.where(step < last, jnp.where(even, a, b), none)
 
 
 def strips(rows_of_frames, count):
+    begun = {}
     for f, y, v in rows_of_frames:
         lane = lanes(v.shape)
         group, place = lane // PITCH, lane % PITCH
-        if y == 0:
-            west, east = jnp.zeros_like(v), jnp.zeros_like(v)
+        west, east = begun.pop(f, (jnp.zeros_like(v), jnp.zeros_like(v)))
         here = group == y
         west = jnp.where(here & (place >= DEPTH), turn(v, y * PITCH + DEPTH), west)
         east = jnp.where(here & (place < PITCH - DEPTH), turn(v, y * PITCH + PITCH - DEPTH), east)
         if y == count - 1:
             yield f, west, east
-
-
-def edges_kernel(own_west_ref, own_east_ref, below_ref, above_ref, west_ref, east_ref, send1_ref, send2_ref):
+        else:
+            begun[f] = west, east
+
+
+def edges_kernel(own_west_ref, own_east_ref, far_ref, near_ref, west_ref, east_ref, send1_ref, send2_ref):
     frames = own_west_ref.shape[0]
     even = is_even("space")
 
@@ -184,14 +188,14 @@
 
     for f in range(frames):
         put(DEPTH + f, own_west_ref[f], own_east_ref[f])
-    for f, west, east in strips(beside(below_ref, above_ref), below_ref.shape[2] // LANES):
+    for f, west, east in strips(beside(near_ref, far_ref), near_ref.shape[2] // LANES):
         put(f if f < DEPTH else f + frames, west, east)
 
 
-def make_edges(own_west, own_east, below, above):
+def make_edges(own_west, own_east, near, far):
     frames, chans, _ = own_west.shape
     strip = shape_of((frames + 2 * DEPTH, chans, LANES), BF)
-    return call(edges_kernel, "edges", (strip,) * 4, [VMEM] * 4)(own_west, own_east, below, above)
+    return call(edges_kernel, "edges", (strip,) * 4, [VMEM] * 4)(own_west, own_east, far, near)
 
 
 def spread(dst, f, y, v):
@@ -272,11 +276,11 @@
     )(own, m1, c1)
 
 
-def main_kernel(own1, own2, below_ref, above_ref, m1_ref, m2_ref, c1_ref, c2_ref, s3, far1, far2):
+def main_kernel(own1, own2, far_ref, near_ref, m1_ref, m2_ref, c1_ref, c2_ref, s3, far1, far2):
     frames = own1.shape[0]
-    rows = below_ref.shape[2] // LANES
+    rows = near_ref.shape[2] // LANES
     blank_ends(far1, far2, s3)
-    for f, y, v in beside(below_ref, above_ref):
+    for f, y, v in beside(near_ref, far_ref):
         spread(far1, f, y, v)
 
     def split(own, far, edge):
@@ -289,7 +293,7 @@
     layer(two, plain(s3), m2_ref, c2_ref, pairs_of(range(frames + 2)), rows, lambda f: in_trajectory(f - 1, frames))
 
 
-def make_main(own1, own2, below, above, m1, m2, c1, c2):
+def make_main(own1, own2, near, far, m1, m2, c1, c2):
     frames, rows1, wide = own1.shape
     rows2 = own2.shape[1]
     return call(
@@ -299,7 +303,7 @@
         [VMEM] * 8,
         [pltpu.VMEM((2 * DEPTH, rows1, wide), BF), pltpu.VMEM((2 * DEPTH, rows2, wide), BF)],
         cost=5_000_000_000,
-    )(own1, own2, below, above, m1, m2, c1, c2)[0]
+    )(own1, own2, far, near, m1, m2, c1, c2)[0]
 
 
 def spread_side(dst, f, v):
@@ -498,21 +502,18 @@
     )(mine, theirs, observed, mask, head, day, out)[0]
 
 
-def shifted(value, axis, steps):
-    count = lax.axis_size(axis)
-    return lax.ppermute(value, axis, [(i, (i + steps) % count) for i in range(count)])
-
-
-def swapped(value, start):
-    blocks, strips = lax.axis_size("tm"), lax.axis_size("space")
+def swapped(value, axis, start):
+    sizes = {name: lax.axis_size(name) for name in ("tm", "space")}
+    other = "space" if axis == "tm" else "tm"
     pairs = []
-    for t in range(blocks):
-        for i in range(strips):
-            other = i + 1 if i % 2 == start else i - 1
-            if 0 <= other < strips:
-                pairs.append((t * strips + i, t * strips + other))
-            elif t ^ 1 < blocks:
-                pairs.append((t * strips + i, (t ^ 1) * strips + i))
+    for t in range(sizes["tm"]):
+        for s in range(sizes["space"]):
+            to = {"tm": t, "space": s}
+            to[axis] += 1 if to[axis] % 2 == start else -1
+            if not 0 <= to[axis] < sizes[axis]:
+                to = {"tm": t, "space": s}
+                to[other] ^= 1
+            pairs.append((t * sizes["space"] + s, to["tm"] * sizes["space"] + to["space"]))
     return lax.ppermute(value, ("tm", "space"), pairs)
 
 
@@ -525,16 +526,17 @@
     w1 = conv_one.transpose(2, 3, 4, 1, 0).reshape(27 * chans, hid)
     w2 = conv_two.transpose(2, 3, 4, 0, 1).reshape(27, hid, hid)
     w3 = conv_three.transpose(2, 3, 4, 0, 1).reshape(27, fields, hid)
-    own, low, high = make_rows(state)
-    below, above = shifted(high, "tm", 1), shifted(low, "tm", -1)
+    own, send2, send1 = make_rows(state)
+    far = swapped(send2, "tm", 1)
+    near = swapped(send1, "tm", 0)
     small = jnp.concatenate([bias_one, bias_two, bias_three, day_of_frame.astype(F32)])[None]
     m1, m2, m3, s1, s2, s3, c1, c2, c3, days, head = make_weights(w1, w2, w3, small, state.shape[0])
     own1, own2, west, east = make_inner(own, m1, c1)
-    west, east, send1, send2 = make_edges(west, east, below, above)
-    near, far = swapped(send1, 0), swapped(send2, 1)
-    wide = make_main(own1, own2, below, above, m1, m2, c1, c2)
+    west, east, send1, send2 = make_edges(west, east, near, far)
+    first, second = swapped(send1, "space", 0), swapped(send2, "space", 1)
+    wide = make_main(own1, own2, near, far, m1, m2, c1, c2)
     t3, mine = make_side(
-        wide, west, east, near, far, s1, s2, head, c1, c2, c3, state, days, observed.shape[0]
+        wide, west, east, first, second, s1, s2, head, c1, c2, c3, state, days, observed.shape[0]
     )
     score, side = make_early(wide, t3, m3, s3, EARLY)
     out, first = make_update(wide, m3, score, side, c3, state, noise)

time: 22.2 us -> 21.7 us (0.977)
  waiting for transfers between devices: 2.44 us -> 1.35 us
  starting transfers between devices: 6.17 us -> 6.75 us
    ppermute x2 -> x0, starting transfers between devices: 2.49 us -> none  [shifted(): lax.ppermute(value, axis, [(i, (i + steps) % count) for i in range(count)])]
    ppermute x2 -> x4, starting transfers between devices: 2.85 us -> 5.21 us  [swapped(): return lax.ppermute(value, ('tm', 'space'), pairs)]
    ppermute x2 -> x0, waiting for transfers between devices: 1.2 us -> none  [shifted(): lax.ppermute(value, axis, [(i, (i + steps) % count) for i in range(count)])]
    ppermute x2, starting transfers between devices: 0.83 us -> 1.54 us  [body(): theirs = lax.ppermute(mine, 'tm', [(i, i ^ reach) for i in range(count)])]
    ppermute x2 -> x4, waiting for transfers between devices: 0.01 us -> 0.61 us  [swapped(): return lax.ppermute(value, ('tm', 'space'), pairs)]
    ppermute x2, waiting for transfers between devices: 1.23 us -> 0.74 us  [body(): theirs = lax.ppermute(mine, 'tm', [(i, i ^ reach) for i in range(count)])]
  transfers between devices with their start and end apart: 6 -> 6, of which waited for: 4 -> 2; matrix products, arithmetic and copies ran while one was open for 0% -> 0% of each run, Pallas kernels for 39% -> 40%
where the time goes in v7:
time: 21.7 us; the launch traced here: 21.6 us
  Pallas kernels  12.3 us (57%)
  starting transfers between devices  6.75 us (31%)
  waiting for transfers between devices  1.35 us (6%)
  local copies, waits for them, and re-layouts  0.98 us (5%)
    ppermute x4, starting transfers between devices, swapped(): return lax.ppermute(value, ('tm', 'space'), pairs)  5.21 us
    pallas_call x1, Pallas kernels, make_main(): call(main_kernel, 'main', (shape_of((frames + 2, rows2, wide), BF),), [VM...  4.13 us
    pallas_call x1, Pallas kernels, make_side(): call(side_kernel, 'side', (shape_of((frames + 2, 3 * hid, 2 * LANES), BF)...  2.65 us
    pallas_call x1, Pallas kernels, make_update(): call(update_kernel, 'update', (shape_of(state.shape, BF), shape_of((frame...  2.02 us
    ppermute x2, starting transfers between devices, body(): theirs = lax.ppermute(mine, 'tm', [(i, i ^ reach) for i in range(count)])  1.54 us
    unnamed x24, local copies, waits for them, and re-layouts  0.98 us
    pallas_call x1, Pallas kernels, make_inner(): call(inner_kernel, 'inner', (shape_of((frames, 3 * chans, wide), BF), sha...  0.91 us
    pallas_call x1, Pallas kernels, make_weights(): call(weights_kernel, 'weights', (shape_of((2 * hid, 4 * 9 * chans), BF),...  0.88 us
  transfers between devices with their start and end apart: 6, of which 2 were waited for; matrix products, arithmetic and copies ran while one was open for 0% of the time, Pallas kernels for 40%

profile of v7, /device:TPU:0, one launch (start us, length us, event | category | flops | bytes accessed | tf_op | source)
XLA Modules:
  0.0 21.6 jit_solution(12327954292263192205)
XLA Ops:
  0.0 0.9 %copy-done = bf16[6,16,1,8,128]{4,3,2,1,0:T(8,128)(2,1)S(1)} copy-done((bf16[6,16,1,8,128]{4,3,2,1,0:T(8,128)(2,1)S(1)}, bf16[6,16,1,8,128]{4,3,2,1,0:T(8,128)(2,1)}, u32[]{:S(2)}) %copy-start) | copy-done | bytes 196632
  0.9 0.0 copy-start.4
  0.9 0.0 copy-start.6
  1.0 0.0 copy-start.7
  1.0 0.1 rows.1
  1.1 3.0 %collective-permute-start = (bf16[3,16,1024]{2,1,0:T(8,128)(2,1)S(1)}, bf16[3,16,1024]{2,1,0:T(8,128)(2,1)S(1)}, u32[]{:S(2)}, u32[]{:S(2)}) collective-permute-start(bf16[3,16,1024]{2,1,0:T(8,128)(2,1)S(1)} %get-tuple-element.38), channel_id=1, source_target_pairs={{0,1},{1,0},{2,3},{3,2},{4,5},{5,4},{6,7},{7,6},{8,16},{9,17},{10,... | collective-permute-start | bytes 294920 | tf_op jit(solution)/shard_map/ppermute | solution.py:517
  4.1 0.1 collective-permute-start.1
  4.2 0.0 copy-done.11
  4.2 0.1 pad_maximum_fusion
  4.3 0.0 copy-done.4
  4.3 0.9 %weights.1 = (bf16[128,576]{1,0:T(8,128)(2,1)S(1)}, bf16[128,2304]{1,0:T(8,128)(2,1)S(1)}, bf16[96,4608]{1,0:T(8,128)(2,1)S(1)}, bf16[384,192]{1,0:T(8,128)(2,1)...) custom-call(bf16[432,64]{1,0:T(8,128)(2,1)S(1)} %bitcast.25, ...), custom_call_target="tpu_custom_call" | custom-call | flops 1000000000 | bytes 1000000 | tf_op jit(solution)/shard_map/weights/pallas_call | solution.py:133
  5.2 0.9 %inner.1 = (bf16[6,48,1280]{2,1,0:T(8,128)(2,1)S(1)}, bf16[4,192,1280]{2,1,0:T(8,128)(2,1)S(1)}, bf16[6,16,128]{2,1,0:T(8,128)(2,1)S(1)}, bf16[6,16,128]{2,1,0:T(8,128)(2,1)S(1)}) custom-call(bf16[6,16,1024]{2,1,0:T(8,128)(2,1)S(1)} %get-tuple-element.33.own_ref, bf16[128,576]{1,0:T(8,128)(2,1)S(1)} %get-tuple-element.34.m1_ref, ...), custom_call_target="tpu_custom_call" | custom-call | flops 1000000000 | bytes 1000000 | tf_op jit(solution)/shard_map/inner/pallas_call | solution.py:270
  6.1 0.6 %collective-permute-done.far_ref = bf16[3,16,1024]{2,1,0:T(8,128)(2,1)S(1)} collective-permute-done((bf16[3,16,1024]{2,1,0:T(8,128)(2,1)S(1)}, bf16[3,16,1024]{2,1,0:T(8,128)(2,1)S(1)}, u32[]{:S(2)}, u32[]{:S(2)}) %collective-permute-start) | collective-permute-done | bytes 98336 | tf_op jit(solution)/shard_map/ppermute | solution.py:517
  6.7 0.0 collective-permute-done.1.near_ref
  6.7 0.2 edges.1
  6.9 2.1 %collective-permute-start.2 = (bf16[12,16,128]{2,1,0:T(8,128)(2,1)S(1)}, bf16[12,16,128]{2,1,0:T(8,128)(2,1)S(1)}, u32[]{:S(2)}, u32[]{:S(2)}) collective-permute-start(bf16[12,16,128]{2,1,0:T(8,128)(2,1)S(1)} %get-tuple-element.46), channel_id=1, source_target_pairs={{0,1},{1,0},{2,3},{3,2},{4,5},{5,4},{6,7},{7,6},{8,9},{9,8},{10,11... | collective-permute-start | bytes 147464 | tf_op jit(solution)/shard_map/ppermute | solution.py:517
  9.0 0.0 collective-permute-start.3
  9.0 4.1 %main.1.wide_ref = bf16[8,192,1280]{2,1,0:T(8,128)(2,1)S(1)} custom-call(bf16[6,48,1280]{2,1,0:T(8,128)(2,1)S(1)} %get-tuple-element.36.own1, bf16[4,192,1280]{2,1,0:T(8,128)(2,1)S(1)} %get-tuple-element.37.own2, bf16[3,16,1024]{2,1,0:T(8,128)(2,1)S(1)} %collective-permute-done.far_ref, bf16[3,16,1024]{2,1,0:T(8,128)(2,1)S(1)} %collective-permute-done.1.near_ref, ...), custom_call_target="tpu_custom_call" | custom-call | flops 5000000000 | bytes 1000000 | tf_op jit(solution)/shard_map/main/pallas_call | solution.py:299
  13.1 0.0 collective-permute-done.2.first_ref
  13.1 0.0 collective-permute-done.3.second_ref
  13.2 0.0 copy-done.1
  13.2 2.6 %side.1 = (bf16[8,192,256]{2,1,0:T(8,128)(2,1)S(1)}, f32[2,8,128]{2,1,0:T(8,128)S(1)}) custom-call(bf16[8,192,1280]{2,1,0:T(8,128)(2,1)S(1)} %main.1.wide_ref, bf16[12,16,128]{2,1,0:T(8,128)(2,1)S(1)} %get-tuple-element.44.west_ref, bf16[12,16,128]{2,1,0:T(8,128)(2,1)S(1)} %get-tuple-element.45.east_ref, ...), custom_call_target="tpu_custom_call" | custom-call | tf_op jit(solution)/shard_map/side/pallas_call | solution.py:402
  15.8 0.0 copy-start.5
  15.8 0.6 %collective-permute-start.4 = (f32[2,8,128]{2,1,0:T(8,128)S(1)}, f32[2,8,128]{2,1,0:T(8,128)S(1)}, u32[]{:S(2)}, u32[]{:S(2)}) collective-permute-start(f32[2,8,128]{2,1,0:T(8,128)S(1)} %get-tuple-element.53), channel_id=1, source_target_pairs={{0,8},{8,0},{16,24},{24,16},{1,9},{9,1},{17,25},{25,17},{2,10},{10... | collective-permute-start | bytes 24584 | tf_op jit(solution)/shard_map/ppermute | solution.py:546
  16.4 0.8 %early.1 = (f32[2,96,128]{2,1,0:T(8,128)S(1)}, f32[2,96,128]{2,1,0:T(8,128)S(1)}) custom-call(bf16[8,192,1280]{2,1,0:T(8,128)(2,1)S(1)} %main.1.wide_ref, bf16[8,192,256]{2,1,0:T(8,128)(2,1)S(1)} %get-tuple-element.55.t3, bf16[96,4608]{1,0:T(8,128)(2,1)S(1)} %get-tuple-element.54.m3_ref, bf16[288,1536]{1,0:T(8,128)(2,1)S(1)} %get-tuple-element.56.s3_ref), custom_call_target="tpu_custom_call" | custom-call | flops 1000000000 | bytes 1000000 | tf_op jit(solution)/shard_map/early/pallas_call | solution.py:435
  17.2 0.0 copy-start.2
  17.2 0.0 copy-start.3
  17.2 0.0 collective-permute-done.4
  17.2 1.0 %collective-permute-start.5 = (f32[2,8,128]{2,1,0:T(8,128)S(1)}, f32[2,8,128]{2,1,0:T(8,128)S(1)}, u32[]{:S(2)}, u32[]{:S(2)}) collective-permute-start(f32[2,8,128]{2,1,0:T(8,128)S(1)} %add.3.mine_ref), channel_id=1, source_target_pairs={{0,16},{8,24},{16,0},{24,8},{1,17},{9,25},{17,1},{25,9},{2,18},{10... | collective-permute-start | bytes 24584 | tf_op jit(solution)/shard_map/ppermute | solution.py:546
  18.2 2.0 %update.1 = (bf16[6,16,8,128]{3,2,1,0:T(8,128)(2,1)}, f32[6,8,128]{2,1,0:T(8,128)S(1)}) custom-call(bf16[8,192,1280]{2,1,0:T(8,128)(2,1)S(1)} %main.1.wide_ref, bf16[96,4608]{1,0:T(8,128)(2,1)S(1)} %get-tuple-element.54.m3_ref, f32[2,96,128]{2,1,0:T(8,128)S(1)} %get-tuple-element.57.score_ref, f32[2,96,128]{2,1,0:T(8,128)S(1)} %get-tuple-element.58.side_ref, ...), custom_call_target="tpu_custom_call" | custom-call | flops 2000000000 | bytes 1000000 | tf_op jit(solution)/shard_map/update/pallas_call | solution.py:464
  20.2 0.7 %collective-permute-done.5.theirs_ref = f32[2,8,128]{2,1,0:T(8,128)S(1)} collective-permute-done((f32[2,8,128]{2,1,0:T(8,128)S(1)}, f32[2,8,128]{2,1,0:T(8,128)S(1)}, u32[]{:S(2)}, u32[]{:S(2)}) %collective-permute-start.5) | collective-permute-done | bytes 8224 | tf_op jit(solution)/shard_map/ppermute | solution.py:546
  20.9 0.6 %correct.1 = bf16[6,16,8,128]{3,2,1,0:T(8,128)(2,1)} custom-call(f32[2,8,128]{2,1,0:T(8,128)S(1)} %add.3.mine_ref, f32[2,8,128]{2,1,0:T(8,128)S(1)} %collective-permute-done.5.theirs_ref, f32[2,8,128]{2,1,0:T(8,128)S(1)} %bitcast.20, s32[8,128]{1,0:T(8,128)S(1)} %bitcast.21, ...), custom_call_target="tpu_custom_call", output_to_operand_aliasing={{}: (6, {})} | custom-call | tf_op jit(solution)/shard_map/correct/pallas_call | solution.py:494
  (16 shorter events, 0.0 us)
Async XLA Ops:
  0.0 0.9 %copy-start = (bf16[6,16,1,8,128]{4,3,2,1,0:T(8,128)(2,1)S(1)}, bf16[6,16,1,8,128]{4,3,2,1,0:T(8,128)(2,1)}, u32[]{:S(2)}) copy-start(bf16[6,16,1,8,128]{4,3,2,1,0:T(8,128)(2,1)} %param.11) | copy-start | bytes 589828
  0.9 3.3 %copy-start.11 = (s32[6]{0:T(128)S(1)}, s32[6]{0:T(128)}, u32[]{:S(2)}) copy-start(s32[6]{0:T(128)} %param.19) | copy-start | bytes 76
  0.9 3.3 %copy-start.8 = (f32[16]{0:T(128)S(1)}, f32[16]{0:T(128)}, u32[]{:S(2)}) copy-start(f32[16]{0:T(128)} %param.18) | copy-start | bytes 196
  0.9 3.3 %copy-start.9 = (f32[64]{0:T(128)S(1)}, f32[64]{0:T(128)}, u32[]{:S(2)}) copy-start(f32[64]{0:T(128)} %param.16) | copy-start | bytes 772
  0.9 3.3 %copy-start.10 = (f32[64]{0:T(128)S(1)}, f32[64]{0:T(128)}, u32[]{:S(2)}) copy-start(f32[64]{0:T(128)} %param.14) | copy-start | bytes 772
  0.9 3.4 %copy-start.4 = (bf16[64,64,3,3,3]{1,0,4,3,2:T(8,128)(2,1)S(1)}, bf16[64,64,3,3,3]{1,0,4,3,2:T(8,128)(2,1)}, u32[]{:S(2)}) copy-start(bf16[64,64,3,3,3]{1,0,4,3,2:T(8,128)(2,1)} %param.15) | copy-start | bytes 663556
  0.9 3.4 %copy-start.6 = (bf16[64,16,3,3,3]{0,1,4,3,2:T(8,128)(2,1)S(1)}, bf16[64,16,3,3,3]{0,1,4,3,2:T(8,128)(2,1)}, u32[]{:S(2)}) copy-start(bf16[64,16,3,3,3]{0,1,4,3,2:T(8,128)(2,1)} %param.13) | copy-start | bytes 165892
  1.0 3.4 %copy-start.7 = (bf16[16,64,3,3,3]{1,0,4,3,2:T(8,128)(2,1)S(1)}, bf16[16,64,3,3,3]{1,0,4,3,2:T(8,128)(2,1)}, u32[]{:S(2)}) copy-start(bf16[16,64,3,3,3]{1,0,4,3,2:T(8,128)(2,1)} %param.17) | copy-start | bytes 165892
  1.1 5.6 %collective-permute-start = (bf16[3,16,1024]{2,1,0:T(8,128)(2,1)S(1)}, bf16[3,16,1024]{2,1,0:T(8,128)(2,1)S(1)}, u32[]{:S(2)}, u32[]{:S(2)}) collective-permute-start(bf16[3,16,1024]{2,1,0:T(8,128)(2,1)S(1)} %get-tuple-element.38), channel_id=1, source_target_pairs={{0,1},{1,0},{2,3},{3,2},{4,5},{5,4},{6,7},{7,6},{8,16},{9,17},{10,... | collective-permute-start | bytes 294920 | tf_op jit(solution)/shard_map/ppermute | solution.py:517
  4.1 2.6 %collective-permute-start.1 = (bf16[3,16,1024]{2,1,0:T(8,128)(2,1)S(1)}, bf16[3,16,1024]{2,1,0:T(8,128)(2,1)S(1)}, u32[]{:S(2)}, u32[]{:S(2)}) collective-permute-start(bf16[3,16,1024]{2,1,0:T(8,128)(2,1)S(1)} %get-tuple-element.39), channel_id=1, source_target_pairs={{0,8},{1,9},{2,10},{3,11},{4,12},{5,13},{6,14},{7,15},{8,0},{9,1},... | collective-permute-start | bytes 294920 | tf_op jit(solution)/shard_map/ppermute | solution.py:517
  6.9 6.2 %collective-permute-start.2 = (bf16[12,16,128]{2,1,0:T(8,128)(2,1)S(1)}, bf16[12,16,128]{2,1,0:T(8,128)(2,1)S(1)}, u32[]{:S(2)}, u32[]{:S(2)}) collective-permute-start(bf16[12,16,128]{2,1,0:T(8,128)(2,1)S(1)} %get-tuple-element.46), channel_id=1, source_target_pairs={{0,1},{1,0},{2,3},{3,2},{4,5},{5,4},{6,7},{7,6},{8,9},{9,8},{10,11... | collective-permute-start | bytes 147464 | tf_op jit(solution)/shard_map/ppermute | solution.py:517
  9.0 4.1 %collective-permute-start.3 = (bf16[12,16,128]{2,1,0:T(8,128)(2,1)S(1)}, bf16[12,16,128]{2,1,0:T(8,128)(2,1)S(1)}, u32[]{:S(2)}, u32[]{:S(2)}) collective-permute-start(bf16[12,16,128]{2,1,0:T(8,128)(2,1)S(1)} %get-tuple-element.47), channel_id=1, source_target_pairs={{0,8},{1,2},{2,1},{3,4},{4,3},{5,6},{6,5},{7,15},{8,0},{9,10},{10,... | collective-permute-start | bytes 147464 | tf_op jit(solution)/shard_map/ppermute | solution.py:517
  9.0 4.2 %copy-start.1 = (bf16[6,16,1,8,128]{4,3,2,1,0:T(8,128)(2,1)S(1)}, bf16[6,16,1,8,128]{4,3,2,1,0:T(8,128)(2,1)}, u32[]{:S(2)}) copy-start(bf16[6,16,1,8,128]{4,3,2,1,0:T(8,128)(2,1)} %param.11) | copy-start | bytes 589828
  15.8 2.4 %copy-start.5 = (bf16[6,16,1,8,128]{4,3,2,1,0:T(8,128)(2,1)S(1)}, bf16[6,16,1,8,128]{4,3,2,1,0:T(8,128)(2,1)}, u32[]{:S(2)}) copy-start(bf16[6,16,1,8,128]{4,3,2,1,0:T(8,128)(2,1)} %param.12) | copy-start | bytes 589828
  15.8 1.4 %collective-permute-start.4 = (f32[2,8,128]{2,1,0:T(8,128)S(1)}, f32[2,8,128]{2,1,0:T(8,128)S(1)}, u32[]{:S(2)}, u32[]{:S(2)}) collective-permute-start(f32[2,8,128]{2,1,0:T(8,128)S(1)} %get-tuple-element.53), channel_id=1, source_target_pairs={{0,8},{8,0},{16,24},{24,16},{1,9},{9,1},{17,25},{25,17},{2,10},{10... | collective-permute-start | bytes 24584 | tf_op jit(solution)/shard_map/ppermute | solution.py:546
  17.2 3.8 %copy-start.2 = (f32[2,1,8,128]{3,2,1,0:T(8,128)S(1)}, f32[2,1,8,128]{3,2,1,0:T(8,128)}, u32[]{:S(2)}) copy-start(f32[2,1,8,128]{3,2,1,0:T(8,128)} %param.20) | copy-start | bytes 24580
  17.2 3.8 %copy-start.3 = (s32[1,8,128]{2,1,0:T(8,128)S(1)}, s32[1,8,128]{2,1,0:T(8,128)}, u32[]{:S(2)}) copy-start(s32[1,8,128]{2,1,0:T(8,128)} %param.21) | copy-start | bytes 12292
  17.2 3.7 %collective-permute-start.5 = (f32[2,8,128]{2,1,0:T(8,128)S(1)}, f32[2,8,128]{2,1,0:T(8,128)S(1)}, u32[]{:S(2)}, u32[]{:S(2)}) collective-permute-start(f32[2,8,128]{2,1,0:T(8,128)S(1)} %add.3.mine_ref), channel_id=1, source_target_pairs={{0,16},{8,24},{16,0},{24,8},{1,17},{9,25},{17,1},{25,9},{2,18},{10... | collective-permute-start | bytes 24584 | tf_op jit(solution)/shard_map/ppermute | solution.py:546

commit v8 on v7

--- a/solution.py
+++ b/solution.py
@@ -178,7 +178,7 @@
             begun[f] = west, east
 
 
-def edges_kernel(own_west_ref, own_east_ref, far_ref, near_ref, west_ref, east_ref, send1_ref, send2_ref):
+def edges_kernel(own_west_ref, own_east_ref, far_ref, near_ref, west_ref, east_ref, send2_ref, send1_ref):
     frames = own_west_ref.shape[0]
     even = is_even("space")
 
@@ -217,6 +217,11 @@
 
 def plain(ref):
     return lambda f: (ref, f)
+
+
+def split(own, far, count=None):
+    count = own.shape[0] if count is None else count
+    return lambda f: (own, f - DEPTH) if DEPTH <= f < DEPTH + count else (far, f if f < DEPTH else f - count)
 
 
 def in_trajectory(local, frames):
@@ -251,29 +256,36 @@
     return groups + [(frames[-1], 1)] * (len(frames) % 2)
 
 
-def inner_kernel(own_ref, m1_ref, c1_ref, s1, s2, west_ref, east_ref):
+def inner_kernel(own_ref, m1_ref, m2_ref, c1_ref, c2_ref, s1, s2, s3, west_ref, east_ref):
     frames = own_ref.shape[0]
     rows = own_ref.shape[2] // LANES
     each = [(f, y, own_ref[f, :, tile(y)]) for f in range(frames) for y in range(rows)]
-    blank_ends(s1, s2)
+    blank_ends(s1, s2, s3)
     for f, y, v in each:
         spread(s1, f, y, v)
     for f, west, east in strips(each, rows):
         west_ref[f], east_ref[f] = west, east
     layer(plain(s1), plain(s2), m1_ref, c1_ref, pairs_of(range(frames - 2)), rows, lambda f: None)
-
-
-def make_inner(own, m1, c1):
+    layer(plain(s2), plain(s3), m2_ref, c2_ref, pairs_of(range(frames - 4)), rows, lambda f: None)
+
+
+def make_inner(own, m1, m2, c1, c2):
     frames, chans, width = own.shape
     hid, wide = c1.shape[0], width + 2 * LANES
     strip = shape_of((frames, chans, LANES), BF)
     return call(
         inner_kernel,
         "inner",
-        (shape_of((frames, 3 * chans, wide), BF), shape_of((frames - 2, 3 * hid, wide), BF), strip, strip),
-        [VMEM] * 3,
-        cost=1_000_000_000,
-    )(own, m1, c1)
+        (
+            shape_of((frames, 3 * chans, wide), BF),
+            shape_of((frames - 2, 3 * hid, wide), BF),
+            shape_of((frames - 4, 3 * hid, wide), BF),
+            strip,
+            strip,
+        ),
+        [VMEM] * 5,
+        cost=1_500_000_000,
+    )(own, m1, m2, c1, c2)
 
 
 def main_kernel(own1, own2, far_ref, near_ref, m1_ref, m2_ref, c1_ref, c2_ref, s3, far1, far2):
@@ -283,14 +295,11 @@
     for f, y, v in beside(near_ref, far_ref):
         spread(far1, f, y, v)
 
-    def split(own, far, edge):
-        count = own.shape[0]
-        return lambda f: (own, f - edge) if edge <= f < edge + count else (far, f if f < edge else f - count)
-
-    one, two = split(own1, far1, DEPTH), split(own2, far2, DEPTH)
+    one, two, three = split(own1, far1), split(own2, far2), split(None, s3, frames - 4)
     groups = pairs_of(range(DEPTH)) + pairs_of(range(frames + 1, frames + 4))
     layer(one, two, m1_ref, c1_ref, groups, rows, lambda f: in_trajectory(f - 2, frames))
-    layer(two, plain(s3), m2_ref, c2_ref, pairs_of(range(frames + 2)), rows, lambda f: in_trajectory(f - 1, frames))
+    groups = pairs_of(range(DEPTH)) + pairs_of(range(frames - 1, frames + 2))
+    layer(two, three, m2_ref, c2_ref, groups, rows, lambda f: in_trajectory(f - 1, frames))
 
 
 def make_main(own1, own2, near, far, m1, m2, c1, c2):
@@ -299,7 +308,7 @@
     return call(
         main_kernel,
         "main",
-        (shape_of((frames + 2, rows2, wide), BF),),
+        (shape_of((2 * DEPTH, rows2, wide), BF),),
         [VMEM] * 8,
         [pltpu.VMEM((2 * DEPTH, rows1, wide), BF), pltpu.VMEM((2 * DEPTH, rows2, wide), BF)],
         cost=5_000_000_000,
@@ -337,7 +346,7 @@
 
 
 def side_kernel(
-    wide_ref, west_ref, east_ref, first_ref, second_ref, s1_ref, s2_ref, head_ref, c1_ref, c2_ref, c3_ref,
+    own3, far3, west_ref, east_ref, second_ref, first_ref, s1_ref, s2_ref, head_ref, c1_ref, c2_ref, c3_ref,
     state_ref, day_ref, t3, part_ref, t1, t2, own, ends,
 ):
     frames, fields, rows, _ = state_ref.shape
@@ -374,7 +383,8 @@
     own[0] = jnp.zeros(own.shape[1:], F32)
     own[rows + 1] = jnp.zeros(own.shape[1:], F32)
     for y in range(0, rows, 2):
-        z = jnp.concatenate([wide_ref[j, :, (y + 1) * LANES : (y + 3) * LANES] for j in range(frames + 2)], axis=0)
+        places = [split(own3, far3)(j) for j in range(frames + 2)]
+        z = jnp.concatenate([ref[at, :, (y + 1) * LANES : (y + 3) * LANES] for ref, at in places], axis=0)
         acc = jnp.dot(head_ref[...], z, preferred_element_type=F32)
         own[y + 1], own[y + 2] = acc[:, tile(0)], acc[:, tile(1)]
     z = jnp.concatenate([t3[j] for j in range(frames + 2)], axis=0)
@@ -396,33 +406,33 @@
         part_ref[d] = total
 
 
-def make_side(wide, west, east, first, second, s1, s2, head, c1, c2, c3, state, day, days):
+def make_side(own3, far3, west, east, first, second, s1, s2, head, c1, c2, c3, state, day, days):
     frames, fields, rows, _ = state.shape
     chans, hid = west.shape[1], c1.shape[0]
     return call(
         side_kernel,
         "side",
         (shape_of((frames + 2, 3 * hid, 2 * LANES), BF), shape_of((days, rows, LANES), F32)),
-        [VMEM] * 13,
+        [VMEM] * 14,
         [
             pltpu.VMEM((frames + 6, 3 * chans, 2 * LANES), BF),
             pltpu.VMEM((frames + 4, 3 * hid, 2 * LANES), BF),
             pltpu.VMEM((rows + 2, head.shape[0], LANES), F32),
             pltpu.VMEM((2, head.shape[0], LANES), F32),
         ],
-    )(wide, west, east, first, second, s1, s2, head, c1, c2, c3, state, day)
-
-
-def own_score(wide_ref, m3_ref, frames, y):
-    acc = jnp.dot(m3_ref[...], window(plain(wide_ref), range(frames + 2), y), preferred_element_type=F32)
+    )(own3, far3, west, east, second, first, s1, s2, head, c1, c2, c3, state, day)
+
+
+def own_score(own3, far3, m3_ref, frames, y):
+    acc = jnp.dot(m3_ref[...], window(split(own3, far3), range(frames + 2), y), preferred_element_type=F32)
     return acc[:, tile(0)], acc[:, tile(1)]
 
 
-def early_kernel(wide_ref, t3, m3_ref, s3_ref, score_ref, side_ref):
+def early_kernel(own3, far3, t3, m3_ref, s3_ref, score_ref, side_ref):
     frames = t3.shape[0] - 2
     fields = m3_ref.shape[0] // frames
     for y in range(0, score_ref.shape[0], 2):
-        score_ref[y], score_ref[y + 1] = own_score(wide_ref, m3_ref, frames, y)
+        score_ref[y], score_ref[y + 1] = own_score(own3, far3, m3_ref, frames, y)
     z = jnp.concatenate([t3[j] for j in range(frames + 2)], axis=0)
     acc = jnp.dot(s3_ref[...], z, preferred_element_type=F32)
     for f in range(frames):
@@ -431,21 +441,21 @@
             side_ref[half, f * fields : (f + 1) * fields] = both[:, tile(half)]
 
 
-def make_early(wide, t3, m3, s3, count):
+def make_early(own3, far3, t3, m3, s3, count):
     return call(
         early_kernel,
         "early",
         (shape_of((count, m3.shape[0], LANES), F32), shape_of((2, m3.shape[0], LANES), F32)),
-        [VMEM] * 4,
+        [VMEM] * 5,
         cost=1_000_000_000,
-    )(wide, t3, m3, s3)
-
-
-def update_kernel(wide_ref, m3_ref, score_ref, side_ref, c3_ref, state_ref, noise_ref, out_ref, head_ref, rest, scr):
+    )(own3, far3, t3, m3, s3)
+
+
+def update_kernel(own3, far3, m3_ref, score_ref, side_ref, c3_ref, state_ref, noise_ref, out_ref, head_ref, rest, scr):
     frames, fields, rows, _ = state_ref.shape
     done = score_ref.shape[0]
     for y in range(done, rows, 2):
-        rest[y - done], rest[y - done + 1] = own_score(wide_ref, m3_ref, frames, y)
+        rest[y - done], rest[y - done + 1] = own_score(own3, far3, m3_ref, frames, y)
     bias = c3_ref[...]
     for f in range(frames):
         at = slice(f * fields, (f + 1) * fields)
@@ -459,19 +469,19 @@
         head_ref[f] = moved[0]
 
 
-def make_update(wide, m3, score, side, c3, state, noise):
+def make_update(own3, far3, m3, score, side, c3, state, noise):
     frames, fields, rows, _ = state.shape
     return call(
         update_kernel,
         "update",
         (shape_of(state.shape, BF), shape_of((frames, rows, LANES), F32)),
-        [VMEM] * 7,
+        [VMEM] * 8,
         [
             pltpu.VMEM((rows - score.shape[0], frames * fields, LANES), F32),
             pltpu.VMEM((frames, fields * rows, LANES), F32),
         ],
         cost=2_000_000_000,
-    )(wide, m3, score, side, c3, state, noise)
+    )(own3, far3, m3, score, side, c3, state, noise)
 
 
 def correct_kernel(mine_ref, theirs_ref, observed_ref, mask_ref, head_ref, day_ref, _, out_ref, buf, sem):
@@ -531,15 +541,16 @@
     near = swapped(send1, "tm", 0)
     small = jnp.concatenate([bias_one, bias_two, bias_three, day_of_frame.astype(F32)])[None]
     m1, m2, m3, s1, s2, s3, c1, c2, c3, days, head = make_weights(w1, w2, w3, small, state.shape[0])
-    own1, own2, west, east = make_inner(own, m1, c1)
-    west, east, send1, send2 = make_edges(west, east, near, far)
-    first, second = swapped(send1, "space", 0), swapped(send2, "space", 1)
-    wide = make_main(own1, own2, near, far, m1, m2, c1, c2)
+    own1, own2, own3, west, east = make_inner(own, m1, m2, c1, c2)
+    west, east, send2, send1 = make_edges(west, east, near, far)
+    second = swapped(send2, "space", 1)
+    first = swapped(send1, "space", 0)
+    far3 = make_main(own1, own2, near, far, m1, m2, c1, c2)
     t3, mine = make_side(
-        wide, west, east, first, second, s1, s2, head, c1, c2, c3, state, days, observed.shape[0]
+        own3, far3, west, east, first, second, s1, s2, head, c1, c2, c3, state, days, observed.shape[0]
     )
-    score, side = make_early(wide, t3, m3, s3, EARLY)
-    out, first = make_update(wide, m3, score, side, c3, state, noise)
+    score, side = make_early(own3, far3, t3, m3, s3, EARLY)
+    out, first = make_update(own3, far3, m3, score, side, c3, state, noise)
     count = lax.axis_size("tm")
     reach = 1
     while True:

time: 21.7 us -> 22.8 us (1.051)
  starting transfers between devices: 6.75 us -> 7.44 us
  Pallas kernels: 12.3 us -> 12.9 us
  waiting for transfers between devices: 1.35 us -> 1.09 us
    ppermute x4, starting transfers between devices: 5.21 us -> 6.46 us  [swapped(): return lax.ppermute(value, ('tm', 'space'), pairs)]
    pallas_call x1, Pallas kernels: 0.91 us -> 1.75 us  [make_inner(): call(inner_kernel, 'inner', (shape_of((frames, 3 * chans, wide), BF), sha...]
    ppermute x4, waiting for transfers between devices: 0.61 us -> 0.01 us  [swapped(): return lax.ppermute(value, ('tm', 'space'), pairs)]
    ppermute x2, starting transfers between devices: 1.54 us -> 0.99 us  [body(): theirs = lax.ppermute(mine, 'tm', [(i, i ^ reach) for i in range(count)])]
    ppermute x2, waiting for transfers between devices: 0.74 us -> 1.08 us  [body(): theirs = lax.ppermute(mine, 'tm', [(i, i ^ reach) for i in range(count)])]
  transfers between devices with their start and end apart: 6 -> 6, of which waited for: 2 -> 2; matrix products, arithmetic and copies ran while one was open for 0% -> 0% of each run, Pallas kernels for 40% -> 41%
where the time goes in v8:
time: 22.8 us; the launch traced here: 22.7 us
  Pallas kernels  12.9 us (57%)
  starting transfers between devices  7.44 us (33%)
  waiting for transfers between devices  1.09 us (5%)
  local copies, waits for them, and re-layouts  0.97 us (4%)
    ppermute x4, starting transfers between devices, swapped(): return lax.ppermute(value, ('tm', 'space'), pairs)  6.46 us
    pallas_call x1, Pallas kernels, make_main(): call(main_kernel, 'main', (shape_of((2 * DEPTH, rows2, wide), BF),), [VME...  3.92 us
    pallas_call x1, Pallas kernels, make_side(): call(side_kernel, 'side', (shape_of((frames + 2, 3 * hid, 2 * LANES), BF)...  2.66 us
    pallas_call x1, Pallas kernels, make_update(): call(update_kernel, 'update', (shape_of(state.shape, BF), shape_of((frame...  2.01 us
    pallas_call x1, Pallas kernels, make_inner(): call(inner_kernel, 'inner', (shape_of((frames, 3 * chans, wide), BF), sha...  1.75 us
    ppermute x2, waiting for transfers between devices, body(): theirs = lax.ppermute(mine, 'tm', [(i, i ^ reach) for i in range(count)])  1.08 us
    ppermute x2, starting transfers between devices, body(): theirs = lax.ppermute(mine, 'tm', [(i, i ^ reach) for i in range(count)])  0.99 us
    unnamed x24, local copies, waits for them, and re-layouts  0.97 us
  transfers between devices with their start and end apart: 6, of which 2 were waited for; matrix products, arithmetic and copies ran while one was open for 0% of the time, Pallas kernels for 41%

profile of v8, /device:TPU:0, one launch (start us, length us, event | category | flops | bytes accessed | tf_op | source)
XLA Modules:
  0.0 22.7 jit_solution(14088733742675354114)
XLA Ops:
  0.0 0.9 %copy-done = bf16[6,16,1,8,128]{4,3,2,1,0:T(8,128)(2,1)S(1)} copy-done((bf16[6,16,1,8,128]{4,3,2,1,0:T(8,128)(2,1)S(1)}, bf16[6,16,1,8,128]{4,3,2,1,0:T(8,128)(2,1)}, u32[]{:S(2)}) %copy-start) | copy-done | bytes 196632
  0.9 0.0 copy-start.4
  0.9 0.0 copy-start.6
  1.0 0.0 copy-start.7
  1.0 0.1 rows.1
  1.1 3.0 %collective-permute-start = (bf16[3,16,1024]{2,1,0:T(8,128)(2,1)S(1)}, bf16[3,16,1024]{2,1,0:T(8,128)(2,1)S(1)}, u32[]{:S(2)}, u32[]{:S(2)}) collective-permute-start(bf16[3,16,1024]{2,1,0:T(8,128)(2,1)S(1)} %get-tuple-element.42), channel_id=1, source_target_pairs={{0,1},{1,0},{2,3},{3,2},{4,5},{5,4},{6,7},{7,6},{8,16},{9,17},{10,... | collective-permute-start | bytes 294920 | tf_op jit(solution)/shard_map/ppermute | solution.py:527
  4.1 0.1 collective-permute-start.1
  4.2 0.0 copy-done.11
  4.2 0.0 copy-done.8
  4.2 0.0 copy-done.9
  4.2 0.0 copy-done.10
  4.2 0.1 pad_maximum_fusion
  4.3 0.0 copy-done.6
  4.3 0.9 %weights.1 = (bf16[128,576]{1,0:T(8,128)(2,1)S(1)}, bf16[128,2304]{1,0:T(8,128)(2,1)S(1)}, bf16[96,4608]{1,0:T(8,128)(2,1)S(1)}, bf16[384,192]{1,0:T(8,128)(2,1)...) custom-call(bf16[432,64]{1,0:T(8,128)(2,1)S(1)} %bitcast.25, ...), custom_call_target="tpu_custom_call" | custom-call | flops 1000000000 | bytes 1000000 | tf_op jit(solution)/shard_map/weights/pallas_call | solution.py:133
  5.2 1.8 %inner.1 = (bf16[6,48,1280]{2,1,0:T(8,128)(2,1)S(1)}, bf16[4,192,1280]{2,1,0:T(8,128)(2,1)S(1)}, bf16[2,192,1280]{2,1,0:T(8,128)(2,1)S(1)}, bf16[6,16,128]{2,1,0:T(8,128)(2,1)S(1)}, bf16[6,16,128]{2,1,0:T(8,128)(2,1)S(1)}) custom-call(bf16[6,16,1024]{2,1,0:T(8,128)(2,1)S(1)} %get-tuple-element.34.own_ref, bf16[128,576]{1,0:T(8,128)(2,1)S(1)} %get-tuple-element.35.m1_ref, ...), custom_call_target="tpu_custom_call" | custom-call | flops 1500000000 | bytes 1000000 | tf_op jit(solution)/shard_map/inner/pallas_call | solution.py:276
  7.0 0.0 collective-permute-done.far_ref
  7.0 0.0 collective-permute-done.1.near_ref
  7.0 0.2 edges.1
  7.2 0.5 %collective-permute-start.2 = (bf16[12,16,128]{2,1,0:T(8,128)(2,1)S(1)}, bf16[12,16,128]{2,1,0:T(8,128)(2,1)S(1)}, u32[]{:S(2)}, u32[]{:S(2)}) collective-permute-start(bf16[12,16,128]{2,1,0:T(8,128)(2,1)S(1)} %get-tuple-element.48), channel_id=1, source_target_pairs={{0,8},{1,2},{2,1},{3,4},{4,3},{5,6},{6,5},{7,15},{8,0},{9,10},{10,... | collective-permute-start | bytes 147464 | tf_op jit(solution)/shard_map/ppermute | solution.py:527
  7.7 2.8 %collective-permute-start.3 = (bf16[12,16,128]{2,1,0:T(8,128)(2,1)S(1)}, bf16[12,16,128]{2,1,0:T(8,128)(2,1)S(1)}, u32[]{:S(2)}, u32[]{:S(2)}) collective-permute-start(bf16[12,16,128]{2,1,0:T(8,128)(2,1)S(1)} %get-tuple-element.49), channel_id=1, source_target_pairs={{0,1},{1,0},{2,3},{3,2},{4,5},{5,4},{6,7},{7,6},{8,9},{9,8},{10,11... | collective-permute-start | bytes 147464 | tf_op jit(solution)/shard_map/ppermute | solution.py:527
  10.5 3.9 %main.1.far3 = bf16[6,192,1280]{2,1,0:T(8,128)(2,1)S(1)} custom-call(bf16[6,48,1280]{2,1,0:T(8,128)(2,1)S(1)} %get-tuple-element.40.own1, bf16[4,192,1280]{2,1,0:T(8,128)(2,1)S(1)} %get-tuple-element.41.own2, bf16[3,16,1024]{2,1,0:T(8,128)(2,1)S(1)} %collective-permute-done.far_ref, bf16[3,16,1024]{2,1,0:T(8,128)(2,1)S(1)} %collective-permute-done.1.near_ref, ...), custom_call_target="tpu_custom_call" | custom-call | flops 5000000000 | bytes 1000000 | tf_op jit(solution)/shard_map/main/pallas_call | solution.py:308
  14.4 0.0 collective-permute-done.2.second_ref
  14.5 0.0 collective-permute-done.3.first_ref
  14.5 2.7 %side.1 = (bf16[8,192,256]{2,1,0:T(8,128)(2,1)S(1)}, f32[2,8,128]{2,1,0:T(8,128)S(1)}) custom-call(bf16[2,192,1280]{2,1,0:T(8,128)(2,1)S(1)} %get-tuple-element.39.own3, bf16[6,192,1280]{2,1,0:T(8,128)(2,1)S(1)} %main.1.far3, bf16[12,16,128]{2,1,0:T(8,128)(2,1)S(1)} %get-tuple-element.46.west_ref, bf16[12,16,128]{2,1,0:T(8,128)(2,1)S(1)} %get-tuple-element.47.east_ref, ...), custom_call_target="tpu_custom_call" | custom-call | tf_op jit(solution)/shard_map/side/pallas_call | solution.py:412
  17.1 0.1 collective-permute-start.4
  17.2 0.0 copy-start.5
  17.2 0.8 %early.1 = (f32[2,96,128]{2,1,0:T(8,128)S(1)}, f32[2,96,128]{2,1,0:T(8,128)S(1)}) custom-call(bf16[2,192,1280]{2,1,0:T(8,128)(2,1)S(1)} %get-tuple-element.39.own3, bf16[6,192,1280]{2,1,0:T(8,128)(2,1)S(1)} %main.1.far3, bf16[8,192,256]{2,1,0:T(8,128)(2,1)S(1)} %get-tuple-element.57.t3, bf16[96,4608]{1,0:T(8,128)(2,1)S(1)} %get-tuple-element.56.m3_ref, ...), custom_call_target="tpu_custom_call" | custom-call | flops 1000000000 | bytes 1000000 | tf_op jit(solution)/shard_map/early/pallas_call | solution.py:445
  18.0 0.4 %collective-permute-done.4 = f32[2,8,128]{2,1,0:T(8,128)S(1)} collective-permute-done((f32[2,8,128]{2,1,0:T(8,128)S(1)}, f32[2,8,128]{2,1,0:T(8,128)S(1)}, u32[]{:S(2)}, u32[]{:S(2)}) %collective-permute-start.4) | collective-permute-done | bytes 8224 | tf_op jit(solution)/shard_map/ppermute | solution.py:557
  18.4 0.9 %collective-permute-start.5 = (f32[2,8,128]{2,1,0:T(8,128)S(1)}, f32[2,8,128]{2,1,0:T(8,128)S(1)}, u32[]{:S(2)}, u32[]{:S(2)}) collective-permute-start(f32[2,8,128]{2,1,0:T(8,128)S(1)} %add.3.mine_ref), channel_id=1, source_target_pairs={{0,16},{8,24},{16,0},{24,8},{1,17},{9,25},{17,1},{25,9},{2,18},{10... | collective-permute-start | bytes 24584 | tf_op jit(solution)/shard_map/ppermute | solution.py:557
  19.3 2.0 %update.1 = (bf16[6,16,8,128]{3,2,1,0:T(8,128)(2,1)}, f32[6,8,128]{2,1,0:T(8,128)S(1)}) custom-call(bf16[2,192,1280]{2,1,0:T(8,128)(2,1)S(1)} %get-tuple-element.39.own3, bf16[6,192,1280]{2,1,0:T(8,128)(2,1)S(1)} %main.1.far3, bf16[96,4608]{1,0:T(8,128)(2,1)S(1)} %get-tuple-element.56.m3_ref, f32[2,96,128]{2,1,0:T(8,128)S(1)} %get-tuple-element.59.score_ref, ...), custom_call_target="tpu_custom_call" | custom-call | flops 2000000000 | bytes 1000000 | tf_op jit(solution)/shard_map/update/pallas_call | solution.py:474
  21.3 0.7 %collective-permute-done.5.theirs_ref = f32[2,8,128]{2,1,0:T(8,128)S(1)} collective-permute-done((f32[2,8,128]{2,1,0:T(8,128)S(1)}, f32[2,8,128]{2,1,0:T(8,128)S(1)}, u32[]{:S(2)}, u32[]{:S(2)}) %collective-permute-start.5) | collective-permute-done | bytes 8224 | tf_op jit(solution)/shard_map/ppermute | solution.py:557
  22.0 0.6 %correct.1 = bf16[6,16,8,128]{3,2,1,0:T(8,128)(2,1)} custom-call(f32[2,8,128]{2,1,0:T(8,128)S(1)} %add.3.mine_ref, f32[2,8,128]{2,1,0:T(8,128)S(1)} %collective-permute-done.5.theirs_ref, f32[2,8,128]{2,1,0:T(8,128)S(1)} %bitcast.20, s32[8,128]{1,0:T(8,128)S(1)} %bitcast.21, ...), custom_call_target="tpu_custom_call", output_to_operand_aliasing={{}: (6, {})} | custom-call | tf_op jit(solution)/shard_map/correct/pallas_call | solution.py:504
  (16 shorter events, 0.0 us)
Async XLA Ops:
  0.0 0.9 %copy-start = (bf16[6,16,1,8,128]{4,3,2,1,0:T(8,128)(2,1)S(1)}, bf16[6,16,1,8,128]{4,3,2,1,0:T(8,128)(2,1)}, u32[]{:S(2)}) copy-start(bf16[6,16,1,8,128]{4,3,2,1,0:T(8,128)(2,1)} %param.11) | copy-start | bytes 589828
  0.9 3.3 %copy-start.11 = (s32[6]{0:T(128)S(1)}, s32[6]{0:T(128)}, u32[]{:S(2)}) copy-start(s32[6]{0:T(128)} %param.19) | copy-start | bytes 76
  0.9 3.3 %copy-start.8 = (f32[16]{0:T(128)S(1)}, f32[16]{0:T(128)}, u32[]{:S(2)}) copy-start(f32[16]{0:T(128)} %param.18) | copy-start | bytes 196
  0.9 3.3 %copy-start.9 = (f32[64]{0:T(128)S(1)}, f32[64]{0:T(128)}, u32[]{:S(2)}) copy-start(f32[64]{0:T(128)} %param.16) | copy-start | bytes 772
  0.9 3.3 %copy-start.10 = (f32[64]{0:T(128)S(1)}, f32[64]{0:T(128)}, u32[]{:S(2)}) copy-start(f32[64]{0:T(128)} %param.14) | copy-start | bytes 772
  0.9 3.4 %copy-start.4 = (bf16[64,64,3,3,3]{1,0,4,3,2:T(8,128)(2,1)S(1)}, bf16[64,64,3,3,3]{1,0,4,3,2:T(8,128)(2,1)}, u32[]{:S(2)}) copy-start(bf16[64,64,3,3,3]{1,0,4,3,2:T(8,128)(2,1)} %param.15) | copy-start | bytes 663556
  0.9 3.4 %copy-start.6 = (bf16[64,16,3,3,3]{0,1,4,3,2:T(8,128)(2,1)S(1)}, bf16[64,16,3,3,3]{0,1,4,3,2:T(8,128)(2,1)}, u32[]{:S(2)}) copy-start(bf16[64,16,3,3,3]{0,1,4,3,2:T(8,128)(2,1)} %param.13) | copy-start | bytes 165892
  1.0 3.4 %copy-start.7 = (bf16[16,64,3,3,3]{1,0,4,3,2:T(8,128)(2,1)S(1)}, bf16[16,64,3,3,3]{1,0,4,3,2:T(8,128)(2,1)}, u32[]{:S(2)}) copy-start(bf16[16,64,3,3,3]{1,0,4,3,2:T(8,128)(2,1)} %param.17) | copy-start | bytes 165892
  1.1 5.9 %collective-permute-start = (bf16[3,16,1024]{2,1,0:T(8,128)(2,1)S(1)}, bf16[3,16,1024]{2,1,0:T(8,128)(2,1)S(1)}, u32[]{:S(2)}, u32[]{:S(2)}) collective-permute-start(bf16[3,16,1024]{2,1,0:T(8,128)(2,1)S(1)} %get-tuple-element.42), channel_id=1, source_target_pairs={{0,1},{1,0},{2,3},{3,2},{4,5},{5,4},{6,7},{7,6},{8,16},{9,17},{10,... | collective-permute-start | bytes 294920 | tf_op jit(solution)/shard_map/ppermute | solution.py:527
  4.1 2.9 %collective-permute-start.1 = (bf16[3,16,1024]{2,1,0:T(8,128)(2,1)S(1)}, bf16[3,16,1024]{2,1,0:T(8,128)(2,1)S(1)}, u32[]{:S(2)}, u32[]{:S(2)}) collective-permute-start(bf16[3,16,1024]{2,1,0:T(8,128)(2,1)S(1)} %get-tuple-element.43), channel_id=1, source_target_pairs={{0,8},{1,9},{2,10},{3,11},{4,12},{5,13},{6,14},{7,15},{8,0},{9,1},... | collective-permute-start | bytes 294920 | tf_op jit(solution)/shard_map/ppermute | solution.py:527
  7.2 7.3 %collective-permute-start.2 = (bf16[12,16,128]{2,1,0:T(8,128)(2,1)S(1)}, bf16[12,16,128]{2,1,0:T(8,128)(2,1)S(1)}, u32[]{:S(2)}, u32[]{:S(2)}) collective-permute-start(bf16[12,16,128]{2,1,0:T(8,128)(2,1)S(1)} %get-tuple-element.48), channel_id=1, source_target_pairs={{0,8},{1,2},{2,1},{3,4},{4,3},{5,6},{6,5},{7,15},{8,0},{9,10},{10,... | collective-permute-start | bytes 147464 | tf_op jit(solution)/shard_map/ppermute | solution.py:527
  7.7 6.8 %collective-permute-start.3 = (bf16[12,16,128]{2,1,0:T(8,128)(2,1)S(1)}, bf16[12,16,128]{2,1,0:T(8,128)(2,1)S(1)}, u32[]{:S(2)}, u32[]{:S(2)}) collective-permute-start(bf16[12,16,128]{2,1,0:T(8,128)(2,1)S(1)} %get-tuple-element.49), channel_id=1, source_target_pairs={{0,1},{1,0},{2,3},{3,2},{4,5},{5,4},{6,7},{7,6},{8,9},{9,8},{10,11... | collective-permute-start | bytes 147464 | tf_op jit(solution)/shard_map/ppermute | solution.py:527
  10.5 3.9 %copy-start.1 = (bf16[6,16,1,8,128]{4,3,2,1,0:T(8,128)(2,1)S(1)}, bf16[6,16,1,8,128]{4,3,2,1,0:T(8,128)(2,1)}, u32[]{:S(2)}) copy-start(bf16[6,16,1,8,128]{4,3,2,1,0:T(8,128)(2,1)} %param.11) | copy-start | bytes 589828
  17.1 1.2 %collective-permute-start.4 = (f32[2,8,128]{2,1,0:T(8,128)S(1)}, f32[2,8,128]{2,1,0:T(8,128)S(1)}, u32[]{:S(2)}, u32[]{:S(2)}) collective-permute-start(f32[2,8,128]{2,1,0:T(8,128)S(1)} %get-tuple-element.55), channel_id=1, source_target_pairs={{0,8},{8,0},{16,24},{24,16},{1,9},{9,1},{17,25},{25,17},{2,10},{10... | collective-permute-start | bytes 24584 | tf_op jit(solution)/shard_map/ppermute | solution.py:557
  17.2 2.1 %copy-start.5 = (bf16[6,16,1,8,128]{4,3,2,1,0:T(8,128)(2,1)S(1)}, bf16[6,16,1,8,128]{4,3,2,1,0:T(8,128)(2,1)}, u32[]{:S(2)}) copy-start(bf16[6,16,1,8,128]{4,3,2,1,0:T(8,128)(2,1)} %param.12) | copy-start | bytes 589828
  18.4 3.7 %collective-permute-start.5 = (f32[2,8,128]{2,1,0:T(8,128)S(1)}, f32[2,8,128]{2,1,0:T(8,128)S(1)}, u32[]{:S(2)}, u32[]{:S(2)}) collective-permute-start(f32[2,8,128]{2,1,0:T(8,128)S(1)} %add.3.mine_ref), channel_id=1, source_target_pairs={{0,16},{8,24},{16,0},{24,8},{1,17},{9,25},{17,1},{25,9},{2,18},{10... | collective-permute-start | bytes 24584 | tf_op jit(solution)/shard_map/ppermute | solution.py:557
  19.3 2.7 %copy-start.2 = (f32[2,1,8,128]{3,2,1,0:T(8,128)S(1)}, f32[2,1,8,128]{3,2,1,0:T(8,128)}, u32[]{:S(2)}) copy-start(f32[2,1,8,128]{3,2,1,0:T(8,128)} %param.20) | copy-start | bytes 24580
  19.3 2.7 %copy-start.3 = (s32[1,8,128]{2,1,0:T(8,128)S(1)}, s32[1,8,128]{2,1,0:T(8,128)}, u32[]{:S(2)}) copy-start(s32[1,8,128]{2,1,0:T(8,128)} %param.21) | copy-start | bytes 12292

commit v9 on v7

--- a/solution.py
+++ b/solution.py
@@ -1,3 +1,5 @@
+import functools
+
 import jax
 import jax.numpy as jnp
 from jax import lax
@@ -12,7 +14,6 @@
 PITCH = 16
 VMEM = pl.BlockSpec(memory_space=pltpu.VMEM)
 ANYWHERE = pl.BlockSpec(memory_space=pltpu.HBM)
-EARLY = 2
 LIMIT = 24 * 1024 * 1024
 
 
@@ -418,48 +419,31 @@
     return acc[:, tile(0)], acc[:, tile(1)]
 
 
-def early_kernel(wide_ref, t3, m3_ref, s3_ref, score_ref, side_ref):
-    frames = t3.shape[0] - 2
-    fields = m3_ref.shape[0] // frames
-    for y in range(0, score_ref.shape[0], 2):
-        score_ref[y], score_ref[y + 1] = own_score(wide_ref, m3_ref, frames, y)
+def update_kernel(
+    wide_ref, t3, m3_ref, s3_ref, c3_ref, state_ref, noise_ref, out_ref, head_ref, rest, side, scr
+):
+    frames, fields, rows, _ = state_ref.shape
     z = jnp.concatenate([t3[j] for j in range(frames + 2)], axis=0)
     acc = jnp.dot(s3_ref[...], z, preferred_element_type=F32)
     for f in range(frames):
         both = over_rows(acc, f * 3 * fields, fields)
         for half in range(2):
-            side_ref[half, f * fields : (f + 1) * fields] = both[:, tile(half)]
-
-
-def make_early(wide, t3, m3, s3, count):
-    return call(
-        early_kernel,
-        "early",
-        (shape_of((count, m3.shape[0], LANES), F32), shape_of((2, m3.shape[0], LANES), F32)),
-        [VMEM] * 4,
-        cost=1_000_000_000,
-    )(wide, t3, m3, s3)
-
-
-def update_kernel(wide_ref, m3_ref, score_ref, side_ref, c3_ref, state_ref, noise_ref, out_ref, head_ref, rest, scr):
-    frames, fields, rows, _ = state_ref.shape
-    done = score_ref.shape[0]
-    for y in range(done, rows, 2):
-        rest[y - done], rest[y - done + 1] = own_score(wide_ref, m3_ref, frames, y)
+            side[half, f * fields : (f + 1) * fields] = both[:, tile(half)]
+    for y in range(0, rows, 2):
+        rest[y], rest[y + 1] = own_score(wide_ref, m3_ref, frames, y)
     bias = c3_ref[...]
     for f in range(frames):
         at = slice(f * fields, (f + 1) * fields)
-        west, east = side_ref[0, at], side_ref[1, at]
+        west, east = side[0, at], side[1, at]
         for y in range(rows):
-            v = score_ref[y, at] if y < done else rest[y - done, at]
-            scr[f, pl.ds(y, fields, stride=rows), :] = patched(v, west, east, y) + bias
+            scr[f, pl.ds(y, fields, stride=rows), :] = patched(rest[y, at], west, east, y) + bias
         score = scr[f].reshape(fields, rows, LANES)
         moved = state_ref[f].astype(F32) + 0.8 * score + 0.5 * noise_ref[f].astype(F32)
         out_ref[f] = moved.astype(BF)
         head_ref[f] = moved[0]
 
 
-def make_update(wide, m3, score, side, c3, state, noise):
+def make_update(wide, t3, m3, s3, c3, state, noise):
     frames, fields, rows, _ = state.shape
     return call(
         update_kernel,
@@ -467,18 +451,21 @@
         (shape_of(state.shape, BF), shape_of((frames, rows, LANES), F32)),
         [VMEM] * 7,
         [
-            pltpu.VMEM((rows - score.shape[0], frames * fields, LANES), F32),
+            pltpu.VMEM((rows, frames * fields, LANES), F32),
+            pltpu.VMEM((2, frames * fields, LANES), F32),
             pltpu.VMEM((frames, fields * rows, LANES), F32),
         ],
-        cost=2_000_000_000,
-    )(wide, m3, score, side, c3, state, noise)
-
-
-def correct_kernel(mine_ref, theirs_ref, observed_ref, mask_ref, head_ref, day_ref, _, out_ref, buf, sem):
+        cost=3_000_000_000,
+    )(wide, t3, m3, s3, c3, state, noise)
+
+
+def correct_kernel(count, *refs):
+    parts = refs[:count]
+    observed_ref, mask_ref, head_ref, day_ref, _, out_ref, buf, sem = refs[count:]
     frames = head_ref.shape[0]
     days = observed_ref.shape[0]
     mask = mask_ref[...].astype(F32)
-    misfit = [0.15 * (mask * (mine_ref[d] + theirs_ref[d] - observed_ref[d])) for d in range(days)]
+    misfit = [0.15 * (mask * (sum(p[d] for p in parts) - observed_ref[d])) for d in range(days)]
     for f in range(frames):
         v = head_ref[f]
         for d in range(days):
@@ -489,17 +476,17 @@
     copy.wait()
 
 
-def make_correct(mine, theirs, observed, mask, head, day, out):
+def make_correct(parts, observed, mask, head, day, out):
     frames, rows, _ = head.shape
     return call(
-        correct_kernel,
+        functools.partial(correct_kernel, len(parts)),
         "correct",
         (shape_of(out.shape, BF),),
-        [VMEM] * 6 + [ANYWHERE],
+        [VMEM] * (len(parts) + 4) + [ANYWHERE],
         [pltpu.VMEM((frames, 1, rows, LANES), BF), pltpu.SemaphoreType.DMA],
-        alias={6: 0},
+        alias={len(parts) + 4: 0},
         out_specs=(ANYWHERE,),
-    )(mine, theirs, observed, mask, head, day, out)[0]
+    )(*parts, observed, mask, head, day, out)[0]
 
 
 def swapped(value, axis, start):
@@ -515,6 +502,21 @@
                 to[other] ^= 1
             pairs.append((t * sizes["space"] + s, to["tm"] * sizes["space"] + to["space"]))
     return lax.ppermute(value, ("tm", "space"), pairs)
+
+
+def totals_of(mine):
+    count = lax.axis_size("tm")
+
+    def partner(value, bits):
+        return lax.ppermute(value, "tm", [(i, i ^ bits) for i in range(count)])
+
+    if count & (count - 1):
+        return [lax.psum(mine, "tm")]
+    far = count // 2
+    while far > 2:
+        mine = mine + partner(mine, far)
+        far //= 2
+    return [partner(mine, bits) for bits in (2, 3, 1) if bits < count] + [mine]
 
 
 def body(
@@ -538,17 +540,9 @@
     t3, mine = make_side(
         wide, west, east, first, second, s1, s2, head, c1, c2, c3, state, days, observed.shape[0]
     )
-    score, side = make_early(wide, t3, m3, s3, EARLY)
-    out, first = make_update(wide, m3, score, side, c3, state, noise)
-    count = lax.axis_size("tm")
-    reach = 1
-    while True:
-        theirs = lax.ppermute(mine, "tm", [(i, i ^ reach) for i in range(count)])
-        reach *= 2
-        if reach >= count:
-            break
-        mine = mine + theirs
-    out = make_correct(mine, theirs, observed[:, 0], obs_mask[0], first, days, out)
+    out, head0 = make_update(wide, t3, m3, s3, c3, state, noise)
+    parts = totals_of(mine)
+    out = make_correct(parts, observed[:, 0], obs_mask[0], head0, days, out)
     return out[:, :, None]
 
 

time: 21.7 us -> 21.8 us (level); the launches traced: 21.6 us -> 21.4 us
  waiting for transfers between devices: 1.35 us -> 0.64 us
  starting transfers between devices: 6.75 us -> 7.41 us
    pallas_call x2 -> x1, Pallas kernels: 1.4 us -> 0.63 us  [make_correct(): call(functools.partial(correct_kernel, len(parts)), 'correct', (shape_of(...]
    ppermute x2 -> x3, waiting for transfers between devices: 0.74 us -> 0.01 us  [partner(): return lax.ppermute(value, 'tm', [(i, i ^ bits) for i in range(count)])]
    ppermute x2 -> x3, starting transfers between devices: 1.54 us -> 2.21 us  [partner(): return lax.ppermute(value, 'tm', [(i, i ^ bits) for i in range(count)])]
    pallas_call x1, Pallas kernels: 2.02 us -> 2.62 us  [make_update(): call(update_kernel, 'update', (shape_of(state.shape, BF), shape_of((frame...]
  transfers between devices with their start and end apart: 6 -> 7, of which waited for: 2 -> 1; matrix products, arithmetic and copies ran while one was open for 0% -> 0% of each run, Pallas kernels for 40% -> 40%
where the time goes in v9:
time: 21.8 us; the launch traced here: 21.4 us
  Pallas kernels  12.2 us (56%)
  starting transfers between devices  7.41 us (34%)
  local copies, waits for them, and re-layouts  0.97 us (4%)
  waiting for transfers between devices  0.64 us (3%)
    ppermute x4, starting transfers between devices, swapped(): return lax.ppermute(value, ('tm', 'space'), pairs)  5.21 us
    pallas_call x1, Pallas kernels, make_main(): call(main_kernel, 'main', (shape_of((frames + 2, rows2, wide), BF),), [VM...  4.19 us
    pallas_call x1, Pallas kernels, make_side(): call(side_kernel, 'side', (shape_of((frames + 2, 3 * hid, 2 * LANES), BF)...  2.65 us
    pallas_call x1, Pallas kernels, make_update(): call(update_kernel, 'update', (shape_of(state.shape, BF), shape_of((frame...  2.62 us
    ppermute x3, starting transfers between devices, partner(): return lax.ppermute(value, 'tm', [(i, i ^ bits) for i in range(count)])  2.21 us
    unnamed x24, local copies, waits for them, and re-layouts  0.97 us
    pallas_call x1, Pallas kernels, make_inner(): call(inner_kernel, 'inner', (shape_of((frames, 3 * chans, wide), BF), sha...  0.88 us
    pallas_call x1, Pallas kernels, make_weights(): call(weights_kernel, 'weights', (shape_of((2 * hid, 4 * 9 * chans), BF),...  0.88 us
  transfers between devices with their start and end apart: 7, of which 1 were waited for; matrix products, arithmetic and copies ran while one was open for 0% of the time, Pallas kernels for 40%

profile of v9, /device:TPU:0, one launch (start us, length us, event | category | flops | bytes accessed | tf_op | source)
XLA Modules:
  0.0 21.4 jit_solution(6737228505683690762)
XLA Ops:
  0.0 0.9 %copy-done = bf16[6,16,1,8,128]{4,3,2,1,0:T(8,128)(2,1)S(1)} copy-done((bf16[6,16,1,8,128]{4,3,2,1,0:T(8,128)(2,1)S(1)}, bf16[6,16,1,8,128]{4,3,2,1,0:T(8,128)(2,1)}, u32[]{:S(2)}) %copy-start) | copy-done | bytes 196632
  0.9 0.0 copy-start.4
  0.9 0.0 copy-start.6
  1.0 0.0 copy-start.7
  1.0 0.1 rows.1
  1.1 3.0 %collective-permute-start = (bf16[3,16,1024]{2,1,0:T(8,128)(2,1)S(1)}, bf16[3,16,1024]{2,1,0:T(8,128)(2,1)S(1)}, u32[]{:S(2)}, u32[]{:S(2)}) collective-permute-start(bf16[3,16,1024]{2,1,0:T(8,128)(2,1)S(1)} %get-tuple-element.36), channel_id=1, source_target_pairs={{0,1},{1,0},{2,3},{3,2},{4,5},{5,4},{6,7},{7,6},{8,16},{9,17},{10,... | collective-permute-start | bytes 294920 | tf_op jit(solution)/shard_map/ppermute | solution.py:504
  4.1 0.1 collective-permute-start.1
  4.2 0.0 copy-done.11
  4.2 0.0 copy-done.8
  4.2 0.0 copy-done.9
  4.2 0.0 copy-done.10
  4.2 0.1 pad_maximum_fusion
  4.3 0.9 %weights.1 = (bf16[128,576]{1,0:T(8,128)(2,1)S(1)}, bf16[128,2304]{1,0:T(8,128)(2,1)S(1)}, bf16[96,4608]{1,0:T(8,128)(2,1)S(1)}, bf16[384,192]{1,0:T(8,128)(2,1)...) custom-call(bf16[432,64]{1,0:T(8,128)(2,1)S(1)} %bitcast.25, ...), custom_call_target="tpu_custom_call" | custom-call | flops 1000000000 | bytes 1000000 | tf_op jit(solution)/shard_map/weights/pallas_call | solution.py:134
  5.2 0.9 %inner.1 = (bf16[6,48,1280]{2,1,0:T(8,128)(2,1)S(1)}, bf16[4,192,1280]{2,1,0:T(8,128)(2,1)S(1)}, bf16[6,16,128]{2,1,0:T(8,128)(2,1)S(1)}, bf16[6,16,128]{2,1,0:T(8,128)(2,1)S(1)}) custom-call(bf16[6,16,1024]{2,1,0:T(8,128)(2,1)S(1)} %get-tuple-element.31.own_ref, bf16[128,576]{1,0:T(8,128)(2,1)S(1)} %get-tuple-element.32.m1_ref, ...), custom_call_target="tpu_custom_call" | custom-call | flops 1000000000 | bytes 1000000 | tf_op jit(solution)/shard_map/inner/pallas_call | solution.py:271
  6.1 0.6 %collective-permute-done.far_ref = bf16[3,16,1024]{2,1,0:T(8,128)(2,1)S(1)} collective-permute-done((bf16[3,16,1024]{2,1,0:T(8,128)(2,1)S(1)}, bf16[3,16,1024]{2,1,0:T(8,128)(2,1)S(1)}, u32[]{:S(2)}, u32[]{:S(2)}) %collective-permute-start) | collective-permute-done | bytes 98336 | tf_op jit(solution)/shard_map/ppermute | solution.py:504
  6.7 0.0 collective-permute-done.1.near_ref
  6.7 0.2 edges.1
  6.9 2.1 %collective-permute-start.2 = (bf16[12,16,128]{2,1,0:T(8,128)(2,1)S(1)}, bf16[12,16,128]{2,1,0:T(8,128)(2,1)S(1)}, u32[]{:S(2)}, u32[]{:S(2)}) collective-permute-start(bf16[12,16,128]{2,1,0:T(8,128)(2,1)S(1)} %get-tuple-element.44), channel_id=1, source_target_pairs={{0,1},{1,0},{2,3},{3,2},{4,5},{5,4},{6,7},{7,6},{8,9},{9,8},{10,11... | collective-permute-start | bytes 147464 | tf_op jit(solution)/shard_map/ppermute | solution.py:504
  9.0 0.0 collective-permute-start.3
  9.0 4.2 %main.1.wide_ref = bf16[8,192,1280]{2,1,0:T(8,128)(2,1)S(1)} custom-call(bf16[6,48,1280]{2,1,0:T(8,128)(2,1)S(1)} %get-tuple-element.34.own1, bf16[4,192,1280]{2,1,0:T(8,128)(2,1)S(1)} %get-tuple-element.35.own2, bf16[3,16,1024]{2,1,0:T(8,128)(2,1)S(1)} %collective-permute-done.far_ref, bf16[3,16,1024]{2,1,0:T(8,128)(2,1)S(1)} %collective-permute-done.1.near_ref, ...), custom_call_target="tpu_custom_call" | custom-call | flops 5000000000 | bytes 1000000 | tf_op jit(solution)/shard_map/main/pallas_call | solution.py:300
  13.2 0.0 copy-start.5
  13.2 0.0 collective-permute-done.2.first_ref
  13.2 0.0 collective-permute-done.3.second_ref
  13.2 2.6 %side.1 = (bf16[8,192,256]{2,1,0:T(8,128)(2,1)S(1)}, f32[2,8,128]{2,1,0:T(8,128)S(1)}) custom-call(bf16[8,192,1280]{2,1,0:T(8,128)(2,1)S(1)} %main.1.wide_ref, bf16[12,16,128]{2,1,0:T(8,128)(2,1)S(1)} %get-tuple-element.42.west_ref, bf16[12,16,128]{2,1,0:T(8,128)(2,1)S(1)} %get-tuple-element.43.east_ref, ...), custom_call_target="tpu_custom_call" | custom-call | tf_op jit(solution)/shard_map/side/pallas_call | solution.py:403
  15.9 1.0 %collective-permute-start.4 = (f32[2,8,128]{2,1,0:T(8,128)S(1)}, f32[2,8,128]{2,1,0:T(8,128)S(1)}, u32[]{:S(2)}, u32[]{:S(2)}) collective-permute-start(f32[2,8,128]{2,1,0:T(8,128)S(1)} %get-tuple-element.51.refs_3_), channel_id=1, source_target_pairs={{0,16},{8,24},{16,0},{24,8},{1,17},{9,25},{17,1},{25,9},{2,18},{10... | collective-permute-start | bytes 24584 | tf_op jit(solution)/shard_map/ppermute | solution.py:511
  16.9 0.9 %collective-permute-start.5 = (f32[2,8,128]{2,1,0:T(8,128)S(1)}, f32[2,8,128]{2,1,0:T(8,128)S(1)}, u32[]{:S(2)}, u32[]{:S(2)}) collective-permute-start(f32[2,8,128]{2,1,0:T(8,128)S(1)} %get-tuple-element.51.refs_3_), channel_id=1, source_target_pairs={{0,24},{8,16},{16,8},{24,0},{1,25},{9,17},{17,9},{25,1},{2,26},{10... | collective-permute-start | bytes 24584 | tf_op jit(solution)/shard_map/ppermute | solution.py:511
  17.8 0.3 %collective-permute-start.6 = (f32[2,8,128]{2,1,0:T(8,128)S(1)}, f32[2,8,128]{2,1,0:T(8,128)S(1)}, u32[]{:S(2)}, u32[]{:S(2)}) collective-permute-start(f32[2,8,128]{2,1,0:T(8,128)S(1)} %get-tuple-element.51.refs_3_), channel_id=1, source_target_pairs={{0,8},{8,0},{16,24},{24,16},{1,9},{9,1},{17,25},{25,17},{2,10},{10... | collective-permute-start | bytes 24584 | tf_op jit(solution)/shard_map/ppermute | solution.py:511
  18.1 2.6 %update.1 = (bf16[6,16,8,128]{3,2,1,0:T(8,128)(2,1)}, f32[6,8,128]{2,1,0:T(8,128)S(1)}) custom-call(bf16[8,192,1280]{2,1,0:T(8,128)(2,1)S(1)} %main.1.wide_ref, bf16[8,192,256]{2,1,0:T(8,128)(2,1)S(1)} %get-tuple-element.52.t3, bf16[96,4608]{1,0:T(8,128)(2,1)S(1)} %get-tuple-element.53.m3_ref, bf16[288,1536]{1,0:T(8,128)(2,1)S(1)} %get-tuple-element.54.s3_ref, ...), custom_call_target="tpu_custom_call" | custom-call | flops 3000000000 | bytes 1000000 | tf_op jit(solution)/shard_map/update/pallas_call | solution.py:448
  20.7 0.0 collective-permute-done.4.refs_0_
  20.7 0.0 collective-permute-done.5.refs_1_
  20.7 0.0 collective-permute-done.6.refs_2_
  20.8 0.6 %correct.1 = bf16[6,16,8,128]{3,2,1,0:T(8,128)(2,1)} custom-call(f32[2,8,128]{2,1,0:T(8,128)S(1)} %collective-permute-done.4.refs_0_, f32[2,8,128]{2,1,0:T(8,128)S(1)} %collective-permute-done.5.refs_1_, f32[2,8,128]{2,1,0:T(8,128)S(1)} %collective-permute-done.6.refs_2_, ...), custom_call_target="tpu_custom_call", output_to_operand_aliasing={{}: (8, {})} | custom-call | tf_op jit(solution)/shard_map/correct/pallas_call | solution.py:481
  (16 shorter events, 0.0 us)
Async XLA Ops:
  0.0 0.9 %copy-start = (bf16[6,16,1,8,128]{4,3,2,1,0:T(8,128)(2,1)S(1)}, bf16[6,16,1,8,128]{4,3,2,1,0:T(8,128)(2,1)}, u32[]{:S(2)}) copy-start(bf16[6,16,1,8,128]{4,3,2,1,0:T(8,128)(2,1)} %param.11) | copy-start | bytes 589828
  0.9 3.3 %copy-start.11 = (s32[6]{0:T(128)S(1)}, s32[6]{0:T(128)}, u32[]{:S(2)}) copy-start(s32[6]{0:T(128)} %param.19) | copy-start | bytes 76
  0.9 3.3 %copy-start.8 = (f32[16]{0:T(128)S(1)}, f32[16]{0:T(128)}, u32[]{:S(2)}) copy-start(f32[16]{0:T(128)} %param.18) | copy-start | bytes 196
  0.9 3.3 %copy-start.9 = (f32[64]{0:T(128)S(1)}, f32[64]{0:T(128)}, u32[]{:S(2)}) copy-start(f32[64]{0:T(128)} %param.16) | copy-start | bytes 772
  0.9 3.3 %copy-start.10 = (f32[64]{0:T(128)S(1)}, f32[64]{0:T(128)}, u32[]{:S(2)}) copy-start(f32[64]{0:T(128)} %param.14) | copy-start | bytes 772
  0.9 3.4 %copy-start.4 = (bf16[64,64,3,3,3]{1,0,4,3,2:T(8,128)(2,1)S(1)}, bf16[64,64,3,3,3]{1,0,4,3,2:T(8,128)(2,1)}, u32[]{:S(2)}) copy-start(bf16[64,64,3,3,3]{1,0,4,3,2:T(8,128)(2,1)} %param.15) | copy-start | bytes 663556
  0.9 3.4 %copy-start.6 = (bf16[64,16,3,3,3]{0,1,4,3,2:T(8,128)(2,1)S(1)}, bf16[64,16,3,3,3]{0,1,4,3,2:T(8,128)(2,1)}, u32[]{:S(2)}) copy-start(bf16[64,16,3,3,3]{0,1,4,3,2:T(8,128)(2,1)} %param.13) | copy-start | bytes 165892
  1.0 3.4 %copy-start.7 = (bf16[16,64,3,3,3]{1,0,4,3,2:T(8,128)(2,1)S(1)}, bf16[16,64,3,3,3]{1,0,4,3,2:T(8,128)(2,1)}, u32[]{:S(2)}) copy-start(bf16[16,64,3,3,3]{1,0,4,3,2:T(8,128)(2,1)} %param.17) | copy-start | bytes 165892
  1.1 5.6 %collective-permute-start = (bf16[3,16,1024]{2,1,0:T(8,128)(2,1)S(1)}, bf16[3,16,1024]{2,1,0:T(8,128)(2,1)S(1)}, u32[]{:S(2)}, u32[]{:S(2)}) collective-permute-start(bf16[3,16,1024]{2,1,0:T(8,128)(2,1)S(1)} %get-tuple-element.36), channel_id=1, source_target_pairs={{0,1},{1,0},{2,3},{3,2},{4,5},{5,4},{6,7},{7,6},{8,16},{9,17},{10,... | collective-permute-start | bytes 294920 | tf_op jit(solution)/shard_map/ppermute | solution.py:504
  4.1 2.6 %collective-permute-start.1 = (bf16[3,16,1024]{2,1,0:T(8,128)(2,1)S(1)}, bf16[3,16,1024]{2,1,0:T(8,128)(2,1)S(1)}, u32[]{:S(2)}, u32[]{:S(2)}) collective-permute-start(bf16[3,16,1024]{2,1,0:T(8,128)(2,1)S(1)} %get-tuple-element.37), channel_id=1, source_target_pairs={{0,8},{1,9},{2,10},{3,11},{4,12},{5,13},{6,14},{7,15},{8,0},{9,1},... | collective-permute-start | bytes 294920 | tf_op jit(solution)/shard_map/ppermute | solution.py:504
  6.9 6.3 %collective-permute-start.2 = (bf16[12,16,128]{2,1,0:T(8,128)(2,1)S(1)}, bf16[12,16,128]{2,1,0:T(8,128)(2,1)S(1)}, u32[]{:S(2)}, u32[]{:S(2)}) collective-permute-start(bf16[12,16,128]{2,1,0:T(8,128)(2,1)S(1)} %get-tuple-element.44), channel_id=1, source_target_pairs={{0,1},{1,0},{2,3},{3,2},{4,5},{5,4},{6,7},{7,6},{8,9},{9,8},{10,11... | collective-permute-start | bytes 147464 | tf_op jit(solution)/shard_map/ppermute | solution.py:504
  9.0 4.2 %collective-permute-start.3 = (bf16[12,16,128]{2,1,0:T(8,128)(2,1)S(1)}, bf16[12,16,128]{2,1,0:T(8,128)(2,1)S(1)}, u32[]{:S(2)}, u32[]{:S(2)}) collective-permute-start(bf16[12,16,128]{2,1,0:T(8,128)(2,1)S(1)} %get-tuple-element.45), channel_id=1, source_target_pairs={{0,8},{1,2},{2,1},{3,4},{4,3},{5,6},{6,5},{7,15},{8,0},{9,10},{10,... | collective-permute-start | bytes 147464 | tf_op jit(solution)/shard_map/ppermute | solution.py:504
  9.0 4.2 %copy-start.1 = (bf16[6,16,1,8,128]{4,3,2,1,0:T(8,128)(2,1)S(1)}, bf16[6,16,1,8,128]{4,3,2,1,0:T(8,128)(2,1)}, u32[]{:S(2)}) copy-start(bf16[6,16,1,8,128]{4,3,2,1,0:T(8,128)(2,1)} %param.11) | copy-start | bytes 589828
  13.2 4.9 %copy-start.5 = (bf16[6,16,1,8,128]{4,3,2,1,0:T(8,128)(2,1)S(1)}, bf16[6,16,1,8,128]{4,3,2,1,0:T(8,128)(2,1)}, u32[]{:S(2)}) copy-start(bf16[6,16,1,8,128]{4,3,2,1,0:T(8,128)(2,1)} %param.12) | copy-start | bytes 589828
  15.9 4.8 %collective-permute-start.4 = (f32[2,8,128]{2,1,0:T(8,128)S(1)}, f32[2,8,128]{2,1,0:T(8,128)S(1)}, u32[]{:S(2)}, u32[]{:S(2)}) collective-permute-start(f32[2,8,128]{2,1,0:T(8,128)S(1)} %get-tuple-element.51.refs_3_), channel_id=1, source_target_pairs={{0,16},{8,24},{16,0},{24,8},{1,17},{9,25},{17,1},{25,9},{2,18},{10... | collective-permute-start | bytes 24584 | tf_op jit(solution)/shard_map/ppermute | solution.py:511
  16.9 3.9 %collective-permute-start.5 = (f32[2,8,128]{2,1,0:T(8,128)S(1)}, f32[2,8,128]{2,1,0:T(8,128)S(1)}, u32[]{:S(2)}, u32[]{:S(2)}) collective-permute-start(f32[2,8,128]{2,1,0:T(8,128)S(1)} %get-tuple-element.51.refs_3_), channel_id=1, source_target_pairs={{0,24},{8,16},{16,8},{24,0},{1,25},{9,17},{17,9},{25,1},{2,26},{10... | collective-permute-start | bytes 24584 | tf_op jit(solution)/shard_map/ppermute | solution.py:511
  17.8 2.9 %collective-permute-start.6 = (f32[2,8,128]{2,1,0:T(8,128)S(1)}, f32[2,8,128]{2,1,0:T(8,128)S(1)}, u32[]{:S(2)}, u32[]{:S(2)}) collective-permute-start(f32[2,8,128]{2,1,0:T(8,128)S(1)} %get-tuple-element.51.refs_3_), channel_id=1, source_target_pairs={{0,8},{8,0},{16,24},{24,16},{1,9},{9,1},{17,25},{25,17},{2,10},{10... | collective-permute-start | bytes 24584 | tf_op jit(solution)/shard_map/ppermute | solution.py:511
  18.1 2.6 %copy-start.2 = (f32[2,1,8,128]{3,2,1,0:T(8,128)S(1)}, f32[2,1,8,128]{3,2,1,0:T(8,128)}, u32[]{:S(2)}) copy-start(f32[2,1,8,128]{3,2,1,0:T(8,128)} %param.20) | copy-start | bytes 24580
  18.1 2.6 %copy-start.3 = (s32[1,8,128]{2,1,0:T(8,128)S(1)}, s32[1,8,128]{2,1,0:T(8,128)}, u32[]{:S(2)}) copy-start(s32[1,8,128]{2,1,0:T(8,128)} %param.21) | copy-start | bytes 12292

commit v10 on v9

--- a/solution.py
+++ b/solution.py
@@ -420,7 +420,7 @@
 
 
 def update_kernel(
-    wide_ref, t3, m3_ref, s3_ref, c3_ref, state_ref, noise_ref, out_ref, head_ref, rest, side, scr
+    wide_ref, t3, m3_ref, s3_ref, c3_ref, state_ref, noise_ref, out_ref, head_ref, side, scr
 ):
     frames, fields, rows, _ = state_ref.shape
     z = jnp.concatenate([t3[j] for j in range(frames + 2)], axis=0)
@@ -429,14 +429,15 @@
         both = over_rows(acc, f * 3 * fields, fields)
         for half in range(2):
             side[half, f * fields : (f + 1) * fields] = both[:, tile(half)]
+    bias = c3_ref[...]
     for y in range(0, rows, 2):
-        rest[y], rest[y + 1] = own_score(wide_ref, m3_ref, frames, y)
-    bias = c3_ref[...]
+        both = own_score(wide_ref, m3_ref, frames, y)
+        for f in range(frames):
+            at = slice(f * fields, (f + 1) * fields)
+            west, east = side[0, at], side[1, at]
+            for i in range(2):
+                scr[f, pl.ds(y + i, fields, stride=rows), :] = patched(both[i][at], west, east, y + i) + bias
     for f in range(frames):
-        at = slice(f * fields, (f + 1) * fields)
-        west, east = side[0, at], side[1, at]
-        for y in range(rows):
-            scr[f, pl.ds(y, fields, stride=rows), :] = patched(rest[y, at], west, east, y) + bias
         score = scr[f].reshape(fields, rows, LANES)
         moved = state_ref[f].astype(F32) + 0.8 * score + 0.5 * noise_ref[f].astype(F32)
         out_ref[f] = moved.astype(BF)
@@ -451,7 +452,6 @@
         (shape_of(state.shape, BF), shape_of((frames, rows, LANES), F32)),
         [VMEM] * 7,
         [
-            pltpu.VMEM((rows, frames * fields, LANES), F32),
             pltpu.VMEM((2, frames * fields, LANES), F32),
             pltpu.VMEM((frames, fields * rows, LANES), F32),
         ],
@@ -461,8 +461,10 @@
 
 def correct_kernel(count, *refs):
     parts = refs[:count]
-    observed_ref, mask_ref, head_ref, day_ref, _, out_ref, buf, sem = refs[count:]
+    observed_ref, mask_ref, head_ref, day_ref, body_ref, out_ref, buf, sems = refs[count:]
     frames = head_ref.shape[0]
+    others = pltpu.make_async_copy(body_ref.at[:, 1:], out_ref.at[:, 1:], sems.at[0])
+    others.start()
     days = observed_ref.shape[0]
     mask = mask_ref[...].astype(F32)
     misfit = [0.15 * (mask * (sum(p[d] for p in parts) - observed_ref[d])) for d in range(days)]
@@ -471,9 +473,10 @@
         for d in range(days):
             v = v - jnp.where(day_ref[f : f + 1] == d, misfit[d], 0.0)
         buf[f, 0] = v.astype(BF)
-    copy = pltpu.make_async_copy(buf, out_ref.at[:, 0:1], sem)
-    copy.start()
-    copy.wait()
+    first = pltpu.make_async_copy(buf, out_ref.at[:, 0:1], sems.at[1])
+    first.start()
+    others.wait()
+    first.wait()
 
 
 def make_correct(parts, observed, mask, head, day, out):
@@ -482,9 +485,8 @@
         functools.partial(correct_kernel, len(parts)),
         "correct",
         (shape_of(out.shape, BF),),
-        [VMEM] * (len(parts) + 4) + [ANYWHERE],
-        [pltpu.VMEM((frames, 1, rows, LANES), BF), pltpu.SemaphoreType.DMA],
-        alias={len(parts) + 4: 0},
+        [VMEM] * (len(parts) + 5),
+        [pltpu.VMEM((frames, 1, rows, LANES), BF), pltpu.SemaphoreType.DMA((2,))],
         out_specs=(ANYWHERE,),
     )(*parts, observed, mask, head, day, out)[0]
 

time: 21.8 us -> 21.2 us (0.972)
  Pallas kernels: 12.2 us -> 11.6 us
    pallas_call x1, Pallas kernels: 2.62 us -> 1.95 us  [make_update(): call(update_kernel, 'update', (shape_of(state.shape, BF), shape_of((frame...]
  transfers between devices with their start and end apart: 7 -> 7, of which waited for: 1 -> 1; matrix products, arithmetic and copies ran while one was open for 0% -> 0% of each run, Pallas kernels for 40% -> 38%
where the time goes in v10:
time: 21.2 us; the launch traced here: 20.8 us
  Pallas kernels  11.6 us (55%)
  starting transfers between devices  7.41 us (35%)
  local copies, waits for them, and re-layouts  0.97 us (5%)
  waiting for transfers between devices  0.63 us (3%)
    ppermute x4, starting transfers between devices, swapped(): return lax.ppermute(value, ('tm', 'space'), pairs)  5.21 us
    pallas_call x1, Pallas kernels, make_main(): call(main_kernel, 'main', (shape_of((frames + 2, rows2, wide), BF),), [VM...  4.19 us
    pallas_call x1, Pallas kernels, make_side(): call(side_kernel, 'side', (shape_of((frames + 2, 3 * hid, 2 * LANES), BF)...  2.67 us
    ppermute x3, starting transfers between devices, partner(): return lax.ppermute(value, 'tm', [(i, i ^ bits) for i in range(count)])  2.21 us
    pallas_call x1, Pallas kernels, make_update(): call(update_kernel, 'update', (shape_of(state.shape, BF), shape_of((frame...  1.95 us
    unnamed x24, local copies, waits for them, and re-layouts  0.97 us
    pallas_call x1, Pallas kernels, make_inner(): call(inner_kernel, 'inner', (shape_of((frames, 3 * chans, wide), BF), sha...  0.89 us
    pallas_call x1, Pallas kernels, make_weights(): call(weights_kernel, 'weights', (shape_of((2 * hid, 4 * 9 * chans), BF),...  0.88 us
  transfers between devices with their start and end apart: 7, of which 1 were waited for; matrix products, arithmetic and copies ran while one was open for 0% of the time, Pallas kernels for 38%

profile of v10, /device:TPU:0, one launch (start us, length us, event | category | flops | bytes accessed | tf_op | source)
XLA Modules:
  0.0 20.8 jit_solution(9105482371297505776)
XLA Ops:
  0.0 0.9 %copy-done = bf16[6,16,1,8,128]{4,3,2,1,0:T(8,128)(2,1)S(1)} copy-done((bf16[6,16,1,8,128]{4,3,2,1,0:T(8,128)(2,1)S(1)}, bf16[6,16,1,8,128]{4,3,2,1,0:T(8,128)(2,1)}, u32[]{:S(2)}) %copy-start) | copy-done | bytes 196632
  0.9 0.0 copy-start.4
  0.9 0.0 copy-start.6
  1.0 0.0 copy-start.7
  1.0 0.1 rows.1
  1.1 3.0 %collective-permute-start = (bf16[3,16,1024]{2,1,0:T(8,128)(2,1)S(1)}, bf16[3,16,1024]{2,1,0:T(8,128)(2,1)S(1)}, u32[]{:S(2)}, u32[]{:S(2)}) collective-permute-start(bf16[3,16,1024]{2,1,0:T(8,128)(2,1)S(1)} %get-tuple-element.36), channel_id=1, source_target_pairs={{0,1},{1,0},{2,3},{3,2},{4,5},{5,4},{6,7},{7,6},{8,16},{9,17},{10,... | collective-permute-start | bytes 294920 | tf_op jit(solution)/shard_map/ppermute | solution.py:506
  4.1 0.1 collective-permute-start.1
  4.2 0.0 copy-done.11
  4.2 0.0 copy-done.8
  4.2 0.0 copy-done.9
  4.2 0.0 copy-done.10
  4.2 0.1 pad_maximum_fusion
  4.3 0.9 %weights.1 = (bf16[128,576]{1,0:T(8,128)(2,1)S(1)}, bf16[128,2304]{1,0:T(8,128)(2,1)S(1)}, bf16[96,4608]{1,0:T(8,128)(2,1)S(1)}, bf16[384,192]{1,0:T(8,128)(2,1)...) custom-call(bf16[432,64]{1,0:T(8,128)(2,1)S(1)} %bitcast.25, ...), custom_call_target="tpu_custom_call" | custom-call | flops 1000000000 | bytes 1000000 | tf_op jit(solution)/shard_map/weights/pallas_call | solution.py:134
  5.2 0.9 %inner.1 = (bf16[6,48,1280]{2,1,0:T(8,128)(2,1)S(1)}, bf16[4,192,1280]{2,1,0:T(8,128)(2,1)S(1)}, bf16[6,16,128]{2,1,0:T(8,128)(2,1)S(1)}, bf16[6,16,128]{2,1,0:T(8,128)(2,1)S(1)}) custom-call(bf16[6,16,1024]{2,1,0:T(8,128)(2,1)S(1)} %get-tuple-element.31.own_ref, bf16[128,576]{1,0:T(8,128)(2,1)S(1)} %get-tuple-element.32.m1_ref, ...), custom_call_target="tpu_custom_call" | custom-call | flops 1000000000 | bytes 1000000 | tf_op jit(solution)/shard_map/inner/pallas_call | solution.py:271
  6.1 0.6 %collective-permute-done.far_ref = bf16[3,16,1024]{2,1,0:T(8,128)(2,1)S(1)} collective-permute-done((bf16[3,16,1024]{2,1,0:T(8,128)(2,1)S(1)}, bf16[3,16,1024]{2,1,0:T(8,128)(2,1)S(1)}, u32[]{:S(2)}, u32[]{:S(2)}) %collective-permute-start) | collective-permute-done | bytes 98336 | tf_op jit(solution)/shard_map/ppermute | solution.py:506
  6.7 0.0 collective-permute-done.1.near_ref
  6.7 0.2 edges.1
  6.9 2.1 %collective-permute-start.2 = (bf16[12,16,128]{2,1,0:T(8,128)(2,1)S(1)}, bf16[12,16,128]{2,1,0:T(8,128)(2,1)S(1)}, u32[]{:S(2)}, u32[]{:S(2)}) collective-permute-start(bf16[12,16,128]{2,1,0:T(8,128)(2,1)S(1)} %get-tuple-element.44), channel_id=1, source_target_pairs={{0,1},{1,0},{2,3},{3,2},{4,5},{5,4},{6,7},{7,6},{8,9},{9,8},{10,11... | collective-permute-start | bytes 147464 | tf_op jit(solution)/shard_map/ppermute | solution.py:506
  9.0 0.0 collective-permute-start.3
  9.0 4.2 %main.1.wide_ref = bf16[8,192,1280]{2,1,0:T(8,128)(2,1)S(1)} custom-call(bf16[6,48,1280]{2,1,0:T(8,128)(2,1)S(1)} %get-tuple-element.34.own1, bf16[4,192,1280]{2,1,0:T(8,128)(2,1)S(1)} %get-tuple-element.35.own2, bf16[3,16,1024]{2,1,0:T(8,128)(2,1)S(1)} %collective-permute-done.far_ref, bf16[3,16,1024]{2,1,0:T(8,128)(2,1)S(1)} %collective-permute-done.1.near_ref, ...), custom_call_target="tpu_custom_call" | custom-call | flops 5000000000 | bytes 1000000 | tf_op jit(solution)/shard_map/main/pallas_call | solution.py:300
  13.2 0.0 copy-start.5
  13.2 0.0 collective-permute-done.2.first_ref
  13.2 0.0 collective-permute-done.3.second_ref
  13.2 2.7 %side.1 = (bf16[8,192,256]{2,1,0:T(8,128)(2,1)S(1)}, f32[2,8,128]{2,1,0:T(8,128)S(1)}) custom-call(bf16[8,192,1280]{2,1,0:T(8,128)(2,1)S(1)} %main.1.wide_ref, bf16[12,16,128]{2,1,0:T(8,128)(2,1)S(1)} %get-tuple-element.42.west_ref, bf16[12,16,128]{2,1,0:T(8,128)(2,1)S(1)} %get-tuple-element.43.east_ref, ...), custom_call_target="tpu_custom_call" | custom-call | tf_op jit(solution)/shard_map/side/pallas_call | solution.py:403
  15.9 1.0 %collective-permute-start.4 = (f32[2,8,128]{2,1,0:T(8,128)S(1)}, f32[2,8,128]{2,1,0:T(8,128)S(1)}, u32[]{:S(2)}, u32[]{:S(2)}) collective-permute-start(f32[2,8,128]{2,1,0:T(8,128)S(1)} %get-tuple-element.51.refs_3_), channel_id=1, source_target_pairs={{0,16},{8,24},{16,0},{24,8},{1,17},{9,25},{17,1},{25,9},{2,18},{10... | collective-permute-start | bytes 24584 | tf_op jit(solution)/shard_map/ppermute | solution.py:513
  16.9 0.9 %collective-permute-start.5 = (f32[2,8,128]{2,1,0:T(8,128)S(1)}, f32[2,8,128]{2,1,0:T(8,128)S(1)}, u32[]{:S(2)}, u32[]{:S(2)}) collective-permute-start(f32[2,8,128]{2,1,0:T(8,128)S(1)} %get-tuple-element.51.refs_3_), channel_id=1, source_target_pairs={{0,24},{8,16},{16,8},{24,0},{1,25},{9,17},{17,9},{25,1},{2,26},{10... | collective-permute-start | bytes 24584 | tf_op jit(solution)/shard_map/ppermute | solution.py:513
  17.8 0.3 %collective-permute-start.6 = (f32[2,8,128]{2,1,0:T(8,128)S(1)}, f32[2,8,128]{2,1,0:T(8,128)S(1)}, u32[]{:S(2)}, u32[]{:S(2)}) collective-permute-start(f32[2,8,128]{2,1,0:T(8,128)S(1)} %get-tuple-element.51.refs_3_), channel_id=1, source_target_pairs={{0,8},{8,0},{16,24},{24,16},{1,9},{9,1},{17,25},{25,17},{2,10},{10... | collective-permute-start | bytes 24584 | tf_op jit(solution)/shard_map/ppermute | solution.py:513
  18.1 1.9 %update.1 = (bf16[6,16,8,128]{3,2,1,0:T(8,128)(2,1)S(1)}, f32[6,8,128]{2,1,0:T(8,128)S(1)}) custom-call(bf16[8,192,1280]{2,1,0:T(8,128)(2,1)S(1)} %main.1.wide_ref, bf16[8,192,256]{2,1,0:T(8,128)(2,1)S(1)} %get-tuple-element.52.t3, bf16[96,4608]{1,0:T(8,128)(2,1)S(1)} %get-tuple-element.53.m3_ref, bf16[288,1536]{1,0:T(8,128)(2,1)S(1)} %get-tuple-element.54.s3_ref, ...), custom_call_target="tpu_custom_call" | custom-call | flops 3000000000 | bytes 1000000 | tf_op jit(solution)/shard_map/update/pallas_call | solution.py:449
  20.1 0.0 collective-permute-done.4.refs_0_
  20.1 0.0 collective-permute-done.5.refs_1_
  20.1 0.0 collective-permute-done.6.refs_2_
  20.1 0.7 %correct.1 = bf16[6,16,8,128]{3,2,1,0:T(8,128)(2,1)} custom-call(f32[2,8,128]{2,1,0:T(8,128)S(1)} %collective-permute-done.4.refs_0_, f32[2,8,128]{2,1,0:T(8,128)S(1)} %collective-permute-done.5.refs_1_, f32[2,8,128]{2,1,0:T(8,128)S(1)} %collective-permute-done.6.refs_2_, f32[2,8,128]{2,1,0:T(8,128)S(1)} %get-tuple-element.51.refs_3_, ...), custom_call_target="tpu_custom_call" | custom-call | tf_op jit(solution)/shard_map/correct/pallas_call | solution.py:484
  (16 shorter events, 0.0 us)
Async XLA Ops:
  0.0 0.9 %copy-start = (bf16[6,16,1,8,128]{4,3,2,1,0:T(8,128)(2,1)S(1)}, bf16[6,16,1,8,128]{4,3,2,1,0:T(8,128)(2,1)}, u32[]{:S(2)}) copy-start(bf16[6,16,1,8,128]{4,3,2,1,0:T(8,128)(2,1)} %param.11) | copy-start | bytes 589828
  0.9 3.3 %copy-start.11 = (s32[6]{0:T(128)S(1)}, s32[6]{0:T(128)}, u32[]{:S(2)}) copy-start(s32[6]{0:T(128)} %param.19) | copy-start | bytes 76
  0.9 3.3 %copy-start.8 = (f32[16]{0:T(128)S(1)}, f32[16]{0:T(128)}, u32[]{:S(2)}) copy-start(f32[16]{0:T(128)} %param.18) | copy-start | bytes 196
  0.9 3.3 %copy-start.9 = (f32[64]{0:T(128)S(1)}, f32[64]{0:T(128)}, u32[]{:S(2)}) copy-start(f32[64]{0:T(128)} %param.16) | copy-start | bytes 772
  0.9 3.3 %copy-start.10 = (f32[64]{0:T(128)S(1)}, f32[64]{0:T(128)}, u32[]{:S(2)}) copy-start(f32[64]{0:T(128)} %param.14) | copy-start | bytes 772
  0.9 3.4 %copy-start.4 = (bf16[64,64,3,3,3]{1,0,4,3,2:T(8,128)(2,1)S(1)}, bf16[64,64,3,3,3]{1,0,4,3,2:T(8,128)(2,1)}, u32[]{:S(2)}) copy-start(bf16[64,64,3,3,3]{1,0,4,3,2:T(8,128)(2,1)} %param.15) | copy-start | bytes 663556
  0.9 3.4 %copy-start.6 = (bf16[64,16,3,3,3]{0,1,4,3,2:T(8,128)(2,1)S(1)}, bf16[64,16,3,3,3]{0,1,4,3,2:T(8,128)(2,1)}, u32[]{:S(2)}) copy-start(bf16[64,16,3,3,3]{0,1,4,3,2:T(8,128)(2,1)} %param.13) | copy-start | bytes 165892
  1.0 3.4 %copy-start.7 = (bf16[16,64,3,3,3]{1,0,4,3,2:T(8,128)(2,1)S(1)}, bf16[16,64,3,3,3]{1,0,4,3,2:T(8,128)(2,1)}, u32[]{:S(2)}) copy-start(bf16[16,64,3,3,3]{1,0,4,3,2:T(8,128)(2,1)} %param.17) | copy-start | bytes 165892
  1.1 5.6 %collective-permute-start = (bf16[3,16,1024]{2,1,0:T(8,128)(2,1)S(1)}, bf16[3,16,1024]{2,1,0:T(8,128)(2,1)S(1)}, u32[]{:S(2)}, u32[]{:S(2)}) collective-permute-start(bf16[3,16,1024]{2,1,0:T(8,128)(2,1)S(1)} %get-tuple-element.36), channel_id=1, source_target_pairs={{0,1},{1,0},{2,3},{3,2},{4,5},{5,4},{6,7},{7,6},{8,16},{9,17},{10,... | collective-permute-start | bytes 294920 | tf_op jit(solution)/shard_map/ppermute | solution.py:506
  4.1 2.6 %collective-permute-start.1 = (bf16[3,16,1024]{2,1,0:T(8,128)(2,1)S(1)}, bf16[3,16,1024]{2,1,0:T(8,128)(2,1)S(1)}, u32[]{:S(2)}, u32[]{:S(2)}) collective-permute-start(bf16[3,16,1024]{2,1,0:T(8,128)(2,1)S(1)} %get-tuple-element.37), channel_id=1, source_target_pairs={{0,8},{1,9},{2,10},{3,11},{4,12},{5,13},{6,14},{7,15},{8,0},{9,1},... | collective-permute-start | bytes 294920 | tf_op jit(solution)/shard_map/ppermute | solution.py:506
  6.9 6.3 %collective-permute-start.2 = (bf16[12,16,128]{2,1,0:T(8,128)(2,1)S(1)}, bf16[12,16,128]{2,1,0:T(8,128)(2,1)S(1)}, u32[]{:S(2)}, u32[]{:S(2)}) collective-permute-start(bf16[12,16,128]{2,1,0:T(8,128)(2,1)S(1)} %get-tuple-element.44), channel_id=1, source_target_pairs={{0,1},{1,0},{2,3},{3,2},{4,5},{5,4},{6,7},{7,6},{8,9},{9,8},{10,11... | collective-permute-start | bytes 147464 | tf_op jit(solution)/shard_map/ppermute | solution.py:506
  9.0 4.2 %collective-permute-start.3 = (bf16[12,16,128]{2,1,0:T(8,128)(2,1)S(1)}, bf16[12,16,128]{2,1,0:T(8,128)(2,1)S(1)}, u32[]{:S(2)}, u32[]{:S(2)}) collective-permute-start(bf16[12,16,128]{2,1,0:T(8,128)(2,1)S(1)} %get-tuple-element.45), channel_id=1, source_target_pairs={{0,8},{1,2},{2,1},{3,4},{4,3},{5,6},{6,5},{7,15},{8,0},{9,10},{10,... | collective-permute-start | bytes 147464 | tf_op jit(solution)/shard_map/ppermute | solution.py:506
  9.0 4.2 %copy-start.1 = (bf16[6,16,1,8,128]{4,3,2,1,0:T(8,128)(2,1)S(1)}, bf16[6,16,1,8,128]{4,3,2,1,0:T(8,128)(2,1)}, u32[]{:S(2)}) copy-start(bf16[6,16,1,8,128]{4,3,2,1,0:T(8,128)(2,1)} %param.11) | copy-start | bytes 589828
  13.2 4.9 %copy-start.5 = (bf16[6,16,1,8,128]{4,3,2,1,0:T(8,128)(2,1)S(1)}, bf16[6,16,1,8,128]{4,3,2,1,0:T(8,128)(2,1)}, u32[]{:S(2)}) copy-start(bf16[6,16,1,8,128]{4,3,2,1,0:T(8,128)(2,1)} %param.12) | copy-start | bytes 589828
  15.9 4.2 %collective-permute-start.4 = (f32[2,8,128]{2,1,0:T(8,128)S(1)}, f32[2,8,128]{2,1,0:T(8,128)S(1)}, u32[]{:S(2)}, u32[]{:S(2)}) collective-permute-start(f32[2,8,128]{2,1,0:T(8,128)S(1)} %get-tuple-element.51.refs_3_), channel_id=1, source_target_pairs={{0,16},{8,24},{16,0},{24,8},{1,17},{9,25},{17,1},{25,9},{2,18},{10... | collective-permute-start | bytes 24584 | tf_op jit(solution)/shard_map/ppermute | solution.py:513
  16.9 3.2 %collective-permute-start.5 = (f32[2,8,128]{2,1,0:T(8,128)S(1)}, f32[2,8,128]{2,1,0:T(8,128)S(1)}, u32[]{:S(2)}, u32[]{:S(2)}) collective-permute-start(f32[2,8,128]{2,1,0:T(8,128)S(1)} %get-tuple-element.51.refs_3_), channel_id=1, source_target_pairs={{0,24},{8,16},{16,8},{24,0},{1,25},{9,17},{17,9},{25,1},{2,26},{10... | collective-permute-start | bytes 24584 | tf_op jit(solution)/shard_map/ppermute | solution.py:513
  17.8 2.3 %collective-permute-start.6 = (f32[2,8,128]{2,1,0:T(8,128)S(1)}, f32[2,8,128]{2,1,0:T(8,128)S(1)}, u32[]{:S(2)}, u32[]{:S(2)}) collective-permute-start(f32[2,8,128]{2,1,0:T(8,128)S(1)} %get-tuple-element.51.refs_3_), channel_id=1, source_target_pairs={{0,8},{8,0},{16,24},{24,16},{1,9},{9,1},{17,25},{25,17},{2,10},{10... | collective-permute-start | bytes 24584 | tf_op jit(solution)/shard_map/ppermute | solution.py:513
  18.1 2.0 %copy-start.2 = (f32[2,1,8,128]{3,2,1,0:T(8,128)S(1)}, f32[2,1,8,128]{3,2,1,0:T(8,128)}, u32[]{:S(2)}) copy-start(f32[2,1,8,128]{3,2,1,0:T(8,128)} %param.20) | copy-start | bytes 24580
  18.1 2.0 %copy-start.3 = (s32[1,8,128]{2,1,0:T(8,128)S(1)}, s32[1,8,128]{2,1,0:T(8,128)}, u32[]{:S(2)}) copy-start(s32[1,8,128]{2,1,0:T(8,128)} %param.21) | copy-start | bytes 12292

commit v11 on v10

--- a/solution.py
+++ b/solution.py
@@ -220,6 +220,11 @@
     return lambda f: (ref, f)
 
 
+def split(own, far, count=None):
+    count = own.shape[0] if count is None else count
+    return lambda f: (own, f - DEPTH) if DEPTH <= f < DEPTH + count else (far, f if f < DEPTH else f - count)
+
+
 def in_trajectory(local, frames):
     step = lax.axis_index("tm") * frames + local
     return (step >= 0) & (step < frames * lax.axis_size("tm"))
@@ -252,29 +257,36 @@
     return groups + [(frames[-1], 1)] * (len(frames) % 2)
 
 
-def inner_kernel(own_ref, m1_ref, c1_ref, s1, s2, west_ref, east_ref):
+def inner_kernel(own_ref, m1_ref, m2_ref, c1_ref, c2_ref, s1, s2, s3, west_ref, east_ref):
     frames = own_ref.shape[0]
     rows = own_ref.shape[2] // LANES
     each = [(f, y, own_ref[f, :, tile(y)]) for f in range(frames) for y in range(rows)]
-    blank_ends(s1, s2)
+    blank_ends(s1, s2, s3)
     for f, y, v in each:
         spread(s1, f, y, v)
     for f, west, east in strips(each, rows):
         west_ref[f], east_ref[f] = west, east
     layer(plain(s1), plain(s2), m1_ref, c1_ref, pairs_of(range(frames - 2)), rows, lambda f: None)
-
-
-def make_inner(own, m1, c1):
+    layer(plain(s2), plain(s3), m2_ref, c2_ref, pairs_of(range(frames - 4)), rows, lambda f: None)
+
+
+def make_inner(own, m1, m2, c1, c2):
     frames, chans, width = own.shape
     hid, wide = c1.shape[0], width + 2 * LANES
     strip = shape_of((frames, chans, LANES), BF)
     return call(
         inner_kernel,
         "inner",
-        (shape_of((frames, 3 * chans, wide), BF), shape_of((frames - 2, 3 * hid, wide), BF), strip, strip),
-        [VMEM] * 3,
-        cost=1_000_000_000,
-    )(own, m1, c1)
+        (
+            shape_of((frames, 3 * chans, wide), BF),
+            shape_of((frames - 2, 3 * hid, wide), BF),
+            shape_of((frames - 4, 3 * hid, wide), BF),
+            strip,
+            strip,
+        ),
+        [VMEM] * 5,
+        cost=1_500_000_000,
+    )(own, m1, m2, c1, c2)
 
 
 def main_kernel(own1, own2, far_ref, near_ref, m1_ref, m2_ref, c1_ref, c2_ref, s3, far1, far2):
@@ -284,14 +296,11 @@
     for f, y, v in beside(near_ref, far_ref):
         spread(far1, f, y, v)
 
-    def split(own, far, edge):
-        count = own.shape[0]
-        return lambda f: (own, f - edge) if edge <= f < edge + count else (far, f if f < edge else f - count)
-
-    one, two = split(own1, far1, DEPTH), split(own2, far2, DEPTH)
+    one, two, three = split(own1, far1), split(own2, far2), split(None, s3, frames - 4)
     groups = pairs_of(range(DEPTH)) + pairs_of(range(frames + 1, frames + 4))
     layer(one, two, m1_ref, c1_ref, groups, rows, lambda f: in_trajectory(f - 2, frames))
-    layer(two, plain(s3), m2_ref, c2_ref, pairs_of(range(frames + 2)), rows, lambda f: in_trajectory(f - 1, frames))
+    groups = pairs_of(range(DEPTH)) + pairs_of(range(frames - 1, frames + 2))
+    layer(two, three, m2_ref, c2_ref, groups, rows, lambda f: in_trajectory(f - 1, frames))
 
 
 def make_main(own1, own2, near, far, m1, m2, c1, c2):
@@ -300,7 +309,7 @@
     return call(
         main_kernel,
         "main",
-        (shape_of((frames + 2, rows2, wide), BF),),
+        (shape_of((2 * DEPTH, rows2, wide), BF),),
         [VMEM] * 8,
         [pltpu.VMEM((2 * DEPTH, rows1, wide), BF), pltpu.VMEM((2 * DEPTH, rows2, wide), BF)],
         cost=5_000_000_000,
@@ -338,7 +347,7 @@
 
 
 def side_kernel(
-    wide_ref, west_ref, east_ref, first_ref, second_ref, s1_ref, s2_ref, head_ref, c1_ref, c2_ref, c3_ref,
+    own3, far3, west_ref, east_ref, first_ref, second_ref, s1_ref, s2_ref, head_ref, c1_ref, c2_ref, c3_ref,
     state_ref, day_ref, t3, part_ref, t1, t2, own, ends,
 ):
     frames, fields, rows, _ = state_ref.shape
@@ -375,7 +384,8 @@
     own[0] = jnp.zeros(own.shape[1:], F32)
     own[rows + 1] = jnp.zeros(own.shape[1:], F32)
     for y in range(0, rows, 2):
-        z = jnp.concatenate([wide_ref[j, :, (y + 1) * LANES : (y + 3) * LANES] for j in range(frames + 2)], axis=0)
+        places = [split(own3, far3)(j) for j in range(frames + 2)]
+        z = jnp.concatenate([ref[at, :, (y + 1) * LANES : (y + 3) * LANES] for ref, at in places], axis=0)
         acc = jnp.dot(head_ref[...], z, preferred_element_type=F32)
         own[y + 1], own[y + 2] = acc[:, tile(0)], acc[:, tile(1)]
     z = jnp.concatenate([t3[j] for j in range(frames + 2)], axis=0)
@@ -397,30 +407,30 @@
         part_ref[d] = total
 
 
-def make_side(wide, west, east, first, second, s1, s2, head, c1, c2, c3, state, day, days):
+def make_side(own3, far3, west, east, first, second, s1, s2, head, c1, c2, c3, state, day, days):
     frames, fields, rows, _ = state.shape
     chans, hid = west.shape[1], c1.shape[0]
     return call(
         side_kernel,
         "side",
         (shape_of((frames + 2, 3 * hid, 2 * LANES), BF), shape_of((days, rows, LANES), F32)),
-        [VMEM] * 13,
+        [VMEM] * 14,
         [
             pltpu.VMEM((frames + 6, 3 * chans, 2 * LANES), BF),
             pltpu.VMEM((frames + 4, 3 * hid, 2 * LANES), BF),
             pltpu.VMEM((rows + 2, head.shape[0], LANES), F32),
             pltpu.VMEM((2, head.shape[0], LANES), F32),
         ],
-    )(wide, west, east, first, second, s1, s2, head, c1, c2, c3, state, day)
-
-
-def own_score(wide_ref, m3_ref, frames, y):
-    acc = jnp.dot(m3_ref[...], window(plain(wide_ref), range(frames + 2), y), preferred_element_type=F32)
+    )(own3, far3, west, east, first, second, s1, s2, head, c1, c2, c3, state, day)
+
+
+def own_score(own3, far3, m3_ref, frames, y):
+    acc = jnp.dot(m3_ref[...], window(split(own3, far3), range(frames + 2), y), preferred_element_type=F32)
     return acc[:, tile(0)], acc[:, tile(1)]
 
 
 def update_kernel(
-    wide_ref, t3, m3_ref, s3_ref, c3_ref, state_ref, noise_ref, out_ref, head_ref, side, scr
+    own3, far3, t3, m3_ref, s3_ref, c3_ref, state_ref, noise_ref, out_ref, head_ref, side, scr
 ):
     frames, fields, rows, _ = state_ref.shape
     z = jnp.concatenate([t3[j] for j in range(frames + 2)], axis=0)
@@ -431,7 +441,7 @@
             side[half, f * fields : (f + 1) * fields] = both[:, tile(half)]
     bias = c3_ref[...]
     for y in range(0, rows, 2):
-        both = own_score(wide_ref, m3_ref, frames, y)
+        both = own_score(own3, far3, m3_ref, frames, y)
         for f in range(frames):
             at = slice(f * fields, (f + 1) * fields)
             west, east = side[0, at], side[1, at]
@@ -444,19 +454,19 @@
         head_ref[f] = moved[0]
 
 
-def make_update(wide, t3, m3, s3, c3, state, noise):
+def make_update(own3, far3, t3, m3, s3, c3, state, noise):
     frames, fields, rows, _ = state.shape
     return call(
         update_kernel,
         "update",
         (shape_of(state.shape, BF), shape_of((frames, rows, LANES), F32)),
-        [VMEM] * 7,
+        [VMEM] * 8,
         [
             pltpu.VMEM((2, frames * fields, LANES), F32),
             pltpu.VMEM((frames, fields * rows, LANES), F32),
         ],
         cost=3_000_000_000,
-    )(wide, t3, m3, s3, c3, state, noise)
+    )(own3, far3, t3, m3, s3, c3, state, noise)
 
 
 def correct_kernel(count, *refs):
@@ -535,14 +545,14 @@
     near = swapped(send1, "tm", 0)
     small = jnp.concatenate([bias_one, bias_two, bias_three, day_of_frame.astype(F32)])[None]
     m1, m2, m3, s1, s2, s3, c1, c2, c3, days, head = make_weights(w1, w2, w3, small, state.shape[0])
-    own1, own2, west, east = make_inner(own, m1, c1)
+    own1, own2, own3, west, east = make_inner(own, m1, m2, c1, c2)
     west, east, send1, send2 = make_edges(west, east, near, far)
     first, second = swapped(send1, "space", 0), swapped(send2, "space", 1)
-    wide = make_main(own1, own2, near, far, m1, m2, c1, c2)
+    far3 = make_main(own1, own2, near, far, m1, m2, c1, c2)
     t3, mine = make_side(
-        wide, west, east, first, second, s1, s2, head, c1, c2, c3, state, days, observed.shape[0]
+        own3, far3, west, east, first, second, s1, s2, head, c1, c2, c3, state, days, observed.shape[0]
     )
-    out, head0 = make_update(wide, t3, m3, s3, c3, state, noise)
+    out, head0 = make_update(own3, far3, t3, m3, s3, c3, state, noise)
     parts = totals_of(mine)
     out = make_correct(parts, observed[:, 0], obs_mask[0], head0, days, out)
     return out[:, :, None]

time: 21.2 us -> 21.3 us (level); the launches traced: 20.8 us -> 21.2 us
  Pallas kernels: 11.6 us -> 12.2 us
    pallas_call x1, Pallas kernels: 0.89 us -> 1.76 us  [make_inner(): call(inner_kernel, 'inner', (shape_of((frames, 3 * chans, wide), BF), sha...]
    ppermute x4, waiting for transfers between devices: 0.62 us -> 0.01 us  [swapped(): return lax.ppermute(value, ('tm', 'space'), pairs)]
    ppermute x3, waiting for transfers between devices: 0.01 us -> 0.56 us  [partner(): return lax.ppermute(value, 'tm', [(i, i ^ bits) for i in range(count)])]
    ppermute x4, starting transfers between devices: 5.21 us -> 4.93 us  [swapped(): return lax.ppermute(value, ('tm', 'space'), pairs)]
    pallas_call x1, Pallas kernels: 4.19 us -> 3.94 us  [make_main(): call(main_kernel, 'main', (shape_of((2 * DEPTH, rows2, wide), BF),), [VME...]
  transfers between devices with their start and end apart: 7 -> 7, of which waited for: 1 -> 1; matrix products, arithmetic and copies ran while one was open for 0% -> 0% of each run, Pallas kernels for 38% -> 40%
where the time goes in v11:
time: 21.3 us; the launch traced here: 21.2 us
  Pallas kernels  12.2 us (57%)
  starting transfers between devices  7.21 us (34%)
  local copies, waits for them, and re-layouts  0.97 us (5%)
  waiting for transfers between devices  0.58 us (3%)
    ppermute x4, starting transfers between devices, swapped(): return lax.ppermute(value, ('tm', 'space'), pairs)  4.93 us
    pallas_call x1, Pallas kernels, make_main(): call(main_kernel, 'main', (shape_of((2 * DEPTH, rows2, wide), BF),), [VME...  3.94 us
    pallas_call x1, Pallas kernels, make_side(): call(side_kernel, 'side', (shape_of((frames + 2, 3 * hid, 2 * LANES), BF)...  2.65 us
    ppermute x3, starting transfers between devices, partner(): return lax.ppermute(value, 'tm', [(i, i ^ bits) for i in range(count)])  2.28 us
    pallas_call x1, Pallas kernels, make_update(): call(update_kernel, 'update', (shape_of(state.shape, BF), shape_of((frame...  1.95 us
    pallas_call x1, Pallas kernels, make_inner(): call(inner_kernel, 'inner', (shape_of((frames, 3 * chans, wide), BF), sha...  1.76 us
    unnamed x24, local copies, waits for them, and re-layouts  0.97 us
    pallas_call x1, Pallas kernels, make_weights(): call(weights_kernel, 'weights', (shape_of((2 * hid, 4 * 9 * chans), BF),...  0.88 us
  transfers between devices with their start and end apart: 7, of which 1 were waited for; matrix products, arithmetic and copies ran while one was open for 0% of the time, Pallas kernels for 40%

profile of v11, /device:TPU:0, one launch (start us, length us, event | category | flops | bytes accessed | tf_op | source)
XLA Modules:
  0.0 21.2 jit_solution(8187412941605265644)
XLA Ops:
  0.0 0.9 %copy-done = bf16[6,16,1,8,128]{4,3,2,1,0:T(8,128)(2,1)S(1)} copy-done((bf16[6,16,1,8,128]{4,3,2,1,0:T(8,128)(2,1)S(1)}, bf16[6,16,1,8,128]{4,3,2,1,0:T(8,128)(2,1)}, u32[]{:S(2)}) %copy-start) | copy-done | bytes 196632
  0.9 0.0 copy-start.4
  0.9 0.0 copy-start.6
  1.0 0.0 copy-start.7
  1.0 0.1 rows.1
  1.1 3.0 %collective-permute-start = (bf16[3,16,1024]{2,1,0:T(8,128)(2,1)S(1)}, bf16[3,16,1024]{2,1,0:T(8,128)(2,1)S(1)}, u32[]{:S(2)}, u32[]{:S(2)}) collective-permute-start(bf16[3,16,1024]{2,1,0:T(8,128)(2,1)S(1)} %get-tuple-element.40), channel_id=1, source_target_pairs={{0,1},{1,0},{2,3},{3,2},{4,5},{5,4},{6,7},{7,6},{8,16},{9,17},{10,... | collective-permute-start | bytes 294920 | tf_op jit(solution)/shard_map/ppermute | solution.py:516
  4.1 0.1 collective-permute-start.1
  4.2 0.0 copy-done.11
  4.2 0.0 copy-done.10
  4.2 0.1 pad_maximum_fusion
  4.3 0.0 copy-done.6
  4.3 0.9 %weights.1 = (bf16[128,576]{1,0:T(8,128)(2,1)S(1)}, bf16[128,2304]{1,0:T(8,128)(2,1)S(1)}, bf16[96,4608]{1,0:T(8,128)(2,1)S(1)}, bf16[384,192]{1,0:T(8,128)(2,1)...) custom-call(bf16[432,64]{1,0:T(8,128)(2,1)S(1)} %bitcast.25, ...), custom_call_target="tpu_custom_call" | custom-call | flops 1000000000 | bytes 1000000 | tf_op jit(solution)/shard_map/weights/pallas_call | solution.py:134
  5.2 1.8 %inner.1 = (bf16[6,48,1280]{2,1,0:T(8,128)(2,1)S(1)}, bf16[4,192,1280]{2,1,0:T(8,128)(2,1)S(1)}, bf16[2,192,1280]{2,1,0:T(8,128)(2,1)S(1)}, bf16[6,16,128]{2,1,0:T(8,128)(2,1)S(1)}, bf16[6,16,128]{2,1,0:T(8,128)(2,1)S(1)}) custom-call(bf16[6,16,1024]{2,1,0:T(8,128)(2,1)S(1)} %get-tuple-element.32.own_ref, bf16[128,576]{1,0:T(8,128)(2,1)S(1)} %get-tuple-element.33.m1_ref, ...), custom_call_target="tpu_custom_call" | custom-call | flops 1500000000 | bytes 1000000 | tf_op jit(solution)/shard_map/inner/pallas_call | solution.py:277
  7.0 0.0 collective-permute-done.far_ref
  7.0 0.0 collective-permute-done.1.near_ref
  7.0 0.2 edges.1
  7.2 1.8 %collective-permute-start.2 = (bf16[12,16,128]{2,1,0:T(8,128)(2,1)S(1)}, bf16[12,16,128]{2,1,0:T(8,128)(2,1)S(1)}, u32[]{:S(2)}, u32[]{:S(2)}) collective-permute-start(bf16[12,16,128]{2,1,0:T(8,128)(2,1)S(1)} %get-tuple-element.46), channel_id=1, source_target_pairs={{0,1},{1,0},{2,3},{3,2},{4,5},{5,4},{6,7},{7,6},{8,9},{9,8},{10,11... | collective-permute-start | bytes 147464 | tf_op jit(solution)/shard_map/ppermute | solution.py:516
  9.0 0.0 collective-permute-start.3
  9.0 3.9 %main.1.far3 = bf16[6,192,1280]{2,1,0:T(8,128)(2,1)S(1)} custom-call(bf16[6,48,1280]{2,1,0:T(8,128)(2,1)S(1)} %get-tuple-element.38.own1, bf16[4,192,1280]{2,1,0:T(8,128)(2,1)S(1)} %get-tuple-element.39.own2, bf16[3,16,1024]{2,1,0:T(8,128)(2,1)S(1)} %collective-permute-done.far_ref, bf16[3,16,1024]{2,1,0:T(8,128)(2,1)S(1)} %collective-permute-done.1.near_ref, ...), custom_call_target="tpu_custom_call" | custom-call | flops 5000000000 | bytes 1000000 | tf_op jit(solution)/shard_map/main/pallas_call | solution.py:309
  13.0 0.0 copy-start.5
  13.0 0.0 collective-permute-done.2.first_ref
  13.0 0.0 collective-permute-done.3.second_ref
  13.0 0.0 copy-done.1
  13.0 2.7 %side.1 = (bf16[8,192,256]{2,1,0:T(8,128)(2,1)S(1)}, f32[2,8,128]{2,1,0:T(8,128)S(1)}) custom-call(bf16[2,192,1280]{2,1,0:T(8,128)(2,1)S(1)} %get-tuple-element.37.own3, bf16[6,192,1280]{2,1,0:T(8,128)(2,1)S(1)} %main.1.far3, bf16[12,16,128]{2,1,0:T(8,128)(2,1)S(1)} %get-tuple-element.44.west_ref, bf16[12,16,128]{2,1,0:T(8,128)(2,1)S(1)} %get-tuple-element.45.east_ref, ...), custom_call_target="tpu_custom_call" | custom-call | tf_op jit(solution)/shard_map/side/pallas_call | solution.py:413
  15.7 0.6 %collective-permute-start.6 = (f32[2,8,128]{2,1,0:T(8,128)S(1)}, f32[2,8,128]{2,1,0:T(8,128)S(1)}, u32[]{:S(2)}, u32[]{:S(2)}) collective-permute-start(f32[2,8,128]{2,1,0:T(8,128)S(1)} %get-tuple-element.53.refs_3_), channel_id=1, source_target_pairs={{0,8},{8,0},{16,24},{24,16},{1,9},{9,1},{17,25},{25,17},{2,10},{10... | collective-permute-start | bytes 24584 | tf_op jit(solution)/shard_map/ppermute | solution.py:523
  16.2 0.6 %collective-permute-start.5 = (f32[2,8,128]{2,1,0:T(8,128)S(1)}, f32[2,8,128]{2,1,0:T(8,128)S(1)}, u32[]{:S(2)}, u32[]{:S(2)}) collective-permute-start(f32[2,8,128]{2,1,0:T(8,128)S(1)} %get-tuple-element.53.refs_3_), channel_id=1, source_target_pairs={{0,24},{8,16},{16,8},{24,0},{1,25},{9,17},{17,9},{25,1},{2,26},{10... | collective-permute-start | bytes 24584 | tf_op jit(solution)/shard_map/ppermute | solution.py:523
  16.8 1.1 %collective-permute-start.4 = (f32[2,8,128]{2,1,0:T(8,128)S(1)}, f32[2,8,128]{2,1,0:T(8,128)S(1)}, u32[]{:S(2)}, u32[]{:S(2)}) collective-permute-start(f32[2,8,128]{2,1,0:T(8,128)S(1)} %get-tuple-element.53.refs_3_), channel_id=1, source_target_pairs={{0,16},{8,24},{16,0},{24,8},{1,17},{9,25},{17,1},{25,9},{2,18},{10... | collective-permute-start | bytes 24584 | tf_op jit(solution)/shard_map/ppermute | solution.py:523
  17.9 1.9 %update.1 = (bf16[6,16,8,128]{3,2,1,0:T(8,128)(2,1)S(1)}, f32[6,8,128]{2,1,0:T(8,128)S(1)}) custom-call(bf16[2,192,1280]{2,1,0:T(8,128)(2,1)S(1)} %get-tuple-element.37.own3, bf16[6,192,1280]{2,1,0:T(8,128)(2,1)S(1)} %main.1.far3, bf16[8,192,256]{2,1,0:T(8,128)(2,1)S(1)} %get-tuple-element.54.t3, bf16[96,4608]{1,0:T(8,128)(2,1)S(1)} %get-tuple-element.55.m3_ref, ...), custom_call_target="tpu_custom_call" | custom-call | flops 3000000000 | bytes 1000000 | tf_op jit(solution)/shard_map/update/pallas_call | solution.py:459
  19.9 0.0 collective-permute-done.6.refs_2_
  19.9 0.0 collective-permute-done.5.refs_1_
  19.9 0.6 %collective-permute-done.4.refs_0_ = f32[2,8,128]{2,1,0:T(8,128)S(1)} collective-permute-done((f32[2,8,128]{2,1,0:T(8,128)S(1)}, f32[2,8,128]{2,1,0:T(8,128)S(1)}, u32[]{:S(2)}, u32[]{:S(2)}) %collective-permute-start.4) | collective-permute-done | bytes 8224 | tf_op jit(solution)/shard_map/ppermute | solution.py:523
  20.5 0.7 %correct.1 = bf16[6,16,8,128]{3,2,1,0:T(8,128)(2,1)} custom-call(f32[2,8,128]{2,1,0:T(8,128)S(1)} %collective-permute-done.4.refs_0_, f32[2,8,128]{2,1,0:T(8,128)S(1)} %collective-permute-done.5.refs_1_, f32[2,8,128]{2,1,0:T(8,128)S(1)} %collective-permute-done.6.refs_2_, f32[2,8,128]{2,1,0:T(8,128)S(1)} %get-tuple-element.53.refs_3_, ...), custom_call_target="tpu_custom_call" | custom-call | tf_op jit(solution)/shard_map/correct/pallas_call | solution.py:494
  (16 shorter events, 0.0 us)
Async XLA Ops:
  0.0 0.9 %copy-start = (bf16[6,16,1,8,128]{4,3,2,1,0:T(8,128)(2,1)S(1)}, bf16[6,16,1,8,128]{4,3,2,1,0:T(8,128)(2,1)}, u32[]{:S(2)}) copy-start(bf16[6,16,1,8,128]{4,3,2,1,0:T(8,128)(2,1)} %param.11) | copy-start | bytes 589828
  0.9 3.3 %copy-start.11 = (s32[6]{0:T(128)S(1)}, s32[6]{0:T(128)}, u32[]{:S(2)}) copy-start(s32[6]{0:T(128)} %param.19) | copy-start | bytes 76
  0.9 3.3 %copy-start.8 = (f32[16]{0:T(128)S(1)}, f32[16]{0:T(128)}, u32[]{:S(2)}) copy-start(f32[16]{0:T(128)} %param.18) | copy-start | bytes 196
  0.9 3.3 %copy-start.9 = (f32[64]{0:T(128)S(1)}, f32[64]{0:T(128)}, u32[]{:S(2)}) copy-start(f32[64]{0:T(128)} %param.16) | copy-start | bytes 772
  0.9 3.3 %copy-start.10 = (f32[64]{0:T(128)S(1)}, f32[64]{0:T(128)}, u32[]{:S(2)}) copy-start(f32[64]{0:T(128)} %param.14) | copy-start | bytes 772
  0.9 3.4 %copy-start.4 = (bf16[64,64,3,3,3]{1,0,4,3,2:T(8,128)(2,1)S(1)}, bf16[64,64,3,3,3]{1,0,4,3,2:T(8,128)(2,1)}, u32[]{:S(2)}) copy-start(bf16[64,64,3,3,3]{1,0,4,3,2:T(8,128)(2,1)} %param.15) | copy-start | bytes 663556
  0.9 3.4 %copy-start.6 = (bf16[64,16,3,3,3]{0,1,4,3,2:T(8,128)(2,1)S(1)}, bf16[64,16,3,3,3]{0,1,4,3,2:T(8,128)(2,1)}, u32[]{:S(2)}) copy-start(bf16[64,16,3,3,3]{0,1,4,3,2:T(8,128)(2,1)} %param.13) | copy-start | bytes 165892
  1.0 3.4 %copy-start.7 = (bf16[16,64,3,3,3]{1,0,4,3,2:T(8,128)(2,1)S(1)}, bf16[16,64,3,3,3]{1,0,4,3,2:T(8,128)(2,1)}, u32[]{:S(2)}) copy-start(bf16[16,64,3,3,3]{1,0,4,3,2:T(8,128)(2,1)} %param.17) | copy-start | bytes 165892
  1.1 5.9 %collective-permute-start = (bf16[3,16,1024]{2,1,0:T(8,128)(2,1)S(1)}, bf16[3,16,1024]{2,1,0:T(8,128)(2,1)S(1)}, u32[]{:S(2)}, u32[]{:S(2)}) collective-permute-start(bf16[3,16,1024]{2,1,0:T(8,128)(2,1)S(1)} %get-tuple-element.40), channel_id=1, source_target_pairs={{0,1},{1,0},{2,3},{3,2},{4,5},{5,4},{6,7},{7,6},{8,16},{9,17},{10,... | collective-permute-start | bytes 294920 | tf_op jit(solution)/shard_map/ppermute | solution.py:516
  4.1 2.9 %collective-permute-start.1 = (bf16[3,16,1024]{2,1,0:T(8,128)(2,1)S(1)}, bf16[3,16,1024]{2,1,0:T(8,128)(2,1)S(1)}, u32[]{:S(2)}, u32[]{:S(2)}) collective-permute-start(bf16[3,16,1024]{2,1,0:T(8,128)(2,1)S(1)} %get-tuple-element.41), channel_id=1, source_target_pairs={{0,8},{1,9},{2,10},{3,11},{4,12},{5,13},{6,14},{7,15},{8,0},{9,1},... | collective-permute-start | bytes 294920 | tf_op jit(solution)/shard_map/ppermute | solution.py:516
  7.2 5.8 %collective-permute-start.2 = (bf16[12,16,128]{2,1,0:T(8,128)(2,1)S(1)}, bf16[12,16,128]{2,1,0:T(8,128)(2,1)S(1)}, u32[]{:S(2)}, u32[]{:S(2)}) collective-permute-start(bf16[12,16,128]{2,1,0:T(8,128)(2,1)S(1)} %get-tuple-element.46), channel_id=1, source_target_pairs={{0,1},{1,0},{2,3},{3,2},{4,5},{5,4},{6,7},{7,6},{8,9},{9,8},{10,11... | collective-permute-start | bytes 147464 | tf_op jit(solution)/shard_map/ppermute | solution.py:516
  9.0 4.0 %collective-permute-start.3 = (bf16[12,16,128]{2,1,0:T(8,128)(2,1)S(1)}, bf16[12,16,128]{2,1,0:T(8,128)(2,1)S(1)}, u32[]{:S(2)}, u32[]{:S(2)}) collective-permute-start(bf16[12,16,128]{2,1,0:T(8,128)(2,1)S(1)} %get-tuple-element.47), channel_id=1, source_target_pairs={{0,8},{1,2},{2,1},{3,4},{4,3},{5,6},{6,5},{7,15},{8,0},{9,10},{10,... | collective-permute-start | bytes 147464 | tf_op jit(solution)/shard_map/ppermute | solution.py:516
  9.0 4.0 %copy-start.1 = (bf16[6,16,1,8,128]{4,3,2,1,0:T(8,128)(2,1)S(1)}, bf16[6,16,1,8,128]{4,3,2,1,0:T(8,128)(2,1)}, u32[]{:S(2)}) copy-start(bf16[6,16,1,8,128]{4,3,2,1,0:T(8,128)(2,1)} %param.11) | copy-start | bytes 589828
  13.0 5.0 %copy-start.5 = (bf16[6,16,1,8,128]{4,3,2,1,0:T(8,128)(2,1)S(1)}, bf16[6,16,1,8,128]{4,3,2,1,0:T(8,128)(2,1)}, u32[]{:S(2)}) copy-start(bf16[6,16,1,8,128]{4,3,2,1,0:T(8,128)(2,1)} %param.12) | copy-start | bytes 589828
  15.7 4.2 %collective-permute-start.6 = (f32[2,8,128]{2,1,0:T(8,128)S(1)}, f32[2,8,128]{2,1,0:T(8,128)S(1)}, u32[]{:S(2)}, u32[]{:S(2)}) collective-permute-start(f32[2,8,128]{2,1,0:T(8,128)S(1)} %get-tuple-element.53.refs_3_), channel_id=1, source_target_pairs={{0,8},{8,0},{16,24},{24,16},{1,9},{9,1},{17,25},{25,17},{2,10},{10... | collective-permute-start | bytes 24584 | tf_op jit(solution)/shard_map/ppermute | solution.py:523
  16.2 3.7 %collective-permute-start.5 = (f32[2,8,128]{2,1,0:T(8,128)S(1)}, f32[2,8,128]{2,1,0:T(8,128)S(1)}, u32[]{:S(2)}, u32[]{:S(2)}) collective-permute-start(f32[2,8,128]{2,1,0:T(8,128)S(1)} %get-tuple-element.53.refs_3_), channel_id=1, source_target_pairs={{0,24},{8,16},{16,8},{24,0},{1,25},{9,17},{17,9},{25,1},{2,26},{10... | collective-permute-start | bytes 24584 | tf_op jit(solution)/shard_map/ppermute | solution.py:523
  16.8 3.7 %collective-permute-start.4 = (f32[2,8,128]{2,1,0:T(8,128)S(1)}, f32[2,8,128]{2,1,0:T(8,128)S(1)}, u32[]{:S(2)}, u32[]{:S(2)}) collective-permute-start(f32[2,8,128]{2,1,0:T(8,128)S(1)} %get-tuple-element.53.refs_3_), channel_id=1, source_target_pairs={{0,16},{8,24},{16,0},{24,8},{1,17},{9,25},{17,1},{25,9},{2,18},{10... | collective-permute-start | bytes 24584 | tf_op jit(solution)/shard_map/ppermute | solution.py:523
  17.9 2.5 %copy-start.2 = (f32[2,1,8,128]{3,2,1,0:T(8,128)S(1)}, f32[2,1,8,128]{3,2,1,0:T(8,128)}, u32[]{:S(2)}) copy-start(f32[2,1,8,128]{3,2,1,0:T(8,128)} %param.20) | copy-start | bytes 24580
  17.9 2.5 %copy-start.3 = (s32[1,8,128]{2,1,0:T(8,128)S(1)}, s32[1,8,128]{2,1,0:T(8,128)}, u32[]{:S(2)}) copy-start(s32[1,8,128]{2,1,0:T(8,128)} %param.21) | copy-start | bytes 12292

commit v12 on v11

--- a/solution.py
+++ b/solution.py
@@ -528,7 +528,7 @@
     while far > 2:
         mine = mine + partner(mine, far)
         far //= 2
-    return [partner(mine, bits) for bits in (2, 3, 1) if bits < count] + [mine]
+    return [partner(mine, bits) for bits in (1, 3, 2) if bits < count] + [mine]
 
 
 def body(

time: 21.3 us -> 21 us (0.986); the launches traced: 21.2 us -> 20.6 us
  waiting for transfers between devices: 0.58 us -> 0.02 us
    ppermute x3, waiting for transfers between devices: 0.56 us -> 0.01 us  [partner(): return lax.ppermute(value, 'tm', [(i, i ^ bits) for i in range(count)])]
  transfers between devices with their start and end apart: 7 -> 7, of which waited for: 1 -> 0; matrix products, arithmetic and copies ran while one was open for 0% -> 0% of each run, Pallas kernels for 40% -> 41%
where the time goes in v12:
time: 21 us; the launch traced here: 20.6 us
  Pallas kernels  12.2 us (58%)
  starting transfers between devices  7.14 us (34%)
  local copies, waits for them, and re-layouts  0.97 us (5%)
    ppermute x4, starting transfers between devices, swapped(): return lax.ppermute(value, ('tm', 'space'), pairs)  4.93 us
    pallas_call x1, Pallas kernels, make_main(): call(main_kernel, 'main', (shape_of((2 * DEPTH, rows2, wide), BF),), [VME...  3.94 us
    pallas_call x1, Pallas kernels, make_side(): call(side_kernel, 'side', (shape_of((frames + 2, 3 * hid, 2 * LANES), BF)...  2.65 us
    ppermute x3, starting transfers between devices, partner(): return lax.ppermute(value, 'tm', [(i, i ^ bits) for i in range(count)])  2.21 us
    pallas_call x1, Pallas kernels, make_update(): call(update_kernel, 'update', (shape_of(state.shape, BF), shape_of((frame...  1.95 us
    pallas_call x1, Pallas kernels, make_inner(): call(inner_kernel, 'inner', (shape_of((frames, 3 * chans, wide), BF), sha...  1.76 us
    unnamed x24, local copies, waits for them, and re-layouts  0.97 us
    pallas_call x1, Pallas kernels, make_weights(): call(weights_kernel, 'weights', (shape_of((2 * hid, 4 * 9 * chans), BF),...  0.88 us
  transfers between devices with their start and end apart: 7, of which 0 were waited for; matrix products, arithmetic and copies ran while one was open for 0% of the time, Pallas kernels for 41%

profile of v12, /device:TPU:0, one launch (start us, length us, event | category | flops | bytes accessed | tf_op | source)
XLA Modules:
  0.0 20.6 jit_solution(2065622058936306135)
XLA Ops:
  0.0 0.9 %copy-done = bf16[6,16,1,8,128]{4,3,2,1,0:T(8,128)(2,1)S(1)} copy-done((bf16[6,16,1,8,128]{4,3,2,1,0:T(8,128)(2,1)S(1)}, bf16[6,16,1,8,128]{4,3,2,1,0:T(8,128)(2,1)}, u32[]{:S(2)}) %copy-start) | copy-done | bytes 196632
  0.9 0.0 copy-start.4
  0.9 0.0 copy-start.6
  1.0 0.0 copy-start.7
  1.0 0.1 rows.1
  1.1 3.0 %collective-permute-start = (bf16[3,16,1024]{2,1,0:T(8,128)(2,1)S(1)}, bf16[3,16,1024]{2,1,0:T(8,128)(2,1)S(1)}, u32[]{:S(2)}, u32[]{:S(2)}) collective-permute-start(bf16[3,16,1024]{2,1,0:T(8,128)(2,1)S(1)} %get-tuple-element.40), channel_id=1, source_target_pairs={{0,1},{1,0},{2,3},{3,2},{4,5},{5,4},{6,7},{7,6},{8,16},{9,17},{10,... | collective-permute-start | bytes 294920 | tf_op jit(solution)/shard_map/ppermute | solution.py:516
  4.1 0.1 collective-permute-start.1
  4.2 0.0 copy-done.11
  4.2 0.0 copy-done.8
  4.2 0.0 copy-done.9
  4.2 0.0 copy-done.10
  4.2 0.1 pad_maximum_fusion
  4.3 0.9 %weights.1 = (bf16[128,576]{1,0:T(8,128)(2,1)S(1)}, bf16[128,2304]{1,0:T(8,128)(2,1)S(1)}, bf16[96,4608]{1,0:T(8,128)(2,1)S(1)}, bf16[384,192]{1,0:T(8,128)(2,1)...) custom-call(bf16[432,64]{1,0:T(8,128)(2,1)S(1)} %bitcast.25, ...), custom_call_target="tpu_custom_call" | custom-call | flops 1000000000 | bytes 1000000 | tf_op jit(solution)/shard_map/weights/pallas_call | solution.py:134
  5.2 1.8 %inner.1 = (bf16[6,48,1280]{2,1,0:T(8,128)(2,1)S(1)}, bf16[4,192,1280]{2,1,0:T(8,128)(2,1)S(1)}, bf16[2,192,1280]{2,1,0:T(8,128)(2,1)S(1)}, bf16[6,16,128]{2,1,0:T(8,128)(2,1)S(1)}, bf16[6,16,128]{2,1,0:T(8,128)(2,1)S(1)}) custom-call(bf16[6,16,1024]{2,1,0:T(8,128)(2,1)S(1)} %get-tuple-element.32.own_ref, bf16[128,576]{1,0:T(8,128)(2,1)S(1)} %get-tuple-element.33.m1_ref, ...), custom_call_target="tpu_custom_call" | custom-call | flops 1500000000 | bytes 1000000 | tf_op jit(solution)/shard_map/inner/pallas_call | solution.py:277
  7.0 0.0 collective-permute-done.far_ref
  7.0 0.0 collective-permute-done.1.near_ref
  7.0 0.2 edges.1
  7.2 1.8 %collective-permute-start.2 = (bf16[12,16,128]{2,1,0:T(8,128)(2,1)S(1)}, bf16[12,16,128]{2,1,0:T(8,128)(2,1)S(1)}, u32[]{:S(2)}, u32[]{:S(2)}) collective-permute-start(bf16[12,16,128]{2,1,0:T(8,128)(2,1)S(1)} %get-tuple-element.46), channel_id=1, source_target_pairs={{0,1},{1,0},{2,3},{3,2},{4,5},{5,4},{6,7},{7,6},{8,9},{9,8},{10,11... | collective-permute-start | bytes 147464 | tf_op jit(solution)/shard_map/ppermute | solution.py:516
  9.0 0.0 collective-permute-start.3
  9.0 3.9 %main.1.far3 = bf16[6,192,1280]{2,1,0:T(8,128)(2,1)S(1)} custom-call(bf16[6,48,1280]{2,1,0:T(8,128)(2,1)S(1)} %get-tuple-element.38.own1, bf16[4,192,1280]{2,1,0:T(8,128)(2,1)S(1)} %get-tuple-element.39.own2, bf16[3,16,1024]{2,1,0:T(8,128)(2,1)S(1)} %collective-permute-done.far_ref, bf16[3,16,1024]{2,1,0:T(8,128)(2,1)S(1)} %collective-permute-done.1.near_ref, ...), custom_call_target="tpu_custom_call" | custom-call | flops 5000000000 | bytes 1000000 | tf_op jit(solution)/shard_map/main/pallas_call | solution.py:309
  13.0 0.0 copy-start.5
  13.0 0.0 collective-permute-done.2.first_ref
  13.0 0.0 collective-permute-done.3.second_ref
  13.0 2.7 %side.1 = (bf16[8,192,256]{2,1,0:T(8,128)(2,1)S(1)}, f32[2,8,128]{2,1,0:T(8,128)S(1)}) custom-call(bf16[2,192,1280]{2,1,0:T(8,128)(2,1)S(1)} %get-tuple-element.37.own3, bf16[6,192,1280]{2,1,0:T(8,128)(2,1)S(1)} %main.1.far3, bf16[12,16,128]{2,1,0:T(8,128)(2,1)S(1)} %get-tuple-element.44.west_ref, bf16[12,16,128]{2,1,0:T(8,128)(2,1)S(1)} %get-tuple-element.45.east_ref, ...), custom_call_target="tpu_custom_call" | custom-call | tf_op jit(solution)/shard_map/side/pallas_call | solution.py:413
  15.7 1.0 %collective-permute-start.6 = (f32[2,8,128]{2,1,0:T(8,128)S(1)}, f32[2,8,128]{2,1,0:T(8,128)S(1)}, u32[]{:S(2)}, u32[]{:S(2)}) collective-permute-start(f32[2,8,128]{2,1,0:T(8,128)S(1)} %get-tuple-element.53.refs_3_), channel_id=1, source_target_pairs={{0,16},{8,24},{16,0},{24,8},{1,17},{9,25},{17,1},{25,9},{2,18},{10... | collective-permute-start | bytes 24584 | tf_op jit(solution)/shard_map/ppermute | solution.py:523
  16.6 0.9 %collective-permute-start.5 = (f32[2,8,128]{2,1,0:T(8,128)S(1)}, f32[2,8,128]{2,1,0:T(8,128)S(1)}, u32[]{:S(2)}, u32[]{:S(2)}) collective-permute-start(f32[2,8,128]{2,1,0:T(8,128)S(1)} %get-tuple-element.53.refs_3_), channel_id=1, source_target_pairs={{0,24},{8,16},{16,8},{24,0},{1,25},{9,17},{17,9},{25,1},{2,26},{10... | collective-permute-start | bytes 24584 | tf_op jit(solution)/shard_map/ppermute | solution.py:523
  17.6 0.3 %collective-permute-start.4 = (f32[2,8,128]{2,1,0:T(8,128)S(1)}, f32[2,8,128]{2,1,0:T(8,128)S(1)}, u32[]{:S(2)}, u32[]{:S(2)}) collective-permute-start(f32[2,8,128]{2,1,0:T(8,128)S(1)} %get-tuple-element.53.refs_3_), channel_id=1, source_target_pairs={{0,8},{8,0},{16,24},{24,16},{1,9},{9,1},{17,25},{25,17},{2,10},{10... | collective-permute-start | bytes 24584 | tf_op jit(solution)/shard_map/ppermute | solution.py:523
  17.9 1.9 %update.1 = (bf16[6,16,8,128]{3,2,1,0:T(8,128)(2,1)S(1)}, f32[6,8,128]{2,1,0:T(8,128)S(1)}) custom-call(bf16[2,192,1280]{2,1,0:T(8,128)(2,1)S(1)} %get-tuple-element.37.own3, bf16[6,192,1280]{2,1,0:T(8,128)(2,1)S(1)} %main.1.far3, bf16[8,192,256]{2,1,0:T(8,128)(2,1)S(1)} %get-tuple-element.54.t3, bf16[96,4608]{1,0:T(8,128)(2,1)S(1)} %get-tuple-element.55.m3_ref, ...), custom_call_target="tpu_custom_call" | custom-call | flops 3000000000 | bytes 1000000 | tf_op jit(solution)/shard_map/update/pallas_call | solution.py:459
  19.8 0.0 collective-permute-done.6.refs_2_
  19.8 0.0 collective-permute-done.5.refs_1_
  19.8 0.0 collective-permute-done.4.refs_0_
  19.9 0.7 %correct.1 = bf16[6,16,8,128]{3,2,1,0:T(8,128)(2,1)} custom-call(f32[2,8,128]{2,1,0:T(8,128)S(1)} %collective-permute-done.4.refs_0_, f32[2,8,128]{2,1,0:T(8,128)S(1)} %collective-permute-done.5.refs_1_, f32[2,8,128]{2,1,0:T(8,128)S(1)} %collective-permute-done.6.refs_2_, f32[2,8,128]{2,1,0:T(8,128)S(1)} %get-tuple-element.53.refs_3_, ...), custom_call_target="tpu_custom_call" | custom-call | tf_op jit(solution)/shard_map/correct/pallas_call | solution.py:494
  (16 shorter events, 0.0 us)
Async XLA Ops:
  0.0 0.9 %copy-start = (bf16[6,16,1,8,128]{4,3,2,1,0:T(8,128)(2,1)S(1)}, bf16[6,16,1,8,128]{4,3,2,1,0:T(8,128)(2,1)}, u32[]{:S(2)}) copy-start(bf16[6,16,1,8,128]{4,3,2,1,0:T(8,128)(2,1)} %param.11) | copy-start | bytes 589828
  0.9 3.3 %copy-start.11 = (s32[6]{0:T(128)S(1)}, s32[6]{0:T(128)}, u32[]{:S(2)}) copy-start(s32[6]{0:T(128)} %param.19) | copy-start | bytes 76
  0.9 3.3 %copy-start.8 = (f32[16]{0:T(128)S(1)}, f32[16]{0:T(128)}, u32[]{:S(2)}) copy-start(f32[16]{0:T(128)} %param.18) | copy-start | bytes 196
  0.9 3.3 %copy-start.9 = (f32[64]{0:T(128)S(1)}, f32[64]{0:T(128)}, u32[]{:S(2)}) copy-start(f32[64]{0:T(128)} %param.16) | copy-start | bytes 772
  0.9 3.3 %copy-start.10 = (f32[64]{0:T(128)S(1)}, f32[64]{0:T(128)}, u32[]{:S(2)}) copy-start(f32[64]{0:T(128)} %param.14) | copy-start | bytes 772
  0.9 3.4 %copy-start.4 = (bf16[64,64,3,3,3]{1,0,4,3,2:T(8,128)(2,1)S(1)}, bf16[64,64,3,3,3]{1,0,4,3,2:T(8,128)(2,1)}, u32[]{:S(2)}) copy-start(bf16[64,64,3,3,3]{1,0,4,3,2:T(8,128)(2,1)} %param.15) | copy-start | bytes 663556
  0.9 3.4 %copy-start.6 = (bf16[64,16,3,3,3]{0,1,4,3,2:T(8,128)(2,1)S(1)}, bf16[64,16,3,3,3]{0,1,4,3,2:T(8,128)(2,1)}, u32[]{:S(2)}) copy-start(bf16[64,16,3,3,3]{0,1,4,3,2:T(8,128)(2,1)} %param.13) | copy-start | bytes 165892
  1.0 3.4 %copy-start.7 = (bf16[16,64,3,3,3]{1,0,4,3,2:T(8,128)(2,1)S(1)}, bf16[16,64,3,3,3]{1,0,4,3,2:T(8,128)(2,1)}, u32[]{:S(2)}) copy-start(bf16[16,64,3,3,3]{1,0,4,3,2:T(8,128)(2,1)} %param.17) | copy-start | bytes 165892
  1.1 5.9 %collective-permute-start = (bf16[3,16,1024]{2,1,0:T(8,128)(2,1)S(1)}, bf16[3,16,1024]{2,1,0:T(8,128)(2,1)S(1)}, u32[]{:S(2)}, u32[]{:S(2)}) collective-permute-start(bf16[3,16,1024]{2,1,0:T(8,128)(2,1)S(1)} %get-tuple-element.40), channel_id=1, source_target_pairs={{0,1},{1,0},{2,3},{3,2},{4,5},{5,4},{6,7},{7,6},{8,16},{9,17},{10,... | collective-permute-start | bytes 294920 | tf_op jit(solution)/shard_map/ppermute | solution.py:516
  4.1 2.9 %collective-permute-start.1 = (bf16[3,16,1024]{2,1,0:T(8,128)(2,1)S(1)}, bf16[3,16,1024]{2,1,0:T(8,128)(2,1)S(1)}, u32[]{:S(2)}, u32[]{:S(2)}) collective-permute-start(bf16[3,16,1024]{2,1,0:T(8,128)(2,1)S(1)} %get-tuple-element.41), channel_id=1, source_target_pairs={{0,8},{1,9},{2,10},{3,11},{4,12},{5,13},{6,14},{7,15},{8,0},{9,1},... | collective-permute-start | bytes 294920 | tf_op jit(solution)/shard_map/ppermute | solution.py:516
  7.2 5.8 %collective-permute-start.2 = (bf16[12,16,128]{2,1,0:T(8,128)(2,1)S(1)}, bf16[12,16,128]{2,1,0:T(8,128)(2,1)S(1)}, u32[]{:S(2)}, u32[]{:S(2)}) collective-permute-start(bf16[12,16,128]{2,1,0:T(8,128)(2,1)S(1)} %get-tuple-element.46), channel_id=1, source_target_pairs={{0,1},{1,0},{2,3},{3,2},{4,5},{5,4},{6,7},{7,6},{8,9},{9,8},{10,11... | collective-permute-start | bytes 147464 | tf_op jit(solution)/shard_map/ppermute | solution.py:516
  9.0 4.0 %collective-permute-start.3 = (bf16[12,16,128]{2,1,0:T(8,128)(2,1)S(1)}, bf16[12,16,128]{2,1,0:T(8,128)(2,1)S(1)}, u32[]{:S(2)}, u32[]{:S(2)}) collective-permute-start(bf16[12,16,128]{2,1,0:T(8,128)(2,1)S(1)} %get-tuple-element.47), channel_id=1, source_target_pairs={{0,8},{1,2},{2,1},{3,4},{4,3},{5,6},{6,5},{7,15},{8,0},{9,10},{10,... | collective-permute-start | bytes 147464 | tf_op jit(solution)/shard_map/ppermute | solution.py:516
  9.0 4.0 %copy-start.1 = (bf16[6,16,1,8,128]{4,3,2,1,0:T(8,128)(2,1)S(1)}, bf16[6,16,1,8,128]{4,3,2,1,0:T(8,128)(2,1)}, u32[]{:S(2)}) copy-start(bf16[6,16,1,8,128]{4,3,2,1,0:T(8,128)(2,1)} %param.11) | copy-start | bytes 589828
  13.0 4.9 %copy-start.5 = (bf16[6,16,1,8,128]{4,3,2,1,0:T(8,128)(2,1)S(1)}, bf16[6,16,1,8,128]{4,3,2,1,0:T(8,128)(2,1)}, u32[]{:S(2)}) copy-start(bf16[6,16,1,8,128]{4,3,2,1,0:T(8,128)(2,1)} %param.12) | copy-start | bytes 589828
  15.7 4.2 %collective-permute-start.6 = (f32[2,8,128]{2,1,0:T(8,128)S(1)}, f32[2,8,128]{2,1,0:T(8,128)S(1)}, u32[]{:S(2)}, u32[]{:S(2)}) collective-permute-start(f32[2,8,128]{2,1,0:T(8,128)S(1)} %get-tuple-element.53.refs_3_), channel_id=1, source_target_pairs={{0,16},{8,24},{16,0},{24,8},{1,17},{9,25},{17,1},{25,9},{2,18},{10... | collective-permute-start | bytes 24584 | tf_op jit(solution)/shard_map/ppermute | solution.py:523
  16.6 3.2 %collective-permute-start.5 = (f32[2,8,128]{2,1,0:T(8,128)S(1)}, f32[2,8,128]{2,1,0:T(8,128)S(1)}, u32[]{:S(2)}, u32[]{:S(2)}) collective-permute-start(f32[2,8,128]{2,1,0:T(8,128)S(1)} %get-tuple-element.53.refs_3_), channel_id=1, source_target_pairs={{0,24},{8,16},{16,8},{24,0},{1,25},{9,17},{17,9},{25,1},{2,26},{10... | collective-permute-start | bytes 24584 | tf_op jit(solution)/shard_map/ppermute | solution.py:523
  17.6 2.3 %collective-permute-start.4 = (f32[2,8,128]{2,1,0:T(8,128)S(1)}, f32[2,8,128]{2,1,0:T(8,128)S(1)}, u32[]{:S(2)}, u32[]{:S(2)}) collective-permute-start(f32[2,8,128]{2,1,0:T(8,128)S(1)} %get-tuple-element.53.refs_3_), channel_id=1, source_target_pairs={{0,8},{8,0},{16,24},{24,16},{1,9},{9,1},{17,25},{25,17},{2,10},{10... | collective-permute-start | bytes 24584 | tf_op jit(solution)/shard_map/ppermute | solution.py:523
  17.9 2.0 %copy-start.2 = (f32[2,1,8,128]{3,2,1,0:T(8,128)S(1)}, f32[2,1,8,128]{3,2,1,0:T(8,128)}, u32[]{:S(2)}) copy-start(f32[2,1,8,128]{3,2,1,0:T(8,128)} %param.20) | copy-start | bytes 24580
  17.9 2.0 %copy-start.3 = (s32[1,8,128]{2,1,0:T(8,128)S(1)}, s32[1,8,128]{2,1,0:T(8,128)}, u32[]{:S(2)}) copy-start(s32[1,8,128]{2,1,0:T(8,128)} %param.21) | copy-start | bytes 12292

commit v13 on v12

--- a/solution.py
+++ b/solution.py
@@ -57,10 +57,14 @@
     return lax.axis_index(axis) % 2 == 0
 
 
-def rows_kernel(state_ref, own_ref, far_ref, near_ref, scr):
+def rows_kernel(state_ref, own_ref, far_ref, near_ref, raw, scr, sems):
     frames, chans, rows, _ = state_ref.shape
+    copies = [pltpu.make_async_copy(state_ref.at[f], raw.at[f], sems.at[f]) for f in range(frames)]
+    for c in copies:
+        c.start()
     for f in range(frames):
-        scr[f] = state_ref[f].astype(F32).reshape(chans * rows, LANES)
+        copies[f].wait()
+        scr[f] = raw[f].astype(F32).reshape(chans * rows, LANES)
         for y in range(rows):
             v = scr[f, pl.ds(y, chans, stride=rows), :].astype(BF)
             own_ref[f, :, tile(y)] = v
@@ -77,10 +81,14 @@
         rows_kernel,
         "rows",
         (shape_of((frames, chans, rows * LANES), BF), slab, slab),
-        [VMEM],
-        [pltpu.VMEM((frames, chans * rows, LANES), F32)],
+        [ANYWHERE],
+        [
+            pltpu.VMEM(state.shape, BF),
+            pltpu.VMEM((frames, chans * rows, LANES), F32),
+            pltpu.SemaphoreType.DMA((frames,)),
+        ],
         cost=4_000_000_000,
-    )(state)
+    )(pltpu.with_memory_space_constraint(state, pltpu.HBM))
 
 
 def weights_kernel(

time: 21 us -> 21 us (level)
  local copies, waits for them, and re-layouts: 0.97 us -> 0.04 us
  Pallas kernels: 12.2 us -> 13.1 us
    unnamed x24 -> x22, local copies, waits for them, and re-layouts: 0.97 us -> 0.04 us
    pallas_call x1, Pallas kernels: 0.12 us -> 1.03 us  [make_rows(): call(rows_kernel, 'rows', (shape_of((frames, chans, rows * LANES), BF), s...]
where the time goes in v13:
time: 21 us; the launch traced here: 20.6 us
  Pallas kernels  13.1 us (62%)
  starting transfers between devices  7.16 us (34%)
    ppermute x4, starting transfers between devices, swapped(): return lax.ppermute(value, ('tm', 'space'), pairs)  4.95 us
    pallas_call x1, Pallas kernels, make_main(): call(main_kernel, 'main', (shape_of((2 * DEPTH, rows2, wide), BF),), [VME...  3.95 us
    pallas_call x1, Pallas kernels, make_side(): call(side_kernel, 'side', (shape_of((frames + 2, 3 * hid, 2 * LANES), BF)...  2.65 us
    ppermute x3, starting transfers between devices, partner(): return lax.ppermute(value, 'tm', [(i, i ^ bits) for i in range(count)])  2.21 us
    pallas_call x1, Pallas kernels, make_update(): call(update_kernel, 'update', (shape_of(state.shape, BF), shape_of((frame...  1.95 us
    pallas_call x1, Pallas kernels, make_inner(): call(inner_kernel, 'inner', (shape_of((frames, 3 * chans, wide), BF), sha...  1.75 us
    pallas_call x1, Pallas kernels, make_rows(): call(rows_kernel, 'rows', (shape_of((frames, chans, rows * LANES), BF), s...  1.03 us
    pallas_call x1, Pallas kernels, make_weights(): call(weights_kernel, 'weights', (shape_of((2 * hid, 4 * 9 * chans), BF),...  0.88 us
  transfers between devices with their start and end apart: 7, of which 0 were waited for; matrix products, arithmetic and copies ran while one was open for 0% of the time, Pallas kernels for 41%

profile of v13, /device:TPU:0, one launch (start us, length us, event | category | flops | bytes accessed | tf_op | source)
XLA Modules:
  0.0 20.6 jit_solution(4325272308296021274)
XLA Ops:
  0.0 0.0 copy-start.5
  0.0 0.0 copy-start.6
  0.0 1.0 %rows.1 = (bf16[6,16,1024]{2,1,0:T(8,128)(2,1)S(1)}, bf16[3,16,1024]{2,1,0:T(8,128)(2,1)S(1)}, bf16[3,16,1024]{2,1,0:T(8,128)(2,1)S(1)}) custom-call(bf16[6,16,8,128]{3,2,1,0:T(8,128)(2,1)} %bitcast.17), custom_call_target="tpu_custom_call" | custom-call | flops 4000000000 | bytes 1000000 | tf_op jit(solution)/shard_map/rows/pallas_call | solution.py:80
  1.1 3.0 %collective-permute-start = (bf16[3,16,1024]{2,1,0:T(8,128)(2,1)S(1)}, bf16[3,16,1024]{2,1,0:T(8,128)(2,1)S(1)}, u32[]{:S(2)}, u32[]{:S(2)}) collective-permute-start(bf16[3,16,1024]{2,1,0:T(8,128)(2,1)S(1)} %get-tuple-element.40), channel_id=1, source_target_pairs={{0,1},{1,0},{2,3},{3,2},{4,5},{5,4},{6,7},{7,6},{8,16},{9,17},{10,... | collective-permute-start | bytes 294920 | tf_op jit(solution)/shard_map/ppermute | solution.py:524
  4.1 0.1 collective-permute-start.1
  4.2 0.0 copy-done.10
  4.2 0.0 copy-done.7
  4.2 0.0 copy-done.8
  4.2 0.0 copy-done.9
  4.2 0.1 pad_maximum_fusion
  4.3 0.0 copy-done.3
  4.3 0.0 copy-done.5
  4.3 0.9 %weights.1 = (bf16[128,576]{1,0:T(8,128)(2,1)S(1)}, bf16[128,2304]{1,0:T(8,128)(2,1)S(1)}, bf16[96,4608]{1,0:T(8,128)(2,1)S(1)}, bf16[384,192]{1,0:T(8,128)(2,1)...) custom-call(bf16[432,64]{1,0:T(8,128)(2,1)S(1)} %bitcast.25, ...), custom_call_target="tpu_custom_call" | custom-call | flops 1000000000 | bytes 1000000 | tf_op jit(solution)/shard_map/weights/pallas_call | solution.py:142
  5.2 1.7 %inner.1 = (bf16[6,48,1280]{2,1,0:T(8,128)(2,1)S(1)}, bf16[4,192,1280]{2,1,0:T(8,128)(2,1)S(1)}, bf16[2,192,1280]{2,1,0:T(8,128)(2,1)S(1)}, bf16[6,16,128]{2,1,0:T(8,128)(2,1)S(1)}, bf16[6,16,128]{2,1,0:T(8,128)(2,1)S(1)}) custom-call(bf16[6,16,1024]{2,1,0:T(8,128)(2,1)S(1)} %get-tuple-element.32.own_ref, bf16[128,576]{1,0:T(8,128)(2,1)S(1)} %get-tuple-element.33.m1_ref, ...), custom_call_target="tpu_custom_call" | custom-call | flops 1500000000 | bytes 1000000 | tf_op jit(solution)/shard_map/inner/pallas_call | solution.py:285
  7.0 0.0 collective-permute-done.far_ref
  7.0 0.0 collective-permute-done.1.near_ref
  7.0 0.2 edges.1
  7.2 1.8 %collective-permute-start.2 = (bf16[12,16,128]{2,1,0:T(8,128)(2,1)S(1)}, bf16[12,16,128]{2,1,0:T(8,128)(2,1)S(1)}, u32[]{:S(2)}, u32[]{:S(2)}) collective-permute-start(bf16[12,16,128]{2,1,0:T(8,128)(2,1)S(1)} %get-tuple-element.46), channel_id=1, source_target_pairs={{0,1},{1,0},{2,3},{3,2},{4,5},{5,4},{6,7},{7,6},{8,9},{9,8},{10,11... | collective-permute-start | bytes 147464 | tf_op jit(solution)/shard_map/ppermute | solution.py:524
  9.0 0.0 collective-permute-start.3
  9.0 4.0 %main.1.far3 = bf16[6,192,1280]{2,1,0:T(8,128)(2,1)S(1)} custom-call(bf16[6,48,1280]{2,1,0:T(8,128)(2,1)S(1)} %get-tuple-element.38.own1, bf16[4,192,1280]{2,1,0:T(8,128)(2,1)S(1)} %get-tuple-element.39.own2, bf16[3,16,1024]{2,1,0:T(8,128)(2,1)S(1)} %collective-permute-done.far_ref, bf16[3,16,1024]{2,1,0:T(8,128)(2,1)S(1)} %collective-permute-done.1.near_ref, ...), custom_call_target="tpu_custom_call" | custom-call | flops 5000000000 | bytes 1000000 | tf_op jit(solution)/shard_map/main/pallas_call | solution.py:317
  13.0 0.0 copy-start.4
  13.0 0.0 collective-permute-done.2.first_ref
  13.0 0.0 collective-permute-done.3.second_ref
  13.0 2.7 %side.1 = (bf16[8,192,256]{2,1,0:T(8,128)(2,1)S(1)}, f32[2,8,128]{2,1,0:T(8,128)S(1)}) custom-call(bf16[2,192,1280]{2,1,0:T(8,128)(2,1)S(1)} %get-tuple-element.37.own3, bf16[6,192,1280]{2,1,0:T(8,128)(2,1)S(1)} %main.1.far3, bf16[12,16,128]{2,1,0:T(8,128)(2,1)S(1)} %get-tuple-element.44.west_ref, bf16[12,16,128]{2,1,0:T(8,128)(2,1)S(1)} %get-tuple-element.45.east_ref, ...), custom_call_target="tpu_custom_call" | custom-call | tf_op jit(solution)/shard_map/side/pallas_call | solution.py:421
  15.7 1.0 %collective-permute-start.6 = (f32[2,8,128]{2,1,0:T(8,128)S(1)}, f32[2,8,128]{2,1,0:T(8,128)S(1)}, u32[]{:S(2)}, u32[]{:S(2)}) collective-permute-start(f32[2,8,128]{2,1,0:T(8,128)S(1)} %get-tuple-element.53.refs_3_), channel_id=1, source_target_pairs={{0,16},{8,24},{16,0},{24,8},{1,17},{9,25},{17,1},{25,9},{2,18},{10... | collective-permute-start | bytes 24584 | tf_op jit(solution)/shard_map/ppermute | solution.py:531
  16.6 0.9 %collective-permute-start.5 = (f32[2,8,128]{2,1,0:T(8,128)S(1)}, f32[2,8,128]{2,1,0:T(8,128)S(1)}, u32[]{:S(2)}, u32[]{:S(2)}) collective-permute-start(f32[2,8,128]{2,1,0:T(8,128)S(1)} %get-tuple-element.53.refs_3_), channel_id=1, source_target_pairs={{0,24},{8,16},{16,8},{24,0},{1,25},{9,17},{17,9},{25,1},{2,26},{10... | collective-permute-start | bytes 24584 | tf_op jit(solution)/shard_map/ppermute | solution.py:531
  17.6 0.3 %collective-permute-start.4 = (f32[2,8,128]{2,1,0:T(8,128)S(1)}, f32[2,8,128]{2,1,0:T(8,128)S(1)}, u32[]{:S(2)}, u32[]{:S(2)}) collective-permute-start(f32[2,8,128]{2,1,0:T(8,128)S(1)} %get-tuple-element.53.refs_3_), channel_id=1, source_target_pairs={{0,8},{8,0},{16,24},{24,16},{1,9},{9,1},{17,25},{25,17},{2,10},{10... | collective-permute-start | bytes 24584 | tf_op jit(solution)/shard_map/ppermute | solution.py:531
  17.9 1.9 %update.1 = (bf16[6,16,8,128]{3,2,1,0:T(8,128)(2,1)S(1)}, f32[6,8,128]{2,1,0:T(8,128)S(1)}) custom-call(bf16[2,192,1280]{2,1,0:T(8,128)(2,1)S(1)} %get-tuple-element.37.own3, bf16[6,192,1280]{2,1,0:T(8,128)(2,1)S(1)} %main.1.far3, bf16[8,192,256]{2,1,0:T(8,128)(2,1)S(1)} %get-tuple-element.54.t3, bf16[96,4608]{1,0:T(8,128)(2,1)S(1)} %get-tuple-element.55.m3_ref, ...), custom_call_target="tpu_custom_call" | custom-call | flops 3000000000 | bytes 1000000 | tf_op jit(solution)/shard_map/update/pallas_call | solution.py:467
  19.8 0.0 collective-permute-done.6.refs_2_
  19.8 0.0 collective-permute-done.5.refs_1_
  19.9 0.0 collective-permute-done.4.refs_0_
  19.9 0.7 %correct.1 = bf16[6,16,8,128]{3,2,1,0:T(8,128)(2,1)} custom-call(f32[2,8,128]{2,1,0:T(8,128)S(1)} %collective-permute-done.4.refs_0_, f32[2,8,128]{2,1,0:T(8,128)S(1)} %collective-permute-done.5.refs_1_, f32[2,8,128]{2,1,0:T(8,128)S(1)} %collective-permute-done.6.refs_2_, f32[2,8,128]{2,1,0:T(8,128)S(1)} %get-tuple-element.53.refs_3_, ...), custom_call_target="tpu_custom_call" | custom-call | tf_op jit(solution)/shard_map/correct/pallas_call | solution.py:502
  (14 shorter events, 0.0 us)
Async XLA Ops:
  0.0 4.2 %copy-start.10 = (s32[6]{0:T(128)S(1)}, s32[6]{0:T(128)}, u32[]{:S(2)}) copy-start(s32[6]{0:T(128)} %param.19) | copy-start | bytes 76
  0.0 4.2 %copy-start.7 = (f32[16]{0:T(128)S(1)}, f32[16]{0:T(128)}, u32[]{:S(2)}) copy-start(f32[16]{0:T(128)} %param.18) | copy-start | bytes 196
  0.0 4.2 %copy-start.8 = (f32[64]{0:T(128)S(1)}, f32[64]{0:T(128)}, u32[]{:S(2)}) copy-start(f32[64]{0:T(128)} %param.16) | copy-start | bytes 772
  0.0 4.2 %copy-start.9 = (f32[64]{0:T(128)S(1)}, f32[64]{0:T(128)}, u32[]{:S(2)}) copy-start(f32[64]{0:T(128)} %param.14) | copy-start | bytes 772
  0.0 4.3 %copy-start.3 = (bf16[64,64,3,3,3]{1,0,4,3,2:T(8,128)(2,1)S(1)}, bf16[64,64,3,3,3]{1,0,4,3,2:T(8,128)(2,1)}, u32[]{:S(2)}) copy-start(bf16[64,64,3,3,3]{1,0,4,3,2:T(8,128)(2,1)} %param.15) | copy-start | bytes 663556
  0.0 4.3 %copy-start.5 = (bf16[64,16,3,3,3]{0,1,4,3,2:T(8,128)(2,1)S(1)}, bf16[64,16,3,3,3]{0,1,4,3,2:T(8,128)(2,1)}, u32[]{:S(2)}) copy-start(bf16[64,16,3,3,3]{0,1,4,3,2:T(8,128)(2,1)} %param.13) | copy-start | bytes 165892
  0.0 4.3 %copy-start.6 = (bf16[16,64,3,3,3]{1,0,4,3,2:T(8,128)(2,1)S(1)}, bf16[16,64,3,3,3]{1,0,4,3,2:T(8,128)(2,1)}, u32[]{:S(2)}) copy-start(bf16[16,64,3,3,3]{1,0,4,3,2:T(8,128)(2,1)} %param.17) | copy-start | bytes 165892
  1.1 5.9 %collective-permute-start = (bf16[3,16,1024]{2,1,0:T(8,128)(2,1)S(1)}, bf16[3,16,1024]{2,1,0:T(8,128)(2,1)S(1)}, u32[]{:S(2)}, u32[]{:S(2)}) collective-permute-start(bf16[3,16,1024]{2,1,0:T(8,128)(2,1)S(1)} %get-tuple-element.40), channel_id=1, source_target_pairs={{0,1},{1,0},{2,3},{3,2},{4,5},{5,4},{6,7},{7,6},{8,16},{9,17},{10,... | collective-permute-start | bytes 294920 | tf_op jit(solution)/shard_map/ppermute | solution.py:524
  4.1 2.9 %collective-permute-start.1 = (bf16[3,16,1024]{2,1,0:T(8,128)(2,1)S(1)}, bf16[3,16,1024]{2,1,0:T(8,128)(2,1)S(1)}, u32[]{:S(2)}, u32[]{:S(2)}) collective-permute-start(bf16[3,16,1024]{2,1,0:T(8,128)(2,1)S(1)} %get-tuple-element.41), channel_id=1, source_target_pairs={{0,8},{1,9},{2,10},{3,11},{4,12},{5,13},{6,14},{7,15},{8,0},{9,1},... | collective-permute-start | bytes 294920 | tf_op jit(solution)/shard_map/ppermute | solution.py:524
  7.2 5.8 %collective-permute-start.2 = (bf16[12,16,128]{2,1,0:T(8,128)(2,1)S(1)}, bf16[12,16,128]{2,1,0:T(8,128)(2,1)S(1)}, u32[]{:S(2)}, u32[]{:S(2)}) collective-permute-start(bf16[12,16,128]{2,1,0:T(8,128)(2,1)S(1)} %get-tuple-element.46), channel_id=1, source_target_pairs={{0,1},{1,0},{2,3},{3,2},{4,5},{5,4},{6,7},{7,6},{8,9},{9,8},{10,11... | collective-permute-start | bytes 147464 | tf_op jit(solution)/shard_map/ppermute | solution.py:524
  9.0 4.0 %collective-permute-start.3 = (bf16[12,16,128]{2,1,0:T(8,128)(2,1)S(1)}, bf16[12,16,128]{2,1,0:T(8,128)(2,1)S(1)}, u32[]{:S(2)}, u32[]{:S(2)}) collective-permute-start(bf16[12,16,128]{2,1,0:T(8,128)(2,1)S(1)} %get-tuple-element.47), channel_id=1, source_target_pairs={{0,8},{1,2},{2,1},{3,4},{4,3},{5,6},{6,5},{7,15},{8,0},{9,10},{10,... | collective-permute-start | bytes 147464 | tf_op jit(solution)/shard_map/ppermute | solution.py:524
  9.0 4.0 %copy-start = (bf16[6,16,1,8,128]{4,3,2,1,0:T(8,128)(2,1)S(1)}, bf16[6,16,1,8,128]{4,3,2,1,0:T(8,128)(2,1)}, u32[]{:S(2)}) copy-start(bf16[6,16,1,8,128]{4,3,2,1,0:T(8,128)(2,1)} %param.11) | copy-start | bytes 589828
  13.0 4.9 %copy-start.4 = (bf16[6,16,1,8,128]{4,3,2,1,0:T(8,128)(2,1)S(1)}, bf16[6,16,1,8,128]{4,3,2,1,0:T(8,128)(2,1)}, u32[]{:S(2)}) copy-start(bf16[6,16,1,8,128]{4,3,2,1,0:T(8,128)(2,1)} %param.12) | copy-start | bytes 589828
  15.7 4.2 %collective-permute-start.6 = (f32[2,8,128]{2,1,0:T(8,128)S(1)}, f32[2,8,128]{2,1,0:T(8,128)S(1)}, u32[]{:S(2)}, u32[]{:S(2)}) collective-permute-start(f32[2,8,128]{2,1,0:T(8,128)S(1)} %get-tuple-element.53.refs_3_), channel_id=1, source_target_pairs={{0,16},{8,24},{16,0},{24,8},{1,17},{9,25},{17,1},{25,9},{2,18},{10... | collective-permute-start | bytes 24584 | tf_op jit(solution)/shard_map/ppermute | solution.py:531
  16.6 3.2 %collective-permute-start.5 = (f32[2,8,128]{2,1,0:T(8,128)S(1)}, f32[2,8,128]{2,1,0:T(8,128)S(1)}, u32[]{:S(2)}, u32[]{:S(2)}) collective-permute-start(f32[2,8,128]{2,1,0:T(8,128)S(1)} %get-tuple-element.53.refs_3_), channel_id=1, source_target_pairs={{0,24},{8,16},{16,8},{24,0},{1,25},{9,17},{17,9},{25,1},{2,26},{10... | collective-permute-start | bytes 24584 | tf_op jit(solution)/shard_map/ppermute | solution.py:531
  17.6 2.3 %collective-permute-start.4 = (f32[2,8,128]{2,1,0:T(8,128)S(1)}, f32[2,8,128]{2,1,0:T(8,128)S(1)}, u32[]{:S(2)}, u32[]{:S(2)}) collective-permute-start(f32[2,8,128]{2,1,0:T(8,128)S(1)} %get-tuple-element.53.refs_3_), channel_id=1, source_target_pairs={{0,8},{8,0},{16,24},{24,16},{1,9},{9,1},{17,25},{25,17},{2,10},{10... | collective-permute-start | bytes 24584 | tf_op jit(solution)/shard_map/ppermute | solution.py:531
  17.9 2.0 %copy-start.1 = (f32[2,1,8,128]{3,2,1,0:T(8,128)S(1)}, f32[2,1,8,128]{3,2,1,0:T(8,128)}, u32[]{:S(2)}) copy-start(f32[2,1,8,128]{3,2,1,0:T(8,128)} %param.20) | copy-start | bytes 24580
  17.9 2.0 %copy-start.2 = (s32[1,8,128]{2,1,0:T(8,128)S(1)}, s32[1,8,128]{2,1,0:T(8,128)}, u32[]{:S(2)}) copy-start(s32[1,8,128]{2,1,0:T(8,128)} %param.21) | copy-start | bytes 12292
